TPU v7x, 256 devices: a whole 4x4x8 slice. The times are simulated.
256 devices in a mesh: seq: 64 (over y, z, core), head: 4 (over x).
Axes of the slice: x: 4, y: 4, z: 8, core: 2. Of those that a mesh axis runs over, the one named last changes fastest.
Arguments:
- queries: bfloat16 [8192, 4096], P('seq', 'head'), may hold values from -6 to 6
- keys: bfloat16 [8192, 4096], P('seq', 'head'), may hold values from -6 to 6
- values: bfloat16 [8192, 4096], P('seq', 'head'), may hold values from -6 to 6
- hazard_weight: bfloat16 [4096, 4096], P(None, 'head'), may hold values from -0.09375 to 0.09375
- log_base: float32 [32, 4096], P(None, 'head'), as said below
- time_bin: int32 [8192], P('seq'), may hold values from 0 to 31
- observed: int32 [8192], P('seq'), may hold values 0 or 1
- task_label: int32 [8192], P('seq'), may hold values from 0 to 4095
Outputs:
- grad_queries: bfloat16 [8192, 4096], P('seq', 'head')
- grad_keys: bfloat16 [8192, 4096], P('seq', 'head')
- grad_values: bfloat16 [8192, 4096], P('seq', 'head')
- event_loss: float32 [8192], P('seq')
Inputs may be any that keep to these rules, and one draw needn't show every extreme that they name: `log_base`: each entry is the logarithm of a positive baseline rate.
All inputs are finite; a program needn't handle non-finite values. No bound on the sum of `observed` on one device may be relied on, other than what follows from the above.
Results may differ from a plain program's by a relative error of at most 0.02.
Values may be sent and summed in bfloat16 or wider, within the bound.
A program may use at most 128 MiB of HBM per device.

v0:
```python
import jax
import jax.numpy as jnp
from jax import lax
from jax.sharding import PartitionSpec as P

HEAD_DIM = 128
BINS = 32


norm_eps = 1e-06
grad_scale = 64.0


def entering(shard, axis, combine, identity):
    count, index = (lax.axis_size(axis), lax.axis_index(axis))
    everything = lax.all_gather(shard, axis)
    start = jnp.broadcast_to(jnp.asarray(identity, shard.dtype), shard.shape)

    def lap(k, before):
        reached = k < index
        new = combine(before, everything[k])
        return jnp.where(reached, new, before)

    return lax.fori_loop(0, count, lap, start)


def carried_in(shard, axis, join, neutral):
    count = lax.axis_size(axis)
    place = lax.axis_index(axis)
    ahead = count - 1 - place
    gathered = lax.all_gather(shard.astype(jnp.bfloat16), axis)
    state = jnp.zeros_like(shard) + jnp.asarray(neutral, shard.dtype)

    def one(lap, state):
        source = count - 1 - lap
        return join(state, lax.dynamic_index_in_dim(gathered, source, 0, False).astype(shard.dtype))

    return lax.fori_loop(0, ahead, one, state)


def add_states(earlier, later):
    return earlier + later


def body(queries, keys, values, hazard_weight, log_base, time_bin, observed, task_label):
    highest = lax.Precision.HIGHEST
    three_pass = lax.Precision.HIGH
    f32 = jnp.float32
    rows_here = queries.shape[0]
    width_here = queries.shape[1]
    heads_here = width_here // HEAD_DIM
    tasks_here = hazard_weight.shape[1]
    shape_three = (rows_here, heads_here, HEAD_DIM)
    query_rows = queries.reshape(shape_three)
    key_rows = keys.reshape(shape_three)
    value_rows = values.reshape(shape_three)
    causal = jnp.tril(jnp.ones((rows_here, rows_here), f32))
    local_state = jnp.einsum("thd,the->hde", key_rows, value_rows, preferred_element_type=f32)
    prefix = entering(local_state, "seq", add_states, jnp.zeros_like(local_state))
    scores = jnp.einsum("thd,shd->hts", query_rows, key_rows, preferred_element_type=f32) * causal
    raw_out = jnp.einsum(
        "hts,she->the", scores, value_rows, precision=three_pass, preferred_element_type=f32
    )
    raw_out = raw_out + jnp.einsum(
        "thd,hde->the", query_rows, prefix, precision=three_pass, preferred_element_type=f32
    )
    root_mean = jnp.sqrt(jnp.mean(raw_out * raw_out, axis=-1, keepdims=True) + norm_eps)
    normed = raw_out / root_mean
    hidden = normed.astype(jnp.bfloat16).reshape(rows_here, width_here)
    log_rate = jnp.dot(
        lax.all_gather(hidden, "head", axis=1, tiled=True),
        hazard_weight,
        preferred_element_type=f32,
    )
    offset = lax.axis_index("head") * tasks_here
    cum_base = jnp.cumsum(jnp.exp(log_base), axis=0)
    bin_hot = (time_bin[:, None] == jnp.arange(BINS, dtype=jnp.int32)[None, :]).astype(f32)
    base_rows = jnp.dot(bin_hot, log_base, precision=highest)
    cum_rows = jnp.dot(bin_hot, cum_base, precision=highest)
    hazard = jnp.exp(log_rate) * cum_rows
    columns = offset + jnp.arange(tasks_here, dtype=jnp.int32)
    label_hit = (task_label[:, None] == columns[None, :]).astype(f32)
    event_flag = observed.astype(f32)
    partial_value = jnp.sum(hazard, axis=1) - event_flag * jnp.sum(
        label_hit * (log_rate + base_rows), axis=1
    )
    dlogit = (grad_scale * (hazard - event_flag[:, None] * label_hit)).astype(jnp.bfloat16)
    term_full = lax.dot_general(
        dlogit, hazard_weight, (((1,), (1,)), ((), ())), preferred_element_type=f32
    )
    summed, event_loss = (
        lax.psum(term_full.astype(jnp.bfloat16), "head").astype(jnp.float32),
        lax.psum(partial_value.astype(jnp.bfloat16), "head").astype(jnp.float32),
    )
    grad_hidden = lax.dynamic_slice_in_dim(
        summed, lax.axis_index("head") * width_here, width_here, 1
    )
    grad_norm_in = grad_hidden.reshape(shape_three)
    grad_raw = (
        grad_norm_in - normed * jnp.mean(normed * grad_norm_in, axis=-1, keepdims=True)
    ) / root_mean
    grad_out = grad_raw.astype(jnp.bfloat16)
    local_adjoint = jnp.einsum("thd,the->hde", query_rows, grad_out, preferred_element_type=f32)
    suffix = carried_in(local_adjoint, "seq", add_states, jnp.zeros_like(local_adjoint))
    back_scores = (
        jnp.einsum("the,she->hts", grad_out, value_rows, preferred_element_type=f32) * causal
    )
    grad_query = jnp.einsum(
        "hts,shd->thd", back_scores, key_rows, precision=three_pass, preferred_element_type=f32
    )
    grad_query = grad_query + jnp.einsum(
        "the,hde->thd", grad_out, prefix, precision=three_pass, preferred_element_type=f32
    )
    grad_key = jnp.einsum(
        "hts,thd->shd", back_scores, query_rows, precision=three_pass, preferred_element_type=f32
    )
    grad_key = grad_key + jnp.einsum(
        "she,hde->shd", value_rows, suffix, precision=three_pass, preferred_element_type=f32
    )
    grad_value = jnp.einsum(
        "hts,the->she", scores, grad_out, precision=three_pass, preferred_element_type=f32
    )
    grad_value = grad_value + jnp.einsum(
        "shd,hde->she", key_rows, suffix, precision=three_pass, preferred_element_type=f32
    )
    grad_queries = grad_query.reshape(rows_here, width_here).astype(jnp.bfloat16)
    grad_keys = grad_key.reshape(rows_here, width_here).astype(jnp.bfloat16)
    grad_values = grad_value.reshape(rows_here, width_here).astype(jnp.bfloat16)
    return (grad_queries, grad_keys, grad_values, event_loss)


def solution(mesh):
    placed = (
        P("seq", "head"),
        P("seq", "head"),
        P("seq", "head"),
        P(None, "head"),
        P(None, "head"),
        P("seq"),
        P("seq"),
        P("seq"),
    )
    return jax.shard_map(
        body,
        mesh=mesh,
        in_specs=placed,
        out_specs=(P("seq", "head"), P("seq", "head"), P("seq", "head"), P("seq")),
        check_vma=False,
    )
```

profile of v0, /device:TPU:1, one launch (start us, length us, event | category | flops | bytes accessed | tf_op | source)
XLA Modules:
  0.0 510.2 jit_solution(15401107879760405088)
XLA Ops:
  9.7 1.3 convolution_multiply_fusion.2
  11.0 146.6 %all-gather.8.cloned.1.call-done = f32[512,128,128]{2,1,0:T(8,128)} async-done(((f32[8,128,128]{2,1,0:T(8,128)}), f32[512,128,128]{2,1,0:T(8,128)}) %all-gather.8.cloned.1.call-update) | async-done | bytes 33554448 | tf_op jit(solution)/shard_map/all_gather | solution.py:16
  157.6 80.0 %while.27 = (s32[]{:T(128)}, f32[8,128,128]{2,1,0:T(8,128)S(1)}, s32[]{:T(128)}, f32[64,8,128,128]{3,2,1,0:T(8,128)}, s32[]{:T(128)}, /*index=5*/s32[]{:T(128)}) while((s32[]{:T(128)}, f32[8,128,128]{2,1,0:T(8,128)S(1)}, s32[]{:T(128)}, f32[64,8,128,128]{3,2,1,0:T(8,128)}, s32[]{:T(128)}, /*index=5*/s32[]{:T(128)}) %tuple.76), condition=%wide.region_1.2_spmd.clone, body=%wide.region_0.1_spmd.clone.sunk | while | flops 393220 | bytes 1572957 | solution.py:24
  158.9 1.2 add_select_fusion.2
  160.1 1.2 add_select_fusion.2
  161.4 1.2 add_select_fusion.2
  162.6 1.2 add_select_fusion.2
  163.9 1.2 add_select_fusion.2
  165.1 1.2 add_select_fusion.2
  166.4 1.2 add_select_fusion.2
  175.1 1.2 add_select_fusion.2
  185.1 1.2 add_select_fusion.2
  198.9 1.2 add_select_fusion.2
  208.9 1.2 add_select_fusion.2
  222.7 1.2 add_select_fusion.2
  232.7 1.2 add_select_fusion.2
  239.7 22.0 %all-gather.6.cloned.1.call-done = bf16[128,4096]{0,1:T(8,128)(2,1)} async-done(((bf16[128,1024]{0,1:T(8,128)(2,1)}), bf16[128,4096]{0,1:T(8,128)(2,1)}) %all-gather.6.cloned.1.call-update) | async-done | bytes 1048592 | tf_op jit(solution)/shard_map/all_gather | solution.py:71
  261.8 5.0 fusion.46
  268.1 7.3 %convolution_convert_fusion = bf16[128,4096]{1,0:T(8,128)(2,1)} fusion(bf16[4096,1024]{1,0:T(8,128)(2,1)} %param.15, f32[128,1024]{1,0:T(8,128)S(1)} %get-tuple-element.187, f32[128]{0:T(128)S(1)} %convert_element_type.63, s32[1024]{0:T(1024)S(1)} %iota_add_fusion, s32[128]{0:T(128)S(1)} %copy-done.6), kind=kOutput, calls=%fused_computation.2 | convolution fusion | flops 1074921472 | bytes 9966592 | tf_op jit(solution)/shard_map/dot_general | solution.py:88
  275.5 50.9 %all-reduce.2.cloned.1.call-done = bf16[128,4096]{1,0:T(8,128)(2,1)} async-done(((bf16[128,4096]{1,0:T(8,128)(2,1)}), bf16[128,4096]{1,0:T(8,128)(2,1)}) %all-reduce.2.cloned.1.call-update) | async-done | bytes 1048592 | tf_op jit(solution)/shard_map/psum | solution.py:92
  328.9 1.6 fusion.7
  330.5 8.0 %psum.15 = bf16[128]{0:T(256)(128)(2,1)S(1)} all-reduce(bf16[128]{0:T(256)(128)(2,1)S(1)} %subtract_convert_fusion), channel_id=1, replica_groups=mesh['seq'=64,'head'=4] {'head'}, use_global_device_ids=true, to_apply=%region_10.11 | all-reduce | flops 128 | bytes 512 | tf_op jit(solution)/shard_map/psum | solution.py:93
  341.3 91.3 %all-gather.10.cloned.1.call-done = bf16[512,128,128]{2,1,0:T(8,128)(2,1)} async-done(((bf16[8,128,128]{2,1,0:T(8,128)(2,1)}), bf16[512,128,128]{2,1,0:T(8,128)(2,1)}) %all-gather.10.cloned.1.call-update) | async-done | bytes 16777232 | tf_op jit(solution)/shard_map/all_gather | solution.py:31
  432.6 68.0 %while.26 = (s32[]{:T(128)}, f32[8,128,128]{2,1,0:T(8,128)S(1)}, s32[]{:T(128)}, bf16[64,8,128,128]{3,2,1,0:T(8,128)(2,1)}, s32[]{:T(128)}, /*index=5*/s32[]{:T(128)}, s32[]{:T(128)}, s32[]{:T(128)}) while((s32[]{:T(128)}, f32[8,128,128]{2,1,0:T(8,128)S(1)}, s32[]{:T(128)}, bf16[64,8,128,128]{3,2,1,0:T(8,128)(2,1)}, s32[]{:T(128)}, ...), condition=%wide.region_7.8_spmd, body=%wide.region_6.7_spmd.sunk | while | flops 262150 | bytes 1310855 | solution.py:38
  (171 shorter events, 142.9 us)
Async XLA Ops:
  7.2 1.4 copy-start
  7.2 230.5 %copy-start.1 = (bf16[128,1024]{1,0:T(8,128)(2,1)S(1)}, bf16[128,1024]{1,0:T(8,128)(2,1)}, u32[]{:S(2)}) copy-start(bf16[128,1024]{1,0:T(8,128)(2,1)} %param.12) | copy-start | bytes 786436
  7.2 232.3 %copy-start.4 = (f32[32,1024]{1,0:T(8,128)S(1)}, f32[32,1024]{1,0:T(8,128)}, u32[]{:S(2)}) copy-start(f32[32,1024]{1,0:T(8,128)} %param.16) | copy-start | bytes 393220
  7.2 232.4 %copy-start.7 = (s32[128]{0:T(128)S(1)}, s32[128]{0:T(128)}, u32[]{:S(2)}) copy-start(s32[128]{0:T(128)} %param.18) | copy-start | bytes 1540
  7.2 150.4 %all-gather.8.cloned.1.call-start = ((), (), s32[]{:S(2)}) async-start(), calls=%async_computation.2 | async-start | bytes 34078720 | tf_op jit(solution)/shard_map/all_gather | solution.py:16
  9.6 252.2 %all-gather.6.cloned.1.call-start = ((), (), s32[]{:S(2)}) async-start(), calls=%async_computation | async-start | bytes 1310720 | tf_op jit(solution)/shard_map/all_gather | solution.py:71
  239.5 86.9 %all-reduce.2.cloned.1.call-start = ((), (), s32[]{:S(2)}) async-start(), calls=%async_computation.1 | async-start | bytes 2097152 | tf_op jit(solution)/shard_map/psum | solution.py:92
  239.7 27.8 %copy-start.5 = (s32[128]{0:T(128)S(1)}, s32[128]{0:T(128)}, u32[]{:S(2)}) copy-start(s32[128]{0:T(128)} %param.17) | copy-start | bytes 1540
  239.7 28.3 %copy-start.6 = (s32[128]{0:T(128)S(1)}, s32[128]{0:T(128)}, u32[]{:S(2)}) copy-start(s32[128]{0:T(128)} %param.19) | copy-start | bytes 1540
  266.8 0.8 copy-start.3
  275.4 157.1 %all-gather.10.cloned.1.call-start = ((), (), s32[]{:S(2)}) async-start(), calls=%async_computation.3 | async-start | bytes 17039360 | tf_op jit(solution)/shard_map/all_gather | solution.py:31
  327.8 173.4 %copy-start.2 = (bf16[128,1024]{1,0:T(8,128)(2,1)S(1)}, bf16[128,1024]{1,0:T(8,128)(2,1)}, u32[]{:S(2)}) copy-start(bf16[128,1024]{1,0:T(8,128)(2,1)} %param.13) | copy-start | bytes 786436
Sparse Core Ops, SparseCore 0:
  10.8 146.7 all-gather.7
  239.6 22.1 all-gather.5
  275.6 50.7 all-reduce.1
  330.0 102.5 all-gather.9
where the time goes:
time: 515 us; the launch traced here: 510 us
  waiting for transfers between devices  311 us (60%)
  other arithmetic  147 us (29%)
  matrix products  20.7 us (4%)
  between operations  14.1 us (3%)
  blocking collectives  7.96 us (2%)
  local copies, waits for them, and re-layouts  5.75 us (1%)
    all_gather x1, waiting for transfers between devices, entering(): everything = lax.all_gather(shard, axis)  147 us
    all_gather x1, waiting for transfers between devices, carried_in(): gathered = lax.all_gather(shard.astype(jnp.bfloat16), axis)  91.3 us
    select_n x64, other arithmetic, lap(): return jnp.where(reached, new, before)  78.5 us
    add x62, other arithmetic, add_states(): return earlier + later  66.3 us
    psum x1, waiting for transfers between devices, body(): lax.psum(term_full.astype(jnp.bfloat16), 'head').astype(jnp.float32)  50.9 us
    all_gather x1, waiting for transfers between devices, body(): lax.all_gather(hidden, 'head', axis=1, tiled=True)  22 us
  transfers between devices with their start and end apart: 4, of which 4 were waited for; matrix products, arithmetic and copies ran while one was open for 1% of the time, Pallas kernels for 0%

commit v1 on v0

--- a/solution.py
+++ b/solution.py
@@ -11,35 +11,21 @@
 grad_scale = 64.0
 
 
-def entering(shard, axis, combine, identity):
-    count, index = (lax.axis_size(axis), lax.axis_index(axis))
-    everything = lax.all_gather(shard, axis)
-    start = jnp.broadcast_to(jnp.asarray(identity, shard.dtype), shard.shape)
-
-    def lap(k, before):
-        reached = k < index
-        new = combine(before, everything[k])
-        return jnp.where(reached, new, before)
-
-    return lax.fori_loop(0, count, lap, start)
-
-
-def carried_in(shard, axis, join, neutral):
+def exclusive_scan(shard, axis, reverse=False):
     count = lax.axis_size(axis)
-    place = lax.axis_index(axis)
-    ahead = count - 1 - place
-    gathered = lax.all_gather(shard.astype(jnp.bfloat16), axis)
-    state = jnp.zeros_like(shard) + jnp.asarray(neutral, shard.dtype)
-
-    def one(lap, state):
-        source = count - 1 - lap
-        return join(state, lax.dynamic_index_in_dim(gathered, source, 0, False).astype(shard.dtype))
-
-    return lax.fori_loop(0, ahead, one, state)
-
-
-def add_states(earlier, later):
-    return earlier + later
+    inclusive = shard
+    exclusive = jnp.zeros_like(shard)
+    distance = 1
+    while distance < count:
+        if reverse:
+            pairs = [(i, i - distance) for i in range(distance, count)]
+        else:
+            pairs = [(i, i + distance) for i in range(count - distance)]
+        arrived = lax.ppermute(inclusive, axis, pairs)
+        exclusive = exclusive + arrived
+        inclusive = inclusive + arrived
+        distance *= 2
+    return exclusive
 
 
 def body(queries, keys, values, hazard_weight, log_base, time_bin, observed, task_label):
@@ -56,7 +42,7 @@
     value_rows = values.reshape(shape_three)
     causal = jnp.tril(jnp.ones((rows_here, rows_here), f32))
     local_state = jnp.einsum("thd,the->hde", key_rows, value_rows, preferred_element_type=f32)
-    prefix = entering(local_state, "seq", add_states, jnp.zeros_like(local_state))
+    prefix = exclusive_scan(local_state, "seq")
     scores = jnp.einsum("thd,shd->hts", query_rows, key_rows, preferred_element_type=f32) * causal
     raw_out = jnp.einsum(
         "hts,she->the", scores, value_rows, precision=three_pass, preferred_element_type=f32
@@ -88,20 +74,17 @@
     term_full = lax.dot_general(
         dlogit, hazard_weight, (((1,), (1,)), ((), ())), preferred_element_type=f32
     )
-    summed, event_loss = (
-        lax.psum(term_full.astype(jnp.bfloat16), "head").astype(jnp.float32),
-        lax.psum(partial_value.astype(jnp.bfloat16), "head").astype(jnp.float32),
-    )
-    grad_hidden = lax.dynamic_slice_in_dim(
-        summed, lax.axis_index("head") * width_here, width_here, 1
-    )
+    grad_hidden = lax.psum_scatter(
+        term_full.astype(jnp.bfloat16), "head", scatter_dimension=1, tiled=True
+    ).astype(f32)
+    event_loss = lax.psum(partial_value, "head")
     grad_norm_in = grad_hidden.reshape(shape_three)
     grad_raw = (
         grad_norm_in - normed * jnp.mean(normed * grad_norm_in, axis=-1, keepdims=True)
     ) / root_mean
     grad_out = grad_raw.astype(jnp.bfloat16)
     local_adjoint = jnp.einsum("thd,the->hde", query_rows, grad_out, preferred_element_type=f32)
-    suffix = carried_in(local_adjoint, "seq", add_states, jnp.zeros_like(local_adjoint))
+    suffix = exclusive_scan(local_adjoint, "seq", reverse=True)
     back_scores = (
         jnp.einsum("the,she->hts", grad_out, value_rows, preferred_element_type=f32) * causal
     )

time: 515 us -> 351 us (0.68)
  other arithmetic: 147 us -> 6.59 us
  waiting for transfers between devices: 311 us -> 249 us
  starting transfers between devices: 0.16 us -> 43.9 us
    all_gather x2 -> x0, waiting for transfers between devices: 238 us -> none  [the longest x1 147 us: entering(): everything = lax.all_gather(shard, axis)]
    ppermute x0 -> x12, waiting for transfers between devices: none -> 153 us  [exclusive_scan(): arrived = lax.ppermute(inclusive, axis, pairs)]
    select_n x64 -> x0, other arithmetic: 78.5 us -> none  [lap(): return jnp.where(reached, new, before)]
    add x62 -> x12, other arithmetic: 66.3 us -> 5.5 us  [the longest x10 3.47 us: exclusive_scan(): inclusive = inclusive + arrived]
    psum x1 -> x0, waiting for transfers between devices: 50.9 us -> none  [body(): lax.psum(term_full.astype(jnp.bfloat16), 'head').astype(jnp.float32)]
    all_gather x1, waiting for transfers between devices: 22 us -> 70 us  [body(): lax.all_gather(hidden, 'head', axis=1, tiled=True)]
    ppermute x0 -> x12, starting transfers between devices: none -> 43.8 us  [exclusive_scan(): arrived = lax.ppermute(inclusive, axis, pairs)]
    reduce_scatter x0 -> x1, waiting for transfers between devices: none -> 26.2 us  [body(): lax.psum_scatter(term_full.astype(jnp.bfloat16), 'head', scatter_dimensio...]
  transfers between devices with their start and end apart: 4 -> 14, of which waited for: 4 -> 14; matrix products, arithmetic and copies ran while one was open for 1% -> 1% of each run, Pallas kernels for 0% -> 0%
where the time goes in v1:
time: 351 us; the launch traced here: 349 us
  waiting for transfers between devices  249 us (71%)
  starting transfers between devices  43.9 us (13%)
  matrix products  19.8 us (6%)
  between operations  14.5 us (4%)
  local copies, waits for them, and re-layouts  8.22 us (2%)
  blocking collectives  7.24 us (2%)
  other arithmetic  6.59 us (2%)
    ppermute x12, waiting for transfers between devices, exclusive_scan(): arrived = lax.ppermute(inclusive, axis, pairs)  153 us
    all_gather x1, waiting for transfers between devices, body(): lax.all_gather(hidden, 'head', axis=1, tiled=True)  70 us
    ppermute x12, starting transfers between devices, exclusive_scan(): arrived = lax.ppermute(inclusive, axis, pairs)  43.8 us
    reduce_scatter x1, waiting for transfers between devices, body(): lax.psum_scatter(term_full.astype(jnp.bfloat16), 'head', scatter_dimensio...  26.2 us
    dot_general x1, matrix products, body(): lax.dot_general(dlogit, hazard_weight, (((1,), (1,)), ((), ())), preferre...  7.28 us
    psum x1, blocking collectives, body(): event_loss = lax.psum(partial_value, 'head')  7.24 us
  transfers between devices with their start and end apart: 14, of which 14 were waited for; matrix products, arithmetic and copies ran while one was open for 1% of the time, Pallas kernels for 0%

profile of v1, /device:TPU:1, one launch (start us, length us, event | category | flops | bytes accessed | tf_op | source)
XLA Modules:
  0.0 348.9 jit_solution(7701577139190305905)
XLA Ops:
  9.7 5.1 %collective-permute-start = (f32[8,128,128]{2,1,0:T(8,128)S(1)}, f32[8,128,128]{2,1,0:T(8,128)S(1)}, u32[]{:S(2)}, u32[]{:S(2)}) collective-permute-start(f32[8,128,128]{2,1,0:T(8,128)S(1)} %fusion.15), channel_id=1, source_target_pairs={{0,4},{4,8},{8,12},{12,16},{16,20},{20,24},{24,28},{28,32},{32,36}... | collective-permute-start | bytes 1572872 | tf_op jit(solution)/shard_map/ppermute | solution.py:24
  14.8 6.1 %collective-permute-done = f32[8,128,128]{2,1,0:T(8,128)S(1)} collective-permute-done((f32[8,128,128]{2,1,0:T(8,128)S(1)}, f32[8,128,128]{2,1,0:T(8,128)S(1)}, u32[]{:S(2)}, u32[]{:S(2)}) %collective-permute-start) | collective-permute-done | bytes 524320 | tf_op jit(solution)/shard_map/ppermute | solution.py:24
  21.0 3.6 %collective-permute-start.1 = (f32[8,128,128]{2,1,0:T(8,128)S(1)}, f32[8,128,128]{2,1,0:T(8,128)S(1)}, u32[]{:S(2)}, u32[]{:S(2)}) collective-permute-start(f32[8,128,128]{2,1,0:T(8,128)S(1)} %add.101), channel_id=1, source_target_pairs={{0,8},{4,12},{8,16},{12,20},{16,24},{20,28},{24,32},{28,36},{32,40... | collective-permute-start | bytes 1572872 | tf_op jit(solution)/shard_map/ppermute | solution.py:24
  24.6 10.2 %collective-permute-done.1 = f32[8,128,128]{2,1,0:T(8,128)S(1)} collective-permute-done((f32[8,128,128]{2,1,0:T(8,128)S(1)}, f32[8,128,128]{2,1,0:T(8,128)S(1)}, u32[]{:S(2)}, u32[]{:S(2)}) %collective-permute-start.1) | collective-permute-done | bytes 524320 | tf_op jit(solution)/shard_map/ppermute | solution.py:24
  34.9 7.4 %collective-permute-start.2 = (f32[8,128,128]{2,1,0:T(8,128)S(1)}, f32[8,128,128]{2,1,0:T(8,128)S(1)}, u32[]{:S(2)}, u32[]{:S(2)}) collective-permute-start(f32[8,128,128]{2,1,0:T(8,128)S(1)} %add.103), channel_id=1, source_target_pairs={{0,16},{4,20},{8,24},{12,28},{16,32},{20,36},{24,40},{28,44},{32,4... | collective-permute-start | bytes 1572872 | tf_op jit(solution)/shard_map/ppermute | solution.py:24
  42.3 14.2 %collective-permute-done.2 = f32[8,128,128]{2,1,0:T(8,128)S(1)} collective-permute-done((f32[8,128,128]{2,1,0:T(8,128)S(1)}, f32[8,128,128]{2,1,0:T(8,128)S(1)}, u32[]{:S(2)}, u32[]{:S(2)}) %collective-permute-start.2) | collective-permute-done | bytes 524320 | tf_op jit(solution)/shard_map/ppermute | solution.py:24
  57.9 15.7 %collective-permute-done.3 = f32[8,128,128]{2,1,0:T(8,128)S(1)} collective-permute-done((f32[8,128,128]{2,1,0:T(8,128)S(1)}, f32[8,128,128]{2,1,0:T(8,128)S(1)}, u32[]{:S(2)}, u32[]{:S(2)}) %collective-permute-start.3) | collective-permute-done | bytes 524320 | tf_op jit(solution)/shard_map/ppermute | solution.py:24
  73.6 4.4 %collective-permute-start.4 = (f32[8,128,128]{2,1,0:T(8,128)S(1)}, f32[8,128,128]{2,1,0:T(8,128)S(1)}, u32[]{:S(2)}, u32[]{:S(2)}) collective-permute-start(f32[8,128,128]{2,1,0:T(8,128)S(1)} %add.107), channel_id=1, source_target_pairs={{0,64},{4,68},{8,72},{12,76},{16,80},{20,84},{24,88},{28,92},{32,9... | collective-permute-start | bytes 1572872 | tf_op jit(solution)/shard_map/ppermute | solution.py:24
  78.1 7.5 %collective-permute-done.4 = f32[8,128,128]{2,1,0:T(8,128)S(1)} collective-permute-done((f32[8,128,128]{2,1,0:T(8,128)S(1)}, f32[8,128,128]{2,1,0:T(8,128)S(1)}, u32[]{:S(2)}, u32[]{:S(2)}) %collective-permute-start.4) | collective-permute-done | bytes 524320 | tf_op jit(solution)/shard_map/ppermute | solution.py:24
  85.6 11.6 %collective-permute-start.5 = (f32[8,128,128]{2,1,0:T(8,128)S(1)}, f32[8,128,128]{2,1,0:T(8,128)S(1)}, u32[]{:S(2)}, u32[]{:S(2)}) collective-permute-start(f32[8,128,128]{2,1,0:T(8,128)S(1)} %add.109), channel_id=1, source_target_pairs={{0,128},{4,132},{8,136},{12,140},{16,144},{20,148},{24,152},{28,15... | collective-permute-start | bytes 1572872 | tf_op jit(solution)/shard_map/ppermute | solution.py:24
  98.1 5.2 %collective-permute-done.5 = f32[8,128,128]{2,1,0:T(8,128)S(1)} collective-permute-done((f32[8,128,128]{2,1,0:T(8,128)S(1)}, f32[8,128,128]{2,1,0:T(8,128)S(1)}, u32[]{:S(2)}, u32[]{:S(2)}) %collective-permute-start.5) | collective-permute-done | bytes 524320 | tf_op jit(solution)/shard_map/ppermute | solution.py:24
  105.1 70.0 %all-gather.2.cloned.1.call-done = bf16[128,4096]{0,1:T(8,128)(2,1)} async-done(((bf16[128,1024]{0,1:T(8,128)(2,1)}), bf16[128,4096]{0,1:T(8,128)(2,1)}) %all-gather.2.cloned.1.call-update) | async-done | bytes 1048592 | tf_op jit(solution)/shard_map/all_gather | solution.py:57
  175.1 5.0 %fusion.45 = f32[128,1024]{1,0:T(8,128)S(1)} fusion(bf16[128,4096]{0,1:T(8,128)(2,1)} %all-gather.2.cloned.1.call-done, bf16[4096,1024]{1,0:T(8,128)(2,1)} %param.11), kind=kOutput, calls=%fused_computation.70 | convolution fusion | flops 1073741824 | bytes 9961472 | tf_op jit(solution)/shard_map/dot_general | solution.py:56
  181.4 7.3 %convolution_convert_fusion = bf16[128,4096]{1,0:T(8,128)(2,1)} fusion(bf16[4096,1024]{1,0:T(8,128)(2,1)} %param.11, f32[128,1024]{1,0:T(8,128)S(1)} %get-tuple-element.11, f32[128]{0:T(128)S(1)} %convert_element_type.40, s32[1024]{0:T(1024)S(1)} %iota_add_fusion, s32[128]{0:T(128)S(1)} %copy-done.9), kind=kOutput, calls=%fused_computation | convolution fusion | flops 1074921472 | bytes 9966592 | tf_op jit(solution)/shard_map/dot_general | solution.py:74
  188.7 26.2 %reduce-scatter.2.cloned.1.call-done = bf16[128,1024]{1,0:T(8,128)(2,1)} async-done(((bf16[128,4096]{1,0:T(8,128)(2,1)}), bf16[128,1024]{1,0:T(8,128)(2,1)}) %reduce-scatter.2.cloned.1.call-update) | async-done | bytes 262160 | tf_op jit(solution)/shard_map/reduce_scatter | solution.py:77
  216.4 3.9 %collective-permute-start.6 = (f32[8,128,128]{1,2,0:T(8,128)S(1)}, f32[8,128,128]{1,2,0:T(8,128)S(1)}, u32[]{:S(2)}, u32[]{:S(2)}) collective-permute-start(f32[8,128,128]{1,2,0:T(8,128)S(1)} %convolution_bitcast_fusion.1), channel_id=1, source_target_pairs={{4,0},{8,4},{12,8},{16,12},{20,16},{24,20},{28,24},{32,28},{36,32}... | collective-permute-start | bytes 1572872 | tf_op jit(solution)/shard_map/ppermute | solution.py:24
  220.3 8.0 %collective-permute-done.6 = f32[8,128,128]{1,2,0:T(8,128)S(1)} collective-permute-done((f32[8,128,128]{1,2,0:T(8,128)S(1)}, f32[8,128,128]{1,2,0:T(8,128)S(1)}, u32[]{:S(2)}, u32[]{:S(2)}) %collective-permute-start.6) | collective-permute-done | bytes 524320 | tf_op jit(solution)/shard_map/ppermute | solution.py:24
  229.7 12.9 %collective-permute-done.7 = f32[8,128,128]{1,2,0:T(8,128)S(1)} collective-permute-done((f32[8,128,128]{1,2,0:T(8,128)S(1)}, f32[8,128,128]{1,2,0:T(8,128)S(1)}, u32[]{:S(2)}, u32[]{:S(2)}) %collective-permute-start.7) | collective-permute-done | bytes 524320 | tf_op jit(solution)/shard_map/ppermute | solution.py:24
  244.7 26.2 %collective-permute-done.8 = f32[8,128,128]{1,2,0:T(8,128)S(1)} collective-permute-done((f32[8,128,128]{1,2,0:T(8,128)S(1)}, f32[8,128,128]{1,2,0:T(8,128)S(1)}, u32[]{:S(2)}, u32[]{:S(2)}) %collective-permute-start.8) | collective-permute-done | bytes 524320 | tf_op jit(solution)/shard_map/ppermute | solution.py:24
  274.7 16.9 %collective-permute-done.9 = f32[8,128,128]{1,2,0:T(8,128)S(1)} collective-permute-done((f32[8,128,128]{1,2,0:T(8,128)S(1)}, f32[8,128,128]{1,2,0:T(8,128)S(1)}, u32[]{:S(2)}, u32[]{:S(2)}) %collective-permute-start.9) | collective-permute-done | bytes 524320 | tf_op jit(solution)/shard_map/ppermute | solution.py:24
  294.6 7.2 %psum.7 = f32[128]{0:T(128)} all-reduce(f32[128]{0:T(128)S(1)} %multiply_subtract_fusion), channel_id=1, replica_groups=mesh['seq'=64,'head'=4] {'head'}, use_global_device_ids=true, to_apply=%region_6.7 | all-reduce | flops 128 | bytes 1024 | tf_op jit(solution)/shard_map/psum | solution.py:80
  302.7 15.6 %collective-permute-done.10 = f32[8,128,128]{1,2,0:T(8,128)} collective-permute-done((f32[8,128,128]{1,2,0:T(8,128)}, f32[8,128,128]{1,2,0:T(8,128)}, u32[]{:S(2)}, u32[]{:S(2)}) %collective-permute-start.10) | collective-permute-done | bytes 524320 | tf_op jit(solution)/shard_map/ppermute | solution.py:24
  318.2 2.1 add.125
  323.4 14.1 %collective-permute-done.11 = f32[8,128,128]{1,2,0:T(8,128)} collective-permute-done((f32[8,128,128]{1,2,0:T(8,128)}, f32[8,128,128]{1,2,0:T(8,128)}, u32[]{:S(2)}, u32[]{:S(2)}) %collective-permute-start.11) | collective-permute-done | bytes 524320 | tf_op jit(solution)/shard_map/ppermute | solution.py:24
  (74 shorter events, 28.1 us)
Async XLA Ops:
  7.2 90.1 %copy-start = (bf16[128,1024]{1,0:T(8,128)(2,1)S(1)}, bf16[128,1024]{1,0:T(8,128)(2,1)}, u32[]{:S(2)}) copy-start(bf16[128,1024]{1,0:T(8,128)(2,1)} %param.8) | copy-start | bytes 786436
  7.2 90.1 %copy-start.2 = (bf16[128,1024]{1,0:T(8,128)(2,1)S(1)}, bf16[128,1024]{1,0:T(8,128)(2,1)}, u32[]{:S(2)}) copy-start(bf16[128,1024]{1,0:T(8,128)(2,1)} %param.9) | copy-start | bytes 786436
  7.2 90.4 %copy-start.1 = (bf16[128,1024]{1,0:T(8,128)(2,1)S(1)}, bf16[128,1024]{1,0:T(8,128)(2,1)}, u32[]{:S(2)}) copy-start(bf16[128,1024]{1,0:T(8,128)(2,1)} %param.10) | copy-start | bytes 786436
  7.2 167.9 %all-gather.2.cloned.1.call-start = ((), (), s32[]{:S(2)}) async-start(), calls=%async_computation.1 | async-start | bytes 1310720 | tf_op jit(solution)/shard_map/all_gather | solution.py:57
  9.7 95.1 %copy-start.10 = (s32[128]{0:T(128)S(1)}, s32[128]{0:T(128)}, u32[]{:S(2)}) copy-start(s32[128]{0:T(128)} %param.14) | copy-start | bytes 1540
  9.7 95.1 %copy-start.7 = (f32[32,1024]{1,0:T(8,128)S(1)}, f32[32,1024]{1,0:T(8,128)}, u32[]{:S(2)}) copy-start(f32[32,1024]{1,0:T(8,128)} %param.12) | copy-start | bytes 393220
  9.7 11.2 %collective-permute-start = (f32[8,128,128]{2,1,0:T(8,128)S(1)}, f32[8,128,128]{2,1,0:T(8,128)S(1)}, u32[]{:S(2)}, u32[]{:S(2)}) collective-permute-start(f32[8,128,128]{2,1,0:T(8,128)S(1)} %fusion.15), channel_id=1, source_target_pairs={{0,4},{4,8},{8,12},{12,16},{16,20},{20,24},{24,28},{28,32},{32,36}... | collective-permute-start | bytes 1572872 | tf_op jit(solution)/shard_map/ppermute | solution.py:24
  21.0 13.8 %collective-permute-start.1 = (f32[8,128,128]{2,1,0:T(8,128)S(1)}, f32[8,128,128]{2,1,0:T(8,128)S(1)}, u32[]{:S(2)}, u32[]{:S(2)}) collective-permute-start(f32[8,128,128]{2,1,0:T(8,128)S(1)} %add.101), channel_id=1, source_target_pairs={{0,8},{4,12},{8,16},{12,20},{16,24},{20,28},{24,32},{28,36},{32,40... | collective-permute-start | bytes 1572872 | tf_op jit(solution)/shard_map/ppermute | solution.py:24
  34.9 21.6 %collective-permute-start.2 = (f32[8,128,128]{2,1,0:T(8,128)S(1)}, f32[8,128,128]{2,1,0:T(8,128)S(1)}, u32[]{:S(2)}, u32[]{:S(2)}) collective-permute-start(f32[8,128,128]{2,1,0:T(8,128)S(1)} %add.103), channel_id=1, source_target_pairs={{0,16},{4,20},{8,24},{12,28},{16,32},{20,36},{24,40},{28,44},{32,4... | collective-permute-start | bytes 1572872 | tf_op jit(solution)/shard_map/ppermute | solution.py:24
  56.6 17.0 %collective-permute-start.3 = (f32[8,128,128]{2,1,0:T(8,128)S(1)}, f32[8,128,128]{2,1,0:T(8,128)S(1)}, u32[]{:S(2)}, u32[]{:S(2)}) collective-permute-start(f32[8,128,128]{2,1,0:T(8,128)S(1)} %add.105), channel_id=1, source_target_pairs={{0,32},{4,36},{8,40},{12,44},{16,48},{20,52},{24,56},{28,60},{32,6... | collective-permute-start | bytes 1572872 | tf_op jit(solution)/shard_map/ppermute | solution.py:24
  73.6 11.9 %collective-permute-start.4 = (f32[8,128,128]{2,1,0:T(8,128)S(1)}, f32[8,128,128]{2,1,0:T(8,128)S(1)}, u32[]{:S(2)}, u32[]{:S(2)}) collective-permute-start(f32[8,128,128]{2,1,0:T(8,128)S(1)} %add.107), channel_id=1, source_target_pairs={{0,64},{4,68},{8,72},{12,76},{16,80},{20,84},{24,88},{28,92},{32,9... | collective-permute-start | bytes 1572872 | tf_op jit(solution)/shard_map/ppermute | solution.py:24
  85.6 17.7 %collective-permute-start.5 = (f32[8,128,128]{2,1,0:T(8,128)S(1)}, f32[8,128,128]{2,1,0:T(8,128)S(1)}, u32[]{:S(2)}, u32[]{:S(2)}) collective-permute-start(f32[8,128,128]{2,1,0:T(8,128)S(1)} %add.109), channel_id=1, source_target_pairs={{0,128},{4,132},{8,136},{12,140},{16,144},{20,148},{24,152},{28,15... | collective-permute-start | bytes 1572872 | tf_op jit(solution)/shard_map/ppermute | solution.py:24
  104.8 110.1 %reduce-scatter.2.cloned.1.call-start = ((), (), s32[]{:S(2)}) async-start(), calls=%async_computation.2 | async-start | bytes 1310720 | tf_op jit(solution)/shard_map/reduce_scatter | solution.py:77
  105.0 75.9 %copy-start.8 = (s32[128]{0:T(128)S(1)}, s32[128]{0:T(128)}, u32[]{:S(2)}) copy-start(s32[128]{0:T(128)} %param.13) | copy-start | bytes 1540
  105.1 76.4 %copy-start.9 = (s32[128]{0:T(128)S(1)}, s32[128]{0:T(128)}, u32[]{:S(2)}) copy-start(s32[128]{0:T(128)} %param.15) | copy-start | bytes 1540
  180.1 0.8 copy-start.6
  216.4 11.9 %collective-permute-start.6 = (f32[8,128,128]{1,2,0:T(8,128)S(1)}, f32[8,128,128]{1,2,0:T(8,128)S(1)}, u32[]{:S(2)}, u32[]{:S(2)}) collective-permute-start(f32[8,128,128]{1,2,0:T(8,128)S(1)} %convolution_bitcast_fusion.1), channel_id=1, source_target_pairs={{4,0},{8,4},{12,8},{16,12},{20,16},{24,20},{28,24},{32,28},{36,32}... | collective-permute-start | bytes 1572872 | tf_op jit(solution)/shard_map/ppermute | solution.py:24
  228.4 14.2 %collective-permute-start.7 = (f32[8,128,128]{1,2,0:T(8,128)S(1)}, f32[8,128,128]{1,2,0:T(8,128)S(1)}, u32[]{:S(2)}, u32[]{:S(2)}) collective-permute-start(f32[8,128,128]{1,2,0:T(8,128)S(1)} %add.117), channel_id=1, source_target_pairs={{8,0},{12,4},{16,8},{20,12},{24,16},{28,20},{32,24},{36,28},{40,32... | collective-permute-start | bytes 1572872 | tf_op jit(solution)/shard_map/ppermute | solution.py:24
  243.4 27.5 %collective-permute-start.8 = (f32[8,128,128]{1,2,0:T(8,128)S(1)}, f32[8,128,128]{1,2,0:T(8,128)S(1)}, u32[]{:S(2)}, u32[]{:S(2)}) collective-permute-start(f32[8,128,128]{1,2,0:T(8,128)S(1)} %add.119), channel_id=1, source_target_pairs={{16,0},{20,4},{24,8},{28,12},{32,16},{36,20},{40,24},{44,28},{48,3... | collective-permute-start | bytes 1572872 | tf_op jit(solution)/shard_map/ppermute | solution.py:24
  270.9 0.8 copy-start.4
  271.8 19.9 %collective-permute-start.9 = (f32[8,128,128]{1,2,0:T(8,128)S(1)}, f32[8,128,128]{1,2,0:T(8,128)S(1)}, u32[]{:S(2)}, u32[]{:S(2)}) collective-permute-start(f32[8,128,128]{1,2,0:T(8,128)S(1)} %add.121), channel_id=1, source_target_pairs={{32,0},{36,4},{40,8},{44,12},{48,16},{52,20},{56,24},{60,28},{64,3... | collective-permute-start | bytes 1572872 | tf_op jit(solution)/shard_map/ppermute | solution.py:24
  291.6 0.8 copy-start.5
  293.3 24.9 %collective-permute-start.10 = (f32[8,128,128]{1,2,0:T(8,128)}, f32[8,128,128]{1,2,0:T(8,128)}, u32[]{:S(2)}, u32[]{:S(2)}) collective-permute-start(f32[8,128,128]{1,2,0:T(8,128)} %add.123), channel_id=1, source_target_pairs={{64,0},{68,4},{72,8},{76,12},{80,16},{84,20},{88,24},{92,28},{96,3... | collective-permute-start | bytes 1572872 | tf_op jit(solution)/shard_map/ppermute | solution.py:24
  320.3 17.2 %collective-permute-start.11 = (f32[8,128,128]{1,2,0:T(8,128)}, f32[8,128,128]{1,2,0:T(8,128)}, u32[]{:S(2)}, u32[]{:S(2)}) collective-permute-start(f32[8,128,128]{1,2,0:T(8,128)} %add.125), channel_id=1, source_target_pairs={{128,0},{132,4},{136,8},{140,12},{144,16},{148,20},{152,24},{156,2... | collective-permute-start | bytes 1572872 | tf_op jit(solution)/shard_map/ppermute | solution.py:24
  (1 other events, 0.8 us)
Sparse Core Ops, SparseCore 0:
  104.9 70.1 all-gather.1
  188.9 25.9 reduce-scatter.1

commit v2 on v1

--- a/solution.py
+++ b/solution.py
@@ -13,9 +13,15 @@
 
 def exclusive_scan(shard, axis, reverse=False):
     count = lax.axis_size(axis)
-    inclusive = shard
-    exclusive = jnp.zeros_like(shard)
-    distance = 1
+    core = lax.axis_index(axis) % 2
+    pair = [(i, i ^ 1) for i in range(count)]
+    other = lax.ppermute(shard, axis, pair)
+    keep_other = (core == 0) if reverse else (core == 1)
+    within = jnp.where(keep_other, other, jnp.zeros_like(other))
+    half = shard.shape[0] // 2
+    inclusive = lax.dynamic_slice_in_dim(shard + other, core * half, half, 0)
+    exclusive = jnp.zeros_like(inclusive)
+    distance = 2
     while distance < count:
         if reverse:
             pairs = [(i, i - distance) for i in range(distance, count)]
@@ -25,7 +31,13 @@
         exclusive = exclusive + arrived
         inclusive = inclusive + arrived
         distance *= 2
-    return exclusive
+    partner = lax.ppermute(exclusive, axis, pair)
+    joined = jnp.where(
+        core == 0,
+        jnp.concatenate([exclusive, partner], axis=0),
+        jnp.concatenate([partner, exclusive], axis=0),
+    )
+    return joined + within
 
 
 def body(queries, keys, values, hazard_weight, log_base, time_bin, observed, task_label):

time: 351 us -> 240 us (0.68)
  waiting for transfers between devices: 249 us -> 129 us
  starting transfers between devices: 43.9 us -> 49.7 us
  matrix products: 19.8 us -> 24.9 us
  other arithmetic: 6.59 us -> 2.7 us
    ppermute x12 -> x10, waiting for transfers between devices: 153 us -> 75.4 us  [exclusive_scan(): arrived = lax.ppermute(inclusive, axis, pairs)]
    all_gather x1, waiting for transfers between devices: 70 us -> 24.9 us  [body(): lax.all_gather(hidden, 'head', axis=1, tiled=True)]
    ppermute x0 -> x4, starting transfers between devices: none -> 12.7 us  [the longest x2 7.16 us: exclusive_scan(): partner = lax.ppermute(exclusive, axis, pair)]
    ppermute x12 -> x10, starting transfers between devices: 43.8 us -> 36.9 us  [exclusive_scan(): arrived = lax.ppermute(inclusive, axis, pairs)]
  transfers between devices with their start and end apart: 14 -> 16, of which waited for: 14 -> 14; matrix products, arithmetic and copies ran while one was open for 1% -> 4% of each run, Pallas kernels for 0% -> 0%
where the time goes in v2:
time: 240 us; the launch traced here: 236 us
  waiting for transfers between devices  129 us (54%)
  starting transfers between devices  49.7 us (21%)
  matrix products  24.9 us (10%)
  between operations  14.4 us (6%)
  local copies, waits for them, and re-layouts  7.58 us (3%)
  blocking collectives  7 us (3%)
  other arithmetic  2.7 us (1%)
    ppermute x10, waiting for transfers between devices, exclusive_scan(): arrived = lax.ppermute(inclusive, axis, pairs)  75.4 us
    ppermute x10, starting transfers between devices, exclusive_scan(): arrived = lax.ppermute(inclusive, axis, pairs)  36.9 us
    reduce_scatter x1, waiting for transfers between devices, body(): lax.psum_scatter(term_full.astype(jnp.bfloat16), 'head', scatter_dimensio...  26.1 us
    all_gather x1, waiting for transfers between devices, body(): lax.all_gather(hidden, 'head', axis=1, tiled=True)  24.9 us
    dot_general x1, matrix products, body(): lax.dot_general(dlogit, hazard_weight, (((1,), (1,)), ((), ())), preferre...  7.29 us
    ppermute x2, starting transfers between devices, exclusive_scan(): partner = lax.ppermute(exclusive, axis, pair)  7.16 us
    psum x1, blocking collectives, body(): event_loss = lax.psum(partial_value, 'head')  7 us
    unnamed x30, local copies, waits for them, and re-layouts  6.25 us
  transfers between devices with their start and end apart: 16, of which 14 were waited for; matrix products, arithmetic and copies ran while one was open for 4% of the time, Pallas kernels for 0%

profile of v2, /device:TPU:1, one launch (start us, length us, event | category | flops | bytes accessed | tf_op | source)
XLA Modules:
  0.0 235.7 jit_solution(16217477352183363238)
XLA Ops:
  9.7 3.3 %collective-permute-start = (f32[8,128,128]{2,1,0:T(8,128)S(1)}, f32[8,128,128]{2,1,0:T(8,128)S(1)}, u32[]{:S(2)}, u32[]{:S(2)}) collective-permute-start(f32[8,128,128]{2,1,0:T(8,128)S(1)} %fusion.17), channel_id=1, source_target_pairs={{0,4},{4,0},{8,12},{12,8},{16,20},{20,16},{24,28},{28,24},{32,36},... | collective-permute-start | bytes 1572872 | tf_op jit(solution)/shard_map/ppermute | solution.py:18
  16.4 5.3 %collective-permute-done.1 = f32[4,128,128]{2,1,0:T(8,128)S(1)} collective-permute-done((f32[4,128,128]{2,1,0:T(8,128)S(1)}, f32[4,128,128]{2,1,0:T(8,128)S(1)}, u32[]{:S(2)}, u32[]{:S(2)}) %collective-permute-start.1) | collective-permute-done | bytes 262176 | tf_op jit(solution)/shard_map/ppermute | solution.py:30
  21.8 5.5 %collective-permute-start.2 = (f32[4,128,128]{2,1,0:T(8,128)S(1)}, f32[4,128,128]{2,1,0:T(8,128)S(1)}, u32[]{:S(2)}, u32[]{:S(2)}) collective-permute-start(f32[4,128,128]{2,1,0:T(8,128)S(1)} %add.113), channel_id=1, source_target_pairs={{0,16},{4,20},{8,24},{12,28},{16,32},{20,36},{24,40},{28,44},{32,4... | collective-permute-start | bytes 786440 | tf_op jit(solution)/shard_map/ppermute | solution.py:30
  27.2 9.9 %collective-permute-done.2 = f32[4,128,128]{2,1,0:T(8,128)S(1)} collective-permute-done((f32[4,128,128]{2,1,0:T(8,128)S(1)}, f32[4,128,128]{2,1,0:T(8,128)S(1)}, u32[]{:S(2)}, u32[]{:S(2)}) %collective-permute-start.2) | collective-permute-done | bytes 262176 | tf_op jit(solution)/shard_map/ppermute | solution.py:30
  37.2 12.2 %collective-permute-start.3 = (f32[4,128,128]{2,1,0:T(8,128)S(1)}, f32[4,128,128]{2,1,0:T(8,128)S(1)}, u32[]{:S(2)}, u32[]{:S(2)}) collective-permute-start(f32[4,128,128]{2,1,0:T(8,128)S(1)} %add.115), channel_id=1, source_target_pairs={{0,32},{4,36},{8,40},{12,44},{16,48},{20,52},{24,56},{28,60},{32,6... | collective-permute-start | bytes 786440 | tf_op jit(solution)/shard_map/ppermute | solution.py:30
  49.4 11.4 %collective-permute-done.3 = f32[4,128,128]{2,1,0:T(8,128)S(1)} collective-permute-done((f32[4,128,128]{2,1,0:T(8,128)S(1)}, f32[4,128,128]{2,1,0:T(8,128)S(1)}, u32[]{:S(2)}, u32[]{:S(2)}) %collective-permute-start.3) | collective-permute-done | bytes 262176 | tf_op jit(solution)/shard_map/ppermute | solution.py:30
  60.8 5.3 %collective-permute-start.4 = (f32[4,128,128]{2,1,0:T(8,128)S(1)}, f32[4,128,128]{2,1,0:T(8,128)S(1)}, u32[]{:S(2)}, u32[]{:S(2)}) collective-permute-start(f32[4,128,128]{2,1,0:T(8,128)S(1)} %add.117), channel_id=1, source_target_pairs={{0,64},{4,68},{8,72},{12,76},{16,80},{20,84},{24,88},{28,92},{32,9... | collective-permute-start | bytes 786440 | tf_op jit(solution)/shard_map/ppermute | solution.py:30
  66.1 5.1 %collective-permute-done.4 = f32[4,128,128]{2,1,0:T(8,128)S(1)} collective-permute-done((f32[4,128,128]{2,1,0:T(8,128)S(1)}, f32[4,128,128]{2,1,0:T(8,128)S(1)}, u32[]{:S(2)}, u32[]{:S(2)}) %collective-permute-start.4) | collective-permute-done | bytes 262176 | tf_op jit(solution)/shard_map/ppermute | solution.py:30
  71.3 5.7 %collective-permute-start.5 = (f32[4,128,128]{2,1,0:T(8,128)S(1)}, f32[4,128,128]{2,1,0:T(8,128)S(1)}, u32[]{:S(2)}, u32[]{:S(2)}) collective-permute-start(f32[4,128,128]{2,1,0:T(8,128)S(1)} %add.119), channel_id=1, source_target_pairs={{0,128},{4,132},{8,136},{12,140},{16,144},{20,148},{24,152},{28,15... | collective-permute-start | bytes 786440 | tf_op jit(solution)/shard_map/ppermute | solution.py:30
  77.0 4.2 %collective-permute-done.5 = f32[4,128,128]{2,1,0:T(8,128)S(1)} collective-permute-done((f32[4,128,128]{2,1,0:T(8,128)S(1)}, f32[4,128,128]{2,1,0:T(8,128)S(1)}, u32[]{:S(2)}, u32[]{:S(2)}) %collective-permute-start.5) | collective-permute-done | bytes 262176 | tf_op jit(solution)/shard_map/ppermute | solution.py:30
  81.3 2.3 collective-permute-start.6
  87.0 24.9 %all-gather.2.cloned.1.call-done = bf16[128,4096]{0,1:T(8,128)(2,1)} async-done(((bf16[128,1024]{0,1:T(8,128)(2,1)}), bf16[128,4096]{0,1:T(8,128)(2,1)}) %all-gather.2.cloned.1.call-update) | async-done | bytes 1048592 | tf_op jit(solution)/shard_map/all_gather | solution.py:69
  111.9 5.0 %fusion.51 = f32[128,1024]{1,0:T(8,128)S(1)} fusion(bf16[128,4096]{0,1:T(8,128)(2,1)} %all-gather.2.cloned.1.call-done, bf16[4096,1024]{1,0:T(8,128)(2,1)} %param.11), kind=kOutput, calls=%fused_computation.76 | convolution fusion | flops 1073741824 | bytes 9961472 | tf_op jit(solution)/shard_map/dot_general | solution.py:68
  117.8 7.3 %convolution_convert_fusion = bf16[128,4096]{1,0:T(8,128)(2,1)} fusion(bf16[4096,1024]{1,0:T(8,128)(2,1)} %param.11, f32[128,1024]{1,0:T(8,128)S(1)} %get-tuple-element.11, f32[128]{0:T(128)S(1)} %convert_element_type.40, s32[1024]{0:T(1024)S(1)} %iota_add_fusion, s32[128]{0:T(128)S(1)} %copy-done.11), kind=kOutput, calls=%fused_computation | convolution fusion | flops 1074921472 | bytes 9966592 | tf_op jit(solution)/shard_map/dot_general | solution.py:86
  125.1 26.1 %reduce-scatter.2.cloned.1.call-done = bf16[128,1024]{1,0:T(8,128)(2,1)} async-done(((bf16[128,4096]{1,0:T(8,128)(2,1)}), bf16[128,1024]{1,0:T(8,128)(2,1)}) %reduce-scatter.2.cloned.1.call-update) | async-done | bytes 262160 | tf_op jit(solution)/shard_map/reduce_scatter | solution.py:89
  152.8 2.2 collective-permute-start.7
  157.9 8.1 %collective-permute-done.8 = f32[4,128,128]{2,1,0:T(8,128)S(1)} collective-permute-done((f32[4,128,128]{2,1,0:T(8,128)S(1)}, f32[4,128,128]{2,1,0:T(8,128)S(1)}, u32[]{:S(2)}, u32[]{:S(2)}) %collective-permute-start.8) | collective-permute-done | bytes 262176 | tf_op jit(solution)/shard_map/ppermute | solution.py:30
  167.3 9.2 %collective-permute-done.9 = f32[4,128,128]{2,1,0:T(8,128)S(1)} collective-permute-done((f32[4,128,128]{2,1,0:T(8,128)S(1)}, f32[4,128,128]{2,1,0:T(8,128)S(1)}, u32[]{:S(2)}, u32[]{:S(2)}) %collective-permute-start.9) | collective-permute-done | bytes 262176 | tf_op jit(solution)/shard_map/ppermute | solution.py:30
  180.1 7.0 %psum.7 = f32[128]{0:T(128)} all-reduce(f32[128]{0:T(128)S(1)} %multiply_subtract_fusion), channel_id=1, replica_groups=mesh['seq'=64,'head'=4] {'head'}, use_global_device_ids=true, to_apply=%region_6.7 | all-reduce | flops 128 | bytes 1024 | tf_op jit(solution)/shard_map/psum | solution.py:92
  187.1 8.7 %collective-permute-done.10 = f32[4,128,128]{2,1,0:T(8,128)S(1)} collective-permute-done((f32[4,128,128]{2,1,0:T(8,128)S(1)}, f32[4,128,128]{2,1,0:T(8,128)S(1)}, u32[]{:S(2)}, u32[]{:S(2)}) %collective-permute-start.10) | collective-permute-done | bytes 262176 | tf_op jit(solution)/shard_map/ppermute | solution.py:30
  198.6 8.4 %collective-permute-done.11 = f32[4,128,128]{2,1,0:T(8,128)S(1)} collective-permute-done((f32[4,128,128]{2,1,0:T(8,128)S(1)}, f32[4,128,128]{2,1,0:T(8,128)S(1)}, u32[]{:S(2)}, u32[]{:S(2)}) %collective-permute-start.11) | collective-permute-done | bytes 262176 | tf_op jit(solution)/shard_map/ppermute | solution.py:30
  208.4 2.2 fusion.6
  210.6 5.1 %collective-permute-done.12 = f32[4,128,128]{2,1,0:T(8,128)S(1)} collective-permute-done((f32[4,128,128]{2,1,0:T(8,128)S(1)}, f32[4,128,128]{2,1,0:T(8,128)S(1)}, u32[]{:S(2)}, u32[]{:S(2)}) %collective-permute-start.12) | collective-permute-done | bytes 262176 | tf_op jit(solution)/shard_map/ppermute | solution.py:30
  216.9 4.8 %collective-permute-start.13 = (f32[4,128,128]{2,1,0:T(8,128)S(1)}, f32[4,128,128]{2,1,0:T(8,128)}, u32[]{:S(2)}, u32[]{:S(2)}) collective-permute-start(f32[4,128,128]{2,1,0:T(8,128)S(1)} %add_add_fusion), channel_id=1, source_target_pairs={{0,4},{4,0},{8,12},{12,8},{16,20},{20,16},{24,28},{28,24},{32,36},... | collective-permute-start | bytes 786440 | tf_op jit(solution)/shard_map/ppermute | solution.py:34
  (82 shorter events, 32.1 us)
Async XLA Ops:
  7.2 76.5 %copy-start = (bf16[128,1024]{1,0:T(8,128)(2,1)S(1)}, bf16[128,1024]{1,0:T(8,128)(2,1)}, u32[]{:S(2)}) copy-start(bf16[128,1024]{1,0:T(8,128)(2,1)} %param.8) | copy-start | bytes 786436
  7.2 77.7 %copy-start.1 = (bf16[128,1024]{1,0:T(8,128)(2,1)S(1)}, bf16[128,1024]{1,0:T(8,128)(2,1)}, u32[]{:S(2)}) copy-start(bf16[128,1024]{1,0:T(8,128)(2,1)} %param.10) | copy-start | bytes 786436
  7.2 79.6 %copy-start.12 = (s32[128]{0:T(128)S(1)}, s32[128]{0:T(128)}, u32[]{:S(2)}) copy-start(s32[128]{0:T(128)} %param.14) | copy-start | bytes 1540
  7.2 79.6 %copy-start.9 = (f32[32,1024]{1,0:T(8,128)S(1)}, f32[32,1024]{1,0:T(8,128)}, u32[]{:S(2)}) copy-start(f32[32,1024]{1,0:T(8,128)} %param.12) | copy-start | bytes 393220
  7.2 104.7 %all-gather.2.cloned.1.call-start = ((), (), s32[]{:S(2)}) async-start(), calls=%async_computation.1 | async-start | bytes 1310720 | tf_op jit(solution)/shard_map/all_gather | solution.py:69
  9.7 4.9 %collective-permute-start = (f32[8,128,128]{2,1,0:T(8,128)S(1)}, f32[8,128,128]{2,1,0:T(8,128)S(1)}, u32[]{:S(2)}, u32[]{:S(2)}) collective-permute-start(f32[8,128,128]{2,1,0:T(8,128)S(1)} %fusion.17), channel_id=1, source_target_pairs={{0,4},{4,0},{8,12},{12,8},{16,20},{20,16},{24,28},{28,24},{32,36},... | collective-permute-start | bytes 1572872 | tf_op jit(solution)/shard_map/ppermute | solution.py:18
  14.6 7.1 %collective-permute-start.1 = (f32[4,128,128]{2,1,0:T(8,128)S(1)}, f32[4,128,128]{2,1,0:T(8,128)S(1)}, u32[]{:S(2)}, u32[]{:S(2)}) collective-permute-start(f32[4,128,128]{2,1,0:T(8,128)S(1)} %dynamic-slice_add_fusion.1), channel_id=1, source_target_pairs={{0,8},{4,12},{8,16},{12,20},{16,24},{20,28},{24,32},{28,36},{32,40... | collective-permute-start | bytes 786440 | tf_op jit(solution)/shard_map/ppermute | solution.py:30
  21.8 15.4 %collective-permute-start.2 = (f32[4,128,128]{2,1,0:T(8,128)S(1)}, f32[4,128,128]{2,1,0:T(8,128)S(1)}, u32[]{:S(2)}, u32[]{:S(2)}) collective-permute-start(f32[4,128,128]{2,1,0:T(8,128)S(1)} %add.113), channel_id=1, source_target_pairs={{0,16},{4,20},{8,24},{12,28},{16,32},{20,36},{24,40},{28,44},{32,4... | collective-permute-start | bytes 786440 | tf_op jit(solution)/shard_map/ppermute | solution.py:30
  37.2 23.6 %collective-permute-start.3 = (f32[4,128,128]{2,1,0:T(8,128)S(1)}, f32[4,128,128]{2,1,0:T(8,128)S(1)}, u32[]{:S(2)}, u32[]{:S(2)}) collective-permute-start(f32[4,128,128]{2,1,0:T(8,128)S(1)} %add.115), channel_id=1, source_target_pairs={{0,32},{4,36},{8,40},{12,44},{16,48},{20,52},{24,56},{28,60},{32,6... | collective-permute-start | bytes 786440 | tf_op jit(solution)/shard_map/ppermute | solution.py:30
  60.8 10.4 %collective-permute-start.4 = (f32[4,128,128]{2,1,0:T(8,128)S(1)}, f32[4,128,128]{2,1,0:T(8,128)S(1)}, u32[]{:S(2)}, u32[]{:S(2)}) collective-permute-start(f32[4,128,128]{2,1,0:T(8,128)S(1)} %add.117), channel_id=1, source_target_pairs={{0,64},{4,68},{8,72},{12,76},{16,80},{20,84},{24,88},{28,92},{32,9... | collective-permute-start | bytes 786440 | tf_op jit(solution)/shard_map/ppermute | solution.py:30
  71.3 10.0 %collective-permute-start.5 = (f32[4,128,128]{2,1,0:T(8,128)S(1)}, f32[4,128,128]{2,1,0:T(8,128)S(1)}, u32[]{:S(2)}, u32[]{:S(2)}) collective-permute-start(f32[4,128,128]{2,1,0:T(8,128)S(1)} %add.119), channel_id=1, source_target_pairs={{0,128},{4,132},{8,136},{12,140},{16,144},{20,148},{24,152},{28,15... | collective-permute-start | bytes 786440 | tf_op jit(solution)/shard_map/ppermute | solution.py:30
  81.3 35.6 %copy-start.3 = (f32[4,128,128]{2,1,0:T(8,128)}, f32[4,128,128]{2,1,0:T(8,128)S(1)}, u32[]{:S(2)}) copy-start(f32[4,128,128]{2,1,0:T(8,128)S(1)} %add_add_fusion.1) | copy-start | bytes 786436
  81.3 4.1 %collective-permute-start.6 = (f32[4,128,128]{2,1,0:T(8,128)S(1)}, f32[4,128,128]{2,1,0:T(8,128)S(1)}, u32[]{:S(2)}, u32[]{:S(2)}) collective-permute-start(f32[4,128,128]{2,1,0:T(8,128)S(1)} %add_add_fusion.1), channel_id=1, source_target_pairs={{0,4},{4,0},{8,12},{12,8},{16,20},{20,16},{24,28},{28,24},{32,36},... | collective-permute-start | bytes 786440 | tf_op jit(solution)/shard_map/ppermute | solution.py:34
  85.5 31.5 %copy-start.8 = (f32[4,128,128]{2,1,0:T(8,128)}, f32[4,128,128]{2,1,0:T(8,128)S(1)}, u32[]{:S(2)}) copy-start(f32[4,128,128]{2,1,0:T(8,128)S(1)} %collective-permute-done.6) | copy-start | bytes 786436
  86.8 64.4 %reduce-scatter.2.cloned.1.call-start = ((), (), s32[]{:S(2)}) async-start(), calls=%async_computation.2 | async-start | bytes 1310720 | tf_op jit(solution)/shard_map/reduce_scatter | solution.py:89
  87.0 30.8 %copy-start.11 = (s32[128]{0:T(128)S(1)}, s32[128]{0:T(128)}, u32[]{:S(2)}) copy-start(s32[128]{0:T(128)} %param.15) | copy-start | bytes 1540
  152.8 73.8 %copy-start.2 = (bf16[128,1024]{1,0:T(8,128)(2,1)S(1)}, bf16[128,1024]{1,0:T(8,128)(2,1)}, u32[]{:S(2)}) copy-start(bf16[128,1024]{1,0:T(8,128)(2,1)} %param.9) | copy-start | bytes 786436
  152.8 3.7 %collective-permute-start.7 = (f32[8,128,128]{2,1,0:T(8,128)S(1)}, f32[8,128,128]{2,1,0:T(8,128)S(1)}, u32[]{:S(2)}, u32[]{:S(2)}) collective-permute-start(f32[8,128,128]{2,1,0:T(8,128)S(1)} %convolution_bitcast_fusion.1), channel_id=1, source_target_pairs={{0,4},{4,0},{8,12},{12,8},{16,20},{20,16},{24,28},{28,24},{32,36},... | collective-permute-start | bytes 1572872 | tf_op jit(solution)/shard_map/ppermute | solution.py:18
  156.6 9.4 %collective-permute-start.8 = (f32[4,128,128]{2,1,0:T(8,128)S(1)}, f32[4,128,128]{2,1,0:T(8,128)S(1)}, u32[]{:S(2)}, u32[]{:S(2)}) collective-permute-start(f32[4,128,128]{2,1,0:T(8,128)S(1)} %dynamic-slice_add_fusion), channel_id=1, source_target_pairs={{8,0},{12,4},{16,8},{20,12},{24,16},{28,20},{32,24},{36,28},{40,32... | collective-permute-start | bytes 786440 | tf_op jit(solution)/shard_map/ppermute | solution.py:30
  166.0 10.5 %collective-permute-start.9 = (f32[4,128,128]{2,1,0:T(8,128)S(1)}, f32[4,128,128]{2,1,0:T(8,128)S(1)}, u32[]{:S(2)}, u32[]{:S(2)}) collective-permute-start(f32[4,128,128]{2,1,0:T(8,128)S(1)} %add.129), channel_id=1, source_target_pairs={{16,0},{20,4},{24,8},{28,12},{32,16},{36,20},{40,24},{44,28},{48,3... | collective-permute-start | bytes 786440 | tf_op jit(solution)/shard_map/ppermute | solution.py:30
  177.2 18.6 %collective-permute-start.10 = (f32[4,128,128]{2,1,0:T(8,128)S(1)}, f32[4,128,128]{2,1,0:T(8,128)S(1)}, u32[]{:S(2)}, u32[]{:S(2)}) collective-permute-start(f32[4,128,128]{2,1,0:T(8,128)S(1)} %add.131), channel_id=1, source_target_pairs={{32,0},{36,4},{40,8},{44,12},{48,16},{52,20},{56,24},{60,28},{64,3... | collective-permute-start | bytes 786440 | tf_op jit(solution)/shard_map/ppermute | solution.py:30
  196.5 10.5 %collective-permute-start.11 = (f32[4,128,128]{2,1,0:T(8,128)S(1)}, f32[4,128,128]{2,1,0:T(8,128)S(1)}, u32[]{:S(2)}, u32[]{:S(2)}) collective-permute-start(f32[4,128,128]{2,1,0:T(8,128)S(1)} %add.133), channel_id=1, source_target_pairs={{64,0},{68,4},{72,8},{76,12},{80,16},{84,20},{88,24},{92,28},{96,3... | collective-permute-start | bytes 786440 | tf_op jit(solution)/shard_map/ppermute | solution.py:30
  207.1 8.6 %collective-permute-start.12 = (f32[4,128,128]{2,1,0:T(8,128)S(1)}, f32[4,128,128]{2,1,0:T(8,128)S(1)}, u32[]{:S(2)}, u32[]{:S(2)}) collective-permute-start(f32[4,128,128]{2,1,0:T(8,128)S(1)} %add.135), channel_id=1, source_target_pairs={{128,0},{132,4},{136,8},{140,12},{144,16},{148,20},{152,24},{156,2... | collective-permute-start | bytes 786440 | tf_op jit(solution)/shard_map/ppermute | solution.py:30
  216.9 7.3 %collective-permute-start.13 = (f32[4,128,128]{2,1,0:T(8,128)S(1)}, f32[4,128,128]{2,1,0:T(8,128)}, u32[]{:S(2)}, u32[]{:S(2)}) collective-permute-start(f32[4,128,128]{2,1,0:T(8,128)S(1)} %add_add_fusion), channel_id=1, source_target_pairs={{0,4},{4,0},{8,12},{12,8},{16,20},{20,16},{24,28},{28,24},{32,36},... | collective-permute-start | bytes 786440 | tf_op jit(solution)/shard_map/ppermute | solution.py:34
  (5 other events, 42.8 us)
Sparse Core Ops, SparseCore 0:
  86.9 25.0 all-gather.1
  125.2 25.8 reduce-scatter.1

commit v3 on v2

--- a/solution.py
+++ b/solution.py
@@ -65,12 +65,23 @@
     root_mean = jnp.sqrt(jnp.mean(raw_out * raw_out, axis=-1, keepdims=True) + norm_eps)
     normed = raw_out / root_mean
     hidden = normed.astype(jnp.bfloat16).reshape(rows_here, width_here)
-    log_rate = jnp.dot(
-        lax.all_gather(hidden, "head", axis=1, tiled=True),
-        hazard_weight,
-        preferred_element_type=f32,
-    )
-    offset = lax.axis_index("head") * tasks_here
+    head_count = lax.axis_size("head")
+    head_index = lax.axis_index("head")
+
+    def shifted(x, k):
+        return lax.ppermute(x, "head", [(m, (m + k) % head_count) for m in range(head_count)])
+
+    def weight_rows(owner):
+        return lax.dynamic_slice_in_dim(hazard_weight, owner * width_here, width_here, 0)
+
+    log_rate = jnp.dot(hidden, weight_rows(head_index), preferred_element_type=f32)
+    for k in range(1, head_count):
+        log_rate = log_rate + jnp.dot(
+            shifted(hidden, k),
+            weight_rows((head_index - k + head_count) % head_count),
+            preferred_element_type=f32,
+        )
+    offset = head_index * tasks_here
     cum_base = jnp.cumsum(jnp.exp(log_base), axis=0)
     bin_hot = (time_bin[:, None] == jnp.arange(BINS, dtype=jnp.int32)[None, :]).astype(f32)
     base_rows = jnp.dot(bin_hot, log_base, precision=highest)
@@ -83,13 +94,17 @@
         label_hit * (log_rate + base_rows), axis=1
     )
     dlogit = (grad_scale * (hazard - event_flag[:, None] * label_hit)).astype(jnp.bfloat16)
-    term_full = lax.dot_general(
-        dlogit, hazard_weight, (((1,), (1,)), ((), ())), preferred_element_type=f32
-    )
-    grad_hidden = lax.psum_scatter(
-        term_full.astype(jnp.bfloat16), "head", scatter_dimension=1, tiled=True
-    ).astype(f32)
-    event_loss = lax.psum(partial_value, "head")
+    def block_term(owner):
+        return lax.dot_general(
+            dlogit, weight_rows(owner), (((1,), (1,)), ((), ())), preferred_element_type=f32
+        )
+
+    grad_hidden = block_term(head_index)
+    event_loss = partial_value
+    for k in range(1, head_count):
+        sent = block_term((head_index + k) % head_count).astype(jnp.bfloat16)
+        grad_hidden = grad_hidden + shifted(sent, k).astype(f32)
+        event_loss = event_loss + shifted(partial_value, k)
     grad_norm_in = grad_hidden.reshape(shape_three)
     grad_raw = (
         grad_norm_in - normed * jnp.mean(normed * grad_norm_in, axis=-1, keepdims=True)

time: 240 us -> 197 us (0.82)
  the two profiles are of different devices: /device:TPU:1 before, /device:TPU:225 now
where the time goes in v3:
time: 197 us; the launch traced here: 196 us
  waiting for transfers between devices  119 us (60%)
  starting transfers between devices  42.2 us (21%)
  matrix products  24.6 us (12%)
  local copies, waits for them, and re-layouts  7.19 us (4%)
  other arithmetic  2.05 us (1%)
    ppermute x10, waiting for transfers between devices, exclusive_scan(): arrived = lax.ppermute(inclusive, axis, pairs)  97.2 us
    ppermute x10, starting transfers between devices, exclusive_scan(): arrived = lax.ppermute(inclusive, axis, pairs)  21.7 us
    ppermute x9, waiting for transfers between devices, shifted(): lax.ppermute(x, 'head', [(m, (m + k) % head_count) for m in range(head_co...  18.6 us
    ppermute x9, starting transfers between devices, shifted(): lax.ppermute(x, 'head', [(m, (m + k) % head_count) for m in range(head_co...  11.7 us
    ppermute x2, starting transfers between devices, exclusive_scan(): partner = lax.ppermute(exclusive, axis, pair)  6.67 us
    dot_general x3, matrix products, body(): jnp.dot(shifted(hidden, k), weight_rows((head_index - k + head_count) % h...  6.31 us
    dot_general x4, matrix products, block_term(): lax.dot_general(dlogit, weight_rows(owner), (((1,), (1,)), ((), ())), pre...  5.82 us
    unnamed x26, local copies, waits for them, and re-layouts  4.81 us
  transfers between devices with their start and end apart: 23, of which 19 were waited for; matrix products, arithmetic and copies ran while one was open for 9% of the time, Pallas kernels for 0%

profile of v3, /device:TPU:225, one launch (start us, length us, event | category | flops | bytes accessed | tf_op | source)
XLA Modules:
  0.0 196.2 jit_solution(12192493504789772732)
XLA Ops:
  7.4 7.5 %collective-permute-done.1 = f32[4,128,128]{2,1,0:T(8,128)S(1)} collective-permute-done((f32[4,128,128]{2,1,0:T(8,128)S(1)}, f32[4,128,128]{2,1,0:T(8,128)S(1)}, u32[]{:S(2)}, u32[]{:S(2)}) %collective-permute-start.1) | collective-permute-done | bytes 262176 | tf_op jit(solution)/shard_map/ppermute | solution.py:30
  16.8 11.4 %collective-permute-done.2 = f32[4,128,128]{2,1,0:T(8,128)S(1)} collective-permute-done((f32[4,128,128]{2,1,0:T(8,128)S(1)}, f32[4,128,128]{2,1,0:T(8,128)S(1)}, u32[]{:S(2)}, u32[]{:S(2)}) %collective-permute-start.2) | collective-permute-done | bytes 262176 | tf_op jit(solution)/shard_map/ppermute | solution.py:30
  28.3 4.0 %collective-permute-start.3 = (f32[4,128,128]{2,1,0:T(8,128)S(1)}, f32[4,128,128]{2,1,0:T(8,128)S(1)}, u32[]{:S(2)}, u32[]{:S(2)}) collective-permute-start(f32[4,128,128]{2,1,0:T(8,128)S(1)} %add.187), channel_id=1, source_target_pairs={{0,32},{4,36},{8,40},{12,44},{16,48},{20,52},{24,56},{28,60},{32,6... | collective-permute-start | bytes 786440 | tf_op jit(solution)/shard_map/ppermute | solution.py:30
  32.4 14.9 %collective-permute-done.3 = f32[4,128,128]{2,1,0:T(8,128)S(1)} collective-permute-done((f32[4,128,128]{2,1,0:T(8,128)S(1)}, f32[4,128,128]{2,1,0:T(8,128)S(1)}, u32[]{:S(2)}, u32[]{:S(2)}) %collective-permute-start.3) | collective-permute-done | bytes 262176 | tf_op jit(solution)/shard_map/ppermute | solution.py:30
  47.3 3.2 %collective-permute-start.4 = (f32[4,128,128]{2,1,0:T(8,128)S(1)}, f32[4,128,128]{2,1,0:T(8,128)S(1)}, u32[]{:S(2)}, u32[]{:S(2)}) collective-permute-start(f32[4,128,128]{2,1,0:T(8,128)S(1)} %add.189), channel_id=1, source_target_pairs={{0,64},{4,68},{8,72},{12,76},{16,80},{20,84},{24,88},{28,92},{32,9... | collective-permute-start | bytes 786440 | tf_op jit(solution)/shard_map/ppermute | solution.py:30
  50.5 5.1 %collective-permute-done.4 = f32[4,128,128]{2,1,0:T(8,128)S(1)} collective-permute-done((f32[4,128,128]{2,1,0:T(8,128)S(1)}, f32[4,128,128]{2,1,0:T(8,128)S(1)}, u32[]{:S(2)}, u32[]{:S(2)}) %collective-permute-start.4) | collective-permute-done | bytes 262176 | tf_op jit(solution)/shard_map/ppermute | solution.py:30
  55.7 2.3 %collective-permute-start.5 = (f32[4,128,128]{2,1,0:T(8,128)S(1)}, f32[4,128,128]{2,1,0:T(8,128)S(1)}, u32[]{:S(2)}, u32[]{:S(2)}) collective-permute-start(f32[4,128,128]{2,1,0:T(8,128)S(1)} %add.191), channel_id=1, source_target_pairs={{0,128},{4,132},{8,136},{12,140},{16,144},{20,148},{24,152},{28,15... | collective-permute-start | bytes 786440 | tf_op jit(solution)/shard_map/ppermute | solution.py:30
  58.0 3.3 %collective-permute-done.5 = f32[4,128,128]{2,1,0:T(8,128)S(1)} collective-permute-done((f32[4,128,128]{2,1,0:T(8,128)S(1)}, f32[4,128,128]{2,1,0:T(8,128)S(1)}, u32[]{:S(2)}, u32[]{:S(2)}) %collective-permute-start.5) | collective-permute-done | bytes 262176 | tf_op jit(solution)/shard_map/ppermute | solution.py:30
  61.3 4.6 %collective-permute-start.6 = (f32[4,128,128]{2,1,0:T(8,128)S(1)}, f32[4,128,128]{2,1,0:T(8,128)S(1)}, u32[]{:S(2)}, u32[]{:S(2)}) collective-permute-start(f32[4,128,128]{2,1,0:T(8,128)S(1)} %add_add_fusion.1), channel_id=1, source_target_pairs={{0,4},{4,0},{8,12},{12,8},{16,20},{20,16},{24,28},{28,24},{32,36},... | collective-permute-start | bytes 786440 | tf_op jit(solution)/shard_map/ppermute | solution.py:34
  68.6 2.8 %collective-permute-start.8 = (bf16[128,1024]{0,1:T(8,128)(2,1)S(1)}, bf16[128,1024]{0,1:T(8,128)(2,1)}, u32[]{:S(2)}, u32[]{:S(2)}) collective-permute-start(bf16[128,1024]{0,1:T(8,128)(2,1)S(1)} %bitcast.116), channel_id=1, source_target_pairs={{0,2},{1,3},{2,0},{3,1},{4,6},{5,7},{6,4},{7,5},{8,10},{9,11},{10,... | collective-permute-start | bytes 786440 | tf_op jit(solution)/shard_map/ppermute | solution.py:72
  78.2 2.2 %fusion.6 = f32[128,1024]{1,0:T(8,128)S(1)} fusion(bf16[128,1024]{0,1:T(8,128)(2,1)} %collective-permute-done.8, bf16[4096,1024]{1,0:T(8,128)(2,1)} %param.11, s32[]{:T(128)S(6)} %select_n.90), kind=kOutput, calls=%fused_computation.6 | convolution fusion | flops 268435456 | bytes 2883588 | tf_op jit(solution)/shard_map/dot_general | solution.py:79
  80.4 3.5 %collective-permute-done.9 = bf16[128,1024]{0,1:T(8,128)(2,1)S(1)} collective-permute-done((bf16[128,1024]{0,1:T(8,128)(2,1)S(1)}, bf16[128,1024]{0,1:T(8,128)(2,1)S(1)}, u32[]{:S(2)}, u32[]{:S(2)}) %collective-permute-start.9) | collective-permute-done | bytes 262176 | tf_op jit(solution)/shard_map/ppermute | solution.py:72
  85.9 2.1 %fusion.26 = f32[128,1024]{1,0:T(8,128)S(1)} fusion(f32[128,1024]{1,0:T(8,128)S(1)} %fusion.2, f32[128,1024]{1,0:T(8,128)S(1)} %fusion.6, f32[128,1024]{1,0:T(8,128)S(1)} %fusion.14, bf16[128,1024]{0,1:T(8,128)(2,1)S(1)} %collective-permute-done.7, bf16[4096,1024]{1,0:T(8,128)(2,1)} %param.11, s32[]{:T(128)S(6)} %select_n.88), kind=kOutput, calls=%fused_computation.32 | convolution fusion | flops 268828672 | bytes 4456452 | tf_op jit(solution)/shard_map/dot_general | solution.py:79
  88.6 2.4 %fusion.38 = bf16[128,1024]{1,0:T(8,128)(2,1)S(1)} fusion(bf16[128,1024]{1,0:T(8,128)(2,1)S(1)} %get-tuple-element.9, bf16[4096,1024]{1,0:T(8,128)(2,1)} %param.11, s32[]{:T(128)S(6)} %select_n.92), kind=kOutput, calls=%fused_computation.39 | convolution fusion | flops 268566528 | bytes 2621444 | tf_op jit(solution)/shard_map/dot_general | solution.py:98
  94.3 2.5 %collective-permute-start.11 = (bf16[128,1024]{1,0:T(8,128)(2,1)S(1)}, bf16[128,1024]{1,0:T(8,128)(2,1)S(1)}, u32[]{:S(2)}, u32[]{:S(2)}) collective-permute-start(bf16[128,1024]{1,0:T(8,128)(2,1)S(1)} %fusion.35), channel_id=1, source_target_pairs={{0,2},{1,3},{2,0},{3,1},{4,6},{5,7},{6,4},{7,5},{8,10},{9,11},{10,... | collective-permute-start | bytes 786440 | tf_op jit(solution)/shard_map/ppermute | solution.py:72
  96.8 4.4 %collective-permute-done.10 = bf16[128,1024]{1,0:T(8,128)(2,1)S(1)} collective-permute-done((bf16[128,1024]{1,0:T(8,128)(2,1)S(1)}, bf16[128,1024]{1,0:T(8,128)(2,1)S(1)}, u32[]{:S(2)}, u32[]{:S(2)}) %collective-permute-start.10) | collective-permute-done | bytes 262176 | tf_op jit(solution)/shard_map/ppermute | solution.py:72
  101.2 7.2 %collective-permute-done.11 = bf16[128,1024]{1,0:T(8,128)(2,1)S(1)} collective-permute-done((bf16[128,1024]{1,0:T(8,128)(2,1)S(1)}, bf16[128,1024]{1,0:T(8,128)(2,1)S(1)}, u32[]{:S(2)}, u32[]{:S(2)}) %collective-permute-start.11) | collective-permute-done | bytes 262176 | tf_op jit(solution)/shard_map/ppermute | solution.py:72
  116.7 14.1 %collective-permute-done.14 = f32[4,128,128]{2,1,0:T(8,128)S(1)} collective-permute-done((f32[4,128,128]{2,1,0:T(8,128)S(1)}, f32[4,128,128]{2,1,0:T(8,128)S(1)}, u32[]{:S(2)}, u32[]{:S(2)}) %collective-permute-start.14) | collective-permute-done | bytes 262176 | tf_op jit(solution)/shard_map/ppermute | solution.py:30
  134.4 12.9 %collective-permute-done.15 = f32[4,128,128]{2,1,0:T(8,128)S(1)} collective-permute-done((f32[4,128,128]{2,1,0:T(8,128)S(1)}, f32[4,128,128]{2,1,0:T(8,128)S(1)}, u32[]{:S(2)}, u32[]{:S(2)}) %collective-permute-start.15) | collective-permute-done | bytes 262176 | tf_op jit(solution)/shard_map/ppermute | solution.py:30
  149.9 2.5 %collective-permute-start.21 = (f32[128]{0:T(128)S(1)}, f32[128]{0:T(128)S(1)}, u32[]{:S(2)}, u32[]{:S(2)}) collective-permute-start(f32[128]{0:T(128)S(1)} %multiply_subtract_fusion), channel_id=1, source_target_pairs={{0,2},{1,3},{2,0},{3,1},{4,6},{5,7},{6,4},{7,5},{8,10},{9,11},{10,... | collective-permute-start | bytes 1544 | tf_op jit(solution)/shard_map/ppermute | solution.py:72
  155.3 11.6 %collective-permute-done.16 = f32[4,128,128]{2,1,0:T(8,128)S(1)} collective-permute-done((f32[4,128,128]{2,1,0:T(8,128)S(1)}, f32[4,128,128]{2,1,0:T(8,128)S(1)}, u32[]{:S(2)}, u32[]{:S(2)}) %collective-permute-start.16) | collective-permute-done | bytes 262176 | tf_op jit(solution)/shard_map/ppermute | solution.py:30
  169.0 9.7 %collective-permute-done.17 = f32[4,128,128]{2,1,0:T(8,128)S(1)} collective-permute-done((f32[4,128,128]{2,1,0:T(8,128)S(1)}, f32[4,128,128]{2,1,0:T(8,128)S(1)}, u32[]{:S(2)}, u32[]{:S(2)}) %collective-permute-start.17) | collective-permute-done | bytes 262176 | tf_op jit(solution)/shard_map/ppermute | solution.py:30
  180.1 2.1 %fusion.31 = bf16[128,8,128]{0,2,1:T(8,128)(2,1)} fusion(f32[128,8,128]{0,2,1:T(8,128)S(1)} %convolution_bitcast_fusion.4, bf16[128,8,128]{0,2,1:T(8,128)(2,1)S(1)} %divide_convert_fusion, f32[4,128,128]{2,1,0:T(8,128)} %copy-done.3, f32[4,128,128]{2,1,0:T(8,128)S(1)} %add_add_fusion.1, f32[8,128,128]{2,1,0:T(8,128)S(1)} %collective-permute-done, ...), kind=kOutput, calls=%fused_computation.36 | convolution fusion | flops 101580800 | bytes 2097154 | tf_op jit(solution)/shard_map/the,hde->thd/dot_general | solution.py:121
  182.2 6.8 %collective-permute-done.18 = f32[4,128,128]{2,1,0:T(8,128)S(1)} collective-permute-done((f32[4,128,128]{2,1,0:T(8,128)S(1)}, f32[4,128,128]{2,1,0:T(8,128)S(1)}, u32[]{:S(2)}, u32[]{:S(2)}) %collective-permute-start.18) | collective-permute-done | bytes 262176 | tf_op jit(solution)/shard_map/ppermute | solution.py:30
  (97 shorter events, 52.1 us)
Async XLA Ops:
  3.1 2.3 %collective-permute-start = (f32[8,128,128]{2,1,0:T(8,128)S(1)}, f32[8,128,128]{2,1,0:T(8,128)S(1)}, u32[]{:S(2)}, u32[]{:S(2)}) collective-permute-start(f32[8,128,128]{2,1,0:T(8,128)S(1)} %fusion.50), channel_id=1, source_target_pairs={{0,4},{4,0},{8,12},{12,8},{16,20},{20,16},{24,28},{28,24},{32,36},... | collective-permute-start | bytes 1572872 | tf_op jit(solution)/shard_map/ppermute | solution.py:18
  5.5 9.4 %collective-permute-start.1 = (f32[4,128,128]{2,1,0:T(8,128)S(1)}, f32[4,128,128]{2,1,0:T(8,128)S(1)}, u32[]{:S(2)}, u32[]{:S(2)}) collective-permute-start(f32[4,128,128]{2,1,0:T(8,128)S(1)} %dynamic-slice_add_fusion.1), channel_id=1, source_target_pairs={{0,8},{4,12},{8,16},{12,20},{16,24},{20,28},{24,32},{28,36},{32,40... | collective-permute-start | bytes 786440 | tf_op jit(solution)/shard_map/ppermute | solution.py:30
  14.9 13.4 %collective-permute-start.2 = (f32[4,128,128]{2,1,0:T(8,128)S(1)}, f32[4,128,128]{2,1,0:T(8,128)S(1)}, u32[]{:S(2)}, u32[]{:S(2)}) collective-permute-start(f32[4,128,128]{2,1,0:T(8,128)S(1)} %add.185), channel_id=1, source_target_pairs={{0,16},{4,20},{8,24},{12,28},{16,32},{20,36},{24,40},{28,44},{32,4... | collective-permute-start | bytes 786440 | tf_op jit(solution)/shard_map/ppermute | solution.py:30
  28.3 18.9 %collective-permute-start.3 = (f32[4,128,128]{2,1,0:T(8,128)S(1)}, f32[4,128,128]{2,1,0:T(8,128)S(1)}, u32[]{:S(2)}, u32[]{:S(2)}) collective-permute-start(f32[4,128,128]{2,1,0:T(8,128)S(1)} %add.187), channel_id=1, source_target_pairs={{0,32},{4,36},{8,40},{12,44},{16,48},{20,52},{24,56},{28,60},{32,6... | collective-permute-start | bytes 786440 | tf_op jit(solution)/shard_map/ppermute | solution.py:30
  47.3 8.4 %collective-permute-start.4 = (f32[4,128,128]{2,1,0:T(8,128)S(1)}, f32[4,128,128]{2,1,0:T(8,128)S(1)}, u32[]{:S(2)}, u32[]{:S(2)}) collective-permute-start(f32[4,128,128]{2,1,0:T(8,128)S(1)} %add.189), channel_id=1, source_target_pairs={{0,64},{4,68},{8,72},{12,76},{16,80},{20,84},{24,88},{28,92},{32,9... | collective-permute-start | bytes 786440 | tf_op jit(solution)/shard_map/ppermute | solution.py:30
  55.7 5.6 %collective-permute-start.5 = (f32[4,128,128]{2,1,0:T(8,128)S(1)}, f32[4,128,128]{2,1,0:T(8,128)S(1)}, u32[]{:S(2)}, u32[]{:S(2)}) collective-permute-start(f32[4,128,128]{2,1,0:T(8,128)S(1)} %add.191), channel_id=1, source_target_pairs={{0,128},{4,132},{8,136},{12,140},{16,144},{20,148},{24,152},{28,15... | collective-permute-start | bytes 786440 | tf_op jit(solution)/shard_map/ppermute | solution.py:30
  61.3 6.5 %collective-permute-start.6 = (f32[4,128,128]{2,1,0:T(8,128)S(1)}, f32[4,128,128]{2,1,0:T(8,128)S(1)}, u32[]{:S(2)}, u32[]{:S(2)}) collective-permute-start(f32[4,128,128]{2,1,0:T(8,128)S(1)} %add_add_fusion.1), channel_id=1, source_target_pairs={{0,4},{4,0},{8,12},{12,8},{16,20},{20,16},{24,28},{28,24},{32,36},... | collective-permute-start | bytes 786440 | tf_op jit(solution)/shard_map/ppermute | solution.py:34
  68.6 9.6 %collective-permute-start.8 = (bf16[128,1024]{0,1:T(8,128)(2,1)S(1)}, bf16[128,1024]{0,1:T(8,128)(2,1)}, u32[]{:S(2)}, u32[]{:S(2)}) collective-permute-start(bf16[128,1024]{0,1:T(8,128)(2,1)S(1)} %bitcast.116), channel_id=1, source_target_pairs={{0,2},{1,3},{2,0},{3,1},{4,6},{5,7},{6,4},{7,5},{8,10},{9,11},{10,... | collective-permute-start | bytes 786440 | tf_op jit(solution)/shard_map/ppermute | solution.py:72
  73.2 10.7 %collective-permute-start.9 = (bf16[128,1024]{0,1:T(8,128)(2,1)S(1)}, bf16[128,1024]{0,1:T(8,128)(2,1)S(1)}, u32[]{:S(2)}, u32[]{:S(2)}) collective-permute-start(bf16[128,1024]{0,1:T(8,128)(2,1)S(1)} %bitcast.117), channel_id=1, source_target_pairs={{0,3},{1,0},{2,1},{3,2},{4,7},{5,4},{6,5},{7,6},{8,11},{9,8},{10,9... | collective-permute-start | bytes 786440 | tf_op jit(solution)/shard_map/ppermute | solution.py:72
  74.0 11.9 %collective-permute-start.7 = (bf16[128,1024]{0,1:T(8,128)(2,1)S(1)}, bf16[128,1024]{0,1:T(8,128)(2,1)S(1)}, u32[]{:S(2)}, u32[]{:S(2)}) collective-permute-start(bf16[128,1024]{0,1:T(8,128)(2,1)S(1)} %bitcast.118), channel_id=1, source_target_pairs={{0,1},{1,2},{2,3},{3,0},{4,5},{5,6},{6,7},{7,4},{8,9},{9,10},{10,1... | collective-permute-start | bytes 786440 | tf_op jit(solution)/shard_map/ppermute | solution.py:72
  92.8 8.3 %collective-permute-start.10 = (bf16[128,1024]{1,0:T(8,128)(2,1)S(1)}, bf16[128,1024]{1,0:T(8,128)(2,1)S(1)}, u32[]{:S(2)}, u32[]{:S(2)}) collective-permute-start(bf16[128,1024]{1,0:T(8,128)(2,1)S(1)} %fusion.38), channel_id=1, source_target_pairs={{0,1},{1,2},{2,3},{3,0},{4,5},{5,6},{6,7},{7,4},{8,9},{9,10},{10,1... | collective-permute-start | bytes 786440 | tf_op jit(solution)/shard_map/ppermute | solution.py:72
  94.3 14.0 %collective-permute-start.11 = (bf16[128,1024]{1,0:T(8,128)(2,1)S(1)}, bf16[128,1024]{1,0:T(8,128)(2,1)S(1)}, u32[]{:S(2)}, u32[]{:S(2)}) collective-permute-start(bf16[128,1024]{1,0:T(8,128)(2,1)S(1)} %fusion.35), channel_id=1, source_target_pairs={{0,2},{1,3},{2,0},{3,1},{4,6},{5,7},{6,4},{7,5},{8,10},{9,11},{10,... | collective-permute-start | bytes 786440 | tf_op jit(solution)/shard_map/ppermute | solution.py:72
  96.8 11.6 %collective-permute-start.12 = (bf16[128,1024]{1,0:T(8,128)(2,1)S(1)}, bf16[128,1024]{1,0:T(8,128)(2,1)S(1)}, u32[]{:S(2)}, u32[]{:S(2)}) collective-permute-start(bf16[128,1024]{1,0:T(8,128)(2,1)S(1)} %fusion.32), channel_id=1, source_target_pairs={{0,3},{1,0},{2,1},{3,2},{4,7},{5,4},{6,5},{7,6},{8,11},{9,8},{10,9... | collective-permute-start | bytes 786440 | tf_op jit(solution)/shard_map/ppermute | solution.py:72
  111.2 82.3 %copy-start.2 = (bf16[128,1024]{1,0:T(8,128)(2,1)S(1)}, bf16[128,1024]{1,0:T(8,128)(2,1)}, u32[]{:S(2)}) copy-start(bf16[128,1024]{1,0:T(8,128)(2,1)} %param.9) | copy-start | bytes 786436
  111.8 2.9 %collective-permute-start.13 = (f32[8,128,128]{2,1,0:T(8,128)S(1)}, f32[8,128,128]{2,1,0:T(8,128)S(1)}, u32[]{:S(2)}, u32[]{:S(2)}) collective-permute-start(f32[8,128,128]{2,1,0:T(8,128)S(1)} %convolution_bitcast_fusion.1), channel_id=1, source_target_pairs={{0,4},{4,0},{8,12},{12,8},{16,20},{20,16},{24,28},{28,24},{32,36},... | collective-permute-start | bytes 1572872 | tf_op jit(solution)/shard_map/ppermute | solution.py:18
  114.8 16.0 %collective-permute-start.14 = (f32[4,128,128]{2,1,0:T(8,128)S(1)}, f32[4,128,128]{2,1,0:T(8,128)S(1)}, u32[]{:S(2)}, u32[]{:S(2)}) collective-permute-start(f32[4,128,128]{2,1,0:T(8,128)S(1)} %dynamic-slice_add_fusion), channel_id=1, source_target_pairs={{8,0},{12,4},{16,8},{20,12},{24,16},{28,20},{32,24},{36,28},{40,32... | collective-permute-start | bytes 786440 | tf_op jit(solution)/shard_map/ppermute | solution.py:30
  130.8 16.4 %collective-permute-start.15 = (f32[4,128,128]{2,1,0:T(8,128)S(1)}, f32[4,128,128]{2,1,0:T(8,128)S(1)}, u32[]{:S(2)}, u32[]{:S(2)}) collective-permute-start(f32[4,128,128]{2,1,0:T(8,128)S(1)} %add.217), channel_id=1, source_target_pairs={{16,0},{20,4},{24,8},{28,12},{32,16},{36,20},{40,24},{44,28},{48,3... | collective-permute-start | bytes 786440 | tf_op jit(solution)/shard_map/ppermute | solution.py:30
  147.3 19.5 %collective-permute-start.16 = (f32[4,128,128]{2,1,0:T(8,128)S(1)}, f32[4,128,128]{2,1,0:T(8,128)S(1)}, u32[]{:S(2)}, u32[]{:S(2)}) collective-permute-start(f32[4,128,128]{2,1,0:T(8,128)S(1)} %add.219), channel_id=1, source_target_pairs={{32,0},{36,4},{40,8},{44,12},{48,16},{52,20},{56,24},{60,28},{64,3... | collective-permute-start | bytes 786440 | tf_op jit(solution)/shard_map/ppermute | solution.py:30
  149.2 3.7 %collective-permute-start.20 = (f32[128]{0:T(128)S(1)}, f32[128]{0:T(128)S(1)}, u32[]{:S(2)}, u32[]{:S(2)}) collective-permute-start(f32[128]{0:T(128)S(1)} %multiply_subtract_fusion), channel_id=1, source_target_pairs={{0,1},{1,2},{2,3},{3,0},{4,5},{5,6},{6,7},{7,4},{8,9},{9,10},{10,1... | collective-permute-start | bytes 1544 | tf_op jit(solution)/shard_map/ppermute | solution.py:72
  149.9 3.9 %collective-permute-start.21 = (f32[128]{0:T(128)S(1)}, f32[128]{0:T(128)S(1)}, u32[]{:S(2)}, u32[]{:S(2)}) collective-permute-start(f32[128]{0:T(128)S(1)} %multiply_subtract_fusion), channel_id=1, source_target_pairs={{0,2},{1,3},{2,0},{3,1},{4,6},{5,7},{6,4},{7,5},{8,10},{9,11},{10,... | collective-permute-start | bytes 1544 | tf_op jit(solution)/shard_map/ppermute | solution.py:72
  152.4 2.4 %collective-permute-start.22 = (f32[128]{0:T(128)S(1)}, f32[128]{0:T(128)S(1)}, u32[]{:S(2)}, u32[]{:S(2)}) collective-permute-start(f32[128]{0:T(128)S(1)} %multiply_subtract_fusion), channel_id=1, source_target_pairs={{0,3},{1,0},{2,1},{3,2},{4,7},{5,4},{6,5},{7,6},{8,11},{9,8},{10,9... | collective-permute-start | bytes 1544 | tf_op jit(solution)/shard_map/ppermute | solution.py:72
  166.9 11.8 %collective-permute-start.17 = (f32[4,128,128]{2,1,0:T(8,128)S(1)}, f32[4,128,128]{2,1,0:T(8,128)S(1)}, u32[]{:S(2)}, u32[]{:S(2)}) collective-permute-start(f32[4,128,128]{2,1,0:T(8,128)S(1)} %add.221), channel_id=1, source_target_pairs={{64,0},{68,4},{72,8},{76,12},{80,16},{84,20},{88,24},{92,28},{96,3... | collective-permute-start | bytes 786440 | tf_op jit(solution)/shard_map/ppermute | solution.py:30
  178.8 10.2 %collective-permute-start.18 = (f32[4,128,128]{2,1,0:T(8,128)S(1)}, f32[4,128,128]{2,1,0:T(8,128)S(1)}, u32[]{:S(2)}, u32[]{:S(2)}) collective-permute-start(f32[4,128,128]{2,1,0:T(8,128)S(1)} %add.223), channel_id=1, source_target_pairs={{128,0},{132,4},{136,8},{140,12},{144,16},{148,20},{152,24},{156,2... | collective-permute-start | bytes 786440 | tf_op jit(solution)/shard_map/ppermute | solution.py:30
  189.0 4.5 %collective-permute-start.19 = (f32[4,128,128]{2,1,0:T(8,128)S(1)}, f32[4,128,128]{2,1,0:T(8,128)S(1)}, u32[]{:S(2)}, u32[]{:S(2)}) collective-permute-start(f32[4,128,128]{2,1,0:T(8,128)S(1)} %add_add_fusion), channel_id=1, source_target_pairs={{0,4},{4,0},{8,12},{12,8},{16,20},{20,16},{24,28},{28,24},{32,36},... | collective-permute-start | bytes 786440 | tf_op jit(solution)/shard_map/ppermute | solution.py:34
  (10 other events, 308.6 us)

commit v4 on v3

--- a/solution.py
+++ b/solution.py
@@ -1,43 +1,130 @@
+import functools
+
 import jax
 import jax.numpy as jnp
 from jax import lax
+from jax.experimental import pallas as pl
+from jax.experimental.pallas import tpu as pltpu
 from jax.sharding import PartitionSpec as P
 
 HEAD_DIM = 128
 BINS = 32
+MESH = pl.DeviceIdType.MESH
 
 
 norm_eps = 1e-06
 grad_scale = 64.0
 
 
+def scan_kernel(reverse, count, state_ref, out_ref, other, inclusive, arrived, exclusive, partner,
+                send_sems, recv_sems):
+    me = lax.axis_index("seq")
+    head = lax.axis_index("head")
+    core = me % 2
+    mate = me + 1 - 2 * core
+    half = exclusive.shape[0]
+    distances = []
+    distance = 2
+    while distance < count:
+        distances.append(distance)
+        distance *= 2
+    step = -1 if reverse else 1
+    targets = [me + step * d for d in distances]
+    sources = [me - step * d for d in distances]
+    sends = [(t >= 0) & (t < count) for t in targets]
+    receives = [(s >= 0) & (s < count) for s in sources]
+
+    barrier = pltpu.get_barrier_semaphore()
+    pl.semaphore_signal(barrier, 1, device_id=(mate, head), device_id_type=MESH)
+    expected = jnp.int32(1)
+    for target, source, send, receive in zip(targets, sources, sends, receives):
+        @pl.when(send)
+        def _():
+            pl.semaphore_signal(barrier, 1, device_id=(target, head), device_id_type=MESH)
+
+        @pl.when(receive)
+        def _():
+            pl.semaphore_signal(barrier, 1, device_id=(source, head), device_id_type=MESH)
+
+        expected = expected + send.astype(jnp.int32) + receive.astype(jnp.int32)
+    pl.semaphore_wait(barrier, expected)
+
+    swap = pltpu.make_async_remote_copy(
+        state_ref, other, send_sems.at[0], recv_sems.at[0], device_id=(mate, head), device_id_type=MESH
+    )
+    swap.start()
+    swap.wait()
+    mine = pl.ds(core * half, half)
+    inclusive[0] = state_ref[mine] + other[mine]
+    exclusive[...] = jnp.zeros_like(exclusive)
+    copies = []
+    for r, (target, send, receive) in enumerate(zip(targets, sends, receives)):
+        copy = pltpu.make_async_remote_copy(
+            inclusive.at[r], arrived.at[r], send_sems.at[r + 1], recv_sems.at[r + 1],
+            device_id=(target, head), device_id_type=MESH,
+        )
+        copies.append(copy)
+
+        @pl.when(send)
+        def _():
+            copy.start()
+
+        @pl.when(receive)
+        def _():
+            copy.wait_recv()
+            got = arrived[r]
+            inclusive[r + 1] = inclusive[r] + got
+            exclusive[...] = exclusive[...] + got
+
+        @pl.when(jnp.logical_not(receive))
+        def _():
+            inclusive[r + 1] = inclusive[r]
+
+    last = len(distances) + 1
+    back = pltpu.make_async_remote_copy(
+        exclusive, partner, send_sems.at[last], recv_sems.at[last], device_id=(mate, head), device_id_type=MESH
+    )
+    back.start()
+    for copy, send in zip(copies, sends):
+        @pl.when(send)
+        def _():
+            copy.wait_send()
+    back.wait()
+    theirs = pl.ds((1 - core) * half, half)
+    take_other = (core == 0) if reverse else (core == 1)
+
+    @pl.when(take_other)
+    def _():
+        out_ref[mine] = exclusive[...] + other[mine]
+        out_ref[theirs] = partner[...] + other[theirs]
+
+    @pl.when(jnp.logical_not(take_other))
+    def _():
+        out_ref[mine] = exclusive[...]
+        out_ref[theirs] = partner[...]
+
+
 def exclusive_scan(shard, axis, reverse=False):
     count = lax.axis_size(axis)
-    core = lax.axis_index(axis) % 2
-    pair = [(i, i ^ 1) for i in range(count)]
-    other = lax.ppermute(shard, axis, pair)
-    keep_other = (core == 0) if reverse else (core == 1)
-    within = jnp.where(keep_other, other, jnp.zeros_like(other))
-    half = shard.shape[0] // 2
-    inclusive = lax.dynamic_slice_in_dim(shard + other, core * half, half, 0)
-    exclusive = jnp.zeros_like(inclusive)
-    distance = 2
-    while distance < count:
-        if reverse:
-            pairs = [(i, i - distance) for i in range(distance, count)]
-        else:
-            pairs = [(i, i + distance) for i in range(count - distance)]
-        arrived = lax.ppermute(inclusive, axis, pairs)
-        exclusive = exclusive + arrived
-        inclusive = inclusive + arrived
-        distance *= 2
-    partner = lax.ppermute(exclusive, axis, pair)
-    joined = jnp.where(
-        core == 0,
-        jnp.concatenate([exclusive, partner], axis=0),
-        jnp.concatenate([partner, exclusive], axis=0),
-    )
-    return joined + within
+    heads, rows, cols = shard.shape
+    half = heads // 2
+    rounds = max(count.bit_length() - 2, 0)
+    return pl.pallas_call(
+        functools.partial(scan_kernel, reverse, count),
+        out_shape=jax.ShapeDtypeStruct(shard.shape, shard.dtype),
+        in_specs=[pl.BlockSpec(memory_space=pltpu.VMEM)],
+        out_specs=pl.BlockSpec(memory_space=pltpu.VMEM),
+        scratch_shapes=[
+            pltpu.VMEM((heads, rows, cols), shard.dtype),
+            pltpu.VMEM((rounds + 1, half, rows, cols), shard.dtype),
+            pltpu.VMEM((max(rounds, 1), half, rows, cols), shard.dtype),
+            pltpu.VMEM((half, rows, cols), shard.dtype),
+            pltpu.VMEM((half, rows, cols), shard.dtype),
+            pltpu.SemaphoreType.DMA((rounds + 2,)),
+            pltpu.SemaphoreType.DMA((rounds + 2,)),
+        ],
+        compiler_params=pltpu.CompilerParams(collective_id=1 if reverse else 0, has_side_effects=True),
+    )(shard)
 
 
 def body(queries, keys, values, hazard_weight, log_base, time_bin, observed, task_label):

time: 197 us -> 184 us (0.934)
  the two profiles are of different devices: /device:TPU:225 before, /device:TPU:1 now
where the time goes in v4:
time: 184 us
  Pallas kernels  121 us (66%)
  matrix products  28.5 us (15%)
  starting transfers between devices  14.2 us (8%)
  waiting for transfers between devices  12 us (7%)
  local copies, waits for them, and re-layouts  5.13 us (3%)
    pallas_call x2, Pallas kernels, exclusive_scan(): pl.pallas_call(functools.partial(scan_kernel, reverse, count), out_shape=...  121 us
    ppermute x9, starting transfers between devices, shifted(): lax.ppermute(x, 'head', [(m, (m + k) % head_count) for m in range(head_co...  14.2 us
    ppermute x9, waiting for transfers between devices, shifted(): lax.ppermute(x, 'head', [(m, (m + k) % head_count) for m in range(head_co...  12 us
    dot_general x4, matrix products, block_term(): lax.dot_general(dlogit, weight_rows(owner), (((1,), (1,)), ((), ())), pre...  7.44 us
    dot_general x3, matrix products, body(): jnp.dot(shifted(hidden, k), weight_rows((head_index - k + head_count) % h...  6.72 us
  transfers between devices with their start and end apart: 9, of which 4 were waited for; matrix products, arithmetic and copies ran while one was open for 4% of the time, Pallas kernels for 0%

profile of v4, /device:TPU:1, one launch (start us, length us, event | category | flops | bytes accessed | tf_op | source)
XLA Modules:
  0.0 183.5 jit_solution(5273014819932976641)
XLA Ops:
  0.7 1.0 copy.41
  3.0 38.6 %shard_map.111 = f32[8,128,128]{2,1,0:T(8,128)} custom-call(f32[8,128,128]{2,1,0:T(8,128)} %fusion.48.state_ref), custom_call_target="tpu_custom_call" | custom-call | tf_op jit(solution)/shard_map/pallas_call | solution.py:112
  41.6 1.6 convolution_bitcast_fusion.5
  43.2 1.3 convolution_multiply_fusion.1
  45.1 2.7 %collective-permute-start.1 = (bf16[128,1024]{0,1:T(8,128)(2,1)S(1)}, bf16[128,1024]{0,1:T(8,128)(2,1)S(1)}, u32[]{:S(2)}, u32[]{:S(2)}) collective-permute-start(bf16[128,1024]{0,1:T(8,128)(2,1)S(1)} %bitcast.120), channel_id=1, source_target_pairs={{0,2},{1,3},{2,0},{3,1},{4,6},{5,7},{6,4},{7,5},{8,10},{9,11},{10,... | collective-permute-start | bytes 786440 | tf_op jit(solution)/shard_map/ppermute | solution.py:159
  49.3 2.1 %fusion.14 = f32[128,1024]{1,0:T(8,128)S(1)} fusion(bf16[128,1024]{0,1:T(8,128)(2,1)S(1)} %bitcast.123, bf16[4096,1024]{1,0:T(8,128)(2,1)} %param.11, s32[]{:T(128)S(6)} %select_n.48), kind=kOutput, calls=%fused_computation.14 | convolution fusion | flops 268435456 | bytes 2883588 | tf_op jit(solution)/shard_map/dot_general | solution.py:164
  52.9 2.4 %fusion.6 = f32[128,1024]{1,0:T(8,128)S(1)} fusion(bf16[128,1024]{0,1:T(8,128)(2,1)S(1)} %collective-permute-done.1, bf16[4096,1024]{1,0:T(8,128)(2,1)} %param.11, s32[]{:T(128)S(6)} %select_n.52), kind=kOutput, calls=%fused_computation.6 | convolution fusion | flops 268435456 | bytes 2883588 | tf_op jit(solution)/shard_map/dot_general | solution.py:166
  55.4 4.1 %collective-permute-done.2 = bf16[128,1024]{0,1:T(8,128)(2,1)S(1)} collective-permute-done((bf16[128,1024]{0,1:T(8,128)(2,1)S(1)}, bf16[128,1024]{0,1:T(8,128)(2,1)S(1)}, u32[]{:S(2)}, u32[]{:S(2)}) %collective-permute-start.2) | collective-permute-done | bytes 262176 | tf_op jit(solution)/shard_map/ppermute | solution.py:159
  59.5 2.1 %fusion.2 = f32[128,1024]{1,0:T(8,128)S(1)} fusion(bf16[128,1024]{0,1:T(8,128)(2,1)S(1)} %collective-permute-done.2, bf16[4096,1024]{1,0:T(8,128)(2,1)} %param.11, s32[]{:T(128)S(6)} %select_n.54), kind=kOutput, calls=%fused_computation.2 | convolution fusion | flops 268435456 | bytes 2883588 | tf_op jit(solution)/shard_map/dot_general | solution.py:166
  61.6 2.2 %fusion.26 = f32[128,1024]{1,0:T(8,128)S(1)} fusion(f32[128,1024]{1,0:T(8,128)S(1)} %fusion.2, f32[128,1024]{1,0:T(8,128)S(1)} %fusion.6, f32[128,1024]{1,0:T(8,128)S(1)} %fusion.14, bf16[128,1024]{0,1:T(8,128)(2,1)S(1)} %collective-permute-done, bf16[4096,1024]{1,0:T(8,128)(2,1)} %param.11, s32[]{:T(128)S(6)} %select_n.50), kind=kOutput, calls=%fused_computation.32 | convolution fusion | flops 268828672 | bytes 4456452 | tf_op jit(solution)/shard_map/dot_general | solution.py:166
  63.9 1.4 fusion.41
  65.9 2.5 %fusion.38 = bf16[128,1024]{1,0:T(8,128)(2,1)S(1)} fusion(bf16[128,1024]{1,0:T(8,128)(2,1)S(1)} %get-tuple-element.9, bf16[4096,1024]{1,0:T(8,128)(2,1)} %param.11, s32[]{:T(128)S(6)} %select_n.54), kind=kOutput, calls=%fused_computation.39 | convolution fusion | flops 268566528 | bytes 2621444 | tf_op jit(solution)/shard_map/dot_general | solution.py:185
  68.4 2.5 %fusion.35 = bf16[128,1024]{1,0:T(8,128)(2,1)S(1)} fusion(bf16[128,1024]{1,0:T(8,128)(2,1)S(1)} %get-tuple-element.9, bf16[4096,1024]{1,0:T(8,128)(2,1)} %param.11, s32[]{:T(128)S(6)} %select_n.52), kind=kOutput, calls=%fused_computation.38 | convolution fusion | flops 268566528 | bytes 2621444 | tf_op jit(solution)/shard_map/dot_general | solution.py:185
  71.7 2.2 %collective-permute-start.3 = (bf16[128,1024]{1,0:T(8,128)(2,1)S(1)}, bf16[128,1024]{1,0:T(8,128)(2,1)S(1)}, u32[]{:S(2)}, u32[]{:S(2)}) collective-permute-start(bf16[128,1024]{1,0:T(8,128)(2,1)S(1)} %fusion.38), channel_id=1, source_target_pairs={{0,1},{1,2},{2,3},{3,0},{4,5},{5,6},{6,7},{7,4},{8,9},{9,10},{10,1... | collective-permute-start | bytes 786440 | tf_op jit(solution)/shard_map/ppermute | solution.py:159
  73.9 2.5 %collective-permute-start.4 = (bf16[128,1024]{1,0:T(8,128)(2,1)S(1)}, bf16[128,1024]{1,0:T(8,128)(2,1)S(1)}, u32[]{:S(2)}, u32[]{:S(2)}) collective-permute-start(bf16[128,1024]{1,0:T(8,128)(2,1)S(1)} %fusion.35), channel_id=1, source_target_pairs={{0,2},{1,3},{2,0},{3,1},{4,6},{5,7},{6,4},{7,5},{8,10},{9,11},{10,... | collective-permute-start | bytes 786440 | tf_op jit(solution)/shard_map/ppermute | solution.py:159
  76.4 1.5 collective-permute-start.6
  78.4 6.4 %collective-permute-done.6 = f32[128]{0:T(128)S(1)} collective-permute-done((f32[128]{0:T(128)S(1)}, f32[128]{0:T(128)S(1)}, u32[]{:S(2)}, u32[]{:S(2)}) %collective-permute-start.6) | collective-permute-done | bytes 544 | tf_op jit(solution)/shard_map/ppermute | solution.py:159
  84.8 3.4 %collective-permute-start.8 = (f32[128]{0:T(128)S(1)}, f32[128]{0:T(128)S(1)}, u32[]{:S(2)}, u32[]{:S(2)}) collective-permute-start(f32[128]{0:T(128)S(1)} %multiply_subtract_fusion), channel_id=1, source_target_pairs={{0,3},{1,0},{2,1},{3,2},{4,7},{5,4},{6,5},{7,6},{8,11},{9,8},{10,9... | collective-permute-start | bytes 1544 | tf_op jit(solution)/shard_map/ppermute | solution.py:159
  89.5 1.7 convert_add_fusion
  91.1 1.2 copy.19
  92.9 1.1 convolution_bitcast_fusion.1.state_ref
  94.6 82.4 %shard_map.112 = f32[8,128,128]{2,1,0:T(8,128)} custom-call(f32[8,128,128]{2,1,0:T(8,128)} %convolution_bitcast_fusion.1.state_ref), custom_call_target="tpu_custom_call" | custom-call | tf_op jit(solution)/shard_map/pallas_call | solution.py:112
  177.1 1.5 convolution_bitcast_fusion
  178.6 1.5 fusion.29
  (59 shorter events, 12.5 us)
Async XLA Ops:
  0.6 1.3 copy-start
  0.6 50.7 %copy-start.4 = (f32[32,1024]{1,0:T(8,128)S(1)}, f32[32,1024]{1,0:T(8,128)}, u32[]{:S(2)}) copy-start(f32[32,1024]{1,0:T(8,128)} %param.12) | copy-start | bytes 393220
  0.7 50.8 %copy-start.6 = (s32[128]{0:T(128)S(1)}, s32[128]{0:T(128)}, u32[]{:S(2)}) copy-start(s32[128]{0:T(128)} %param.14) | copy-start | bytes 1540
  44.5 19.4 %copy-start.7 = (s32[128]{0:T(128)S(1)}, s32[128]{0:T(128)}, u32[]{:S(2)}) copy-start(s32[128]{0:T(128)} %param.15) | copy-start | bytes 1540
  44.5 19.4 %copy-start.8 = (s32[128]{0:T(128)S(1)}, s32[128]{0:T(128)}, u32[]{:S(2)}) copy-start(s32[128]{0:T(128)} %param.13) | copy-start | bytes 1540
  45.1 7.8 %collective-permute-start.1 = (bf16[128,1024]{0,1:T(8,128)(2,1)S(1)}, bf16[128,1024]{0,1:T(8,128)(2,1)S(1)}, u32[]{:S(2)}, u32[]{:S(2)}) collective-permute-start(bf16[128,1024]{0,1:T(8,128)(2,1)S(1)} %bitcast.120), channel_id=1, source_target_pairs={{0,2},{1,3},{2,0},{3,1},{4,6},{5,7},{6,4},{7,5},{8,10},{9,11},{10,... | collective-permute-start | bytes 786440 | tf_op jit(solution)/shard_map/ppermute | solution.py:159
  47.8 11.7 %collective-permute-start.2 = (bf16[128,1024]{0,1:T(8,128)(2,1)S(1)}, bf16[128,1024]{0,1:T(8,128)(2,1)S(1)}, u32[]{:S(2)}, u32[]{:S(2)}) collective-permute-start(bf16[128,1024]{0,1:T(8,128)(2,1)S(1)} %bitcast.121), channel_id=1, source_target_pairs={{0,3},{1,0},{2,1},{3,2},{4,7},{5,4},{6,5},{7,6},{8,11},{9,8},{10,9... | collective-permute-start | bytes 786440 | tf_op jit(solution)/shard_map/ppermute | solution.py:159
  48.7 12.9 %collective-permute-start = (bf16[128,1024]{0,1:T(8,128)(2,1)S(1)}, bf16[128,1024]{0,1:T(8,128)(2,1)S(1)}, u32[]{:S(2)}, u32[]{:S(2)}) collective-permute-start(bf16[128,1024]{0,1:T(8,128)(2,1)S(1)} %bitcast.122), channel_id=1, source_target_pairs={{0,1},{1,2},{2,3},{3,0},{4,5},{5,6},{6,7},{7,4},{8,9},{9,10},{10,1... | collective-permute-start | bytes 786440 | tf_op jit(solution)/shard_map/ppermute | solution.py:159
  52.2 13.1 %copy-start.5 = (f32[32,1024]{1,0:T(8,128)S(1)}, f32[32,1024]{1,0:T(8,128)}, u32[]{:S(2)}) copy-start(f32[32,1024]{1,0:T(8,128)} %reduce_window_sum.11) | copy-start | bytes 393220
  52.2 18.6 %slice-start = ((s8[8388608]{0:T(1024)(128)(4,1)}), s8[4194304]{0:T(1024)(128)(4,1)S(1)}, s32[]{:S(2)}) async-start(s8[8388608]{0:T(1024)(128)(4,1)} %bitcast.117), calls=%async_computation | async-start | bytes 8388608
  61.6 9.3 %slice-start.1 = ((s8[8388608]{0:T(1024)(128)(4,1)}), s8[4194304]{0:T(1024)(128)(4,1)S(1)}, s32[]{:S(2)}) async-start(s8[8388608]{0:T(1024)(128)(4,1)} %bitcast.117), calls=%async_computation.1 | async-start | bytes 8388608
  65.9 27.0 %copy-start.2 = (bf16[128,1024]{1,0:T(8,128)(2,1)S(1)}, bf16[128,1024]{1,0:T(8,128)(2,1)}, u32[]{:S(2)}) copy-start(bf16[128,1024]{1,0:T(8,128)(2,1)} %param.8) | copy-start | bytes 786436
  68.4 26.0 %copy-start.1 = (f32[8,128,128]{2,1,0:T(8,128)S(1)}, f32[8,128,128]{2,1,0:T(8,128)}, u32[]{:S(2)}) copy-start(f32[8,128,128]{2,1,0:T(8,128)} %shard_map.111) | copy-start | bytes 1572868
  70.9 107.7 %copy-start.3 = (bf16[128,1024]{1,0:T(8,128)(2,1)S(1)}, bf16[128,1024]{1,0:T(8,128)(2,1)}, u32[]{:S(2)}) copy-start(bf16[128,1024]{1,0:T(8,128)(2,1)} %param.9) | copy-start | bytes 786436
  71.7 17.7 %collective-permute-start.3 = (bf16[128,1024]{1,0:T(8,128)(2,1)S(1)}, bf16[128,1024]{1,0:T(8,128)(2,1)S(1)}, u32[]{:S(2)}, u32[]{:S(2)}) collective-permute-start(bf16[128,1024]{1,0:T(8,128)(2,1)S(1)} %fusion.38), channel_id=1, source_target_pairs={{0,1},{1,2},{2,3},{3,0},{4,5},{5,6},{6,7},{7,4},{8,9},{9,10},{10,1... | collective-permute-start | bytes 786440 | tf_op jit(solution)/shard_map/ppermute | solution.py:159
  73.9 15.5 %collective-permute-start.4 = (bf16[128,1024]{1,0:T(8,128)(2,1)S(1)}, bf16[128,1024]{1,0:T(8,128)(2,1)S(1)}, u32[]{:S(2)}, u32[]{:S(2)}) collective-permute-start(bf16[128,1024]{1,0:T(8,128)(2,1)S(1)} %fusion.35), channel_id=1, source_target_pairs={{0,2},{1,3},{2,0},{3,1},{4,6},{5,7},{6,4},{7,5},{8,10},{9,11},{10,... | collective-permute-start | bytes 786440 | tf_op jit(solution)/shard_map/ppermute | solution.py:159
  76.4 13.1 %collective-permute-start.5 = (bf16[128,1024]{1,0:T(8,128)(2,1)S(1)}, bf16[128,1024]{1,0:T(8,128)(2,1)S(1)}, u32[]{:S(2)}, u32[]{:S(2)}) collective-permute-start(bf16[128,1024]{1,0:T(8,128)(2,1)S(1)} %fusion.32), channel_id=1, source_target_pairs={{0,3},{1,0},{2,1},{3,2},{4,7},{5,4},{6,5},{7,6},{8,11},{9,8},{10,9... | collective-permute-start | bytes 786440 | tf_op jit(solution)/shard_map/ppermute | solution.py:159
  76.4 8.4 %collective-permute-start.6 = (f32[128]{0:T(128)S(1)}, f32[128]{0:T(128)S(1)}, u32[]{:S(2)}, u32[]{:S(2)}) collective-permute-start(f32[128]{0:T(128)S(1)} %multiply_subtract_fusion), channel_id=1, source_target_pairs={{0,1},{1,2},{2,3},{3,0},{4,5},{5,6},{6,7},{7,4},{8,9},{9,10},{10,1... | collective-permute-start | bytes 1544 | tf_op jit(solution)/shard_map/ppermute | solution.py:159
  77.9 10.3 %collective-permute-start.7 = (f32[128]{0:T(128)S(1)}, f32[128]{0:T(128)S(1)}, u32[]{:S(2)}, u32[]{:S(2)}) collective-permute-start(f32[128]{0:T(128)S(1)} %multiply_subtract_fusion), channel_id=1, source_target_pairs={{0,2},{1,3},{2,0},{3,1},{4,6},{5,7},{6,4},{7,5},{8,10},{9,11},{10,... | collective-permute-start | bytes 1544 | tf_op jit(solution)/shard_map/ppermute | solution.py:159
  84.8 4.2 %collective-permute-start.8 = (f32[128]{0:T(128)S(1)}, f32[128]{0:T(128)S(1)}, u32[]{:S(2)}, u32[]{:S(2)}) collective-permute-start(f32[128]{0:T(128)S(1)} %multiply_subtract_fusion), channel_id=1, source_target_pairs={{0,3},{1,0},{2,1},{3,2},{4,7},{5,4},{6,5},{7,6},{8,11},{9,8},{10,9... | collective-permute-start | bytes 1544 | tf_op jit(solution)/shard_map/ppermute | solution.py:159

commit v5 on v4

--- a/solution.py
+++ b/solution.py
@@ -16,13 +16,14 @@
 grad_scale = 64.0
 
 
-def scan_kernel(reverse, count, state_ref, out_ref, other, inclusive, arrived, exclusive, partner,
+def scan_kernel(reverse, count, state_ref, out_ref, other, running, exclusive, outgoing, arrived, handed, partner,
                 send_sems, recv_sems):
     me = lax.axis_index("seq")
     head = lax.axis_index("head")
     core = me % 2
     mate = me + 1 - 2 * core
     half = exclusive.shape[0]
+    wire = outgoing.dtype
     distances = []
     distance = 2
     while distance < count:
@@ -55,12 +56,13 @@
     swap.start()
     swap.wait()
     mine = pl.ds(core * half, half)
-    inclusive[0] = state_ref[mine] + other[mine]
+    running[...] = state_ref[mine] + other[mine]
     exclusive[...] = jnp.zeros_like(exclusive)
     copies = []
     for r, (target, send, receive) in enumerate(zip(targets, sends, receives)):
+        outgoing[r] = running[...].astype(wire)
         copy = pltpu.make_async_remote_copy(
-            inclusive.at[r], arrived.at[r], send_sems.at[r + 1], recv_sems.at[r + 1],
+            outgoing.at[r], arrived.at[r], send_sems.at[r + 1], recv_sems.at[r + 1],
             device_id=(target, head), device_id_type=MESH,
         )
         copies.append(copy)
@@ -72,17 +74,14 @@
         @pl.when(receive)
         def _():
             copy.wait_recv()
-            got = arrived[r]
-            inclusive[r + 1] = inclusive[r] + got
+            got = arrived[r].astype(running.dtype)
+            running[...] = running[...] + got
             exclusive[...] = exclusive[...] + got
 
-        @pl.when(jnp.logical_not(receive))
-        def _():
-            inclusive[r + 1] = inclusive[r]
-
     last = len(distances) + 1
+    handed[...] = exclusive[...].astype(wire)
     back = pltpu.make_async_remote_copy(
-        exclusive, partner, send_sems.at[last], recv_sems.at[last], device_id=(mate, head), device_id_type=MESH
+        handed, partner, send_sems.at[last], recv_sems.at[last], device_id=(mate, head), device_id_type=MESH
     )
     back.start()
     for copy, send in zip(copies, sends):
@@ -96,19 +95,20 @@
     @pl.when(take_other)
     def _():
         out_ref[mine] = exclusive[...] + other[mine]
-        out_ref[theirs] = partner[...] + other[theirs]
+        out_ref[theirs] = partner[...].astype(out_ref.dtype) + other[theirs]
 
     @pl.when(jnp.logical_not(take_other))
     def _():
         out_ref[mine] = exclusive[...]
-        out_ref[theirs] = partner[...]
-
-
-def exclusive_scan(shard, axis, reverse=False):
+        out_ref[theirs] = partner[...].astype(out_ref.dtype)
+
+
+def exclusive_scan(shard, axis, reverse=False, wire=jnp.float32):
     count = lax.axis_size(axis)
     heads, rows, cols = shard.shape
     half = heads // 2
-    rounds = max(count.bit_length() - 2, 0)
+    rounds = max(count.bit_length() - 2, 1)
+    block = (half, rows, cols)
     return pl.pallas_call(
         functools.partial(scan_kernel, reverse, count),
         out_shape=jax.ShapeDtypeStruct(shard.shape, shard.dtype),
@@ -116,10 +116,12 @@
         out_specs=pl.BlockSpec(memory_space=pltpu.VMEM),
         scratch_shapes=[
             pltpu.VMEM((heads, rows, cols), shard.dtype),
-            pltpu.VMEM((rounds + 1, half, rows, cols), shard.dtype),
-            pltpu.VMEM((max(rounds, 1), half, rows, cols), shard.dtype),
-            pltpu.VMEM((half, rows, cols), shard.dtype),
-            pltpu.VMEM((half, rows, cols), shard.dtype),
+            pltpu.VMEM(block, shard.dtype),
+            pltpu.VMEM(block, shard.dtype),
+            pltpu.VMEM((rounds,) + block, wire),
+            pltpu.VMEM((rounds,) + block, wire),
+            pltpu.VMEM(block, wire),
+            pltpu.VMEM(block, wire),
             pltpu.SemaphoreType.DMA((rounds + 2,)),
             pltpu.SemaphoreType.DMA((rounds + 2,)),
         ],
@@ -198,7 +200,7 @@
     ) / root_mean
     grad_out = grad_raw.astype(jnp.bfloat16)
     local_adjoint = jnp.einsum("thd,the->hde", query_rows, grad_out, preferred_element_type=f32)
-    suffix = exclusive_scan(local_adjoint, "seq", reverse=True)
+    suffix = exclusive_scan(local_adjoint, "seq", reverse=True, wire=jnp.bfloat16)
     back_scores = (
         jnp.einsum("the,she->hts", grad_out, value_rows, preferred_element_type=f32) * causal
     )

time: 184 us -> 164 us (0.89)
  Pallas kernels: 121 us -> 101 us
    pallas_call x2, Pallas kernels: 121 us -> 101 us  [exclusive_scan(): pl.pallas_call(functools.partial(scan_kernel, reverse, count), out_shape=...]
  transfers between devices with their start and end apart: 9 -> 9, of which waited for: 4 -> 4; matrix products, arithmetic and copies ran while one was open for 4% -> 5% of each run, Pallas kernels for 0% -> 0%
where the time goes in v5:
time: 164 us; the launch traced here: 163 us
  Pallas kernels  101 us (62%)
  matrix products  28.5 us (17%)
  starting transfers between devices  14.2 us (9%)
  waiting for transfers between devices  12 us (7%)
  local copies, waits for them, and re-layouts  5.13 us (3%)
    pallas_call x2, Pallas kernels, exclusive_scan(): pl.pallas_call(functools.partial(scan_kernel, reverse, count), out_shape=...  101 us
    ppermute x9, starting transfers between devices, shifted(): lax.ppermute(x, 'head', [(m, (m + k) % head_count) for m in range(head_co...  14.2 us
    ppermute x9, waiting for transfers between devices, shifted(): lax.ppermute(x, 'head', [(m, (m + k) % head_count) for m in range(head_co...  12 us
    dot_general x4, matrix products, block_term(): lax.dot_general(dlogit, weight_rows(owner), (((1,), (1,)), ((), ())), pre...  7.45 us
    dot_general x3, matrix products, body(): jnp.dot(shifted(hidden, k), weight_rows((head_index - k + head_count) % h...  6.74 us
    unnamed x26, local copies, waits for them, and re-layouts  3.65 us
  transfers between devices with their start and end apart: 9, of which 4 were waited for; matrix products, arithmetic and copies ran while one was open for 5% of the time, Pallas kernels for 0%

profile of v5, /device:TPU:1, one launch (start us, length us, event | category | flops | bytes accessed | tf_op | source)
XLA Modules:
  0.0 163.1 jit_solution(15598818291975005482)
XLA Ops:
  0.7 1.0 copy.41
  3.0 38.6 %shard_map.111 = f32[8,128,128]{2,1,0:T(8,128)} custom-call(f32[8,128,128]{2,1,0:T(8,128)} %fusion.48.state_ref), custom_call_target="tpu_custom_call" | custom-call | tf_op jit(solution)/shard_map/pallas_call | solution.py:112
  41.6 1.6 convolution_bitcast_fusion.5
  43.1 1.3 convolution_multiply_fusion.1
  45.1 2.7 %collective-permute-start.1 = (bf16[128,1024]{0,1:T(8,128)(2,1)S(1)}, bf16[128,1024]{0,1:T(8,128)(2,1)S(1)}, u32[]{:S(2)}, u32[]{:S(2)}) collective-permute-start(bf16[128,1024]{0,1:T(8,128)(2,1)S(1)} %bitcast.120), channel_id=1, source_target_pairs={{0,2},{1,3},{2,0},{3,1},{4,6},{5,7},{6,4},{7,5},{8,10},{9,11},{10,... | collective-permute-start | bytes 786440 | tf_op jit(solution)/shard_map/ppermute | solution.py:161
  49.3 2.1 %fusion.14 = f32[128,1024]{1,0:T(8,128)S(1)} fusion(bf16[128,1024]{0,1:T(8,128)(2,1)S(1)} %bitcast.123, bf16[4096,1024]{1,0:T(8,128)(2,1)} %param.11, s32[]{:T(128)S(6)} %select_n.48), kind=kOutput, calls=%fused_computation.14 | convolution fusion | flops 268435456 | bytes 2883588 | tf_op jit(solution)/shard_map/dot_general | solution.py:166
  53.0 2.4 %fusion.6 = f32[128,1024]{1,0:T(8,128)S(1)} fusion(bf16[128,1024]{0,1:T(8,128)(2,1)S(1)} %collective-permute-done.1, bf16[4096,1024]{1,0:T(8,128)(2,1)} %param.11, s32[]{:T(128)S(6)} %select_n.52), kind=kOutput, calls=%fused_computation.6 | convolution fusion | flops 268435456 | bytes 2883588 | tf_op jit(solution)/shard_map/dot_general | solution.py:168
  55.4 4.1 %collective-permute-done.2 = bf16[128,1024]{0,1:T(8,128)(2,1)S(1)} collective-permute-done((bf16[128,1024]{0,1:T(8,128)(2,1)S(1)}, bf16[128,1024]{0,1:T(8,128)(2,1)S(1)}, u32[]{:S(2)}, u32[]{:S(2)}) %collective-permute-start.2) | collective-permute-done | bytes 262176 | tf_op jit(solution)/shard_map/ppermute | solution.py:161
  59.5 2.1 %fusion.2 = f32[128,1024]{1,0:T(8,128)S(1)} fusion(bf16[128,1024]{0,1:T(8,128)(2,1)S(1)} %collective-permute-done.2, bf16[4096,1024]{1,0:T(8,128)(2,1)} %param.11, s32[]{:T(128)S(6)} %select_n.54), kind=kOutput, calls=%fused_computation.2 | convolution fusion | flops 268435456 | bytes 2883588 | tf_op jit(solution)/shard_map/dot_general | solution.py:168
  61.6 2.2 %fusion.26 = f32[128,1024]{1,0:T(8,128)S(1)} fusion(f32[128,1024]{1,0:T(8,128)S(1)} %fusion.2, f32[128,1024]{1,0:T(8,128)S(1)} %fusion.6, f32[128,1024]{1,0:T(8,128)S(1)} %fusion.14, bf16[128,1024]{0,1:T(8,128)(2,1)S(1)} %collective-permute-done, bf16[4096,1024]{1,0:T(8,128)(2,1)} %param.11, s32[]{:T(128)S(6)} %select_n.50), kind=kOutput, calls=%fused_computation.32 | convolution fusion | flops 268828672 | bytes 4456452 | tf_op jit(solution)/shard_map/dot_general | solution.py:168
  63.9 1.4 fusion.41
  65.9 2.5 %fusion.38 = bf16[128,1024]{1,0:T(8,128)(2,1)S(1)} fusion(bf16[128,1024]{1,0:T(8,128)(2,1)S(1)} %get-tuple-element.9, bf16[4096,1024]{1,0:T(8,128)(2,1)} %param.11, s32[]{:T(128)S(6)} %select_n.54), kind=kOutput, calls=%fused_computation.39 | convolution fusion | flops 268566528 | bytes 2621444 | tf_op jit(solution)/shard_map/dot_general | solution.py:187
  68.4 2.5 %fusion.35 = bf16[128,1024]{1,0:T(8,128)(2,1)S(1)} fusion(bf16[128,1024]{1,0:T(8,128)(2,1)S(1)} %get-tuple-element.9, bf16[4096,1024]{1,0:T(8,128)(2,1)} %param.11, s32[]{:T(128)S(6)} %select_n.52), kind=kOutput, calls=%fused_computation.38 | convolution fusion | flops 268566528 | bytes 2621444 | tf_op jit(solution)/shard_map/dot_general | solution.py:187
  71.8 2.2 %collective-permute-start.3 = (bf16[128,1024]{1,0:T(8,128)(2,1)S(1)}, bf16[128,1024]{1,0:T(8,128)(2,1)S(1)}, u32[]{:S(2)}, u32[]{:S(2)}) collective-permute-start(bf16[128,1024]{1,0:T(8,128)(2,1)S(1)} %fusion.38), channel_id=1, source_target_pairs={{0,1},{1,2},{2,3},{3,0},{4,5},{5,6},{6,7},{7,4},{8,9},{9,10},{10,1... | collective-permute-start | bytes 786440 | tf_op jit(solution)/shard_map/ppermute | solution.py:161
  73.9 2.5 %collective-permute-start.4 = (bf16[128,1024]{1,0:T(8,128)(2,1)S(1)}, bf16[128,1024]{1,0:T(8,128)(2,1)S(1)}, u32[]{:S(2)}, u32[]{:S(2)}) collective-permute-start(bf16[128,1024]{1,0:T(8,128)(2,1)S(1)} %fusion.35), channel_id=1, source_target_pairs={{0,2},{1,3},{2,0},{3,1},{4,6},{5,7},{6,4},{7,5},{8,10},{9,11},{10,... | collective-permute-start | bytes 786440 | tf_op jit(solution)/shard_map/ppermute | solution.py:161
  76.4 1.5 collective-permute-start.6
  78.4 6.4 %collective-permute-done.6 = f32[128]{0:T(128)S(1)} collective-permute-done((f32[128]{0:T(128)S(1)}, f32[128]{0:T(128)S(1)}, u32[]{:S(2)}, u32[]{:S(2)}) %collective-permute-start.6) | collective-permute-done | bytes 544 | tf_op jit(solution)/shard_map/ppermute | solution.py:161
  84.8 3.5 %collective-permute-start.8 = (f32[128]{0:T(128)S(1)}, f32[128]{0:T(128)S(1)}, u32[]{:S(2)}, u32[]{:S(2)}) collective-permute-start(f32[128]{0:T(128)S(1)} %multiply_subtract_fusion), channel_id=1, source_target_pairs={{0,3},{1,0},{2,1},{3,2},{4,7},{5,4},{6,5},{7,6},{8,11},{9,8},{10,9... | collective-permute-start | bytes 1544 | tf_op jit(solution)/shard_map/ppermute | solution.py:161
  89.5 1.7 %convert_add_fusion = f32[128,1024]{1,0:T(8,128)} fusion(bf16[128,1024]{1,0:T(8,128)(2,1)S(1)} %collective-permute-done.5, bf16[128,1024]{1,0:T(8,128)(2,1)S(1)} %collective-permute-done.4, bf16[128,1024]{1,0:T(8,128)(2,1)S(1)} %collective-permute-done.3, bf16[128,1024]{1,0:T(8,128)(2,1)S(1)} %get-tuple-element.9, bf16[4096,1024]{1,0:T(8,128)(2,1)S(1)} %bitcast.118, ...), kind=kOutput, calls=%fused_computation.47 | convolution fusion | flops 269221888 | bytes 3670020 | tf_op jit(solution)/shard_map/dot_general | solution.py:187
  91.2 1.2 copy.19
  92.9 1.1 convolution_bitcast_fusion.1.state_ref
  94.7 62.0 %shard_map.112 = f32[8,128,128]{2,1,0:T(8,128)} custom-call(f32[8,128,128]{2,1,0:T(8,128)} %convolution_bitcast_fusion.1.state_ref), custom_call_target="tpu_custom_call" | custom-call | tf_op jit(solution)/shard_map/pallas_call | solution.py:112
  156.7 1.5 convolution_bitcast_fusion
  158.2 1.5 fusion.29
  (59 shorter events, 12.5 us)
Async XLA Ops:
  0.6 1.3 copy-start
  0.6 50.7 %copy-start.4 = (f32[32,1024]{1,0:T(8,128)S(1)}, f32[32,1024]{1,0:T(8,128)}, u32[]{:S(2)}) copy-start(f32[32,1024]{1,0:T(8,128)} %param.12) | copy-start | bytes 393220
  0.7 50.8 %copy-start.6 = (s32[128]{0:T(128)S(1)}, s32[128]{0:T(128)}, u32[]{:S(2)}) copy-start(s32[128]{0:T(128)} %param.14) | copy-start | bytes 1540
  44.5 19.4 %copy-start.7 = (s32[128]{0:T(128)S(1)}, s32[128]{0:T(128)}, u32[]{:S(2)}) copy-start(s32[128]{0:T(128)} %param.15) | copy-start | bytes 1540
  44.5 19.4 %copy-start.8 = (s32[128]{0:T(128)S(1)}, s32[128]{0:T(128)}, u32[]{:S(2)}) copy-start(s32[128]{0:T(128)} %param.13) | copy-start | bytes 1540
  45.1 7.8 %collective-permute-start.1 = (bf16[128,1024]{0,1:T(8,128)(2,1)S(1)}, bf16[128,1024]{0,1:T(8,128)(2,1)S(1)}, u32[]{:S(2)}, u32[]{:S(2)}) collective-permute-start(bf16[128,1024]{0,1:T(8,128)(2,1)S(1)} %bitcast.120), channel_id=1, source_target_pairs={{0,2},{1,3},{2,0},{3,1},{4,6},{5,7},{6,4},{7,5},{8,10},{9,11},{10,... | collective-permute-start | bytes 786440 | tf_op jit(solution)/shard_map/ppermute | solution.py:161
  47.8 11.7 %collective-permute-start.2 = (bf16[128,1024]{0,1:T(8,128)(2,1)S(1)}, bf16[128,1024]{0,1:T(8,128)(2,1)S(1)}, u32[]{:S(2)}, u32[]{:S(2)}) collective-permute-start(bf16[128,1024]{0,1:T(8,128)(2,1)S(1)} %bitcast.121), channel_id=1, source_target_pairs={{0,3},{1,0},{2,1},{3,2},{4,7},{5,4},{6,5},{7,6},{8,11},{9,8},{10,9... | collective-permute-start | bytes 786440 | tf_op jit(solution)/shard_map/ppermute | solution.py:161
  48.7 12.9 %collective-permute-start = (bf16[128,1024]{0,1:T(8,128)(2,1)S(1)}, bf16[128,1024]{0,1:T(8,128)(2,1)S(1)}, u32[]{:S(2)}, u32[]{:S(2)}) collective-permute-start(bf16[128,1024]{0,1:T(8,128)(2,1)S(1)} %bitcast.122), channel_id=1, source_target_pairs={{0,1},{1,2},{2,3},{3,0},{4,5},{5,6},{6,7},{7,4},{8,9},{9,10},{10,1... | collective-permute-start | bytes 786440 | tf_op jit(solution)/shard_map/ppermute | solution.py:161
  52.2 13.1 %copy-start.5 = (f32[32,1024]{1,0:T(8,128)S(1)}, f32[32,1024]{1,0:T(8,128)}, u32[]{:S(2)}) copy-start(f32[32,1024]{1,0:T(8,128)} %reduce_window_sum.11) | copy-start | bytes 393220
  52.2 18.6 %slice-start = ((s8[8388608]{0:T(1024)(128)(4,1)}), s8[4194304]{0:T(1024)(128)(4,1)S(1)}, s32[]{:S(2)}) async-start(s8[8388608]{0:T(1024)(128)(4,1)} %bitcast.117), calls=%async_computation | async-start | bytes 8388608
  61.6 9.3 %slice-start.1 = ((s8[8388608]{0:T(1024)(128)(4,1)}), s8[4194304]{0:T(1024)(128)(4,1)S(1)}, s32[]{:S(2)}) async-start(s8[8388608]{0:T(1024)(128)(4,1)} %bitcast.117), calls=%async_computation.1 | async-start | bytes 8388608
  65.9 27.0 %copy-start.2 = (bf16[128,1024]{1,0:T(8,128)(2,1)S(1)}, bf16[128,1024]{1,0:T(8,128)(2,1)}, u32[]{:S(2)}) copy-start(bf16[128,1024]{1,0:T(8,128)(2,1)} %param.8) | copy-start | bytes 786436
  68.4 26.0 %copy-start.1 = (f32[8,128,128]{2,1,0:T(8,128)S(1)}, f32[8,128,128]{2,1,0:T(8,128)}, u32[]{:S(2)}) copy-start(f32[8,128,128]{2,1,0:T(8,128)} %shard_map.111) | copy-start | bytes 1572868
  70.9 87.3 %copy-start.3 = (bf16[128,1024]{1,0:T(8,128)(2,1)S(1)}, bf16[128,1024]{1,0:T(8,128)(2,1)}, u32[]{:S(2)}) copy-start(bf16[128,1024]{1,0:T(8,128)(2,1)} %param.9) | copy-start | bytes 786436
  71.8 17.7 %collective-permute-start.3 = (bf16[128,1024]{1,0:T(8,128)(2,1)S(1)}, bf16[128,1024]{1,0:T(8,128)(2,1)S(1)}, u32[]{:S(2)}, u32[]{:S(2)}) collective-permute-start(bf16[128,1024]{1,0:T(8,128)(2,1)S(1)} %fusion.38), channel_id=1, source_target_pairs={{0,1},{1,2},{2,3},{3,0},{4,5},{5,6},{6,7},{7,4},{8,9},{9,10},{10,1... | collective-permute-start | bytes 786440 | tf_op jit(solution)/shard_map/ppermute | solution.py:161
  73.9 15.6 %collective-permute-start.4 = (bf16[128,1024]{1,0:T(8,128)(2,1)S(1)}, bf16[128,1024]{1,0:T(8,128)(2,1)S(1)}, u32[]{:S(2)}, u32[]{:S(2)}) collective-permute-start(bf16[128,1024]{1,0:T(8,128)(2,1)S(1)} %fusion.35), channel_id=1, source_target_pairs={{0,2},{1,3},{2,0},{3,1},{4,6},{5,7},{6,4},{7,5},{8,10},{9,11},{10,... | collective-permute-start | bytes 786440 | tf_op jit(solution)/shard_map/ppermute | solution.py:161
  76.4 13.1 %collective-permute-start.5 = (bf16[128,1024]{1,0:T(8,128)(2,1)S(1)}, bf16[128,1024]{1,0:T(8,128)(2,1)S(1)}, u32[]{:S(2)}, u32[]{:S(2)}) collective-permute-start(bf16[128,1024]{1,0:T(8,128)(2,1)S(1)} %fusion.32), channel_id=1, source_target_pairs={{0,3},{1,0},{2,1},{3,2},{4,7},{5,4},{6,5},{7,6},{8,11},{9,8},{10,9... | collective-permute-start | bytes 786440 | tf_op jit(solution)/shard_map/ppermute | solution.py:161
  76.4 8.3 %collective-permute-start.6 = (f32[128]{0:T(128)S(1)}, f32[128]{0:T(128)S(1)}, u32[]{:S(2)}, u32[]{:S(2)}) collective-permute-start(f32[128]{0:T(128)S(1)} %multiply_subtract_fusion), channel_id=1, source_target_pairs={{0,1},{1,2},{2,3},{3,0},{4,5},{5,6},{6,7},{7,4},{8,9},{9,10},{10,1... | collective-permute-start | bytes 1544 | tf_op jit(solution)/shard_map/ppermute | solution.py:161
  77.9 10.3 %collective-permute-start.7 = (f32[128]{0:T(128)S(1)}, f32[128]{0:T(128)S(1)}, u32[]{:S(2)}, u32[]{:S(2)}) collective-permute-start(f32[128]{0:T(128)S(1)} %multiply_subtract_fusion), channel_id=1, source_target_pairs={{0,2},{1,3},{2,0},{3,1},{4,6},{5,7},{6,4},{7,5},{8,10},{9,11},{10,... | collective-permute-start | bytes 1544 | tf_op jit(solution)/shard_map/ppermute | solution.py:161
  84.8 4.2 %collective-permute-start.8 = (f32[128]{0:T(128)S(1)}, f32[128]{0:T(128)S(1)}, u32[]{:S(2)}, u32[]{:S(2)}) collective-permute-start(f32[128]{0:T(128)S(1)} %multiply_subtract_fusion), channel_id=1, source_target_pairs={{0,3},{1,0},{2,1},{3,2},{4,7},{5,4},{6,5},{7,6},{8,11},{9,8},{10,9... | collective-permute-start | bytes 1544 | tf_op jit(solution)/shard_map/ppermute | solution.py:161

commit v6 on v5

--- a/solution.py
+++ b/solution.py
@@ -143,7 +143,7 @@
     value_rows = values.reshape(shape_three)
     causal = jnp.tril(jnp.ones((rows_here, rows_here), f32))
     local_state = jnp.einsum("thd,the->hde", key_rows, value_rows, preferred_element_type=f32)
-    prefix = exclusive_scan(local_state, "seq")
+    prefix = exclusive_scan(local_state, "seq", wire=jnp.bfloat16)
     scores = jnp.einsum("thd,shd->hts", query_rows, key_rows, preferred_element_type=f32) * causal
     raw_out = jnp.einsum(
         "hts,she->the", scores, value_rows, precision=three_pass, preferred_element_type=f32

time: 164 us -> 147 us (0.90)
  Pallas kernels: 101 us -> 83.5 us
    pallas_call x2, Pallas kernels: 101 us -> 83.5 us  [exclusive_scan(): pl.pallas_call(functools.partial(scan_kernel, reverse, count), out_shape=...]
where the time goes in v6:
time: 147 us
  Pallas kernels  83.5 us (57%)
  matrix products  28.6 us (19%)
  starting transfers between devices  15 us (10%)
  waiting for transfers between devices  11.9 us (8%)
  local copies, waits for them, and re-layouts  5.13 us (3%)
  other arithmetic  1.53 us (1%)
    pallas_call x2, Pallas kernels, exclusive_scan(): pl.pallas_call(functools.partial(scan_kernel, reverse, count), out_shape=...  83.5 us
    ppermute x9, starting transfers between devices, shifted(): lax.ppermute(x, 'head', [(m, (m + k) % head_count) for m in range(head_co...  15 us
    ppermute x9, waiting for transfers between devices, shifted(): lax.ppermute(x, 'head', [(m, (m + k) % head_count) for m in range(head_co...  11.9 us
    dot_general x4, matrix products, block_term(): lax.dot_general(dlogit, weight_rows(owner), (((1,), (1,)), ((), ())), pre...  7.45 us
    dot_general x3, matrix products, body(): jnp.dot(shifted(hidden, k), weight_rows((head_index - k + head_count) % h...  6.79 us
    unnamed x26, local copies, waits for them, and re-layouts  3.65 us
  transfers between devices with their start and end apart: 9, of which 4 were waited for; matrix products, arithmetic and copies ran while one was open for 5% of the time, Pallas kernels for 0%

profile of v6, /device:TPU:1, one launch (start us, length us, event | category | flops | bytes accessed | tf_op | source)
XLA Modules:
  0.0 146.7 jit_solution(9779254867189506049)
XLA Ops:
  0.7 1.0 copy.41
  3.0 22.8 %shard_map.111 = f32[8,128,128]{2,1,0:T(8,128)} custom-call(f32[8,128,128]{2,1,0:T(8,128)} %fusion.48.state_ref), custom_call_target="tpu_custom_call" | custom-call | tf_op jit(solution)/shard_map/pallas_call | solution.py:112
  25.8 1.6 %convolution_bitcast_fusion.5 = f32[128,8,128]{0,2,1:T(8,128)S(1)} fusion(f32[8,128,128]{2,1,0:T(8,128)} %shard_map.111, bf16[128,1024]{1,0:T(8,128)(2,1)} %param.8), kind=kOutput, calls=%fused_computation.24 | convolution fusion | flops 100663296 | bytes 1310720 | tf_op jit(solution)/shard_map/thd,hde->the/dot_general | solution.py:151
  27.3 1.3 convolution_multiply_fusion.1
  29.3 3.5 %collective-permute-start.1 = (bf16[128,1024]{0,1:T(8,128)(2,1)S(1)}, bf16[128,1024]{0,1:T(8,128)(2,1)S(1)}, u32[]{:S(2)}, u32[]{:S(2)}) collective-permute-start(bf16[128,1024]{0,1:T(8,128)(2,1)S(1)} %bitcast.120), channel_id=1, source_target_pairs={{0,2},{1,3},{2,0},{3,1},{4,6},{5,7},{6,4},{7,5},{8,10},{9,11},{10,... | collective-permute-start | bytes 786440 | tf_op jit(solution)/shard_map/ppermute | solution.py:161
  34.3 2.1 %fusion.14 = f32[128,1024]{1,0:T(8,128)S(1)} fusion(bf16[128,1024]{0,1:T(8,128)(2,1)S(1)} %bitcast.123, bf16[4096,1024]{1,0:T(8,128)(2,1)} %param.11, s32[]{:T(128)S(6)} %select_n.48), kind=kOutput, calls=%fused_computation.14 | convolution fusion | flops 268435456 | bytes 2883588 | tf_op jit(solution)/shard_map/dot_general | solution.py:166
  38.1 2.5 %fusion.6 = f32[128,1024]{1,0:T(8,128)S(1)} fusion(bf16[128,1024]{0,1:T(8,128)(2,1)S(1)} %collective-permute-done.1, bf16[4096,1024]{1,0:T(8,128)(2,1)} %param.11, s32[]{:T(128)S(6)} %select_n.52), kind=kOutput, calls=%fused_computation.6 | convolution fusion | flops 268435456 | bytes 2883588 | tf_op jit(solution)/shard_map/dot_general | solution.py:168
  40.6 3.9 %collective-permute-done.2 = bf16[128,1024]{0,1:T(8,128)(2,1)S(1)} collective-permute-done((bf16[128,1024]{0,1:T(8,128)(2,1)S(1)}, bf16[128,1024]{0,1:T(8,128)(2,1)S(1)}, u32[]{:S(2)}, u32[]{:S(2)}) %collective-permute-start.2) | collective-permute-done | bytes 262176 | tf_op jit(solution)/shard_map/ppermute | solution.py:161
  44.5 2.1 %fusion.2 = f32[128,1024]{1,0:T(8,128)S(1)} fusion(bf16[128,1024]{0,1:T(8,128)(2,1)S(1)} %collective-permute-done.2, bf16[4096,1024]{1,0:T(8,128)(2,1)} %param.11, s32[]{:T(128)S(6)} %select_n.54), kind=kOutput, calls=%fused_computation.2 | convolution fusion | flops 268435456 | bytes 2883588 | tf_op jit(solution)/shard_map/dot_general | solution.py:168
  46.6 2.2 %fusion.26 = f32[128,1024]{1,0:T(8,128)S(1)} fusion(f32[128,1024]{1,0:T(8,128)S(1)} %fusion.2, f32[128,1024]{1,0:T(8,128)S(1)} %fusion.6, f32[128,1024]{1,0:T(8,128)S(1)} %fusion.14, bf16[128,1024]{0,1:T(8,128)(2,1)S(1)} %collective-permute-done, bf16[4096,1024]{1,0:T(8,128)(2,1)} %param.11, s32[]{:T(128)S(6)} %select_n.50), kind=kOutput, calls=%fused_computation.32 | convolution fusion | flops 268828672 | bytes 4456452 | tf_op jit(solution)/shard_map/dot_general | solution.py:168
  48.9 1.4 fusion.41
  50.9 2.5 %fusion.38 = bf16[128,1024]{1,0:T(8,128)(2,1)S(1)} fusion(bf16[128,1024]{1,0:T(8,128)(2,1)S(1)} %get-tuple-element.9, bf16[4096,1024]{1,0:T(8,128)(2,1)} %param.11, s32[]{:T(128)S(6)} %select_n.54), kind=kOutput, calls=%fused_computation.39 | convolution fusion | flops 268566528 | bytes 2621444 | tf_op jit(solution)/shard_map/dot_general | solution.py:187
  53.4 2.5 %fusion.35 = bf16[128,1024]{1,0:T(8,128)(2,1)S(1)} fusion(bf16[128,1024]{1,0:T(8,128)(2,1)S(1)} %get-tuple-element.9, bf16[4096,1024]{1,0:T(8,128)(2,1)} %param.11, s32[]{:T(128)S(6)} %select_n.52), kind=kOutput, calls=%fused_computation.38 | convolution fusion | flops 268566528 | bytes 2621444 | tf_op jit(solution)/shard_map/dot_general | solution.py:187
  56.7 2.2 %collective-permute-start.3 = (bf16[128,1024]{1,0:T(8,128)(2,1)S(1)}, bf16[128,1024]{1,0:T(8,128)(2,1)S(1)}, u32[]{:S(2)}, u32[]{:S(2)}) collective-permute-start(bf16[128,1024]{1,0:T(8,128)(2,1)S(1)} %fusion.38), channel_id=1, source_target_pairs={{0,1},{1,2},{2,3},{3,0},{4,5},{5,6},{6,7},{7,4},{8,9},{9,10},{10,1... | collective-permute-start | bytes 786440 | tf_op jit(solution)/shard_map/ppermute | solution.py:161
  59.0 2.4 %collective-permute-start.4 = (bf16[128,1024]{1,0:T(8,128)(2,1)S(1)}, bf16[128,1024]{1,0:T(8,128)(2,1)S(1)}, u32[]{:S(2)}, u32[]{:S(2)}) collective-permute-start(bf16[128,1024]{1,0:T(8,128)(2,1)S(1)} %fusion.35), channel_id=1, source_target_pairs={{0,2},{1,3},{2,0},{3,1},{4,6},{5,7},{6,4},{7,5},{8,10},{9,11},{10,... | collective-permute-start | bytes 786440 | tf_op jit(solution)/shard_map/ppermute | solution.py:161
  61.5 1.4 collective-permute-start.6
  63.4 6.4 %collective-permute-done.6 = f32[128]{0:T(128)S(1)} collective-permute-done((f32[128]{0:T(128)S(1)}, f32[128]{0:T(128)S(1)}, u32[]{:S(2)}, u32[]{:S(2)}) %collective-permute-start.6) | collective-permute-done | bytes 544 | tf_op jit(solution)/shard_map/ppermute | solution.py:161
  69.8 3.4 %collective-permute-start.8 = (f32[128]{0:T(128)S(1)}, f32[128]{0:T(128)S(1)}, u32[]{:S(2)}, u32[]{:S(2)}) collective-permute-start(f32[128]{0:T(128)S(1)} %multiply_subtract_fusion), channel_id=1, source_target_pairs={{0,3},{1,0},{2,1},{3,2},{4,7},{5,4},{6,5},{7,6},{8,11},{9,8},{10,9... | collective-permute-start | bytes 1544 | tf_op jit(solution)/shard_map/ppermute | solution.py:161
  74.5 1.7 %convert_add_fusion = f32[128,1024]{1,0:T(8,128)} fusion(bf16[128,1024]{1,0:T(8,128)(2,1)S(1)} %collective-permute-done.5, bf16[128,1024]{1,0:T(8,128)(2,1)S(1)} %collective-permute-done.4, bf16[128,1024]{1,0:T(8,128)(2,1)S(1)} %collective-permute-done.3, bf16[128,1024]{1,0:T(8,128)(2,1)S(1)} %get-tuple-element.9, bf16[4096,1024]{1,0:T(8,128)(2,1)S(1)} %bitcast.118, ...), kind=kOutput, calls=%fused_computation.47 | convolution fusion | flops 269221888 | bytes 3670020 | tf_op jit(solution)/shard_map/dot_general | solution.py:187
  76.1 1.2 copy.19
  77.9 1.1 convolution_bitcast_fusion.1.state_ref
  79.6 60.7 %shard_map.112 = f32[8,128,128]{2,1,0:T(8,128)} custom-call(f32[8,128,128]{2,1,0:T(8,128)} %convolution_bitcast_fusion.1.state_ref), custom_call_target="tpu_custom_call" | custom-call | tf_op jit(solution)/shard_map/pallas_call | solution.py:112
  140.3 1.5 %convolution_bitcast_fusion = f32[128,8,128]{0,2,1:T(8,128)S(1)} fusion(f32[8,128,128]{2,1,0:T(8,128)} %shard_map.112, bf16[128,1024]{1,0:T(8,128)(2,1)S(1)} %copy-done), kind=kOutput, calls=%fused_computation.19 | convolution fusion | flops 100663296 | bytes 1310720 | tf_op jit(solution)/shard_map/she,hde->shd/dot_general | solution.py:216
  141.8 1.5 %fusion.29 = bf16[8,128,128]{2,1,0:T(8,128)(2,1)S(1)} fusion(f32[8,128,128]{2,1,0:T(8,128)S(1)} %fusion.82, f32[8,128,128]{2,1,0:T(8,128)} %shard_map.112, bf16[128,1024]{1,0:T(8,128)(2,1)S(1)} %copy-done.3), kind=kOutput, calls=%fused_computation.34 | convolution fusion | flops 100925440 | bytes 1572864 | tf_op jit(solution)/shard_map/shd,hde->she/dot_general | solution.py:222
  (59 shorter events, 12.7 us)
Async XLA Ops:
  0.6 1.3 copy-start
  0.6 35.8 %copy-start.4 = (f32[32,1024]{1,0:T(8,128)S(1)}, f32[32,1024]{1,0:T(8,128)}, u32[]{:S(2)}) copy-start(f32[32,1024]{1,0:T(8,128)} %param.12) | copy-start | bytes 393220
  0.7 35.8 %copy-start.6 = (s32[128]{0:T(128)S(1)}, s32[128]{0:T(128)}, u32[]{:S(2)}) copy-start(s32[128]{0:T(128)} %param.14) | copy-start | bytes 1540
  28.7 20.2 %copy-start.7 = (s32[128]{0:T(128)S(1)}, s32[128]{0:T(128)}, u32[]{:S(2)}) copy-start(s32[128]{0:T(128)} %param.15) | copy-start | bytes 1540
  28.7 20.2 %copy-start.8 = (s32[128]{0:T(128)S(1)}, s32[128]{0:T(128)}, u32[]{:S(2)}) copy-start(s32[128]{0:T(128)} %param.13) | copy-start | bytes 1540
  29.3 8.8 %collective-permute-start.1 = (bf16[128,1024]{0,1:T(8,128)(2,1)S(1)}, bf16[128,1024]{0,1:T(8,128)(2,1)S(1)}, u32[]{:S(2)}, u32[]{:S(2)}) collective-permute-start(bf16[128,1024]{0,1:T(8,128)(2,1)S(1)} %bitcast.120), channel_id=1, source_target_pairs={{0,2},{1,3},{2,0},{3,1},{4,6},{5,7},{6,4},{7,5},{8,10},{9,11},{10,... | collective-permute-start | bytes 786440 | tf_op jit(solution)/shard_map/ppermute | solution.py:161
  32.8 11.7 %collective-permute-start.2 = (bf16[128,1024]{0,1:T(8,128)(2,1)S(1)}, bf16[128,1024]{0,1:T(8,128)(2,1)S(1)}, u32[]{:S(2)}, u32[]{:S(2)}) collective-permute-start(bf16[128,1024]{0,1:T(8,128)(2,1)S(1)} %bitcast.121), channel_id=1, source_target_pairs={{0,3},{1,0},{2,1},{3,2},{4,7},{5,4},{6,5},{7,6},{8,11},{9,8},{10,9... | collective-permute-start | bytes 786440 | tf_op jit(solution)/shard_map/ppermute | solution.py:161
  33.7 12.9 %collective-permute-start = (bf16[128,1024]{0,1:T(8,128)(2,1)S(1)}, bf16[128,1024]{0,1:T(8,128)(2,1)S(1)}, u32[]{:S(2)}, u32[]{:S(2)}) collective-permute-start(bf16[128,1024]{0,1:T(8,128)(2,1)S(1)} %bitcast.122), channel_id=1, source_target_pairs={{0,1},{1,2},{2,3},{3,0},{4,5},{5,6},{6,7},{7,4},{8,9},{9,10},{10,1... | collective-permute-start | bytes 786440 | tf_op jit(solution)/shard_map/ppermute | solution.py:161
  37.3 13.0 %copy-start.5 = (f32[32,1024]{1,0:T(8,128)S(1)}, f32[32,1024]{1,0:T(8,128)}, u32[]{:S(2)}) copy-start(f32[32,1024]{1,0:T(8,128)} %reduce_window_sum.11) | copy-start | bytes 393220
  37.3 18.6 %slice-start = ((s8[8388608]{0:T(1024)(128)(4,1)}), s8[4194304]{0:T(1024)(128)(4,1)S(1)}, s32[]{:S(2)}) async-start(s8[8388608]{0:T(1024)(128)(4,1)} %bitcast.117), calls=%async_computation | async-start | bytes 8388608
  46.6 9.3 %slice-start.1 = ((s8[8388608]{0:T(1024)(128)(4,1)}), s8[4194304]{0:T(1024)(128)(4,1)S(1)}, s32[]{:S(2)}) async-start(s8[8388608]{0:T(1024)(128)(4,1)} %bitcast.117), calls=%async_computation.1 | async-start | bytes 8388608
  50.9 27.0 %copy-start.2 = (bf16[128,1024]{1,0:T(8,128)(2,1)S(1)}, bf16[128,1024]{1,0:T(8,128)(2,1)}, u32[]{:S(2)}) copy-start(bf16[128,1024]{1,0:T(8,128)(2,1)} %param.8) | copy-start | bytes 786436
  53.4 25.9 %copy-start.1 = (f32[8,128,128]{2,1,0:T(8,128)S(1)}, f32[8,128,128]{2,1,0:T(8,128)}, u32[]{:S(2)}) copy-start(f32[8,128,128]{2,1,0:T(8,128)} %shard_map.111) | copy-start | bytes 1572868
  55.9 85.9 %copy-start.3 = (bf16[128,1024]{1,0:T(8,128)(2,1)S(1)}, bf16[128,1024]{1,0:T(8,128)(2,1)}, u32[]{:S(2)}) copy-start(bf16[128,1024]{1,0:T(8,128)(2,1)} %param.9) | copy-start | bytes 786436
  56.7 17.7 %collective-permute-start.3 = (bf16[128,1024]{1,0:T(8,128)(2,1)S(1)}, bf16[128,1024]{1,0:T(8,128)(2,1)S(1)}, u32[]{:S(2)}, u32[]{:S(2)}) collective-permute-start(bf16[128,1024]{1,0:T(8,128)(2,1)S(1)} %fusion.38), channel_id=1, source_target_pairs={{0,1},{1,2},{2,3},{3,0},{4,5},{5,6},{6,7},{7,4},{8,9},{9,10},{10,1... | collective-permute-start | bytes 786440 | tf_op jit(solution)/shard_map/ppermute | solution.py:161
  59.0 15.5 %collective-permute-start.4 = (bf16[128,1024]{1,0:T(8,128)(2,1)S(1)}, bf16[128,1024]{1,0:T(8,128)(2,1)S(1)}, u32[]{:S(2)}, u32[]{:S(2)}) collective-permute-start(bf16[128,1024]{1,0:T(8,128)(2,1)S(1)} %fusion.35), channel_id=1, source_target_pairs={{0,2},{1,3},{2,0},{3,1},{4,6},{5,7},{6,4},{7,5},{8,10},{9,11},{10,... | collective-permute-start | bytes 786440 | tf_op jit(solution)/shard_map/ppermute | solution.py:161
  61.4 13.1 %collective-permute-start.5 = (bf16[128,1024]{1,0:T(8,128)(2,1)S(1)}, bf16[128,1024]{1,0:T(8,128)(2,1)S(1)}, u32[]{:S(2)}, u32[]{:S(2)}) collective-permute-start(bf16[128,1024]{1,0:T(8,128)(2,1)S(1)} %fusion.32), channel_id=1, source_target_pairs={{0,3},{1,0},{2,1},{3,2},{4,7},{5,4},{6,5},{7,6},{8,11},{9,8},{10,9... | collective-permute-start | bytes 786440 | tf_op jit(solution)/shard_map/ppermute | solution.py:161
  61.5 8.4 %collective-permute-start.6 = (f32[128]{0:T(128)S(1)}, f32[128]{0:T(128)S(1)}, u32[]{:S(2)}, u32[]{:S(2)}) collective-permute-start(f32[128]{0:T(128)S(1)} %multiply_subtract_fusion), channel_id=1, source_target_pairs={{0,1},{1,2},{2,3},{3,0},{4,5},{5,6},{6,7},{7,4},{8,9},{9,10},{10,1... | collective-permute-start | bytes 1544 | tf_op jit(solution)/shard_map/ppermute | solution.py:161
  62.9 10.3 %collective-permute-start.7 = (f32[128]{0:T(128)S(1)}, f32[128]{0:T(128)S(1)}, u32[]{:S(2)}, u32[]{:S(2)}) collective-permute-start(f32[128]{0:T(128)S(1)} %multiply_subtract_fusion), channel_id=1, source_target_pairs={{0,2},{1,3},{2,0},{3,1},{4,6},{5,7},{6,4},{7,5},{8,10},{9,11},{10,... | collective-permute-start | bytes 1544 | tf_op jit(solution)/shard_map/ppermute | solution.py:161
  69.8 4.1 %collective-permute-start.8 = (f32[128]{0:T(128)S(1)}, f32[128]{0:T(128)S(1)}, u32[]{:S(2)}, u32[]{:S(2)}) collective-permute-start(f32[128]{0:T(128)S(1)} %multiply_subtract_fusion), channel_id=1, source_target_pairs={{0,3},{1,0},{2,1},{3,2},{4,7},{5,4},{6,5},{7,6},{8,11},{9,8},{10,9... | collective-permute-start | bytes 1544 | tf_op jit(solution)/shard_map/ppermute | solution.py:161

commit v7 on v6

--- a/solution.py
+++ b/solution.py
@@ -129,6 +129,94 @@
     )(shard)
 
 
+def head_barrier(count):
+    me = lax.axis_index("head")
+    seq = lax.axis_index("seq")
+    barrier = pltpu.get_barrier_semaphore()
+    for k in range(1, count):
+        pl.semaphore_signal(barrier, 1, device_id=(seq, (me + k) % count), device_id_type=MESH)
+    pl.semaphore_wait(barrier, count - 1)
+    return me, seq
+
+
+def gather_kernel(count, block_ref, out_ref, slots, send_sems, recv_sems):
+    me, seq = head_barrier(count)
+    copies = []
+    for k in range(1, count):
+        copy = pltpu.make_async_remote_copy(
+            block_ref, slots.at[k], send_sems.at[k], recv_sems.at[k],
+            device_id=(seq, (me + k) % count), device_id_type=MESH,
+        )
+        copy.start()
+        copies.append(copy)
+    out_ref[0] = block_ref[...]
+    for k, copy in enumerate(copies, start=1):
+        copy.wait()
+        out_ref[k] = slots[k]
+
+
+def head_gather(block, count):
+    return pl.pallas_call(
+        functools.partial(gather_kernel, count),
+        out_shape=jax.ShapeDtypeStruct((count,) + block.shape, block.dtype),
+        in_specs=[pl.BlockSpec(memory_space=pltpu.VMEM)],
+        out_specs=pl.BlockSpec(memory_space=pltpu.VMEM),
+        scratch_shapes=[
+            pltpu.VMEM((count,) + block.shape, block.dtype),
+            pltpu.SemaphoreType.DMA((count,)),
+            pltpu.SemaphoreType.DMA((count,)),
+        ],
+        compiler_params=pltpu.CompilerParams(collective_id=2, has_side_effects=True),
+    )(block)
+
+
+def reduce_kernel(count, parts_ref, loss_ref, out_ref, loss_out, slots, loss_slots, send_sems, recv_sems):
+    me, seq = head_barrier(count)
+    copies = []
+    for k in range(1, count):
+        target = (seq, (me + k) % count)
+        copy = pltpu.make_async_remote_copy(
+            parts_ref.at[k], slots.at[k], send_sems.at[0, k], recv_sems.at[0, k],
+            device_id=target, device_id_type=MESH,
+        )
+        copy.start()
+        small = pltpu.make_async_remote_copy(
+            loss_ref, loss_slots.at[k], send_sems.at[1, k], recv_sems.at[1, k],
+            device_id=target, device_id_type=MESH,
+        )
+        small.start()
+        copies.append((copy, small))
+    total = jnp.zeros(out_ref.shape, jnp.float32)
+    loss = loss_ref[...]
+    for k, (copy, small) in enumerate(copies, start=1):
+        copy.wait()
+        total = total + slots[k].astype(jnp.float32)
+        small.wait()
+        loss = loss + loss_slots[k]
+    out_ref[...] = total
+    loss_out[...] = loss
+
+
+def head_reduce(parts, loss, count):
+    block = parts.shape[1:]
+    return pl.pallas_call(
+        functools.partial(reduce_kernel, count),
+        out_shape=(
+            jax.ShapeDtypeStruct(block, jnp.float32),
+            jax.ShapeDtypeStruct(loss.shape, loss.dtype),
+        ),
+        in_specs=[pl.BlockSpec(memory_space=pltpu.VMEM)] * 2,
+        out_specs=(pl.BlockSpec(memory_space=pltpu.VMEM),) * 2,
+        scratch_shapes=[
+            pltpu.VMEM(parts.shape, parts.dtype),
+            pltpu.VMEM((count,) + loss.shape, loss.dtype),
+            pltpu.SemaphoreType.DMA((2, count)),
+            pltpu.SemaphoreType.DMA((2, count)),
+        ],
+        compiler_params=pltpu.CompilerParams(collective_id=3, has_side_effects=True),
+    )(parts, loss)
+
+
 def body(queries, keys, values, hazard_weight, log_base, time_bin, observed, task_label):
     highest = lax.Precision.HIGHEST
     three_pass = lax.Precision.HIGH
@@ -157,16 +245,14 @@
     head_count = lax.axis_size("head")
     head_index = lax.axis_index("head")
 
-    def shifted(x, k):
-        return lax.ppermute(x, "head", [(m, (m + k) % head_count) for m in range(head_count)])
-
     def weight_rows(owner):
         return lax.dynamic_slice_in_dim(hazard_weight, owner * width_here, width_here, 0)
 
-    log_rate = jnp.dot(hidden, weight_rows(head_index), preferred_element_type=f32)
+    gathered = head_gather(hidden, head_count)
+    log_rate = jnp.dot(gathered[0], weight_rows(head_index), preferred_element_type=f32)
     for k in range(1, head_count):
         log_rate = log_rate + jnp.dot(
-            shifted(hidden, k),
+            gathered[k],
             weight_rows((head_index - k + head_count) % head_count),
             preferred_element_type=f32,
         )
@@ -188,12 +274,12 @@
             dlogit, weight_rows(owner), (((1,), (1,)), ((), ())), preferred_element_type=f32
         )
 
-    grad_hidden = block_term(head_index)
-    event_loss = partial_value
-    for k in range(1, head_count):
-        sent = block_term((head_index + k) % head_count).astype(jnp.bfloat16)
-        grad_hidden = grad_hidden + shifted(sent, k).astype(f32)
-        event_loss = event_loss + shifted(partial_value, k)
+    parts = jnp.stack(
+        [block_term((head_index + k) % head_count).astype(jnp.bfloat16) for k in range(head_count)]
+    )
+    received, loss_sum = head_reduce(parts, partial_value.reshape(1, -1), head_count)
+    grad_hidden = block_term(head_index) + received
+    event_loss = loss_sum.reshape(-1)
     grad_norm_in = grad_hidden.reshape(shape_three)
     grad_raw = (
         grad_norm_in - normed * jnp.mean(normed * grad_norm_in, axis=-1, keepdims=True)

time: 147 us -> 158 us (1.075)
  Pallas kernels: 83.5 us -> 118 us
  starting transfers between devices: 15 us -> 0 us
  waiting for transfers between devices: 11.9 us -> 0 us
  local copies, waits for them, and re-layouts: 5.13 us -> 7.36 us
    pallas_call x0 -> x2, Pallas kernels: none -> 34.8 us  [the longest x1 18 us: head_reduce(): pl.pallas_call(functools.partial(reduce_kernel, count), out_shape=(jax.Sh...]
    ppermute x9 -> x0, starting transfers between devices: 15 us -> none  [shifted(): lax.ppermute(x, 'head', [(m, (m + k) % head_count) for m in range(head_co...]
    ppermute x9 -> x0, waiting for transfers between devices: 11.9 us -> none  [shifted(): lax.ppermute(x, 'head', [(m, (m + k) % head_count) for m in range(head_co...]
    reshape x0 -> x2, local copies, waits for them, and re-layouts: none -> 2.08 us  [the longest x1 1.23 us: body(): grad_norm_in = grad_hidden.reshape(shape_three)]
    dot_general x4 -> x5, matrix products: 7.45 us -> 8.26 us  [block_term(): lax.dot_general(dlogit, weight_rows(owner), (((1,), (1,)), ((), ())), pre...]
    unnamed x26 -> x27, local copies, waits for them, and re-layouts: 3.65 us -> 4.12 us
  transfers between devices with their start and end apart: 9 -> 0, of which waited for: 4 -> 0; matrix products, arithmetic and copies ran while one was open for 5% -> 0% of each run, Pallas kernels for 0% -> 0%
where the time goes in v7:
time: 158 us
  Pallas kernels  118 us (75%)
  matrix products  28.5 us (18%)
  local copies, waits for them, and re-layouts  7.36 us (5%)
  other arithmetic  2.69 us (2%)
    pallas_call x2, Pallas kernels, exclusive_scan(): pl.pallas_call(functools.partial(scan_kernel, reverse, count), out_shape=...  83.2 us
    pallas_call x1, Pallas kernels, head_reduce(): pl.pallas_call(functools.partial(reduce_kernel, count), out_shape=(jax.Sh...  18 us
    pallas_call x1, Pallas kernels, head_gather(): pl.pallas_call(functools.partial(gather_kernel, count), out_shape=jax.Sha...  16.8 us
    dot_general x5, matrix products, block_term(): lax.dot_general(dlogit, weight_rows(owner), (((1,), (1,)), ((), ())), pre...  8.26 us
    dot_general x3, matrix products, body(): jnp.dot(gathered[k], weight_rows((head_index - k + head_count) % head_cou...  6.68 us
    unnamed x27, local copies, waits for them, and re-layouts  4.12 us

profile of v7, /device:TPU:1, one launch (start us, length us, event | category | flops | bytes accessed | tf_op | source)
XLA Modules:
  0.0 157.6 jit_solution(11261577573498813380)
XLA Ops:
  1.4 0.9 exp.7
  2.5 1.0 copy.45
  3.7 1.3 convolution_multiply_fusion.2
  5.1 1.0 fusion.68.state_ref
  6.1 23.5 %shard_map.111 = f32[8,128,128]{2,1,0:T(8,128)} custom-call(f32[8,128,128]{2,1,0:T(8,128)} %fusion.68.state_ref), custom_call_target="tpu_custom_call" | custom-call | tf_op jit(solution)/shard_map/pallas_call | solution.py:112
  29.6 1.6 convolution_bitcast_fusion.5
  32.6 16.8 %shard_map.112 = bf16[4,128,1024]{2,1,0:T(8,128)(2,1)} custom-call(bf16[128,1024]{1,0:T(8,128)(2,1)} %copy.40.block_ref), custom_call_target="tpu_custom_call" | custom-call | tf_op jit(solution)/shard_map/pallas_call | solution.py:159
  49.5 2.3 %fusion.12 = f32[128,1024]{1,0:T(8,128)S(1)} fusion(bf16[4096,1024]{1,0:T(8,128)(2,1)} %param.11, s32[]{:T(128)S(6)} %select_n.57, bf16[4,128,1024]{2,1,0:T(8,128)(2,1)} %shard_map.112), kind=kOutput, calls=%fused_computation.12 | convolution fusion | flops 268435456 | bytes 2883588 | tf_op jit(solution)/shard_map/dot_general | solution.py:254
  51.8 2.1 %fusion.18 = f32[128,1024]{1,0:T(8,128)S(1)} fusion(f32[128,1024]{1,0:T(8,128)S(1)} %fusion.12, bf16[4096,1024]{1,0:T(8,128)(2,1)} %param.11, s32[]{:T(128)S(6)} %select_n.55, bf16[4,128,1024]{2,1,0:T(8,128)(2,1)} %shard_map.112), kind=kOutput, calls=%fused_computation.18 | convolution fusion | flops 268566528 | bytes 3407876 | tf_op jit(solution)/shard_map/dot_general | solution.py:252
  53.9 2.3 %fusion.24 = f32[128,1024]{1,0:T(8,128)S(1)} fusion(f32[128,1024]{1,0:T(8,128)S(1)} %fusion.18, bf16[4096,1024]{1,0:T(8,128)(2,1)} %param.11, s32[]{:T(128)S(6)} %select_n.59, bf16[4,128,1024]{2,1,0:T(8,128)(2,1)} %shard_map.112), kind=kOutput, calls=%fused_computation.20 | convolution fusion | flops 268566528 | bytes 3407876 | tf_op jit(solution)/shard_map/dot_general | solution.py:254
  56.2 2.1 %fusion.27 = f32[128,1024]{1,0:T(8,128)S(1)} fusion(f32[128,1024]{1,0:T(8,128)S(1)} %fusion.24, bf16[4096,1024]{1,0:T(8,128)(2,1)} %param.11, s32[]{:T(128)S(6)} %select_n.61, bf16[4,128,1024]{2,1,0:T(8,128)(2,1)} %shard_map.112), kind=kOutput, calls=%fused_computation.21 | convolution fusion | flops 268566528 | bytes 3407876 | tf_op jit(solution)/shard_map/dot_general | solution.py:254
  60.0 2.4 %fusion.59 = bf16[1,128,1024]{2,1,0:T(8,128)(2,1)S(1)} fusion(bf16[128,1024]{1,0:T(8,128)(2,1)S(1)} %get-tuple-element.13, bf16[4096,1024]{1,0:T(8,128)(2,1)} %param.11, s32[]{:T(128)S(6)} %select_n.57), kind=kOutput, calls=%fused_computation.49 | convolution fusion | flops 268566528 | bytes 2621444 | tf_op jit(solution)/shard_map/dot_general | solution.py:273
  62.5 0.9 fusion.56
  63.3 0.9 fusion.53
  64.2 0.9 fusion.50
  65.1 1.1 pad_maximum_fusion.parts_ref
  66.2 18.0 %shard_map.113 = (f32[128,1024]{1,0:T(8,128)}, f32[1,128]{1,0:T(1,128)}) custom-call(bf16[4,128,1024]{2,1,0:T(8,128)(2,1)} %pad_maximum_fusion.parts_ref, f32[1,128]{1,0:T(1,128)} %subtract_bitcast_fusion.loss_ref), custom_call_target="tpu_custom_call" | custom-call | tf_op jit(solution)/shard_map/pallas_call | solution.py:202
  84.1 3.3 %fusion.21 = f32[128,1024]{1,0:T(8,128)} fusion(f32[128,1024]{1,0:T(8,128)} %get-tuple-element.6, bf16[128,1024]{1,0:T(8,128)(2,1)S(1)} %get-tuple-element.13, bf16[4096,1024]{1,0:T(8,128)(2,1)} %param.11, s32[]{:T(128)S(6)} %select_n.55), kind=kOutput, calls=%fused_computation.19 | convolution fusion | flops 268566528 | bytes 3407876 | tf_op jit(solution)/shard_map/dot_general | solution.py:273
  87.4 1.2 copy.41
  90.3 0.9 copy.32
  91.1 1.1 convolution_bitcast_fusion.1.state_ref
  92.3 59.7 %shard_map.114 = f32[8,128,128]{2,1,0:T(8,128)} custom-call(f32[8,128,128]{2,1,0:T(8,128)} %convolution_bitcast_fusion.1.state_ref), custom_call_target="tpu_custom_call" | custom-call | tf_op jit(solution)/shard_map/pallas_call | solution.py:112
  152.0 1.5 fusion.34
  153.5 1.5 convolution_bitcast_fusion
  (46 shorter events, 8.3 us)
Async XLA Ops:
  0.6 4.4 %copy-start = (bf16[128,1024]{1,0:T(8,128)(2,1)S(1)}, bf16[128,1024]{1,0:T(8,128)(2,1)}, u32[]{:S(2)}) copy-start(bf16[128,1024]{1,0:T(8,128)(2,1)} %param.10) | copy-start | bytes 786436
  31.1 27.2 %copy-start.4 = (f32[32,1024]{1,0:T(8,128)S(1)}, f32[32,1024]{1,0:T(8,128)}, u32[]{:S(2)}) copy-start(f32[32,1024]{1,0:T(8,128)} %param.12) | copy-start | bytes 393220
  31.1 27.2 %copy-start.6 = (s32[128]{0:T(128)S(1)}, s32[128]{0:T(128)}, u32[]{:S(2)}) copy-start(s32[128]{0:T(128)} %param.15) | copy-start | bytes 1540
  31.1 27.2 %copy-start.7 = (s32[128]{0:T(128)S(1)}, s32[128]{0:T(128)}, u32[]{:S(2)}) copy-start(s32[128]{0:T(128)} %param.13) | copy-start | bytes 1540
  31.8 27.7 %copy-start.5 = (s32[128]{0:T(128)S(1)}, s32[128]{0:T(128)}, u32[]{:S(2)}) copy-start(s32[128]{0:T(128)} %param.14) | copy-start | bytes 1540
  49.5 13.0 %slice-start = ((s8[8388608]{0:T(1024)(128)(4,1)}), s8[4194304]{0:T(1024)(128)(4,1)S(1)}, s32[]{:S(2)}) async-start(s8[8388608]{0:T(1024)(128)(4,1)} %bitcast.136), calls=%async_computation | async-start | bytes 8388608
  53.9 8.5 %slice-start.1 = ((s8[8388608]{0:T(1024)(128)(4,1)}), s8[4194304]{0:T(1024)(128)(4,1)S(1)}, s32[]{:S(2)}) async-start(s8[8388608]{0:T(1024)(128)(4,1)} %bitcast.136), calls=%async_computation.1 | async-start | bytes 8388608
  63.3 25.9 %copy-start.1 = (f32[8,128,128]{2,1,0:T(8,128)S(1)}, f32[8,128,128]{2,1,0:T(8,128)}, u32[]{:S(2)}) copy-start(f32[8,128,128]{2,1,0:T(8,128)} %shard_map.111) | copy-start | bytes 1572868
  65.0 26.1 %copy-start.2 = (bf16[128,1024]{1,0:T(8,128)(2,1)S(1)}, bf16[128,1024]{1,0:T(8,128)(2,1)}, u32[]{:S(2)}) copy-start(bf16[128,1024]{1,0:T(8,128)(2,1)} %param.8) | copy-start | bytes 786436
  66.2 85.8 %copy-start.3 = (bf16[128,1024]{1,0:T(8,128)(2,1)S(1)}, bf16[128,1024]{1,0:T(8,128)(2,1)}, u32[]{:S(2)}) copy-start(bf16[128,1024]{1,0:T(8,128)(2,1)} %param.9) | copy-start | bytes 786436
  87.4 69.7 %copy-start.8 = (f32[1,128]{1,0:T(1,128)S(1)}, f32[1,128]{1,0:T(1,128)}, u32[]{:S(2)}) copy-start(f32[1,128]{1,0:T(1,128)} %get-tuple-element.7) | copy-start | bytes 1540

commit v8 on v6

--- a/solution.py
+++ b/solution.py
@@ -157,19 +157,15 @@
     head_count = lax.axis_size("head")
     head_index = lax.axis_index("head")
 
-    def shifted(x, k):
-        return lax.ppermute(x, "head", [(m, (m + k) % head_count) for m in range(head_count)])
-
     def weight_rows(owner):
         return lax.dynamic_slice_in_dim(hazard_weight, owner * width_here, width_here, 0)
 
-    log_rate = jnp.dot(hidden, weight_rows(head_index), preferred_element_type=f32)
-    for k in range(1, head_count):
-        log_rate = log_rate + jnp.dot(
-            shifted(hidden, k),
-            weight_rows((head_index - k + head_count) % head_count),
-            preferred_element_type=f32,
-        )
+    gathered = lax.all_to_all(
+        jnp.broadcast_to(hidden[None], (head_count,) + hidden.shape), "head", 0, 0, tiled=True
+    )
+    log_rate = jnp.dot(gathered[0], weight_rows(0), preferred_element_type=f32)
+    for owner in range(1, head_count):
+        log_rate = log_rate + jnp.dot(gathered[owner], weight_rows(owner), preferred_element_type=f32)
     offset = head_index * tasks_here
     cum_base = jnp.cumsum(jnp.exp(log_base), axis=0)
     bin_hot = (time_bin[:, None] == jnp.arange(BINS, dtype=jnp.int32)[None, :]).astype(f32)
@@ -188,12 +184,16 @@
             dlogit, weight_rows(owner), (((1,), (1,)), ((), ())), preferred_element_type=f32
         )
 
-    grad_hidden = block_term(head_index)
-    event_loss = partial_value
-    for k in range(1, head_count):
-        sent = block_term((head_index + k) % head_count).astype(jnp.bfloat16)
-        grad_hidden = grad_hidden + shifted(sent, k).astype(f32)
-        event_loss = event_loss + shifted(partial_value, k)
+    parts = jnp.stack([block_term(owner).astype(jnp.bfloat16) for owner in range(head_count)])
+    received = lax.all_to_all(parts, "head", 0, 0, tiled=True).astype(f32)
+    own = block_term(head_index)
+    grad_hidden = own
+    for owner in range(head_count):
+        grad_hidden = grad_hidden + jnp.where(owner == head_index, 0.0, received[owner])
+    losses = lax.all_to_all(
+        jnp.broadcast_to(partial_value[None], (head_count,) + partial_value.shape), "head", 0, 0, tiled=True
+    )
+    event_loss = jnp.sum(losses, axis=0)
     grad_norm_in = grad_hidden.reshape(shape_three)
     grad_raw = (
         grad_norm_in - normed * jnp.mean(normed * grad_norm_in, axis=-1, keepdims=True)

time: 147 us -> 161 us (1.095)
  waiting for transfers between devices: 11.9 us -> 27.2 us
  starting transfers between devices: 15 us -> 10.8 us
  matrix products: 28.6 us -> 24.7 us
  Pallas kernels: 83.5 us -> 87 us
    all_to_all x0 -> x3, waiting for transfers between devices: none -> 27.2 us  [the longest x1 13.2 us: body(): lax.all_to_all(jnp.broadcast_to(hidden[None], (head_count,) + hidden.shap...]
    ppermute x9 -> x0, starting transfers between devices: 15 us -> none  [shifted(): lax.ppermute(x, 'head', [(m, (m + k) % head_count) for m in range(head_co...]
    ppermute x9 -> x0, waiting for transfers between devices: 11.9 us -> none  [shifted(): lax.ppermute(x, 'head', [(m, (m + k) % head_count) for m in range(head_co...]
    all_to_all x0 -> x3, starting transfers between devices: none -> 10.8 us  [the longest x1 4.02 us: body(): lax.all_to_all(jnp.broadcast_to(hidden[None], (head_count,) + hidden.shap...]
    pallas_call x2, Pallas kernels: 83.5 us -> 87 us  [exclusive_scan(): pl.pallas_call(functools.partial(scan_kernel, reverse, count), out_shape=...]
    broadcast_in_dim x0 -> x3, local copies, waits for them, and re-layouts: none -> 1.83 us  [the longest x2 1.25 us: body(): jnp.broadcast_to(hidden[None], (head_count,) + hidden.shape)]
    dot_general x4 -> x5, matrix products: 7.45 us -> 5.82 us  [block_term(): lax.dot_general(dlogit, weight_rows(owner), (((1,), (1,)), ((), ())), pre...]
    unnamed x26 -> x30, local copies, waits for them, and re-layouts: 3.65 us -> 4.19 us
  transfers between devices with their start and end apart: 9 -> 3, of which waited for: 4 -> 3; matrix products, arithmetic and copies ran while one was open for 5% -> 2% of each run, Pallas kernels for 0% -> 0%
where the time goes in v8:
time: 161 us; the launch traced here: 160 us
  Pallas kernels  87 us (54%)
  waiting for transfers between devices  27.2 us (17%)
  matrix products  24.7 us (15%)
  starting transfers between devices  10.8 us (7%)
  local copies, waits for them, and re-layouts  6.46 us (4%)
  other arithmetic  2.94 us (2%)
    pallas_call x2, Pallas kernels, exclusive_scan(): pl.pallas_call(functools.partial(scan_kernel, reverse, count), out_shape=...  87 us
    all_to_all x1, waiting for transfers between devices, body(): lax.all_to_all(jnp.broadcast_to(hidden[None], (head_count,) + hidden.shap...  13.2 us
    all_to_all x1, waiting for transfers between devices, body(): received = lax.all_to_all(parts, 'head', 0, 0, tiled=True).astype(f32)  11.1 us
    dot_general x3, matrix products, body(): jnp.dot(gathered[owner], weight_rows(owner), preferred_element_type=f32)  6.42 us
    dot_general x5, matrix products, block_term(): lax.dot_general(dlogit, weight_rows(owner), (((1,), (1,)), ((), ())), pre...  5.82 us
    unnamed x30, local copies, waits for them, and re-layouts  4.19 us
    all_to_all x1, starting transfers between devices, body(): lax.all_to_all(jnp.broadcast_to(hidden[None], (head_count,) + hidden.shap...  4.02 us
    all_to_all x1, starting transfers between devices, body(): received = lax.all_to_all(parts, 'head', 0, 0, tiled=True).astype(f32)  3.52 us
  transfers between devices with their start and end apart: 3, of which 3 were waited for; matrix products, arithmetic and copies ran while one was open for 2% of the time, Pallas kernels for 0%

profile of v8, /device:TPU:1, one launch (start us, length us, event | category | flops | bytes accessed | tf_op | source)
XLA Modules:
  0.0 160.1 jit_solution(3660792290632966302)
XLA Ops:
  0.7 1.1 copy.87
  2.0 1.0 fusion.81.state_ref
  3.0 23.5 %shard_map.111 = f32[8,128,128]{2,1,0:T(8,128)} custom-call(f32[8,128,128]{2,1,0:T(8,128)} %fusion.81.state_ref), custom_call_target="tpu_custom_call" | custom-call | tf_op jit(solution)/shard_map/pallas_call | solution.py:112
  26.8 1.5 convolution_bitcast_fusion.5
  29.1 1.1 broadcast_in_dim.20
  30.2 4.0 %all-to-all-start = ((bf16[4,128,1024]{2,1,0:T(8,128)(2,1)}), bf16[4,128,1024]{2,1,0:T(8,128)(2,1)S(1)}, u32[]{:S(2)}, u32[]{:S(2)}) async-start(bf16[4,128,1024]{2,1,0:T(8,128)(2,1)} %broadcast_in_dim.20), calls=%async_computation | async-start | bytes 2097152 | tf_op jit(solution)/shard_map/all_to_all | solution.py:163
  35.1 13.2 %all-to-all-done = bf16[4,128,1024]{2,1,0:T(8,128)(2,1)S(1)} async-done(((bf16[4,128,1024]{2,1,0:T(8,128)(2,1)}), bf16[4,128,1024]{2,1,0:T(8,128)(2,1)S(1)}, u32[]{:S(2)}, u32[]{:S(2)}) %all-to-all-start) | async-done | bytes 1048608 | tf_op jit(solution)/shard_map/all_to_all | solution.py:163
  48.3 2.2 %fusion.4 = f32[128,1024]{1,0:T(8,128)S(1)} fusion(bf16[4096,1024]{1,0:T(8,128)(2,1)} %param.11, bf16[4,128,1024]{2,1,0:T(8,128)(2,1)S(1)} %all-to-all-done), kind=kOutput, calls=%fused_computation.4 | convolution fusion | flops 268435456 | bytes 2883584 | tf_op jit(solution)/shard_map/dot_general | solution.py:168
  50.5 2.0 %fusion.8 = f32[128,1024]{1,0:T(8,128)S(1)} fusion(bf16[4096,1024]{1,0:T(8,128)(2,1)} %param.11, bf16[4,128,1024]{2,1,0:T(8,128)(2,1)S(1)} %all-to-all-done), kind=kOutput, calls=%fused_computation.8 | convolution fusion | flops 268435456 | bytes 2883584 | tf_op jit(solution)/shard_map/dot_general | solution.py:168
  52.6 2.2 %fusion.12 = f32[128,1024]{1,0:T(8,128)S(1)} fusion(bf16[4096,1024]{1,0:T(8,128)(2,1)} %param.11, bf16[4,128,1024]{2,1,0:T(8,128)(2,1)S(1)} %all-to-all-done), kind=kOutput, calls=%fused_computation.12 | convolution fusion | flops 268435456 | bytes 2883584 | tf_op jit(solution)/shard_map/dot_general | solution.py:168
  54.8 2.1 %fusion.28 = f32[128,1024]{1,0:T(8,128)S(1)} fusion(f32[128,1024]{1,0:T(8,128)S(1)} %fusion.4, f32[128,1024]{1,0:T(8,128)S(1)} %fusion.8, f32[128,1024]{1,0:T(8,128)S(1)} %fusion.12, bf16[4096,1024]{1,0:T(8,128)(2,1)} %param.11, bf16[4,128,1024]{2,1,0:T(8,128)(2,1)S(1)} %all-to-all-done), kind=kOutput, calls=%fused_computation.31 | convolution fusion | flops 268828672 | bytes 4456448 | tf_op jit(solution)/shard_map/dot_general | solution.py:166
  62.0 3.2 %all-to-all-start.2 = ((f32[4,1,128]{2,1,0:T(1,128)}), f32[4,1,128]{2,1,0:T(1,128)S(1)}, u32[]{:S(2)}, u32[]{:S(2)}) async-start(f32[4,1,128]{2,1,0:T(1,128)} %broadcast_in_dim.38), calls=%async_computation.2 | async-start | bytes 4096 | tf_op jit(solution)/shard_map/all_to_all | solution.py:193
  65.3 1.1 pad_maximum_fusion
  66.4 2.9 %all-to-all-done.2 = f32[4,1,128]{2,1,0:T(1,128)S(1)} async-done(((f32[4,1,128]{2,1,0:T(1,128)}), f32[4,1,128]{2,1,0:T(1,128)S(1)}, u32[]{:S(2)}, u32[]{:S(2)}) %all-to-all-start.2) | async-done | bytes 2080 | tf_op jit(solution)/shard_map/all_to_all | solution.py:193
  69.3 3.5 %all-to-all-start.1 = ((bf16[4,128,1024]{2,1,0:T(8,128)(2,1)}), bf16[4,128,1024]{2,1,0:T(8,128)(2,1)S(1)}, u32[]{:S(2)}, u32[]{:S(2)}) async-start(bf16[4,128,1024]{2,1,0:T(8,128)(2,1)} %pad_maximum_fusion), calls=%async_computation.1 | async-start | bytes 2097152 | tf_op jit(solution)/shard_map/all_to_all | solution.py:188
  73.3 11.1 %all-to-all-done.1 = bf16[4,128,1024]{2,1,0:T(8,128)(2,1)S(1)} async-done(((bf16[4,128,1024]{2,1,0:T(8,128)(2,1)}), bf16[4,128,1024]{2,1,0:T(8,128)(2,1)S(1)}, u32[]{:S(2)}, u32[]{:S(2)}) %all-to-all-start.1) | async-done | bytes 1048608 | tf_op jit(solution)/shard_map/all_to_all | solution.py:188
  84.7 2.5 %fusion.40 = f32[128,1024]{1,0:T(8,128)S(1)} fusion(bf16[128,1024]{1,0:T(8,128)(2,1)S(1)} %copy-done.10, bf16[4096,1024]{1,0:T(8,128)(2,1)} %param.11, s32[]{:T(128)S(6)} %select_n.52, f32[4,128,1024]{2,1,0:T(8,128)S(1)} %convert_element_type.57, pred[]{:T(512)S(6)} %eq.47, pred[]{:T(512)S(6)} %eq.46, pred[]{:T(512)S(6)} %eq.45, pred[]{:T(512)S(6)} %eq.44), kind=kOutput, calls=%fused_computation.39 | convolution fusion | flops 269484032 | bytes 4980744 | tf_op jit(solution)/shard_map/dot_general | solution.py:183
  89.1 1.1 convolution_bitcast_fusion.1.state_ref
  90.7 0.9 copy.76
  91.5 63.5 %shard_map.112 = f32[8,128,128]{2,1,0:T(8,128)} custom-call(f32[8,128,128]{2,1,0:T(8,128)} %convolution_bitcast_fusion.1.state_ref), custom_call_target="tpu_custom_call" | custom-call | tf_op jit(solution)/shard_map/pallas_call | solution.py:112
  155.0 1.5 convolution_bitcast_fusion
  156.5 1.5 fusion.43
  158.4 0.9 copy.77
  159.3 0.8 copy.78
  (57 shorter events, 10.6 us)
Async XLA Ops:
  0.6 1.4 copy-start
  0.6 25.9 %copy-start.3 = (bf16[128,1024]{1,0:T(8,128)(2,1)S(1)}, bf16[128,1024]{1,0:T(8,128)(2,1)}, u32[]{:S(2)}) copy-start(bf16[128,1024]{1,0:T(8,128)(2,1)} %param.9) | copy-start | bytes 786436
  0.7 25.9 %copy-start.2 = (bf16[128,1024]{1,0:T(8,128)(2,1)S(1)}, bf16[128,1024]{1,0:T(8,128)(2,1)}, u32[]{:S(2)}) copy-start(bf16[128,1024]{1,0:T(8,128)(2,1)} %param.8) | copy-start | bytes 786436
  29.0 5.3 %copy-start.6 = (s32[128]{0:T(128)S(1)}, s32[128]{0:T(128)}, u32[]{:S(2)}) copy-start(s32[128]{0:T(128)} %param.14) | copy-start | bytes 1540
  29.0 5.3 %copy-start.4 = (f32[32,1024]{1,0:T(8,128)S(1)}, f32[32,1024]{1,0:T(8,128)}, u32[]{:S(2)}) copy-start(f32[32,1024]{1,0:T(8,128)} %param.12) | copy-start | bytes 393220
  30.2 18.0 %all-to-all-start = ((bf16[4,128,1024]{2,1,0:T(8,128)(2,1)}), bf16[4,128,1024]{2,1,0:T(8,128)(2,1)S(1)}, u32[]{:S(2)}, u32[]{:S(2)}) async-start(bf16[4,128,1024]{2,1,0:T(8,128)(2,1)} %broadcast_in_dim.20), calls=%async_computation | async-start | bytes 2097152 | tf_op jit(solution)/shard_map/all_to_all | solution.py:163
  48.3 9.8 %slice-start = ((s8[8388608]{0:T(1024)(128)(4,1)}), s8[4194304]{0:T(1024)(128)(4,1)S(1)}, s32[]{:S(2)}) async-start(s8[8388608]{0:T(1024)(128)(4,1)} %bitcast.157), calls=%async_computation.3 | async-start | bytes 8388608
  52.5 5.5 %slice-start.1 = ((s8[8388608]{0:T(1024)(128)(4,1)}), s8[4194304]{0:T(1024)(128)(4,1)S(1)}, s32[]{:S(2)}) async-start(s8[8388608]{0:T(1024)(128)(4,1)} %bitcast.157), calls=%async_computation.4 | async-start | bytes 8388608
  54.8 2.2 %copy-start.7 = (s32[128]{0:T(128)S(1)}, s32[128]{0:T(128)}, u32[]{:S(2)}) copy-start(s32[128]{0:T(128)} %param.15) | copy-start | bytes 1540
  54.8 2.2 %copy-start.8 = (s32[128]{0:T(128)S(1)}, s32[128]{0:T(128)}, u32[]{:S(2)}) copy-start(s32[128]{0:T(128)} %param.13) | copy-start | bytes 1540
  54.8 2.7 %copy-start.5 = (f32[32,1024]{1,0:T(8,128)S(1)}, f32[32,1024]{1,0:T(8,128)}, u32[]{:S(2)}) copy-start(f32[32,1024]{1,0:T(8,128)} %reduce_window_sum.11) | copy-start | bytes 393220
  58.0 2.6 %copy-start.9 = (bf16[128,1024]{1,0:T(8,128)(2,1)}, bf16[128,1024]{1,0:T(8,128)(2,1)S(1)}, u32[]{:S(2)}) copy-start(bf16[128,1024]{1,0:T(8,128)(2,1)S(1)} %get-tuple-element.17) | copy-start | bytes 786436
  62.0 7.2 %all-to-all-start.2 = ((f32[4,1,128]{2,1,0:T(1,128)}), f32[4,1,128]{2,1,0:T(1,128)S(1)}, u32[]{:S(2)}, u32[]{:S(2)}) async-start(f32[4,1,128]{2,1,0:T(1,128)} %broadcast_in_dim.38), calls=%async_computation.2 | async-start | bytes 4096 | tf_op jit(solution)/shard_map/all_to_all | solution.py:193
  69.3 15.2 %all-to-all-start.1 = ((bf16[4,128,1024]{2,1,0:T(8,128)(2,1)}), bf16[4,128,1024]{2,1,0:T(8,128)(2,1)S(1)}, u32[]{:S(2)}, u32[]{:S(2)}) async-start(bf16[4,128,1024]{2,1,0:T(8,128)(2,1)} %pad_maximum_fusion), calls=%async_computation.1 | async-start | bytes 2097152 | tf_op jit(solution)/shard_map/all_to_all | solution.py:188
  72.8 11.9 %copy-start.10 = (bf16[128,1024]{1,0:T(8,128)(2,1)S(1)}, bf16[128,1024]{1,0:T(8,128)(2,1)}, u32[]{:S(2)}) copy-start(bf16[128,1024]{1,0:T(8,128)(2,1)} %copy-done.9) | copy-start | bytes 786436
  87.4 1.0 copy-start.1

commit v9 on v6

--- a/solution.py
+++ b/solution.py
@@ -188,12 +188,14 @@
             dlogit, weight_rows(owner), (((1,), (1,)), ((), ())), preferred_element_type=f32
         )
 
-    grad_hidden = block_term(head_index)
+    blocks = jnp.stack([block_term(owner) for owner in range(head_count)])
+    grad_hidden = lax.dynamic_index_in_dim(blocks, head_index, 0, False)
     event_loss = partial_value
     for k in range(1, head_count):
-        sent = block_term((head_index + k) % head_count).astype(jnp.bfloat16)
-        grad_hidden = grad_hidden + shifted(sent, k).astype(f32)
-        event_loss = event_loss + shifted(partial_value, k)
+        sent = lax.dynamic_index_in_dim(blocks, (head_index + k) % head_count, 0, False)
+        got, got_loss = shifted((sent.astype(jnp.bfloat16), partial_value), k)
+        grad_hidden = grad_hidden + got.astype(f32)
+        event_loss = event_loss + got_loss
     grad_norm_in = grad_hidden.reshape(shape_three)
     grad_raw = (
         grad_norm_in - normed * jnp.mean(normed * grad_norm_in, axis=-1, keepdims=True)

time: 147 us -> 151 us (1.027)
  waiting for transfers between devices: 11.9 us -> 17.1 us
  starting transfers between devices: 15 us -> 11 us
  matrix products: 28.6 us -> 25.4 us
  Pallas kernels: 83.5 us -> 86.1 us
  other arithmetic: 1.53 us -> 3.08 us
    ppermute x9, waiting for transfers between devices: 11.9 us -> 17.1 us  [shifted(): lax.ppermute(x, 'head', [(m, (m + k) % head_count) for m in range(head_co...]
    ppermute x9, starting transfers between devices: 15 us -> 11 us  [shifted(): lax.ppermute(x, 'head', [(m, (m + k) % head_count) for m in range(head_co...]
    pallas_call x2, Pallas kernels: 83.5 us -> 86.1 us  [exclusive_scan(): pl.pallas_call(functools.partial(scan_kernel, reverse, count), out_shape=...]
    add x1 -> x2, other arithmetic: 0.51 us -> 2.55 us  [the longest x1 2.04 us: body(): grad_hidden = grad_hidden + got.astype(f32)]
    unnamed x26 -> x32, local copies, waits for them, and re-layouts: 3.65 us -> 4.21 us
  transfers between devices with their start and end apart: 9 -> 9, of which waited for: 4 -> 5; matrix products, arithmetic and copies ran while one was open for 5% -> 5% of each run, Pallas kernels for 0% -> 0%
where the time goes in v9:
time: 151 us
  Pallas kernels  86.1 us (57%)
  matrix products  25.4 us (17%)
  waiting for transfers between devices  17.1 us (11%)
  starting transfers between devices  11 us (7%)
  local copies, waits for them, and re-layouts  6.61 us (4%)
  other arithmetic  3.08 us (2%)
    pallas_call x2, Pallas kernels, exclusive_scan(): pl.pallas_call(functools.partial(scan_kernel, reverse, count), out_shape=...  86.1 us
    ppermute x9, waiting for transfers between devices, shifted(): lax.ppermute(x, 'head', [(m, (m + k) % head_count) for m in range(head_co...  17.1 us
    ppermute x9, starting transfers between devices, shifted(): lax.ppermute(x, 'head', [(m, (m + k) % head_count) for m in range(head_co...  11 us
    dot_general x4, matrix products, block_term(): lax.dot_general(dlogit, weight_rows(owner), (((1,), (1,)), ((), ())), pre...  6.67 us
    dot_general x3, matrix products, body(): jnp.dot(shifted(hidden, k), weight_rows((head_index - k + head_count) % h...  6.35 us
    unnamed x32, local copies, waits for them, and re-layouts  4.21 us
  transfers between devices with their start and end apart: 9, of which 5 were waited for; matrix products, arithmetic and copies ran while one was open for 5% of the time, Pallas kernels for 0%

profile of v9, /device:TPU:1, one launch (start us, length us, event | category | flops | bytes accessed | tf_op | source)
XLA Modules:
  0.0 150.6 jit_solution(5400012635151195918)
XLA Ops:
  0.7 1.1 copy.41
  3.0 22.8 %shard_map.111 = f32[8,128,128]{2,1,0:T(8,128)} custom-call(f32[8,128,128]{2,1,0:T(8,128)} %fusion.56.state_ref), custom_call_target="tpu_custom_call" | custom-call | tf_op jit(solution)/shard_map/pallas_call | solution.py:112
  26.1 1.5 convolution_bitcast_fusion.5
  28.3 3.2 %collective-permute-start.2 = (bf16[128,1024]{0,1:T(8,128)(2,1)S(1)}, bf16[128,1024]{0,1:T(8,128)(2,1)S(1)}, u32[]{:S(2)}, u32[]{:S(2)}) collective-permute-start(bf16[128,1024]{0,1:T(8,128)(2,1)S(1)} %bitcast.140), channel_id=1, source_target_pairs={{0,3},{1,0},{2,1},{3,2},{4,7},{5,4},{6,5},{7,6},{8,11},{9,8},{10,9... | collective-permute-start | bytes 786440 | tf_op jit(solution)/shard_map/ppermute | solution.py:161
  32.7 2.1 %fusion.14 = f32[128,1024]{1,0:T(8,128)S(1)} fusion(bf16[128,1024]{0,1:T(8,128)(2,1)S(1)} %bitcast.143, bf16[4096,1024]{1,0:T(8,128)(2,1)} %param.11, s32[]{:T(128)S(6)} %select_n.57), kind=kOutput, calls=%fused_computation.15 | convolution fusion | flops 268435456 | bytes 2883588 | tf_op jit(solution)/shard_map/dot_general | solution.py:166
  35.0 2.7 %collective-permute-done.2 = bf16[128,1024]{0,1:T(8,128)(2,1)S(1)} collective-permute-done((bf16[128,1024]{0,1:T(8,128)(2,1)S(1)}, bf16[128,1024]{0,1:T(8,128)(2,1)S(1)}, u32[]{:S(2)}, u32[]{:S(2)}) %collective-permute-start.2) | collective-permute-done | bytes 262176 | tf_op jit(solution)/shard_map/ppermute | solution.py:161
  37.7 2.1 %fusion.8 = f32[128,1024]{1,0:T(8,128)S(1)} fusion(bf16[128,1024]{0,1:T(8,128)(2,1)S(1)} %collective-permute-done.2, bf16[4096,1024]{1,0:T(8,128)(2,1)} %param.11, s32[]{:T(128)S(6)} %select_n.63), kind=kOutput, calls=%fused_computation.9 | convolution fusion | flops 268435456 | bytes 2883588 | tf_op jit(solution)/shard_map/dot_general | solution.py:168
  39.8 2.2 %fusion.10 = f32[128,1024]{1,0:T(8,128)S(1)} fusion(bf16[128,1024]{0,1:T(8,128)(2,1)S(1)} %collective-permute-done.1, bf16[4096,1024]{1,0:T(8,128)(2,1)} %param.11, s32[]{:T(128)S(6)} %select_n.61), kind=kOutput, calls=%fused_computation.11 | convolution fusion | flops 268435456 | bytes 2883588 | tf_op jit(solution)/shard_map/dot_general | solution.py:168
  42.0 4.9 %collective-permute-done = bf16[128,1024]{0,1:T(8,128)(2,1)S(1)} collective-permute-done((bf16[128,1024]{0,1:T(8,128)(2,1)S(1)}, bf16[128,1024]{0,1:T(8,128)(2,1)S(1)}, u32[]{:S(2)}, u32[]{:S(2)}) %collective-permute-start) | collective-permute-done | bytes 262176 | tf_op jit(solution)/shard_map/ppermute | solution.py:161
  46.9 2.1 %fusion.38 = f32[128,1024]{1,0:T(8,128)S(1)} fusion(f32[128,1024]{1,0:T(8,128)S(1)} %fusion.8, f32[128,1024]{1,0:T(8,128)S(1)} %fusion.10, f32[128,1024]{1,0:T(8,128)S(1)} %fusion.14, bf16[128,1024]{0,1:T(8,128)(2,1)S(1)} %collective-permute-done, bf16[4096,1024]{1,0:T(8,128)(2,1)} %param.11, s32[]{:T(128)S(6)} %select_n.59), kind=kOutput, calls=%fused_computation.37 | convolution fusion | flops 268828672 | bytes 4456452 | tf_op jit(solution)/shard_map/dot_general | solution.py:168
  50.1 2.6 %fusion.28 = f32[1,128,1024]{2,1,0:T(8,128)S(1)} fusion(bf16[128,1024]{1,0:T(8,128)(2,1)S(1)} %get-tuple-element.12, bf16[4096,1024]{1,0:T(8,128)(2,1)} %param.11), kind=kOutput, calls=%fused_computation.21 | convolution fusion | flops 268435456 | bytes 2883584 | tf_op jit(solution)/shard_map/dot_general | solution.py:187
  52.7 2.4 %fusion.25 = f32[1,128,1024]{2,1,0:T(8,128)S(1)} fusion(bf16[128,1024]{1,0:T(8,128)(2,1)S(1)} %get-tuple-element.12, bf16[4096,1024]{1,0:T(8,128)(2,1)} %param.11), kind=kOutput, calls=%fused_computation.20 | convolution fusion | flops 268435456 | bytes 2883584 | tf_op jit(solution)/shard_map/dot_general | solution.py:187
  57.9 2.8 %collective-permute-start.5 = (bf16[128,1024]{1,0:T(8,128)(2,1)}, bf16[128,1024]{1,0:T(8,128)(2,1)}, u32[]{:S(2)}, u32[]{:S(2)}) collective-permute-start(bf16[128,1024]{1,0:T(8,128)(2,1)} %get-tuple-element.9), channel_id=1, source_target_pairs={{0,3},{1,0},{2,1},{3,2},{4,7},{5,4},{6,5},{7,6},{8,11},{9,8},{10,9... | collective-permute-start | bytes 786440 | tf_op jit(solution)/shard_map/ppermute | solution.py:161
  60.7 1.2 collective-permute-start.4
  62.2 2.4 %collective-permute-start.7 = (f32[128]{0:T(128)S(1)}, f32[128]{0:T(128)S(1)}, u32[]{:S(2)}, u32[]{:S(2)}) collective-permute-start(f32[128]{0:T(128)S(1)} %multiply_subtract_fusion), channel_id=1, source_target_pairs={{0,2},{1,3},{2,0},{3,1},{4,6},{5,7},{6,4},{7,5},{8,10},{9,11},{10,... | collective-permute-start | bytes 1544 | tf_op jit(solution)/shard_map/ppermute | solution.py:161
  64.6 5.5 %collective-permute-done.8 = f32[128]{0:T(128)S(1)} collective-permute-done((f32[128]{0:T(128)S(1)}, f32[128]{0:T(128)S(1)}, u32[]{:S(2)}, u32[]{:S(2)}) %collective-permute-start.8) | collective-permute-done | bytes 544 | tf_op jit(solution)/shard_map/ppermute | solution.py:161
  70.1 2.4 %collective-permute-done.7 = f32[128]{0:T(128)S(1)} collective-permute-done((f32[128]{0:T(128)S(1)}, f32[128]{0:T(128)S(1)}, u32[]{:S(2)}, u32[]{:S(2)}) %collective-permute-start.7) | collective-permute-done | bytes 544 | tf_op jit(solution)/shard_map/ppermute | solution.py:161
  72.4 1.7 %collective-permute-done.6 = f32[128]{0:T(128)S(1)} collective-permute-done((f32[128]{0:T(128)S(1)}, f32[128]{0:T(128)S(1)}, u32[]{:S(2)}, u32[]{:S(2)}) %collective-permute-start.6) | collective-permute-done | bytes 544 | tf_op jit(solution)/shard_map/ppermute | solution.py:161
  74.7 2.0 %fusion.49 = f32[128,1024]{1,0:T(8,128)} fusion(bf16[128,1024]{1,0:T(8,128)(2,1)} %collective-permute-done.5, bf16[128,1024]{1,0:T(8,128)(2,1)} %collective-permute-done.4, bf16[128,1024]{1,0:T(8,128)(2,1)} %collective-permute-done.3, f32[4,128,1024]{2,1,0:T(8,128)S(1)} %pad_maximum_fusion, s32[]{:T(128)S(6)} %select_n.64), kind=kLoop, calls=%fused_computation.49 | loop fusion | flops 786432 | bytes 1835012 | tf_op jit(solution)/shard_map/add | solution.py:197
  76.7 1.2 copy.19
  79.6 1.1 convolution_bitcast_fusion.1.state_ref
  82.1 63.3 %shard_map.112 = f32[8,128,128]{2,1,0:T(8,128)} custom-call(f32[8,128,128]{2,1,0:T(8,128)} %convolution_bitcast_fusion.1.state_ref), custom_call_target="tpu_custom_call" | custom-call | tf_op jit(solution)/shard_map/pallas_call | solution.py:112
  145.4 1.5 %convolution_bitcast_fusion = f32[128,8,128]{0,2,1:T(8,128)S(1)} fusion(f32[8,128,128]{2,1,0:T(8,128)} %shard_map.112, bf16[128,1024]{1,0:T(8,128)(2,1)S(1)} %copy-done), kind=kOutput, calls=%fused_computation.24 | convolution fusion | flops 100663296 | bytes 1310720 | tf_op jit(solution)/shard_map/she,hde->shd/dot_general | solution.py:218
  147.0 1.5 fusion.41
  (68 shorter events, 13.2 us)
Async XLA Ops:
  0.6 1.4 copy-start
  0.6 25.2 %copy-start.4 = (bf16[128,1024]{1,0:T(8,128)(2,1)S(1)}, bf16[128,1024]{1,0:T(8,128)(2,1)}, u32[]{:S(2)}) copy-start(bf16[128,1024]{1,0:T(8,128)(2,1)} %param.9) | copy-start | bytes 786436
  0.7 25.2 %copy-start.2 = (bf16[128,1024]{1,0:T(8,128)(2,1)S(1)}, bf16[128,1024]{1,0:T(8,128)(2,1)}, u32[]{:S(2)}) copy-start(bf16[128,1024]{1,0:T(8,128)(2,1)} %param.8) | copy-start | bytes 786436
  2.0 1.0 copy-start.6
  28.2 6.6 %copy-start.9 = (s32[128]{0:T(128)S(1)}, s32[128]{0:T(128)}, u32[]{:S(2)}) copy-start(s32[128]{0:T(128)} %param.14) | copy-start | bytes 1540
  28.2 6.6 %copy-start.8 = (f32[32,1024]{1,0:T(8,128)S(1)}, f32[32,1024]{1,0:T(8,128)}, u32[]{:S(2)}) copy-start(f32[32,1024]{1,0:T(8,128)} %param.12) | copy-start | bytes 393220
  28.3 9.4 %collective-permute-start.2 = (bf16[128,1024]{0,1:T(8,128)(2,1)S(1)}, bf16[128,1024]{0,1:T(8,128)(2,1)S(1)}, u32[]{:S(2)}, u32[]{:S(2)}) collective-permute-start(bf16[128,1024]{0,1:T(8,128)(2,1)S(1)} %bitcast.140), channel_id=1, source_target_pairs={{0,3},{1,0},{2,1},{3,2},{4,7},{5,4},{6,5},{7,6},{8,11},{9,8},{10,9... | collective-permute-start | bytes 786440 | tf_op jit(solution)/shard_map/ppermute | solution.py:161
  31.5 8.2 %collective-permute-start.1 = (bf16[128,1024]{0,1:T(8,128)(2,1)S(1)}, bf16[128,1024]{0,1:T(8,128)(2,1)S(1)}, u32[]{:S(2)}, u32[]{:S(2)}) collective-permute-start(bf16[128,1024]{0,1:T(8,128)(2,1)S(1)} %bitcast.141), channel_id=1, source_target_pairs={{0,2},{1,3},{2,0},{3,1},{4,6},{5,7},{6,4},{7,5},{8,10},{9,11},{10,... | collective-permute-start | bytes 786440 | tf_op jit(solution)/shard_map/ppermute | solution.py:161
  32.0 14.8 %collective-permute-start = (bf16[128,1024]{0,1:T(8,128)(2,1)S(1)}, bf16[128,1024]{0,1:T(8,128)(2,1)S(1)}, u32[]{:S(2)}, u32[]{:S(2)}) collective-permute-start(bf16[128,1024]{0,1:T(8,128)(2,1)S(1)} %bitcast.142), channel_id=1, source_target_pairs={{0,1},{1,2},{2,3},{3,0},{4,5},{5,6},{6,7},{7,4},{8,9},{9,10},{10,1... | collective-permute-start | bytes 786440 | tf_op jit(solution)/shard_map/ppermute | solution.py:161
  39.8 15.4 %slice-start = ((s8[8388608]{0:T(1024)(128)(4,1)}), s8[4194304]{0:T(1024)(128)(4,1)S(1)}, s32[]{:S(2)}) async-start(s8[8388608]{0:T(1024)(128)(4,1)} %bitcast.137), calls=%async_computation | async-start | bytes 8388608
  42.0 7.0 %copy-start.10 = (s32[128]{0:T(128)S(1)}, s32[128]{0:T(128)}, u32[]{:S(2)}) copy-start(s32[128]{0:T(128)} %param.15) | copy-start | bytes 1540
  42.0 7.0 %copy-start.11 = (s32[128]{0:T(128)S(1)}, s32[128]{0:T(128)}, u32[]{:S(2)}) copy-start(s32[128]{0:T(128)} %param.13) | copy-start | bytes 1540
  49.0 6.1 %slice-start.1 = ((s8[8388608]{0:T(1024)(128)(4,1)}), s8[4194304]{0:T(1024)(128)(4,1)S(1)}, s32[]{:S(2)}) async-start(s8[8388608]{0:T(1024)(128)(4,1)} %bitcast.137), calls=%async_computation.1 | async-start | bytes 8388608
  57.9 16.8 %collective-permute-start.3 = (bf16[128,1024]{1,0:T(8,128)(2,1)}, bf16[128,1024]{1,0:T(8,128)(2,1)}, u32[]{:S(2)}, u32[]{:S(2)}) collective-permute-start(bf16[128,1024]{1,0:T(8,128)(2,1)} %get-tuple-element.8), channel_id=1, source_target_pairs={{0,1},{1,2},{2,3},{3,0},{4,5},{5,6},{6,7},{7,4},{8,9},{9,10},{10,1... | collective-permute-start | bytes 786440 | tf_op jit(solution)/shard_map/ppermute | solution.py:161
  57.9 16.8 %collective-permute-start.5 = (bf16[128,1024]{1,0:T(8,128)(2,1)}, bf16[128,1024]{1,0:T(8,128)(2,1)}, u32[]{:S(2)}, u32[]{:S(2)}) collective-permute-start(bf16[128,1024]{1,0:T(8,128)(2,1)} %get-tuple-element.9), channel_id=1, source_target_pairs={{0,3},{1,0},{2,1},{3,2},{4,7},{5,4},{6,5},{7,6},{8,11},{9,8},{10,9... | collective-permute-start | bytes 786440 | tf_op jit(solution)/shard_map/ppermute | solution.py:161
  60.7 13.9 %collective-permute-start.4 = (bf16[128,1024]{1,0:T(8,128)(2,1)}, bf16[128,1024]{1,0:T(8,128)(2,1)}, u32[]{:S(2)}, u32[]{:S(2)}) collective-permute-start(bf16[128,1024]{1,0:T(8,128)(2,1)} %get-tuple-element.10), channel_id=1, source_target_pairs={{0,2},{1,3},{2,0},{3,1},{4,6},{5,7},{6,4},{7,5},{8,10},{9,11},{10,... | collective-permute-start | bytes 786440 | tf_op jit(solution)/shard_map/ppermute | solution.py:161
  61.9 8.2 %collective-permute-start.8 = (f32[128]{0:T(128)S(1)}, f32[128]{0:T(128)S(1)}, u32[]{:S(2)}, u32[]{:S(2)}) collective-permute-start(f32[128]{0:T(128)S(1)} %multiply_subtract_fusion), channel_id=1, source_target_pairs={{0,3},{1,0},{2,1},{3,2},{4,7},{5,4},{6,5},{7,6},{8,11},{9,8},{10,9... | collective-permute-start | bytes 1544 | tf_op jit(solution)/shard_map/ppermute | solution.py:161
  62.2 10.2 %collective-permute-start.7 = (f32[128]{0:T(128)S(1)}, f32[128]{0:T(128)S(1)}, u32[]{:S(2)}, u32[]{:S(2)}) collective-permute-start(f32[128]{0:T(128)S(1)} %multiply_subtract_fusion), channel_id=1, source_target_pairs={{0,2},{1,3},{2,0},{3,1},{4,6},{5,7},{6,4},{7,5},{8,10},{9,11},{10,... | collective-permute-start | bytes 1544 | tf_op jit(solution)/shard_map/ppermute | solution.py:161
  70.1 4.1 %collective-permute-start.6 = (f32[128]{0:T(128)S(1)}, f32[128]{0:T(128)S(1)}, u32[]{:S(2)}, u32[]{:S(2)}) collective-permute-start(f32[128]{0:T(128)S(1)} %multiply_subtract_fusion), channel_id=1, source_target_pairs={{0,1},{1,2},{2,3},{3,0},{4,5},{5,6},{6,7},{7,4},{8,9},{9,10},{10,1... | collective-permute-start | bytes 1544 | tf_op jit(solution)/shard_map/ppermute | solution.py:161
  77.9 1.0 copy-start.1
  78.1 1.5 copy-start.3
  78.2 2.6 %copy-start.7 = (bf16[128,8,128]{0,2,1:T(8,128)(2,1)S(1)}, bf16[128,8,128]{0,2,1:T(8,128)(2,1)}, u32[]{:S(2)}) copy-start(bf16[128,8,128]{0,2,1:T(8,128)(2,1)} %copy-done.6) | copy-start | bytes 786436
  80.8 66.2 %copy-start.5 = (bf16[128,1024]{1,0:T(8,128)(2,1)S(1)}, bf16[128,1024]{1,0:T(8,128)(2,1)}, u32[]{:S(2)}) copy-start(bf16[128,1024]{1,0:T(8,128)(2,1)} %param.9) | copy-start | bytes 786436

commit v10 on v5

--- a/solution.py
+++ b/solution.py
@@ -24,14 +24,11 @@
     mate = me + 1 - 2 * core
     half = exclusive.shape[0]
     wire = outgoing.dtype
-    distances = []
-    distance = 2
-    while distance < count:
-        distances.append(distance)
-        distance *= 2
+    rounds = scan_rounds(count)
     step = -1 if reverse else 1
-    targets = [me + step * d for d in distances]
-    sources = [me - step * d for d in distances]
+    flat = [(r, d) for r, group in enumerate(rounds) for d in group]
+    targets = [me + step * d for _, d in flat]
+    sources = [me - step * d for _, d in flat]
     sends = [(t >= 0) & (t < count) for t in targets]
     receives = [(s >= 0) & (s < count) for s in sources]
 
@@ -59,26 +56,29 @@
     running[...] = state_ref[mine] + other[mine]
     exclusive[...] = jnp.zeros_like(exclusive)
     copies = []
-    for r, (target, send, receive) in enumerate(zip(targets, sends, receives)):
+    for r, group in enumerate(rounds):
         outgoing[r] = running[...].astype(wire)
-        copy = pltpu.make_async_remote_copy(
-            outgoing.at[r], arrived.at[r], send_sems.at[r + 1], recv_sems.at[r + 1],
-            device_id=(target, head), device_id_type=MESH,
-        )
-        copies.append(copy)
-
-        @pl.when(send)
-        def _():
-            copy.start()
-
-        @pl.when(receive)
-        def _():
-            copy.wait_recv()
-            got = arrived[r].astype(running.dtype)
-            running[...] = running[...] + got
-            exclusive[...] = exclusive[...] + got
-
-    last = len(distances) + 1
+        members = [c for c, (owner, _) in enumerate(flat) if owner == r]
+        for c in members:
+            copy = pltpu.make_async_remote_copy(
+                outgoing.at[r], arrived.at[c], send_sems.at[c + 1], recv_sems.at[c + 1],
+                device_id=(targets[c], head), device_id_type=MESH,
+            )
+            copies.append(copy)
+
+            @pl.when(sends[c])
+            def _():
+                copy.start()
+
+        for c in members:
+            @pl.when(receives[c])
+            def _():
+                copies[c].wait_recv()
+                got = arrived[c].astype(running.dtype)
+                running[...] = running[...] + got
+                exclusive[...] = exclusive[...] + got
+
+    last = len(flat) + 1
     handed[...] = exclusive[...].astype(wire)
     back = pltpu.make_async_remote_copy(
         handed, partner, send_sems.at[last], recv_sems.at[last], device_id=(mate, head), device_id_type=MESH
@@ -103,11 +103,26 @@
         out_ref[theirs] = partner[...].astype(out_ref.dtype)
 
 
+def scan_rounds(count):
+    chips = count // 2
+    rounds = []
+    window = 1
+    while window < chips:
+        if chips == 4 * window:
+            rounds.append([2 * window, 4 * window, 6 * window])
+            window *= 4
+        else:
+            rounds.append([2 * window])
+            window *= 2
+    return rounds
+
+
 def exclusive_scan(shard, axis, reverse=False, wire=jnp.float32):
     count = lax.axis_size(axis)
     heads, rows, cols = shard.shape
     half = heads // 2
-    rounds = max(count.bit_length() - 2, 1)
+    rounds = scan_rounds(count)
+    copies = max(sum(len(group) for group in rounds), 1)
     block = (half, rows, cols)
     return pl.pallas_call(
         functools.partial(scan_kernel, reverse, count),
@@ -118,12 +133,12 @@
             pltpu.VMEM((heads, rows, cols), shard.dtype),
             pltpu.VMEM(block, shard.dtype),
             pltpu.VMEM(block, shard.dtype),
-            pltpu.VMEM((rounds,) + block, wire),
-            pltpu.VMEM((rounds,) + block, wire),
+            pltpu.VMEM((max(len(rounds), 1),) + block, wire),
+            pltpu.VMEM((copies,) + block, wire),
             pltpu.VMEM(block, wire),
             pltpu.VMEM(block, wire),
-            pltpu.SemaphoreType.DMA((rounds + 2,)),
-            pltpu.SemaphoreType.DMA((rounds + 2,)),
+            pltpu.SemaphoreType.DMA((copies + 2,)),
+            pltpu.SemaphoreType.DMA((copies + 2,)),
         ],
         compiler_params=pltpu.CompilerParams(collective_id=1 if reverse else 0, has_side_effects=True),
     )(shard)
@@ -200,7 +215,7 @@
     ) / root_mean
     grad_out = grad_raw.astype(jnp.bfloat16)
     local_adjoint = jnp.einsum("thd,the->hde", query_rows, grad_out, preferred_element_type=f32)
-    suffix = exclusive_scan(local_adjoint, "seq", reverse=True, wire=jnp.bfloat16)
+    suffix = exclusive_scan(local_adjoint, "seq", reverse=True)
     back_scores = (
         jnp.einsum("the,she->hts", grad_out, value_rows, preferred_element_type=f32) * causal
     )

time: 164 us -> 185 us (1.13)
  Pallas kernels: 101 us -> 121 us
    pallas_call x2, Pallas kernels: 101 us -> 121 us  [exclusive_scan(): pl.pallas_call(functools.partial(scan_kernel, reverse, count), out_shape=...]
  transfers between devices with their start and end apart: 9 -> 9, of which waited for: 4 -> 4; matrix products, arithmetic and copies ran while one was open for 5% -> 4% of each run, Pallas kernels for 0% -> 0%
where the time goes in v10:
time: 185 us; the launch traced here: 183 us
  Pallas kernels  121 us (65%)
  matrix products  28.5 us (15%)
  starting transfers between devices  14.2 us (8%)
  waiting for transfers between devices  12 us (6%)
  local copies, waits for them, and re-layouts  5.13 us (3%)
    pallas_call x2, Pallas kernels, exclusive_scan(): pl.pallas_call(functools.partial(scan_kernel, reverse, count), out_shape=...  121 us
    ppermute x9, starting transfers between devices, shifted(): lax.ppermute(x, 'head', [(m, (m + k) % head_count) for m in range(head_co...  14.2 us
    ppermute x9, waiting for transfers between devices, shifted(): lax.ppermute(x, 'head', [(m, (m + k) % head_count) for m in range(head_co...  12 us
    dot_general x4, matrix products, block_term(): lax.dot_general(dlogit, weight_rows(owner), (((1,), (1,)), ((), ())), pre...  7.44 us
    dot_general x3, matrix products, body(): jnp.dot(shifted(hidden, k), weight_rows((head_index - k + head_count) % h...  6.74 us
  transfers between devices with their start and end apart: 9, of which 4 were waited for; matrix products, arithmetic and copies ran while one was open for 4% of the time, Pallas kernels for 0%

profile of v10, /device:TPU:1, one launch (start us, length us, event | category | flops | bytes accessed | tf_op | source)
XLA Modules:
  0.0 183.1 jit_solution(3881620628535327065)
XLA Ops:
  0.7 1.0 copy.41
  3.0 38.6 %shard_map.111 = f32[8,128,128]{2,1,0:T(8,128)} custom-call(f32[8,128,128]{2,1,0:T(8,128)} %fusion.48.state_ref), custom_call_target="tpu_custom_call" | custom-call | tf_op jit(solution)/shard_map/pallas_call | solution.py:127
  41.6 1.6 convolution_bitcast_fusion.5
  43.2 1.3 convolution_multiply_fusion.1
  45.1 2.7 %collective-permute-start.1 = (bf16[128,1024]{0,1:T(8,128)(2,1)S(1)}, bf16[128,1024]{0,1:T(8,128)(2,1)S(1)}, u32[]{:S(2)}, u32[]{:S(2)}) collective-permute-start(bf16[128,1024]{0,1:T(8,128)(2,1)S(1)} %bitcast.120), channel_id=1, source_target_pairs={{0,2},{1,3},{2,0},{3,1},{4,6},{5,7},{6,4},{7,5},{8,10},{9,11},{10,... | collective-permute-start | bytes 786440 | tf_op jit(solution)/shard_map/ppermute | solution.py:176
  49.3 2.1 %fusion.14 = f32[128,1024]{1,0:T(8,128)S(1)} fusion(bf16[128,1024]{0,1:T(8,128)(2,1)S(1)} %bitcast.123, bf16[4096,1024]{1,0:T(8,128)(2,1)} %param.11, s32[]{:T(128)S(6)} %select_n.48), kind=kOutput, calls=%fused_computation.14 | convolution fusion | flops 268435456 | bytes 2883588 | tf_op jit(solution)/shard_map/dot_general | solution.py:181
  53.0 2.4 %fusion.6 = f32[128,1024]{1,0:T(8,128)S(1)} fusion(bf16[128,1024]{0,1:T(8,128)(2,1)S(1)} %collective-permute-done.1, bf16[4096,1024]{1,0:T(8,128)(2,1)} %param.11, s32[]{:T(128)S(6)} %select_n.52), kind=kOutput, calls=%fused_computation.6 | convolution fusion | flops 268435456 | bytes 2883588 | tf_op jit(solution)/shard_map/dot_general | solution.py:183
  55.4 4.1 %collective-permute-done.2 = bf16[128,1024]{0,1:T(8,128)(2,1)S(1)} collective-permute-done((bf16[128,1024]{0,1:T(8,128)(2,1)S(1)}, bf16[128,1024]{0,1:T(8,128)(2,1)S(1)}, u32[]{:S(2)}, u32[]{:S(2)}) %collective-permute-start.2) | collective-permute-done | bytes 262176 | tf_op jit(solution)/shard_map/ppermute | solution.py:176
  59.6 2.1 %fusion.2 = f32[128,1024]{1,0:T(8,128)S(1)} fusion(bf16[128,1024]{0,1:T(8,128)(2,1)S(1)} %collective-permute-done.2, bf16[4096,1024]{1,0:T(8,128)(2,1)} %param.11, s32[]{:T(128)S(6)} %select_n.54), kind=kOutput, calls=%fused_computation.2 | convolution fusion | flops 268435456 | bytes 2883588 | tf_op jit(solution)/shard_map/dot_general | solution.py:183
  61.6 2.2 %fusion.26 = f32[128,1024]{1,0:T(8,128)S(1)} fusion(f32[128,1024]{1,0:T(8,128)S(1)} %fusion.2, f32[128,1024]{1,0:T(8,128)S(1)} %fusion.6, f32[128,1024]{1,0:T(8,128)S(1)} %fusion.14, bf16[128,1024]{0,1:T(8,128)(2,1)S(1)} %collective-permute-done, bf16[4096,1024]{1,0:T(8,128)(2,1)} %param.11, s32[]{:T(128)S(6)} %select_n.50), kind=kOutput, calls=%fused_computation.32 | convolution fusion | flops 268828672 | bytes 4456452 | tf_op jit(solution)/shard_map/dot_general | solution.py:183
  63.9 1.4 fusion.41
  65.9 2.5 %fusion.38 = bf16[128,1024]{1,0:T(8,128)(2,1)S(1)} fusion(bf16[128,1024]{1,0:T(8,128)(2,1)S(1)} %get-tuple-element.9, bf16[4096,1024]{1,0:T(8,128)(2,1)} %param.11, s32[]{:T(128)S(6)} %select_n.54), kind=kOutput, calls=%fused_computation.39 | convolution fusion | flops 268566528 | bytes 2621444 | tf_op jit(solution)/shard_map/dot_general | solution.py:202
  68.4 2.5 %fusion.35 = bf16[128,1024]{1,0:T(8,128)(2,1)S(1)} fusion(bf16[128,1024]{1,0:T(8,128)(2,1)S(1)} %get-tuple-element.9, bf16[4096,1024]{1,0:T(8,128)(2,1)} %param.11, s32[]{:T(128)S(6)} %select_n.52), kind=kOutput, calls=%fused_computation.38 | convolution fusion | flops 268566528 | bytes 2621444 | tf_op jit(solution)/shard_map/dot_general | solution.py:202
  71.8 2.2 %collective-permute-start.3 = (bf16[128,1024]{1,0:T(8,128)(2,1)S(1)}, bf16[128,1024]{1,0:T(8,128)(2,1)S(1)}, u32[]{:S(2)}, u32[]{:S(2)}) collective-permute-start(bf16[128,1024]{1,0:T(8,128)(2,1)S(1)} %fusion.38), channel_id=1, source_target_pairs={{0,1},{1,2},{2,3},{3,0},{4,5},{5,6},{6,7},{7,4},{8,9},{9,10},{10,1... | collective-permute-start | bytes 786440 | tf_op jit(solution)/shard_map/ppermute | solution.py:176
  74.0 2.5 %collective-permute-start.4 = (bf16[128,1024]{1,0:T(8,128)(2,1)S(1)}, bf16[128,1024]{1,0:T(8,128)(2,1)S(1)}, u32[]{:S(2)}, u32[]{:S(2)}) collective-permute-start(bf16[128,1024]{1,0:T(8,128)(2,1)S(1)} %fusion.35), channel_id=1, source_target_pairs={{0,2},{1,3},{2,0},{3,1},{4,6},{5,7},{6,4},{7,5},{8,10},{9,11},{10,... | collective-permute-start | bytes 786440 | tf_op jit(solution)/shard_map/ppermute | solution.py:176
  76.5 1.5 collective-permute-start.6
  78.4 6.4 %collective-permute-done.6 = f32[128]{0:T(128)S(1)} collective-permute-done((f32[128]{0:T(128)S(1)}, f32[128]{0:T(128)S(1)}, u32[]{:S(2)}, u32[]{:S(2)}) %collective-permute-start.6) | collective-permute-done | bytes 544 | tf_op jit(solution)/shard_map/ppermute | solution.py:176
  84.8 3.4 %collective-permute-start.8 = (f32[128]{0:T(128)S(1)}, f32[128]{0:T(128)S(1)}, u32[]{:S(2)}, u32[]{:S(2)}) collective-permute-start(f32[128]{0:T(128)S(1)} %multiply_subtract_fusion), channel_id=1, source_target_pairs={{0,3},{1,0},{2,1},{3,2},{4,7},{5,4},{6,5},{7,6},{8,11},{9,8},{10,9... | collective-permute-start | bytes 1544 | tf_op jit(solution)/shard_map/ppermute | solution.py:176
  89.5 1.7 convert_add_fusion
  91.2 1.2 copy.19
  92.9 1.1 convolution_bitcast_fusion.1.state_ref
  94.7 82.0 %shard_map.112 = f32[8,128,128]{2,1,0:T(8,128)} custom-call(f32[8,128,128]{2,1,0:T(8,128)} %convolution_bitcast_fusion.1.state_ref), custom_call_target="tpu_custom_call" | custom-call | tf_op jit(solution)/shard_map/pallas_call | solution.py:127
  176.7 1.5 convolution_bitcast_fusion
  178.2 1.5 fusion.29
  (59 shorter events, 12.5 us)
Async XLA Ops:
  0.6 1.3 copy-start
  0.6 50.8 %copy-start.4 = (f32[32,1024]{1,0:T(8,128)S(1)}, f32[32,1024]{1,0:T(8,128)}, u32[]{:S(2)}) copy-start(f32[32,1024]{1,0:T(8,128)} %param.12) | copy-start | bytes 393220
  0.7 50.8 %copy-start.6 = (s32[128]{0:T(128)S(1)}, s32[128]{0:T(128)}, u32[]{:S(2)}) copy-start(s32[128]{0:T(128)} %param.14) | copy-start | bytes 1540
  44.5 19.4 %copy-start.7 = (s32[128]{0:T(128)S(1)}, s32[128]{0:T(128)}, u32[]{:S(2)}) copy-start(s32[128]{0:T(128)} %param.15) | copy-start | bytes 1540
  44.5 19.4 %copy-start.8 = (s32[128]{0:T(128)S(1)}, s32[128]{0:T(128)}, u32[]{:S(2)}) copy-start(s32[128]{0:T(128)} %param.13) | copy-start | bytes 1540
  45.1 7.8 %collective-permute-start.1 = (bf16[128,1024]{0,1:T(8,128)(2,1)S(1)}, bf16[128,1024]{0,1:T(8,128)(2,1)S(1)}, u32[]{:S(2)}, u32[]{:S(2)}) collective-permute-start(bf16[128,1024]{0,1:T(8,128)(2,1)S(1)} %bitcast.120), channel_id=1, source_target_pairs={{0,2},{1,3},{2,0},{3,1},{4,6},{5,7},{6,4},{7,5},{8,10},{9,11},{10,... | collective-permute-start | bytes 786440 | tf_op jit(solution)/shard_map/ppermute | solution.py:176
  47.8 11.7 %collective-permute-start.2 = (bf16[128,1024]{0,1:T(8,128)(2,1)S(1)}, bf16[128,1024]{0,1:T(8,128)(2,1)S(1)}, u32[]{:S(2)}, u32[]{:S(2)}) collective-permute-start(bf16[128,1024]{0,1:T(8,128)(2,1)S(1)} %bitcast.121), channel_id=1, source_target_pairs={{0,3},{1,0},{2,1},{3,2},{4,7},{5,4},{6,5},{7,6},{8,11},{9,8},{10,9... | collective-permute-start | bytes 786440 | tf_op jit(solution)/shard_map/ppermute | solution.py:176
  48.7 12.9 %collective-permute-start = (bf16[128,1024]{0,1:T(8,128)(2,1)S(1)}, bf16[128,1024]{0,1:T(8,128)(2,1)S(1)}, u32[]{:S(2)}, u32[]{:S(2)}) collective-permute-start(bf16[128,1024]{0,1:T(8,128)(2,1)S(1)} %bitcast.122), channel_id=1, source_target_pairs={{0,1},{1,2},{2,3},{3,0},{4,5},{5,6},{6,7},{7,4},{8,9},{9,10},{10,1... | collective-permute-start | bytes 786440 | tf_op jit(solution)/shard_map/ppermute | solution.py:176
  52.2 13.1 %copy-start.5 = (f32[32,1024]{1,0:T(8,128)S(1)}, f32[32,1024]{1,0:T(8,128)}, u32[]{:S(2)}) copy-start(f32[32,1024]{1,0:T(8,128)} %reduce_window_sum.11) | copy-start | bytes 393220
  52.2 18.6 %slice-start = ((s8[8388608]{0:T(1024)(128)(4,1)}), s8[4194304]{0:T(1024)(128)(4,1)S(1)}, s32[]{:S(2)}) async-start(s8[8388608]{0:T(1024)(128)(4,1)} %bitcast.117), calls=%async_computation | async-start | bytes 8388608
  61.6 9.3 %slice-start.1 = ((s8[8388608]{0:T(1024)(128)(4,1)}), s8[4194304]{0:T(1024)(128)(4,1)S(1)}, s32[]{:S(2)}) async-start(s8[8388608]{0:T(1024)(128)(4,1)} %bitcast.117), calls=%async_computation.1 | async-start | bytes 8388608
  65.9 27.0 %copy-start.2 = (bf16[128,1024]{1,0:T(8,128)(2,1)S(1)}, bf16[128,1024]{1,0:T(8,128)(2,1)}, u32[]{:S(2)}) copy-start(bf16[128,1024]{1,0:T(8,128)(2,1)} %param.8) | copy-start | bytes 786436
  68.4 26.0 %copy-start.1 = (f32[8,128,128]{2,1,0:T(8,128)S(1)}, f32[8,128,128]{2,1,0:T(8,128)}, u32[]{:S(2)}) copy-start(f32[8,128,128]{2,1,0:T(8,128)} %shard_map.111) | copy-start | bytes 1572868
  70.9 107.3 %copy-start.3 = (bf16[128,1024]{1,0:T(8,128)(2,1)S(1)}, bf16[128,1024]{1,0:T(8,128)(2,1)}, u32[]{:S(2)}) copy-start(bf16[128,1024]{1,0:T(8,128)(2,1)} %param.9) | copy-start | bytes 786436
  71.8 17.7 %collective-permute-start.3 = (bf16[128,1024]{1,0:T(8,128)(2,1)S(1)}, bf16[128,1024]{1,0:T(8,128)(2,1)S(1)}, u32[]{:S(2)}, u32[]{:S(2)}) collective-permute-start(bf16[128,1024]{1,0:T(8,128)(2,1)S(1)} %fusion.38), channel_id=1, source_target_pairs={{0,1},{1,2},{2,3},{3,0},{4,5},{5,6},{6,7},{7,4},{8,9},{9,10},{10,1... | collective-permute-start | bytes 786440 | tf_op jit(solution)/shard_map/ppermute | solution.py:176
  74.0 15.5 %collective-permute-start.4 = (bf16[128,1024]{1,0:T(8,128)(2,1)S(1)}, bf16[128,1024]{1,0:T(8,128)(2,1)S(1)}, u32[]{:S(2)}, u32[]{:S(2)}) collective-permute-start(bf16[128,1024]{1,0:T(8,128)(2,1)S(1)} %fusion.35), channel_id=1, source_target_pairs={{0,2},{1,3},{2,0},{3,1},{4,6},{5,7},{6,4},{7,5},{8,10},{9,11},{10,... | collective-permute-start | bytes 786440 | tf_op jit(solution)/shard_map/ppermute | solution.py:176
  76.5 13.1 %collective-permute-start.5 = (bf16[128,1024]{1,0:T(8,128)(2,1)S(1)}, bf16[128,1024]{1,0:T(8,128)(2,1)S(1)}, u32[]{:S(2)}, u32[]{:S(2)}) collective-permute-start(bf16[128,1024]{1,0:T(8,128)(2,1)S(1)} %fusion.32), channel_id=1, source_target_pairs={{0,3},{1,0},{2,1},{3,2},{4,7},{5,4},{6,5},{7,6},{8,11},{9,8},{10,9... | collective-permute-start | bytes 786440 | tf_op jit(solution)/shard_map/ppermute | solution.py:176
  76.5 8.4 %collective-permute-start.6 = (f32[128]{0:T(128)S(1)}, f32[128]{0:T(128)S(1)}, u32[]{:S(2)}, u32[]{:S(2)}) collective-permute-start(f32[128]{0:T(128)S(1)} %multiply_subtract_fusion), channel_id=1, source_target_pairs={{0,1},{1,2},{2,3},{3,0},{4,5},{5,6},{6,7},{7,4},{8,9},{9,10},{10,1... | collective-permute-start | bytes 1544 | tf_op jit(solution)/shard_map/ppermute | solution.py:176
  77.9 10.3 %collective-permute-start.7 = (f32[128]{0:T(128)S(1)}, f32[128]{0:T(128)S(1)}, u32[]{:S(2)}, u32[]{:S(2)}) collective-permute-start(f32[128]{0:T(128)S(1)} %multiply_subtract_fusion), channel_id=1, source_target_pairs={{0,2},{1,3},{2,0},{3,1},{4,6},{5,7},{6,4},{7,5},{8,10},{9,11},{10,... | collective-permute-start | bytes 1544 | tf_op jit(solution)/shard_map/ppermute | solution.py:176
  84.8 4.2 %collective-permute-start.8 = (f32[128]{0:T(128)S(1)}, f32[128]{0:T(128)S(1)}, u32[]{:S(2)}, u32[]{:S(2)}) collective-permute-start(f32[128]{0:T(128)S(1)} %multiply_subtract_fusion), channel_id=1, source_target_pairs={{0,3},{1,0},{2,1},{3,2},{4,7},{5,4},{6,5},{7,6},{8,11},{9,8},{10,9... | collective-permute-start | bytes 1544 | tf_op jit(solution)/shard_map/ppermute | solution.py:176

commit v11 on v10

--- a/solution.py
+++ b/solution.py
@@ -24,13 +24,26 @@
     mate = me + 1 - 2 * core
     half = exclusive.shape[0]
     wire = outgoing.dtype
-    rounds = scan_rounds(count)
+    first = scan_rounds(count)
+    second = first[-1:] + first[:-1]
+    width = max(len(group) for group in first)
+    rounds = list(range(len(first)))
     step = -1 if reverse else 1
-    flat = [(r, d) for r, group in enumerate(rounds) for d in group]
-    targets = [me + step * d for _, d in flat]
-    sources = [me - step * d for _, d in flat]
-    sends = [(t >= 0) & (t < count) for t in targets]
-    receives = [(s >= 0) & (s < count) for s in sources]
+    flat = []
+    targets, sources, sends, receives = [], [], [], []
+    for r in rounds:
+        for s in range(width):
+            flat.append((r, s))
+            d0 = first[r][s] if s < len(first[r]) else 0
+            d1 = second[r][s] if s < len(second[r]) else 0
+            distance = jnp.where(core == 0, d0, d1)
+            used = (distance > 0)
+            target = me + step * distance
+            source = me - step * distance
+            targets.append(target)
+            sources.append(source)
+            sends.append(used & (target >= 0) & (target < count))
+            receives.append(used & (source >= 0) & (source < count))
 
     barrier = pltpu.get_barrier_semaphore()
     pl.semaphore_signal(barrier, 1, device_id=(mate, head), device_id_type=MESH)
@@ -122,7 +135,7 @@
     heads, rows, cols = shard.shape
     half = heads // 2
     rounds = scan_rounds(count)
-    copies = max(sum(len(group) for group in rounds), 1)
+    copies = max(len(rounds) * max(len(group) for group in rounds), 1)
     block = (half, rows, cols)
     return pl.pallas_call(
         functools.partial(scan_kernel, reverse, count),

time: 185 us -> 191 us (1.032)
  the two profiles are of different devices: /device:TPU:1 before, /device:TPU:15 now
where the time goes in v11:
time: 191 us
  Pallas kernels  130 us (68%)
  matrix products  28.3 us (15%)
  waiting for transfers between devices  15.9 us (8%)
  starting transfers between devices  9 us (5%)
  local copies, waits for them, and re-layouts  5.13 us (3%)
    pallas_call x2, Pallas kernels, exclusive_scan(): pl.pallas_call(functools.partial(scan_kernel, reverse, count), out_shape=...  130 us
    ppermute x9, waiting for transfers between devices, shifted(): lax.ppermute(x, 'head', [(m, (m + k) % head_count) for m in range(head_co...  15.9 us
    ppermute x9, starting transfers between devices, shifted(): lax.ppermute(x, 'head', [(m, (m + k) % head_count) for m in range(head_co...  9 us
    dot_general x4, matrix products, block_term(): lax.dot_general(dlogit, weight_rows(owner), (((1,), (1,)), ((), ())), pre...  7.45 us
    dot_general x3, matrix products, body(): jnp.dot(shifted(hidden, k), weight_rows((head_index - k + head_count) % h...  6.51 us
  transfers between devices with their start and end apart: 9, of which 5 were waited for; matrix products, arithmetic and copies ran while one was open for 4% of the time, Pallas kernels for 0%

profile of v11, /device:TPU:15, one launch (start us, length us, event | category | flops | bytes accessed | tf_op | source)
XLA Modules:
  0.0 190.5 jit_solution(3038265509736533657)
XLA Ops:
  0.7 1.0 copy.41
  3.0 51.1 %shard_map.111 = f32[8,128,128]{2,1,0:T(8,128)} custom-call(f32[8,128,128]{2,1,0:T(8,128)} %fusion.48.state_ref), custom_call_target="tpu_custom_call" | custom-call | tf_op jit(solution)/shard_map/pallas_call | solution.py:140
  54.1 1.6 convolution_bitcast_fusion.5
  55.6 1.3 convolution_multiply_fusion.1
  57.6 1.2 collective-permute-start.1
  58.8 2.7 %collective-permute-start = (bf16[128,1024]{0,1:T(8,128)(2,1)S(1)}, bf16[128,1024]{0,1:T(8,128)(2,1)S(1)}, u32[]{:S(2)}, u32[]{:S(2)}) collective-permute-start(bf16[128,1024]{0,1:T(8,128)(2,1)S(1)} %bitcast.122), channel_id=1, source_target_pairs={{0,1},{1,2},{2,3},{3,0},{4,5},{5,6},{6,7},{7,4},{8,9},{9,10},{10,1... | collective-permute-start | bytes 786440 | tf_op jit(solution)/shard_map/ppermute | solution.py:189
  61.5 2.1 %fusion.14 = f32[128,1024]{1,0:T(8,128)S(1)} fusion(bf16[128,1024]{0,1:T(8,128)(2,1)S(1)} %bitcast.123, bf16[4096,1024]{1,0:T(8,128)(2,1)} %param.11, s32[]{:T(128)S(6)} %select_n.48), kind=kOutput, calls=%fused_computation.14 | convolution fusion | flops 268435456 | bytes 2883588 | tf_op jit(solution)/shard_map/dot_general | solution.py:194
  64.5 2.2 %fusion.6 = f32[128,1024]{1,0:T(8,128)S(1)} fusion(bf16[128,1024]{0,1:T(8,128)(2,1)S(1)} %collective-permute-done.1, bf16[4096,1024]{1,0:T(8,128)(2,1)} %param.11, s32[]{:T(128)S(6)} %select_n.52), kind=kOutput, calls=%fused_computation.6 | convolution fusion | flops 268435456 | bytes 2883588 | tf_op jit(solution)/shard_map/dot_general | solution.py:196
  66.7 5.3 %collective-permute-done.2 = bf16[128,1024]{0,1:T(8,128)(2,1)S(1)} collective-permute-done((bf16[128,1024]{0,1:T(8,128)(2,1)S(1)}, bf16[128,1024]{0,1:T(8,128)(2,1)S(1)}, u32[]{:S(2)}, u32[]{:S(2)}) %collective-permute-start.2) | collective-permute-done | bytes 262176 | tf_op jit(solution)/shard_map/ppermute | solution.py:189
  72.1 2.1 %fusion.2 = f32[128,1024]{1,0:T(8,128)S(1)} fusion(bf16[128,1024]{0,1:T(8,128)(2,1)S(1)} %collective-permute-done.2, bf16[4096,1024]{1,0:T(8,128)(2,1)} %param.11, s32[]{:T(128)S(6)} %select_n.54), kind=kOutput, calls=%fused_computation.2 | convolution fusion | flops 268435456 | bytes 2883588 | tf_op jit(solution)/shard_map/dot_general | solution.py:196
  74.2 2.2 %fusion.26 = f32[128,1024]{1,0:T(8,128)S(1)} fusion(f32[128,1024]{1,0:T(8,128)S(1)} %fusion.2, f32[128,1024]{1,0:T(8,128)S(1)} %fusion.6, f32[128,1024]{1,0:T(8,128)S(1)} %fusion.14, bf16[128,1024]{0,1:T(8,128)(2,1)S(1)} %collective-permute-done, bf16[4096,1024]{1,0:T(8,128)(2,1)} %param.11, s32[]{:T(128)S(6)} %select_n.50), kind=kOutput, calls=%fused_computation.32 | convolution fusion | flops 268828672 | bytes 4456452 | tf_op jit(solution)/shard_map/dot_general | solution.py:196
  76.4 1.4 fusion.41
  78.4 2.5 %fusion.38 = bf16[128,1024]{1,0:T(8,128)(2,1)S(1)} fusion(bf16[128,1024]{1,0:T(8,128)(2,1)S(1)} %get-tuple-element.9, bf16[4096,1024]{1,0:T(8,128)(2,1)} %param.11, s32[]{:T(128)S(6)} %select_n.54), kind=kOutput, calls=%fused_computation.39 | convolution fusion | flops 268566528 | bytes 2621444 | tf_op jit(solution)/shard_map/dot_general | solution.py:215
  80.9 2.5 %fusion.35 = bf16[128,1024]{1,0:T(8,128)(2,1)S(1)} fusion(bf16[128,1024]{1,0:T(8,128)(2,1)S(1)} %get-tuple-element.9, bf16[4096,1024]{1,0:T(8,128)(2,1)} %param.11, s32[]{:T(128)S(6)} %select_n.52), kind=kOutput, calls=%fused_computation.38 | convolution fusion | flops 268566528 | bytes 2621444 | tf_op jit(solution)/shard_map/dot_general | solution.py:215
  84.4 1.4 collective-permute-start.4
  86.6 1.9 %collective-permute-start.6 = (f32[128]{0:T(128)S(1)}, f32[128]{0:T(128)S(1)}, u32[]{:S(2)}, u32[]{:S(2)}) collective-permute-start(f32[128]{0:T(128)S(1)} %multiply_subtract_fusion), channel_id=1, source_target_pairs={{0,1},{1,2},{2,3},{3,0},{4,5},{5,6},{6,7},{7,4},{8,9},{9,10},{10,1... | collective-permute-start | bytes 1544 | tf_op jit(solution)/shard_map/ppermute | solution.py:189
  89.4 6.9 %collective-permute-done.6 = f32[128]{0:T(128)S(1)} collective-permute-done((f32[128]{0:T(128)S(1)}, f32[128]{0:T(128)S(1)}, u32[]{:S(2)}, u32[]{:S(2)}) %collective-permute-start.6) | collective-permute-done | bytes 544 | tf_op jit(solution)/shard_map/ppermute | solution.py:189
  97.2 2.8 %collective-permute-done.8 = f32[128]{0:T(128)S(1)} collective-permute-done((f32[128]{0:T(128)S(1)}, f32[128]{0:T(128)S(1)}, u32[]{:S(2)}, u32[]{:S(2)}) %collective-permute-start.8) | collective-permute-done | bytes 544 | tf_op jit(solution)/shard_map/ppermute | solution.py:189
  100.5 1.7 convert_add_fusion
  102.1 1.2 copy.19
  103.9 1.1 convolution_bitcast_fusion.1.state_ref
  105.6 78.5 %shard_map.112 = f32[8,128,128]{2,1,0:T(8,128)} custom-call(f32[8,128,128]{2,1,0:T(8,128)} %convolution_bitcast_fusion.1.state_ref), custom_call_target="tpu_custom_call" | custom-call | tf_op jit(solution)/shard_map/pallas_call | solution.py:140
  184.1 1.5 convolution_bitcast_fusion
  185.6 1.5 fusion.29
  (59 shorter events, 11.7 us)
Async XLA Ops:
  0.6 1.3 copy-start
  0.6 63.0 %copy-start.4 = (f32[32,1024]{1,0:T(8,128)S(1)}, f32[32,1024]{1,0:T(8,128)}, u32[]{:S(2)}) copy-start(f32[32,1024]{1,0:T(8,128)} %param.12) | copy-start | bytes 393220
  0.7 63.0 %copy-start.6 = (s32[128]{0:T(128)S(1)}, s32[128]{0:T(128)}, u32[]{:S(2)}) copy-start(s32[128]{0:T(128)} %param.14) | copy-start | bytes 1540
  57.0 19.5 %copy-start.7 = (s32[128]{0:T(128)S(1)}, s32[128]{0:T(128)}, u32[]{:S(2)}) copy-start(s32[128]{0:T(128)} %param.15) | copy-start | bytes 1540
  57.0 19.4 %copy-start.8 = (s32[128]{0:T(128)S(1)}, s32[128]{0:T(128)}, u32[]{:S(2)}) copy-start(s32[128]{0:T(128)} %param.13) | copy-start | bytes 1540
  57.6 6.9 %collective-permute-start.1 = (bf16[128,1024]{0,1:T(8,128)(2,1)S(1)}, bf16[128,1024]{0,1:T(8,128)(2,1)S(1)}, u32[]{:S(2)}, u32[]{:S(2)}) collective-permute-start(bf16[128,1024]{0,1:T(8,128)(2,1)S(1)} %bitcast.120), channel_id=1, source_target_pairs={{0,2},{1,3},{2,0},{3,1},{4,6},{5,7},{6,4},{7,5},{8,10},{9,11},{10,... | collective-permute-start | bytes 786440 | tf_op jit(solution)/shard_map/ppermute | solution.py:189
  58.8 13.3 %collective-permute-start.2 = (bf16[128,1024]{0,1:T(8,128)(2,1)S(1)}, bf16[128,1024]{0,1:T(8,128)(2,1)S(1)}, u32[]{:S(2)}, u32[]{:S(2)}) collective-permute-start(bf16[128,1024]{0,1:T(8,128)(2,1)S(1)} %bitcast.121), channel_id=1, source_target_pairs={{0,3},{1,0},{2,1},{3,2},{4,7},{5,4},{6,5},{7,6},{8,11},{9,8},{10,9... | collective-permute-start | bytes 786440 | tf_op jit(solution)/shard_map/ppermute | solution.py:189
  58.8 15.3 %collective-permute-start = (bf16[128,1024]{0,1:T(8,128)(2,1)S(1)}, bf16[128,1024]{0,1:T(8,128)(2,1)S(1)}, u32[]{:S(2)}, u32[]{:S(2)}) collective-permute-start(bf16[128,1024]{0,1:T(8,128)(2,1)S(1)} %bitcast.122), channel_id=1, source_target_pairs={{0,1},{1,2},{2,3},{3,0},{4,5},{5,6},{6,7},{7,4},{8,9},{9,10},{10,1... | collective-permute-start | bytes 786440 | tf_op jit(solution)/shard_map/ppermute | solution.py:189
  64.4 13.4 %copy-start.5 = (f32[32,1024]{1,0:T(8,128)S(1)}, f32[32,1024]{1,0:T(8,128)}, u32[]{:S(2)}) copy-start(f32[32,1024]{1,0:T(8,128)} %reduce_window_sum.11) | copy-start | bytes 393220
  64.5 19.0 %slice-start = ((s8[8388608]{0:T(1024)(128)(4,1)}), s8[4194304]{0:T(1024)(128)(4,1)S(1)}, s32[]{:S(2)}) async-start(s8[8388608]{0:T(1024)(128)(4,1)} %bitcast.117), calls=%async_computation | async-start | bytes 8388608
  74.1 9.3 %slice-start.1 = ((s8[8388608]{0:T(1024)(128)(4,1)}), s8[4194304]{0:T(1024)(128)(4,1)S(1)}, s32[]{:S(2)}) async-start(s8[8388608]{0:T(1024)(128)(4,1)} %bitcast.117), calls=%async_computation.1 | async-start | bytes 8388608
  78.4 25.4 %copy-start.2 = (bf16[128,1024]{1,0:T(8,128)(2,1)S(1)}, bf16[128,1024]{1,0:T(8,128)(2,1)}, u32[]{:S(2)}) copy-start(bf16[128,1024]{1,0:T(8,128)(2,1)} %param.8) | copy-start | bytes 786436
  80.9 24.4 %copy-start.1 = (f32[8,128,128]{2,1,0:T(8,128)S(1)}, f32[8,128,128]{2,1,0:T(8,128)}, u32[]{:S(2)}) copy-start(f32[8,128,128]{2,1,0:T(8,128)} %shard_map.111) | copy-start | bytes 1572868
  83.4 102.2 %copy-start.3 = (bf16[128,1024]{1,0:T(8,128)(2,1)S(1)}, bf16[128,1024]{1,0:T(8,128)(2,1)}, u32[]{:S(2)}) copy-start(bf16[128,1024]{1,0:T(8,128)(2,1)} %param.9) | copy-start | bytes 786436
  84.3 16.2 %collective-permute-start.3 = (bf16[128,1024]{1,0:T(8,128)(2,1)S(1)}, bf16[128,1024]{1,0:T(8,128)(2,1)S(1)}, u32[]{:S(2)}, u32[]{:S(2)}) collective-permute-start(bf16[128,1024]{1,0:T(8,128)(2,1)S(1)} %fusion.38), channel_id=1, source_target_pairs={{0,1},{1,2},{2,3},{3,0},{4,5},{5,6},{6,7},{7,4},{8,9},{9,10},{10,1... | collective-permute-start | bytes 786440 | tf_op jit(solution)/shard_map/ppermute | solution.py:189
  84.4 16.1 %collective-permute-start.4 = (bf16[128,1024]{1,0:T(8,128)(2,1)S(1)}, bf16[128,1024]{1,0:T(8,128)(2,1)S(1)}, u32[]{:S(2)}, u32[]{:S(2)}) collective-permute-start(bf16[128,1024]{1,0:T(8,128)(2,1)S(1)} %fusion.35), channel_id=1, source_target_pairs={{0,2},{1,3},{2,0},{3,1},{4,6},{5,7},{6,4},{7,5},{8,10},{9,11},{10,... | collective-permute-start | bytes 786440 | tf_op jit(solution)/shard_map/ppermute | solution.py:189
  85.8 14.6 %collective-permute-start.5 = (bf16[128,1024]{1,0:T(8,128)(2,1)S(1)}, bf16[128,1024]{1,0:T(8,128)(2,1)S(1)}, u32[]{:S(2)}, u32[]{:S(2)}) collective-permute-start(bf16[128,1024]{1,0:T(8,128)(2,1)S(1)} %fusion.32), channel_id=1, source_target_pairs={{0,3},{1,0},{2,1},{3,2},{4,7},{5,4},{6,5},{7,6},{8,11},{9,8},{10,9... | collective-permute-start | bytes 786440 | tf_op jit(solution)/shard_map/ppermute | solution.py:189
  86.6 9.7 %collective-permute-start.6 = (f32[128]{0:T(128)S(1)}, f32[128]{0:T(128)S(1)}, u32[]{:S(2)}, u32[]{:S(2)}) collective-permute-start(f32[128]{0:T(128)S(1)} %multiply_subtract_fusion), channel_id=1, source_target_pairs={{0,1},{1,2},{2,3},{3,0},{4,5},{5,6},{6,7},{7,4},{8,9},{9,10},{10,1... | collective-permute-start | bytes 1544 | tf_op jit(solution)/shard_map/ppermute | solution.py:189
  88.5 8.6 %collective-permute-start.7 = (f32[128]{0:T(128)S(1)}, f32[128]{0:T(128)S(1)}, u32[]{:S(2)}, u32[]{:S(2)}) collective-permute-start(f32[128]{0:T(128)S(1)} %multiply_subtract_fusion), channel_id=1, source_target_pairs={{0,2},{1,3},{2,0},{3,1},{4,6},{5,7},{6,4},{7,5},{8,10},{9,11},{10,... | collective-permute-start | bytes 1544 | tf_op jit(solution)/shard_map/ppermute | solution.py:189
  96.3 3.6 %collective-permute-start.8 = (f32[128]{0:T(128)S(1)}, f32[128]{0:T(128)S(1)}, u32[]{:S(2)}, u32[]{:S(2)}) collective-permute-start(f32[128]{0:T(128)S(1)} %multiply_subtract_fusion), channel_id=1, source_target_pairs={{0,3},{1,0},{2,1},{3,2},{4,7},{5,4},{6,5},{7,6},{8,11},{9,8},{10,9... | collective-permute-start | bytes 1544 | tf_op jit(solution)/shard_map/ppermute | solution.py:189

commit v12 on v10

--- a/solution.py
+++ b/solution.py
@@ -205,10 +205,17 @@
 
     grad_hidden = block_term(head_index)
     event_loss = partial_value
+    high = partial_value.astype(jnp.bfloat16)
+    low = (partial_value - high.astype(f32)).astype(jnp.bfloat16)
+    rows_extra = jnp.zeros((8, width_here), jnp.bfloat16)
+    rows_extra = rows_extra.at[0, :rows_here].set(high).at[1, :rows_here].set(low)
     for k in range(1, head_count):
         sent = block_term((head_index + k) % head_count).astype(jnp.bfloat16)
-        grad_hidden = grad_hidden + shifted(sent, k).astype(f32)
-        event_loss = event_loss + shifted(partial_value, k)
+        got = shifted(jnp.concatenate([sent, rows_extra], axis=0), k)
+        grad_hidden = grad_hidden + got[:rows_here].astype(f32)
+        event_loss = event_loss + (
+            got[rows_here, :rows_here].astype(f32) + got[rows_here + 1, :rows_here].astype(f32)
+        )
     grad_norm_in = grad_hidden.reshape(shape_three)
     grad_raw = (
         grad_norm_in - normed * jnp.mean(normed * grad_norm_in, axis=-1, keepdims=True)

time: 185 us -> 190 us (1.027)
  waiting for transfers between devices: 12 us -> 18.1 us
  starting transfers between devices: 14.2 us -> 8.82 us
  matrix products: 28.5 us -> 31 us
    ppermute x9 -> x6, waiting for transfers between devices: 12 us -> 18.1 us  [shifted(): lax.ppermute(x, 'head', [(m, (m + k) % head_count) for m in range(head_co...]
    ppermute x9 -> x6, starting transfers between devices: 14.2 us -> 8.82 us  [shifted(): lax.ppermute(x, 'head', [(m, (m + k) % head_count) for m in range(head_co...]
    dot_general x4, matrix products: 7.44 us -> 11.3 us  [block_term(): lax.dot_general(dlogit, weight_rows(owner), (((1,), (1,)), ((), ())), pre...]
    unnamed x26 -> x28, local copies, waits for them, and re-layouts: 3.65 us -> 5.06 us
  transfers between devices with their start and end apart: 9 -> 6, of which waited for: 4 -> 4; matrix products, arithmetic and copies ran while one was open for 4% -> 3% of each run, Pallas kernels for 0% -> 0%
where the time goes in v12:
time: 190 us; the launch traced here: 188 us
  Pallas kernels  120 us (63%)
  matrix products  31 us (16%)
  waiting for transfers between devices  18.1 us (10%)
  starting transfers between devices  8.82 us (5%)
  local copies, waits for them, and re-layouts  6.72 us (4%)
  other arithmetic  2.67 us (1%)
    pallas_call x2, Pallas kernels, exclusive_scan(): pl.pallas_call(functools.partial(scan_kernel, reverse, count), out_shape=...  120 us
    ppermute x6, waiting for transfers between devices, shifted(): lax.ppermute(x, 'head', [(m, (m + k) % head_count) for m in range(head_co...  18.1 us
    dot_general x4, matrix products, block_term(): lax.dot_general(dlogit, weight_rows(owner), (((1,), (1,)), ((), ())), pre...  11.3 us
    ppermute x6, starting transfers between devices, shifted(): lax.ppermute(x, 'head', [(m, (m + k) % head_count) for m in range(head_co...  8.82 us
    dot_general x3, matrix products, body(): jnp.dot(shifted(hidden, k), weight_rows((head_index - k + head_count) % h...  6.2 us
    unnamed x28, local copies, waits for them, and re-layouts  5.06 us
  transfers between devices with their start and end apart: 6, of which 4 were waited for; matrix products, arithmetic and copies ran while one was open for 3% of the time, Pallas kernels for 0%

profile of v12, /device:TPU:1, one launch (start us, length us, event | category | flops | bytes accessed | tf_op | source)
XLA Modules:
  0.0 188.1 jit_solution(8329288991749807638)
XLA Ops:
  3.0 38.6 %shard_map.111 = f32[8,128,128]{2,1,0:T(8,128)} custom-call(f32[8,128,128]{2,1,0:T(8,128)} %fusion.48.state_ref), custom_call_target="tpu_custom_call" | custom-call | tf_op jit(solution)/shard_map/pallas_call | solution.py:127
  41.6 1.6 convolution_bitcast_fusion.5
  43.2 1.3 convolution_multiply_fusion.1
  45.1 2.7 %collective-permute-start.1 = (bf16[128,1024]{0,1:T(8,128)(2,1)S(1)}, bf16[128,1024]{0,1:T(8,128)(2,1)S(1)}, u32[]{:S(2)}, u32[]{:S(2)}) collective-permute-start(bf16[128,1024]{0,1:T(8,128)(2,1)S(1)} %bitcast.138), channel_id=1, source_target_pairs={{0,2},{1,3},{2,0},{3,1},{4,6},{5,7},{6,4},{7,5},{8,10},{9,11},{10,... | collective-permute-start | bytes 786440 | tf_op jit(solution)/shard_map/ppermute | solution.py:176
  49.3 2.1 %fusion.14 = f32[128,1024]{1,0:T(8,128)S(1)} fusion(bf16[128,1024]{0,1:T(8,128)(2,1)S(1)} %bitcast.141, bf16[4096,1024]{1,0:T(8,128)(2,1)} %param.15, s32[]{:T(128)S(6)} %select_n.48), kind=kOutput, calls=%fused_computation.14 | convolution fusion | flops 268435456 | bytes 2883588 | tf_op jit(solution)/shard_map/dot_general | solution.py:181
  51.6 1.4 collective-permute-done.1
  53.0 2.1 %fusion.6 = f32[128,1024]{1,0:T(8,128)S(1)} fusion(bf16[128,1024]{0,1:T(8,128)(2,1)S(1)} %collective-permute-done.1, bf16[4096,1024]{1,0:T(8,128)(2,1)} %param.15, s32[]{:T(128)S(6)} %select_n.52), kind=kOutput, calls=%fused_computation.6 | convolution fusion | flops 268435456 | bytes 2883588 | tf_op jit(solution)/shard_map/dot_general | solution.py:183
  55.1 4.5 %collective-permute-done.2 = bf16[128,1024]{0,1:T(8,128)(2,1)S(1)} collective-permute-done((bf16[128,1024]{0,1:T(8,128)(2,1)S(1)}, bf16[128,1024]{0,1:T(8,128)(2,1)S(1)}, u32[]{:S(2)}, u32[]{:S(2)}) %collective-permute-start.2) | collective-permute-done | bytes 262176 | tf_op jit(solution)/shard_map/ppermute | solution.py:176
  59.6 2.1 %fusion.2 = f32[128,1024]{1,0:T(8,128)S(1)} fusion(bf16[128,1024]{0,1:T(8,128)(2,1)S(1)} %collective-permute-done.2, bf16[4096,1024]{1,0:T(8,128)(2,1)} %param.15, s32[]{:T(128)S(6)} %select_n.54), kind=kOutput, calls=%fused_computation.2 | convolution fusion | flops 268435456 | bytes 2883588 | tf_op jit(solution)/shard_map/dot_general | solution.py:183
  61.6 2.1 %fusion.26 = f32[128,1024]{1,0:T(8,128)S(1)} fusion(f32[128,1024]{1,0:T(8,128)S(1)} %fusion.2, f32[128,1024]{1,0:T(8,128)S(1)} %fusion.6, f32[128,1024]{1,0:T(8,128)S(1)} %fusion.14, bf16[128,1024]{0,1:T(8,128)(2,1)S(1)} %collective-permute-done, bf16[4096,1024]{1,0:T(8,128)(2,1)} %param.15, s32[]{:T(128)S(6)} %select_n.50), kind=kOutput, calls=%fused_computation.32 | convolution fusion | flops 268828672 | bytes 4456452 | tf_op jit(solution)/shard_map/dot_general | solution.py:183
  64.3 2.4 %fusion.32 = bf16[128,1024]{1,0:T(8,128)(2,1)S(1)} fusion(bf16[128,1024]{1,0:T(8,128)(2,1)S(1)} %get-tuple-element.34, bf16[4096,1024]{1,0:T(8,128)(2,1)} %param.15, s32[]{:T(128)S(6)} %select_n.50), kind=kOutput, calls=%fused_computation.37 | convolution fusion | flops 268566528 | bytes 2621444 | tf_op jit(solution)/shard_map/dot_general | solution.py:202
  66.8 2.5 %fusion.35 = bf16[128,1024]{1,0:T(8,128)(2,1)S(1)} fusion(bf16[128,1024]{1,0:T(8,128)(2,1)S(1)} %get-tuple-element.34, bf16[4096,1024]{1,0:T(8,128)(2,1)} %param.15, s32[]{:T(128)S(6)} %select_n.52), kind=kOutput, calls=%fused_computation.38 | convolution fusion | flops 268566528 | bytes 2621444 | tf_op jit(solution)/shard_map/dot_general | solution.py:202
  69.3 3.2 %fusion.38 = bf16[128,1024]{1,0:T(8,128)(2,1)} fusion(bf16[128,1024]{1,0:T(8,128)(2,1)S(1)} %get-tuple-element.34, bf16[4096,1024]{1,0:T(8,128)(2,1)} %param.15, s32[]{:T(128)S(6)} %select_n.54), kind=kOutput, calls=%fused_computation.39 | convolution fusion | flops 268566528 | bytes 2621444 | tf_op jit(solution)/shard_map/dot_general | solution.py:202
  74.2 2.2 %collective-permute-start.3 = (bf16[136,1024]{1,0:T(8,128)(2,1)S(1)}, bf16[136,1024]{1,0:T(8,128)(2,1)S(1)}, u32[]{:S(2)}, u32[]{:S(2)}) collective-permute-start(bf16[136,1024]{1,0:T(8,128)(2,1)S(1)} %get-tuple-element.36), channel_id=1, source_target_pairs={{0,1},{1,2},{2,3},{3,0},{4,5},{5,6},{6,7},{7,4},{8,9},{9,10},{10,1... | collective-permute-start | bytes 835592 | tf_op jit(solution)/shard_map/ppermute | solution.py:176
  76.4 2.5 %collective-permute-start.4 = (bf16[136,1024]{1,0:T(8,128)(2,1)S(1)}, bf16[136,1024]{1,0:T(8,128)(2,1)S(1)}, u32[]{:S(2)}, u32[]{:S(2)}) collective-permute-start(bf16[136,1024]{1,0:T(8,128)(2,1)S(1)} %get-tuple-element.37), channel_id=1, source_target_pairs={{0,2},{1,3},{2,0},{3,1},{4,6},{5,7},{6,4},{7,5},{8,10},{9,11},{10,... | collective-permute-start | bytes 835592 | tf_op jit(solution)/shard_map/ppermute | solution.py:176
  78.9 4.7 %collective-permute-done.3 = bf16[136,1024]{1,0:T(8,128)(2,1)S(1)} collective-permute-done((bf16[136,1024]{1,0:T(8,128)(2,1)S(1)}, bf16[136,1024]{1,0:T(8,128)(2,1)S(1)}, u32[]{:S(2)}, u32[]{:S(2)}) %collective-permute-start.3) | collective-permute-done | bytes 278560 | tf_op jit(solution)/shard_map/ppermute | solution.py:176
  83.6 7.5 %collective-permute-done.4 = bf16[136,1024]{1,0:T(8,128)(2,1)S(1)} collective-permute-done((bf16[136,1024]{1,0:T(8,128)(2,1)S(1)}, bf16[136,1024]{1,0:T(8,128)(2,1)S(1)}, u32[]{:S(2)}, u32[]{:S(2)}) %collective-permute-start.4) | collective-permute-done | bytes 278560 | tf_op jit(solution)/shard_map/ppermute | solution.py:176
  92.5 3.2 %convert_add_fusion = f32[128,1024]{1,0:T(8,128)} fusion(bf16[136,1024]{1,0:T(8,128)(2,1)S(1)} %collective-permute-done.5, bf16[136,1024]{1,0:T(8,128)(2,1)S(1)} %collective-permute-done.4, bf16[136,1024]{1,0:T(8,128)(2,1)S(1)} %collective-permute-done.3, bf16[128,1024]{1,0:T(8,128)(2,1)S(1)} %get-tuple-element.34, bf16[4096,1024]{1,0:T(8,128)(2,1)} %param.15, ...), kind=kOutput, calls=%fused_computation.47 | convolution fusion | flops 269221888 | bytes 3670020 | tf_op jit(solution)/shard_map/dot_general | solution.py:202
  95.8 1.2 copy.19
  97.5 1.1 convolution_bitcast_fusion.1.state_ref
  99.3 81.1 %shard_map.112 = f32[8,128,128]{2,1,0:T(8,128)} custom-call(f32[8,128,128]{2,1,0:T(8,128)} %convolution_bitcast_fusion.1.state_ref), custom_call_target="tpu_custom_call" | custom-call | tf_op jit(solution)/shard_map/pallas_call | solution.py:127
  180.4 1.5 convolution_bitcast_fusion
  182.0 1.5 fusion.29
  186.9 1.3 fusion.83
  (58 shorter events, 12.8 us)
Async XLA Ops:
  0.6 1.3 copy-start
  0.6 50.8 %copy-start.7 = (f32[32,1024]{1,0:T(8,128)S(1)}, f32[32,1024]{1,0:T(8,128)}, u32[]{:S(2)}) copy-start(f32[32,1024]{1,0:T(8,128)} %param.16) | copy-start | bytes 393220
  0.7 50.8 %copy-start.9 = (s32[128]{0:T(128)S(1)}, s32[128]{0:T(128)}, u32[]{:S(2)}) copy-start(s32[128]{0:T(128)} %param.18) | copy-start | bytes 1540
  44.5 19.2 %copy-start.10 = (s32[128]{0:T(128)S(1)}, s32[128]{0:T(128)}, u32[]{:S(2)}) copy-start(s32[128]{0:T(128)} %param.19) | copy-start | bytes 1540
  44.5 19.2 %copy-start.11 = (s32[128]{0:T(128)S(1)}, s32[128]{0:T(128)}, u32[]{:S(2)}) copy-start(s32[128]{0:T(128)} %param.17) | copy-start | bytes 1540
  45.1 7.8 %collective-permute-start.1 = (bf16[128,1024]{0,1:T(8,128)(2,1)S(1)}, bf16[128,1024]{0,1:T(8,128)(2,1)S(1)}, u32[]{:S(2)}, u32[]{:S(2)}) collective-permute-start(bf16[128,1024]{0,1:T(8,128)(2,1)S(1)} %bitcast.138), channel_id=1, source_target_pairs={{0,2},{1,3},{2,0},{3,1},{4,6},{5,7},{6,4},{7,5},{8,10},{9,11},{10,... | collective-permute-start | bytes 786440 | tf_op jit(solution)/shard_map/ppermute | solution.py:176
  47.8 11.7 %collective-permute-start.2 = (bf16[128,1024]{0,1:T(8,128)(2,1)S(1)}, bf16[128,1024]{0,1:T(8,128)(2,1)S(1)}, u32[]{:S(2)}, u32[]{:S(2)}) collective-permute-start(bf16[128,1024]{0,1:T(8,128)(2,1)S(1)} %bitcast.139), channel_id=1, source_target_pairs={{0,3},{1,0},{2,1},{3,2},{4,7},{5,4},{6,5},{7,6},{8,11},{9,8},{10,9... | collective-permute-start | bytes 786440 | tf_op jit(solution)/shard_map/ppermute | solution.py:176
  48.7 12.9 %collective-permute-start = (bf16[128,1024]{0,1:T(8,128)(2,1)S(1)}, bf16[128,1024]{0,1:T(8,128)(2,1)S(1)}, u32[]{:S(2)}, u32[]{:S(2)}) collective-permute-start(bf16[128,1024]{0,1:T(8,128)(2,1)S(1)} %bitcast.140), channel_id=1, source_target_pairs={{0,1},{1,2},{2,3},{3,0},{4,5},{5,6},{6,7},{7,4},{8,9},{9,10},{10,1... | collective-permute-start | bytes 786440 | tf_op jit(solution)/shard_map/ppermute | solution.py:176
  55.0 17.4 %copy-start.8 = (f32[32,1024]{1,0:T(8,128)S(1)}, f32[32,1024]{1,0:T(8,128)}, u32[]{:S(2)}) copy-start(f32[32,1024]{1,0:T(8,128)} %param.16) | copy-start | bytes 393220
  66.8 30.8 %copy-start.2 = (bf16[128,1024]{1,0:T(8,128)(2,1)S(1)}, bf16[128,1024]{1,0:T(8,128)(2,1)}, u32[]{:S(2)}) copy-start(bf16[128,1024]{1,0:T(8,128)(2,1)} %param.12) | copy-start | bytes 786436
  69.2 29.7 %copy-start.1 = (f32[8,128,128]{2,1,0:T(8,128)S(1)}, f32[8,128,128]{2,1,0:T(8,128)}, u32[]{:S(2)}) copy-start(f32[8,128,128]{2,1,0:T(8,128)} %shard_map.111) | copy-start | bytes 1572868
  72.4 109.5 %copy-start.3 = (bf16[128,1024]{1,0:T(8,128)(2,1)S(1)}, bf16[128,1024]{1,0:T(8,128)(2,1)}, u32[]{:S(2)}) copy-start(bf16[128,1024]{1,0:T(8,128)(2,1)} %param.13) | copy-start | bytes 786436
  74.2 9.4 %collective-permute-start.3 = (bf16[136,1024]{1,0:T(8,128)(2,1)S(1)}, bf16[136,1024]{1,0:T(8,128)(2,1)S(1)}, u32[]{:S(2)}, u32[]{:S(2)}) collective-permute-start(bf16[136,1024]{1,0:T(8,128)(2,1)S(1)} %get-tuple-element.36), channel_id=1, source_target_pairs={{0,1},{1,2},{2,3},{3,0},{4,5},{5,6},{6,7},{7,4},{8,9},{9,10},{10,1... | collective-permute-start | bytes 835592 | tf_op jit(solution)/shard_map/ppermute | solution.py:176
  76.4 14.7 %collective-permute-start.4 = (bf16[136,1024]{1,0:T(8,128)(2,1)S(1)}, bf16[136,1024]{1,0:T(8,128)(2,1)S(1)}, u32[]{:S(2)}, u32[]{:S(2)}) collective-permute-start(bf16[136,1024]{1,0:T(8,128)(2,1)S(1)} %get-tuple-element.37), channel_id=1, source_target_pairs={{0,2},{1,3},{2,0},{3,1},{4,6},{5,7},{6,4},{7,5},{8,10},{9,11},{10,... | collective-permute-start | bytes 835592 | tf_op jit(solution)/shard_map/ppermute | solution.py:176
  78.9 12.2 %collective-permute-start.5 = (bf16[136,1024]{1,0:T(8,128)(2,1)S(1)}, bf16[136,1024]{1,0:T(8,128)(2,1)S(1)}, u32[]{:S(2)}, u32[]{:S(2)}) collective-permute-start(bf16[136,1024]{1,0:T(8,128)(2,1)S(1)} %get-tuple-element.38), channel_id=1, source_target_pairs={{0,3},{1,0},{2,1},{3,2},{4,7},{5,4},{6,5},{7,6},{8,11},{9,8},{10,9... | collective-permute-start | bytes 835592 | tf_op jit(solution)/shard_map/ppermute | solution.py:176
  83.6 7.5 %copy-start.4 = (bf16[136,1024]{1,0:T(8,128)(2,1)}, bf16[136,1024]{1,0:T(8,128)(2,1)S(1)}, u32[]{:S(2)}) copy-start(bf16[136,1024]{1,0:T(8,128)(2,1)S(1)} %collective-permute-done.3) | copy-start | bytes 835588
  91.1 0.7 copy-start.5
  91.8 0.7 copy-start.6

commit v13 on v11

--- a/solution.py
+++ b/solution.py
@@ -25,7 +25,8 @@
     half = exclusive.shape[0]
     wire = outgoing.dtype
     first = scan_rounds(count)
-    second = first[-1:] + first[:-1]
+    turn = min(2, len(first) - 1)
+    second = first[len(first) - turn:] + first[:len(first) - turn]
     width = max(len(group) for group in first)
     rounds = list(range(len(first)))
     step = -1 if reverse else 1
@@ -117,16 +118,11 @@
 
 
 def scan_rounds(count):
-    chips = count // 2
     rounds = []
-    window = 1
-    while window < chips:
-        if chips == 4 * window:
-            rounds.append([2 * window, 4 * window, 6 * window])
-            window *= 4
-        else:
-            rounds.append([2 * window])
-            window *= 2
+    distance = 2
+    while distance < count:
+        rounds.append([distance])
+        distance *= 2
     return rounds
 
 
@@ -135,7 +131,7 @@
     heads, rows, cols = shard.shape
     half = heads // 2
     rounds = scan_rounds(count)
-    copies = max(len(rounds) * max(len(group) for group in rounds), 1)
+    copies = max(len(rounds), 1)
     block = (half, rows, cols)
     return pl.pallas_call(
         functools.partial(scan_kernel, reverse, count),
@@ -146,7 +142,7 @@
             pltpu.VMEM((heads, rows, cols), shard.dtype),
             pltpu.VMEM(block, shard.dtype),
             pltpu.VMEM(block, shard.dtype),
-            pltpu.VMEM((max(len(rounds), 1),) + block, wire),
+            pltpu.VMEM((copies,) + block, wire),
             pltpu.VMEM((copies,) + block, wire),
             pltpu.VMEM(block, wire),
             pltpu.VMEM(block, wire),

time: 191 us -> 191 us (level)
  no operation moved by 1% of the time
where the time goes in v13:
time: 191 us; the launch traced here: 190 us
  Pallas kernels  130 us (68%)
  matrix products  28.3 us (15%)
  waiting for transfers between devices  15.8 us (8%)
  starting transfers between devices  9 us (5%)
  local copies, waits for them, and re-layouts  5.13 us (3%)
    pallas_call x2, Pallas kernels, exclusive_scan(): pl.pallas_call(functools.partial(scan_kernel, reverse, count), out_shape=...  130 us
    ppermute x9, waiting for transfers between devices, shifted(): lax.ppermute(x, 'head', [(m, (m + k) % head_count) for m in range(head_co...  15.8 us
    ppermute x9, starting transfers between devices, shifted(): lax.ppermute(x, 'head', [(m, (m + k) % head_count) for m in range(head_co...  9 us
    dot_general x4, matrix products, block_term(): lax.dot_general(dlogit, weight_rows(owner), (((1,), (1,)), ((), ())), pre...  7.45 us
    dot_general x3, matrix products, body(): jnp.dot(shifted(hidden, k), weight_rows((head_index - k + head_count) % h...  6.5 us
  transfers between devices with their start and end apart: 9, of which 5 were waited for; matrix products, arithmetic and copies ran while one was open for 4% of the time, Pallas kernels for 0%

profile of v13, /device:TPU:15, one launch (start us, length us, event | category | flops | bytes accessed | tf_op | source)
XLA Modules:
  0.0 190.4 jit_solution(5657601412043216925)
XLA Ops:
  0.7 1.0 copy.41
  3.0 50.9 %shard_map.111 = f32[8,128,128]{2,1,0:T(8,128)} custom-call(f32[8,128,128]{2,1,0:T(8,128)} %fusion.48.state_ref), custom_call_target="tpu_custom_call" | custom-call | tf_op jit(solution)/shard_map/pallas_call | solution.py:136
  53.9 1.6 convolution_bitcast_fusion.5
  55.5 1.3 convolution_multiply_fusion.1
  57.4 1.2 collective-permute-start.1
  58.7 2.7 %collective-permute-start = (bf16[128,1024]{0,1:T(8,128)(2,1)S(1)}, bf16[128,1024]{0,1:T(8,128)(2,1)S(1)}, u32[]{:S(2)}, u32[]{:S(2)}) collective-permute-start(bf16[128,1024]{0,1:T(8,128)(2,1)S(1)} %bitcast.122), channel_id=1, source_target_pairs={{0,1},{1,2},{2,3},{3,0},{4,5},{5,6},{6,7},{7,4},{8,9},{9,10},{10,1... | collective-permute-start | bytes 786440 | tf_op jit(solution)/shard_map/ppermute | solution.py:185
  61.3 2.1 %fusion.14 = f32[128,1024]{1,0:T(8,128)S(1)} fusion(bf16[128,1024]{0,1:T(8,128)(2,1)S(1)} %bitcast.123, bf16[4096,1024]{1,0:T(8,128)(2,1)} %param.11, s32[]{:T(128)S(6)} %select_n.48), kind=kOutput, calls=%fused_computation.14 | convolution fusion | flops 268435456 | bytes 2883588 | tf_op jit(solution)/shard_map/dot_general | solution.py:190
  64.4 2.2 %fusion.6 = f32[128,1024]{1,0:T(8,128)S(1)} fusion(bf16[128,1024]{0,1:T(8,128)(2,1)S(1)} %collective-permute-done.1, bf16[4096,1024]{1,0:T(8,128)(2,1)} %param.11, s32[]{:T(128)S(6)} %select_n.52), kind=kOutput, calls=%fused_computation.6 | convolution fusion | flops 268435456 | bytes 2883588 | tf_op jit(solution)/shard_map/dot_general | solution.py:192
  66.6 5.3 %collective-permute-done.2 = bf16[128,1024]{0,1:T(8,128)(2,1)S(1)} collective-permute-done((bf16[128,1024]{0,1:T(8,128)(2,1)S(1)}, bf16[128,1024]{0,1:T(8,128)(2,1)S(1)}, u32[]{:S(2)}, u32[]{:S(2)}) %collective-permute-start.2) | collective-permute-done | bytes 262176 | tf_op jit(solution)/shard_map/ppermute | solution.py:185
  71.8 2.1 %fusion.2 = f32[128,1024]{1,0:T(8,128)S(1)} fusion(bf16[128,1024]{0,1:T(8,128)(2,1)S(1)} %collective-permute-done.2, bf16[4096,1024]{1,0:T(8,128)(2,1)} %param.11, s32[]{:T(128)S(6)} %select_n.54), kind=kOutput, calls=%fused_computation.2 | convolution fusion | flops 268435456 | bytes 2883588 | tf_op jit(solution)/shard_map/dot_general | solution.py:192
  73.9 2.2 %fusion.26 = f32[128,1024]{1,0:T(8,128)S(1)} fusion(f32[128,1024]{1,0:T(8,128)S(1)} %fusion.2, f32[128,1024]{1,0:T(8,128)S(1)} %fusion.6, f32[128,1024]{1,0:T(8,128)S(1)} %fusion.14, bf16[128,1024]{0,1:T(8,128)(2,1)S(1)} %collective-permute-done, bf16[4096,1024]{1,0:T(8,128)(2,1)} %param.11, s32[]{:T(128)S(6)} %select_n.50), kind=kOutput, calls=%fused_computation.32 | convolution fusion | flops 268828672 | bytes 4456452 | tf_op jit(solution)/shard_map/dot_general | solution.py:192
  76.2 1.4 fusion.41
  78.2 2.5 %fusion.38 = bf16[128,1024]{1,0:T(8,128)(2,1)S(1)} fusion(bf16[128,1024]{1,0:T(8,128)(2,1)S(1)} %get-tuple-element.9, bf16[4096,1024]{1,0:T(8,128)(2,1)} %param.11, s32[]{:T(128)S(6)} %select_n.54), kind=kOutput, calls=%fused_computation.39 | convolution fusion | flops 268566528 | bytes 2621444 | tf_op jit(solution)/shard_map/dot_general | solution.py:211
  80.7 2.5 %fusion.35 = bf16[128,1024]{1,0:T(8,128)(2,1)S(1)} fusion(bf16[128,1024]{1,0:T(8,128)(2,1)S(1)} %get-tuple-element.9, bf16[4096,1024]{1,0:T(8,128)(2,1)} %param.11, s32[]{:T(128)S(6)} %select_n.52), kind=kOutput, calls=%fused_computation.38 | convolution fusion | flops 268566528 | bytes 2621444 | tf_op jit(solution)/shard_map/dot_general | solution.py:211
  84.2 1.5 collective-permute-start.4
  86.4 1.9 %collective-permute-start.6 = (f32[128]{0:T(128)S(1)}, f32[128]{0:T(128)S(1)}, u32[]{:S(2)}, u32[]{:S(2)}) collective-permute-start(f32[128]{0:T(128)S(1)} %multiply_subtract_fusion), channel_id=1, source_target_pairs={{0,1},{1,2},{2,3},{3,0},{4,5},{5,6},{6,7},{7,4},{8,9},{9,10},{10,1... | collective-permute-start | bytes 1544 | tf_op jit(solution)/shard_map/ppermute | solution.py:185
  89.2 6.8 %collective-permute-done.6 = f32[128]{0:T(128)S(1)} collective-permute-done((f32[128]{0:T(128)S(1)}, f32[128]{0:T(128)S(1)}, u32[]{:S(2)}, u32[]{:S(2)}) %collective-permute-start.6) | collective-permute-done | bytes 544 | tf_op jit(solution)/shard_map/ppermute | solution.py:185
  96.9 2.8 %collective-permute-done.8 = f32[128]{0:T(128)S(1)} collective-permute-done((f32[128]{0:T(128)S(1)}, f32[128]{0:T(128)S(1)}, u32[]{:S(2)}, u32[]{:S(2)}) %collective-permute-start.8) | collective-permute-done | bytes 544 | tf_op jit(solution)/shard_map/ppermute | solution.py:185
  100.2 1.7 convert_add_fusion
  101.9 1.2 copy.19
  103.6 1.1 convolution_bitcast_fusion.1.state_ref
  105.4 78.6 %shard_map.112 = f32[8,128,128]{2,1,0:T(8,128)} custom-call(f32[8,128,128]{2,1,0:T(8,128)} %convolution_bitcast_fusion.1.state_ref), custom_call_target="tpu_custom_call" | custom-call | tf_op jit(solution)/shard_map/pallas_call | solution.py:136
  184.0 1.5 convolution_bitcast_fusion
  185.5 1.5 fusion.29
  (59 shorter events, 11.7 us)
Async XLA Ops:
  0.6 1.3 copy-start
  0.6 62.8 %copy-start.4 = (f32[32,1024]{1,0:T(8,128)S(1)}, f32[32,1024]{1,0:T(8,128)}, u32[]{:S(2)}) copy-start(f32[32,1024]{1,0:T(8,128)} %param.12) | copy-start | bytes 393220
  0.7 62.8 %copy-start.6 = (s32[128]{0:T(128)S(1)}, s32[128]{0:T(128)}, u32[]{:S(2)}) copy-start(s32[128]{0:T(128)} %param.14) | copy-start | bytes 1540
  56.8 19.4 %copy-start.7 = (s32[128]{0:T(128)S(1)}, s32[128]{0:T(128)}, u32[]{:S(2)}) copy-start(s32[128]{0:T(128)} %param.15) | copy-start | bytes 1540
  56.8 19.4 %copy-start.8 = (s32[128]{0:T(128)S(1)}, s32[128]{0:T(128)}, u32[]{:S(2)}) copy-start(s32[128]{0:T(128)} %param.13) | copy-start | bytes 1540
  57.4 6.9 %collective-permute-start.1 = (bf16[128,1024]{0,1:T(8,128)(2,1)S(1)}, bf16[128,1024]{0,1:T(8,128)(2,1)S(1)}, u32[]{:S(2)}, u32[]{:S(2)}) collective-permute-start(bf16[128,1024]{0,1:T(8,128)(2,1)S(1)} %bitcast.120), channel_id=1, source_target_pairs={{0,2},{1,3},{2,0},{3,1},{4,6},{5,7},{6,4},{7,5},{8,10},{9,11},{10,... | collective-permute-start | bytes 786440 | tf_op jit(solution)/shard_map/ppermute | solution.py:185
  58.7 13.2 %collective-permute-start.2 = (bf16[128,1024]{0,1:T(8,128)(2,1)S(1)}, bf16[128,1024]{0,1:T(8,128)(2,1)S(1)}, u32[]{:S(2)}, u32[]{:S(2)}) collective-permute-start(bf16[128,1024]{0,1:T(8,128)(2,1)S(1)} %bitcast.121), channel_id=1, source_target_pairs={{0,3},{1,0},{2,1},{3,2},{4,7},{5,4},{6,5},{7,6},{8,11},{9,8},{10,9... | collective-permute-start | bytes 786440 | tf_op jit(solution)/shard_map/ppermute | solution.py:185
  58.7 15.3 %collective-permute-start = (bf16[128,1024]{0,1:T(8,128)(2,1)S(1)}, bf16[128,1024]{0,1:T(8,128)(2,1)S(1)}, u32[]{:S(2)}, u32[]{:S(2)}) collective-permute-start(bf16[128,1024]{0,1:T(8,128)(2,1)S(1)} %bitcast.122), channel_id=1, source_target_pairs={{0,1},{1,2},{2,3},{3,0},{4,5},{5,6},{6,7},{7,4},{8,9},{9,10},{10,1... | collective-permute-start | bytes 786440 | tf_op jit(solution)/shard_map/ppermute | solution.py:185
  64.3 13.3 %copy-start.5 = (f32[32,1024]{1,0:T(8,128)S(1)}, f32[32,1024]{1,0:T(8,128)}, u32[]{:S(2)}) copy-start(f32[32,1024]{1,0:T(8,128)} %reduce_window_sum.11) | copy-start | bytes 393220
  64.3 18.9 %slice-start = ((s8[8388608]{0:T(1024)(128)(4,1)}), s8[4194304]{0:T(1024)(128)(4,1)S(1)}, s32[]{:S(2)}) async-start(s8[8388608]{0:T(1024)(128)(4,1)} %bitcast.117), calls=%async_computation | async-start | bytes 8388608
  73.9 9.3 %slice-start.1 = ((s8[8388608]{0:T(1024)(128)(4,1)}), s8[4194304]{0:T(1024)(128)(4,1)S(1)}, s32[]{:S(2)}) async-start(s8[8388608]{0:T(1024)(128)(4,1)} %bitcast.117), calls=%async_computation.1 | async-start | bytes 8388608
  78.2 25.4 %copy-start.2 = (bf16[128,1024]{1,0:T(8,128)(2,1)S(1)}, bf16[128,1024]{1,0:T(8,128)(2,1)}, u32[]{:S(2)}) copy-start(bf16[128,1024]{1,0:T(8,128)(2,1)} %param.8) | copy-start | bytes 786436
  80.7 24.4 %copy-start.1 = (f32[8,128,128]{2,1,0:T(8,128)S(1)}, f32[8,128,128]{2,1,0:T(8,128)}, u32[]{:S(2)}) copy-start(f32[8,128,128]{2,1,0:T(8,128)} %shard_map.111) | copy-start | bytes 1572868
  83.2 102.3 %copy-start.3 = (bf16[128,1024]{1,0:T(8,128)(2,1)S(1)}, bf16[128,1024]{1,0:T(8,128)(2,1)}, u32[]{:S(2)}) copy-start(bf16[128,1024]{1,0:T(8,128)(2,1)} %param.9) | copy-start | bytes 786436
  84.1 16.2 %collective-permute-start.3 = (bf16[128,1024]{1,0:T(8,128)(2,1)S(1)}, bf16[128,1024]{1,0:T(8,128)(2,1)S(1)}, u32[]{:S(2)}, u32[]{:S(2)}) collective-permute-start(bf16[128,1024]{1,0:T(8,128)(2,1)S(1)} %fusion.38), channel_id=1, source_target_pairs={{0,1},{1,2},{2,3},{3,0},{4,5},{5,6},{6,7},{7,4},{8,9},{9,10},{10,1... | collective-permute-start | bytes 786440 | tf_op jit(solution)/shard_map/ppermute | solution.py:185
  84.2 16.1 %collective-permute-start.4 = (bf16[128,1024]{1,0:T(8,128)(2,1)S(1)}, bf16[128,1024]{1,0:T(8,128)(2,1)S(1)}, u32[]{:S(2)}, u32[]{:S(2)}) collective-permute-start(bf16[128,1024]{1,0:T(8,128)(2,1)S(1)} %fusion.35), channel_id=1, source_target_pairs={{0,2},{1,3},{2,0},{3,1},{4,6},{5,7},{6,4},{7,5},{8,10},{9,11},{10,... | collective-permute-start | bytes 786440 | tf_op jit(solution)/shard_map/ppermute | solution.py:185
  85.6 14.6 %collective-permute-start.5 = (bf16[128,1024]{1,0:T(8,128)(2,1)S(1)}, bf16[128,1024]{1,0:T(8,128)(2,1)S(1)}, u32[]{:S(2)}, u32[]{:S(2)}) collective-permute-start(bf16[128,1024]{1,0:T(8,128)(2,1)S(1)} %fusion.32), channel_id=1, source_target_pairs={{0,3},{1,0},{2,1},{3,2},{4,7},{5,4},{6,5},{7,6},{8,11},{9,8},{10,9... | collective-permute-start | bytes 786440 | tf_op jit(solution)/shard_map/ppermute | solution.py:185
  86.4 9.6 %collective-permute-start.6 = (f32[128]{0:T(128)S(1)}, f32[128]{0:T(128)S(1)}, u32[]{:S(2)}, u32[]{:S(2)}) collective-permute-start(f32[128]{0:T(128)S(1)} %multiply_subtract_fusion), channel_id=1, source_target_pairs={{0,1},{1,2},{2,3},{3,0},{4,5},{5,6},{6,7},{7,4},{8,9},{9,10},{10,1... | collective-permute-start | bytes 1544 | tf_op jit(solution)/shard_map/ppermute | solution.py:185
  88.3 8.6 %collective-permute-start.7 = (f32[128]{0:T(128)S(1)}, f32[128]{0:T(128)S(1)}, u32[]{:S(2)}, u32[]{:S(2)}) collective-permute-start(f32[128]{0:T(128)S(1)} %multiply_subtract_fusion), channel_id=1, source_target_pairs={{0,2},{1,3},{2,0},{3,1},{4,6},{5,7},{6,4},{7,5},{8,10},{9,11},{10,... | collective-permute-start | bytes 1544 | tf_op jit(solution)/shard_map/ppermute | solution.py:185
  96.0 3.7 %collective-permute-start.8 = (f32[128]{0:T(128)S(1)}, f32[128]{0:T(128)S(1)}, u32[]{:S(2)}, u32[]{:S(2)}) collective-permute-start(f32[128]{0:T(128)S(1)} %multiply_subtract_fusion), channel_id=1, source_target_pairs={{0,3},{1,0},{2,1},{3,2},{4,7},{5,4},{6,5},{7,6},{8,11},{9,8},{10,9... | collective-permute-start | bytes 1544 | tf_op jit(solution)/shard_map/ppermute | solution.py:185

commit v14 on v10

--- a/solution.py
+++ b/solution.py
@@ -206,9 +206,16 @@
     grad_hidden = block_term(head_index)
     event_loss = partial_value
     for k in range(1, head_count):
-        sent = block_term((head_index + k) % head_count).astype(jnp.bfloat16)
-        grad_hidden = grad_hidden + shifted(sent, k).astype(f32)
         event_loss = event_loss + shifted(partial_value, k)
+    if head_count == 4:
+        ahead = shifted(block_term((head_index + 1) % 4).astype(jnp.bfloat16), 1)
+        relay = shifted(block_term((head_index + 2) % 4).astype(jnp.bfloat16), 3)
+        carried = (relay.astype(f32) + block_term((head_index + 3) % 4)).astype(jnp.bfloat16)
+        grad_hidden = grad_hidden + ahead.astype(f32) + shifted(carried, 3).astype(f32)
+    else:
+        for k in range(1, head_count):
+            sent = block_term((head_index + k) % head_count).astype(jnp.bfloat16)
+            grad_hidden = grad_hidden + shifted(sent, k).astype(f32)
     grad_norm_in = grad_hidden.reshape(shape_three)
     grad_raw = (
         grad_norm_in - normed * jnp.mean(normed * grad_norm_in, axis=-1, keepdims=True)

time: 185 us -> 180 us (0.973)
  waiting for transfers between devices: 12 us -> 7.75 us
    ppermute x9, waiting for transfers between devices: 12 us -> 7.75 us  [shifted(): lax.ppermute(x, 'head', [(m, (m + k) % head_count) for m in range(head_co...]
  transfers between devices with their start and end apart: 9 -> 9, of which waited for: 4 -> 4; matrix products, arithmetic and copies ran while one was open for 4% -> 7% of each run, Pallas kernels for 0% -> 0%
where the time goes in v14:
time: 180 us; the launch traced here: 179 us
  Pallas kernels  121 us (67%)
  matrix products  27.6 us (15%)
  starting transfers between devices  13.9 us (8%)
  waiting for transfers between devices  7.75 us (4%)
  local copies, waits for them, and re-layouts  5.13 us (3%)
  other arithmetic  2.42 us (1%)
    pallas_call x2, Pallas kernels, exclusive_scan(): pl.pallas_call(functools.partial(scan_kernel, reverse, count), out_shape=...  121 us
    ppermute x9, starting transfers between devices, shifted(): lax.ppermute(x, 'head', [(m, (m + k) % head_count) for m in range(head_co...  13.9 us
    ppermute x9, waiting for transfers between devices, shifted(): lax.ppermute(x, 'head', [(m, (m + k) % head_count) for m in range(head_co...  7.75 us
    dot_general x3, matrix products, body(): jnp.dot(shifted(hidden, k), weight_rows((head_index - k + head_count) % h...  6.74 us
    dot_general x4, matrix products, block_term(): lax.dot_general(dlogit, weight_rows(owner), (((1,), (1,)), ((), ())), pre...  6.54 us
    unnamed x26, local copies, waits for them, and re-layouts  3.65 us
  transfers between devices with their start and end apart: 9, of which 4 were waited for; matrix products, arithmetic and copies ran while one was open for 7% of the time, Pallas kernels for 0%

profile of v14, /device:TPU:1, one launch (start us, length us, event | category | flops | bytes accessed | tf_op | source)
XLA Modules:
  0.0 178.6 jit_solution(7447559992301445518)
XLA Ops:
  0.7 1.0 copy.41
  2.0 1.0 fusion.45.state_ref
  3.0 38.6 %shard_map.111 = f32[8,128,128]{2,1,0:T(8,128)} custom-call(f32[8,128,128]{2,1,0:T(8,128)} %fusion.45.state_ref), custom_call_target="tpu_custom_call" | custom-call | tf_op jit(solution)/shard_map/pallas_call | solution.py:127
  41.6 1.6 convolution_bitcast_fusion.5
  43.2 1.3 convolution_multiply_fusion.1
  45.1 2.7 %collective-permute-start.1 = (bf16[128,1024]{0,1:T(8,128)(2,1)S(1)}, bf16[128,1024]{0,1:T(8,128)(2,1)S(1)}, u32[]{:S(2)}, u32[]{:S(2)}) collective-permute-start(bf16[128,1024]{0,1:T(8,128)(2,1)S(1)} %bitcast.120), channel_id=1, source_target_pairs={{0,2},{1,3},{2,0},{3,1},{4,6},{5,7},{6,4},{7,5},{8,10},{9,11},{10,... | collective-permute-start | bytes 786440 | tf_op jit(solution)/shard_map/ppermute | solution.py:176
  49.3 2.1 %fusion.14 = f32[128,1024]{1,0:T(8,128)S(1)} fusion(bf16[128,1024]{0,1:T(8,128)(2,1)S(1)} %bitcast.123, bf16[4096,1024]{1,0:T(8,128)(2,1)} %param.11, s32[]{:T(128)S(6)} %select_n.48), kind=kOutput, calls=%fused_computation.14 | convolution fusion | flops 268435456 | bytes 2883588 | tf_op jit(solution)/shard_map/dot_general | solution.py:181
  53.0 2.4 %fusion.6 = f32[128,1024]{1,0:T(8,128)S(1)} fusion(bf16[128,1024]{0,1:T(8,128)(2,1)S(1)} %collective-permute-done.1, bf16[4096,1024]{1,0:T(8,128)(2,1)} %param.11, s32[]{:T(128)S(6)} %select_n.52), kind=kOutput, calls=%fused_computation.6 | convolution fusion | flops 268435456 | bytes 2883588 | tf_op jit(solution)/shard_map/dot_general | solution.py:183
  55.4 4.1 %collective-permute-done.2 = bf16[128,1024]{0,1:T(8,128)(2,1)S(1)} collective-permute-done((bf16[128,1024]{0,1:T(8,128)(2,1)S(1)}, bf16[128,1024]{0,1:T(8,128)(2,1)S(1)}, u32[]{:S(2)}, u32[]{:S(2)}) %collective-permute-start.2) | collective-permute-done | bytes 262176 | tf_op jit(solution)/shard_map/ppermute | solution.py:176
  59.6 2.1 %fusion.2 = f32[128,1024]{1,0:T(8,128)S(1)} fusion(bf16[128,1024]{0,1:T(8,128)(2,1)S(1)} %collective-permute-done.2, bf16[4096,1024]{1,0:T(8,128)(2,1)} %param.11, s32[]{:T(128)S(6)} %select_n.54), kind=kOutput, calls=%fused_computation.2 | convolution fusion | flops 268435456 | bytes 2883588 | tf_op jit(solution)/shard_map/dot_general | solution.py:183
  61.6 2.2 %fusion.26 = f32[128,1024]{1,0:T(8,128)S(1)} fusion(f32[128,1024]{1,0:T(8,128)S(1)} %fusion.2, f32[128,1024]{1,0:T(8,128)S(1)} %fusion.6, f32[128,1024]{1,0:T(8,128)S(1)} %fusion.14, bf16[128,1024]{0,1:T(8,128)(2,1)S(1)} %collective-permute-done, bf16[4096,1024]{1,0:T(8,128)(2,1)} %param.11, s32[]{:T(128)S(6)} %select_n.50), kind=kOutput, calls=%fused_computation.32 | convolution fusion | flops 268828672 | bytes 4456452 | tf_op jit(solution)/shard_map/dot_general | solution.py:183
  63.9 1.4 fusion.38
  65.9 2.5 %fusion.32 = bf16[128,1024]{1,0:T(8,128)(2,1)S(1)} fusion(bf16[128,1024]{1,0:T(8,128)(2,1)S(1)} %get-tuple-element.9, bf16[4096,1024]{1,0:T(8,128)(2,1)} %param.11, s32[]{:T(128)S(6)} %select_n.52), kind=kOutput, calls=%fused_computation.37 | convolution fusion | flops 268566528 | bytes 2621444 | tf_op jit(solution)/shard_map/dot_general | solution.py:202
  68.4 3.5 %collective-permute-start.4 = (bf16[128,1024]{1,0:T(8,128)(2,1)S(1)}, bf16[128,1024]{1,0:T(8,128)(2,1)S(1)}, u32[]{:S(2)}, u32[]{:S(2)}) collective-permute-start(bf16[128,1024]{1,0:T(8,128)(2,1)S(1)} %fusion.32), channel_id=1, source_target_pairs={{0,3},{1,0},{2,1},{3,2},{4,7},{5,4},{6,5},{7,6},{8,11},{9,8},{10,9... | collective-permute-start | bytes 786440 | tf_op jit(solution)/shard_map/ppermute | solution.py:176
  71.9 1.3 collective-permute-start.7
  73.2 1.4 collective-permute-start.8
  74.6 2.4 %fusion.35 = bf16[128,1024]{1,0:T(8,128)(2,1)S(1)} fusion(bf16[128,1024]{1,0:T(8,128)(2,1)S(1)} %get-tuple-element.9, bf16[4096,1024]{1,0:T(8,128)(2,1)} %param.11, s32[]{:T(128)S(6)} %select_n.54), kind=kOutput, calls=%fused_computation.38 | convolution fusion | flops 268566528 | bytes 2621444 | tf_op jit(solution)/shard_map/dot_general | solution.py:202
  78.7 2.7 %collective-permute-start.5 = (bf16[128,1024]{1,0:T(8,128)(2,1)S(1)}, bf16[128,1024]{1,0:T(8,128)(2,1)S(1)}, u32[]{:S(2)}, u32[]{:S(2)}) collective-permute-start(bf16[128,1024]{1,0:T(8,128)(2,1)S(1)} %add_convert_fusion), channel_id=1, source_target_pairs={{0,3},{1,0},{2,1},{3,2},{4,7},{5,4},{6,5},{7,6},{8,11},{9,8},{10,9... | collective-permute-start | bytes 786440 | tf_op jit(solution)/shard_map/ppermute | solution.py:176
  82.8 2.0 %collective-permute-done.3 = bf16[128,1024]{1,0:T(8,128)(2,1)S(1)} collective-permute-done((bf16[128,1024]{1,0:T(8,128)(2,1)S(1)}, bf16[128,1024]{1,0:T(8,128)(2,1)S(1)}, u32[]{:S(2)}, u32[]{:S(2)}) %collective-permute-start.3) | collective-permute-done | bytes 262176 | tf_op jit(solution)/shard_map/ppermute | solution.py:176
  86.6 1.2 copy.19
  88.3 1.1 convolution_bitcast_fusion.1.state_ref
  90.1 82.1 %shard_map.112 = f32[8,128,128]{2,1,0:T(8,128)} custom-call(f32[8,128,128]{2,1,0:T(8,128)} %convolution_bitcast_fusion.1.state_ref), custom_call_target="tpu_custom_call" | custom-call | tf_op jit(solution)/shard_map/pallas_call | solution.py:127
  172.2 1.5 convolution_bitcast_fusion
  173.7 1.5 fusion.29
  (60 shorter events, 13.7 us)
Async XLA Ops:
  0.6 1.3 copy-start
  0.6 50.8 %copy-start.4 = (f32[32,1024]{1,0:T(8,128)S(1)}, f32[32,1024]{1,0:T(8,128)}, u32[]{:S(2)}) copy-start(f32[32,1024]{1,0:T(8,128)} %param.12) | copy-start | bytes 393220
  0.7 50.8 %copy-start.6 = (s32[128]{0:T(128)S(1)}, s32[128]{0:T(128)}, u32[]{:S(2)}) copy-start(s32[128]{0:T(128)} %param.14) | copy-start | bytes 1540
  44.5 19.4 %copy-start.7 = (s32[128]{0:T(128)S(1)}, s32[128]{0:T(128)}, u32[]{:S(2)}) copy-start(s32[128]{0:T(128)} %param.15) | copy-start | bytes 1540
  44.5 19.4 %copy-start.8 = (s32[128]{0:T(128)S(1)}, s32[128]{0:T(128)}, u32[]{:S(2)}) copy-start(s32[128]{0:T(128)} %param.13) | copy-start | bytes 1540
  45.1 7.8 %collective-permute-start.1 = (bf16[128,1024]{0,1:T(8,128)(2,1)S(1)}, bf16[128,1024]{0,1:T(8,128)(2,1)S(1)}, u32[]{:S(2)}, u32[]{:S(2)}) collective-permute-start(bf16[128,1024]{0,1:T(8,128)(2,1)S(1)} %bitcast.120), channel_id=1, source_target_pairs={{0,2},{1,3},{2,0},{3,1},{4,6},{5,7},{6,4},{7,5},{8,10},{9,11},{10,... | collective-permute-start | bytes 786440 | tf_op jit(solution)/shard_map/ppermute | solution.py:176
  47.8 11.7 %collective-permute-start.2 = (bf16[128,1024]{0,1:T(8,128)(2,1)S(1)}, bf16[128,1024]{0,1:T(8,128)(2,1)S(1)}, u32[]{:S(2)}, u32[]{:S(2)}) collective-permute-start(bf16[128,1024]{0,1:T(8,128)(2,1)S(1)} %bitcast.121), channel_id=1, source_target_pairs={{0,3},{1,0},{2,1},{3,2},{4,7},{5,4},{6,5},{7,6},{8,11},{9,8},{10,9... | collective-permute-start | bytes 786440 | tf_op jit(solution)/shard_map/ppermute | solution.py:176
  48.7 12.9 %collective-permute-start = (bf16[128,1024]{0,1:T(8,128)(2,1)S(1)}, bf16[128,1024]{0,1:T(8,128)(2,1)S(1)}, u32[]{:S(2)}, u32[]{:S(2)}) collective-permute-start(bf16[128,1024]{0,1:T(8,128)(2,1)S(1)} %bitcast.122), channel_id=1, source_target_pairs={{0,1},{1,2},{2,3},{3,0},{4,5},{5,6},{6,7},{7,4},{8,9},{9,10},{10,1... | collective-permute-start | bytes 786440 | tf_op jit(solution)/shard_map/ppermute | solution.py:176
  52.2 13.1 %copy-start.5 = (f32[32,1024]{1,0:T(8,128)S(1)}, f32[32,1024]{1,0:T(8,128)}, u32[]{:S(2)}) copy-start(f32[32,1024]{1,0:T(8,128)} %reduce_window_sum.11) | copy-start | bytes 393220
  52.2 25.6 %slice-start = ((s8[8388608]{0:T(1024)(128)(4,1)}), s8[4194304]{0:T(1024)(128)(4,1)S(1)}, s32[]{:S(2)}) async-start(s8[8388608]{0:T(1024)(128)(4,1)} %bitcast.117), calls=%async_computation | async-start | bytes 8388608
  61.6 16.2 %slice-start.1 = ((s8[8388608]{0:T(1024)(128)(4,1)}), s8[4194304]{0:T(1024)(128)(4,1)S(1)}, s32[]{:S(2)}) async-start(s8[8388608]{0:T(1024)(128)(4,1)} %bitcast.117), calls=%async_computation.1 | async-start | bytes 8388608
  65.9 22.4 %copy-start.2 = (bf16[128,1024]{1,0:T(8,128)(2,1)S(1)}, bf16[128,1024]{1,0:T(8,128)(2,1)}, u32[]{:S(2)}) copy-start(bf16[128,1024]{1,0:T(8,128)(2,1)} %param.8) | copy-start | bytes 786436
  68.4 9.5 %collective-permute-start.4 = (bf16[128,1024]{1,0:T(8,128)(2,1)S(1)}, bf16[128,1024]{1,0:T(8,128)(2,1)S(1)}, u32[]{:S(2)}, u32[]{:S(2)}) collective-permute-start(bf16[128,1024]{1,0:T(8,128)(2,1)S(1)} %fusion.32), channel_id=1, source_target_pairs={{0,3},{1,0},{2,1},{3,2},{4,7},{5,4},{6,5},{7,6},{8,11},{9,8},{10,9... | collective-permute-start | bytes 786440 | tf_op jit(solution)/shard_map/ppermute | solution.py:176
  71.9 17.9 %copy-start.1 = (f32[8,128,128]{2,1,0:T(8,128)S(1)}, f32[8,128,128]{2,1,0:T(8,128)}, u32[]{:S(2)}) copy-start(f32[8,128,128]{2,1,0:T(8,128)} %shard_map.111) | copy-start | bytes 1572868
  71.9 10.4 %collective-permute-start.6 = (f32[128]{0:T(128)S(1)}, f32[128]{0:T(128)S(1)}, u32[]{:S(2)}, u32[]{:S(2)}) collective-permute-start(f32[128]{0:T(128)S(1)} %multiply_subtract_fusion), channel_id=1, source_target_pairs={{0,1},{1,2},{2,3},{3,0},{4,5},{5,6},{6,7},{7,4},{8,9},{9,10},{10,1... | collective-permute-start | bytes 1544 | tf_op jit(solution)/shard_map/ppermute | solution.py:176
  71.9 10.4 %collective-permute-start.7 = (f32[128]{0:T(128)S(1)}, f32[128]{0:T(128)S(1)}, u32[]{:S(2)}, u32[]{:S(2)}) collective-permute-start(f32[128]{0:T(128)S(1)} %multiply_subtract_fusion), channel_id=1, source_target_pairs={{0,2},{1,3},{2,0},{3,1},{4,6},{5,7},{6,4},{7,5},{8,10},{9,11},{10,... | collective-permute-start | bytes 1544 | tf_op jit(solution)/shard_map/ppermute | solution.py:176
  73.2 9.1 %collective-permute-start.8 = (f32[128]{0:T(128)S(1)}, f32[128]{0:T(128)S(1)}, u32[]{:S(2)}, u32[]{:S(2)}) collective-permute-start(f32[128]{0:T(128)S(1)} %multiply_subtract_fusion), channel_id=1, source_target_pairs={{0,3},{1,0},{2,1},{3,2},{4,7},{5,4},{6,5},{7,6},{8,11},{9,8},{10,9... | collective-permute-start | bytes 1544 | tf_op jit(solution)/shard_map/ppermute | solution.py:176
  77.0 96.7 %copy-start.3 = (bf16[128,1024]{1,0:T(8,128)(2,1)S(1)}, bf16[128,1024]{1,0:T(8,128)(2,1)}, u32[]{:S(2)}) copy-start(bf16[128,1024]{1,0:T(8,128)(2,1)} %param.9) | copy-start | bytes 786436
  77.0 7.8 %collective-permute-start.3 = (bf16[128,1024]{1,0:T(8,128)(2,1)S(1)}, bf16[128,1024]{1,0:T(8,128)(2,1)S(1)}, u32[]{:S(2)}, u32[]{:S(2)}) collective-permute-start(bf16[128,1024]{1,0:T(8,128)(2,1)S(1)} %fusion.35), channel_id=1, source_target_pairs={{0,1},{1,2},{2,3},{3,0},{4,5},{5,6},{6,7},{7,4},{8,9},{9,10},{10,1... | collective-permute-start | bytes 786440 | tf_op jit(solution)/shard_map/ppermute | solution.py:176
  78.7 7.0 %collective-permute-start.5 = (bf16[128,1024]{1,0:T(8,128)(2,1)S(1)}, bf16[128,1024]{1,0:T(8,128)(2,1)S(1)}, u32[]{:S(2)}, u32[]{:S(2)}) collective-permute-start(bf16[128,1024]{1,0:T(8,128)(2,1)S(1)} %add_convert_fusion), channel_id=1, source_target_pairs={{0,3},{1,0},{2,1},{3,2},{4,7},{5,4},{6,5},{7,6},{8,11},{9,8},{10,9... | collective-permute-start | bytes 786440 | tf_op jit(solution)/shard_map/ppermute | solution.py:176

commit v15 on v14

--- a/solution.py
+++ b/solution.py
@@ -179,9 +179,14 @@
         return lax.dynamic_slice_in_dim(hazard_weight, owner * width_here, width_here, 0)
 
     log_rate = jnp.dot(hidden, weight_rows(head_index), preferred_element_type=f32)
+    if head_count == 4:
+        behind = shifted(hidden, 1)
+        received = {1: behind, 2: shifted(behind, 1), 3: shifted(hidden, 3)}
+    else:
+        received = {k: shifted(hidden, k) for k in range(1, head_count)}
     for k in range(1, head_count):
         log_rate = log_rate + jnp.dot(
-            shifted(hidden, k),
+            received[k],
             weight_rows((head_index - k + head_count) % head_count),
             preferred_element_type=f32,
         )

time: 180 us -> 176 us (0.978)
  starting transfers between devices: 13.9 us -> 9.64 us
  Pallas kernels: 121 us -> 124 us
  matrix products: 27.6 us -> 24.9 us
    ppermute x9, starting transfers between devices: 13.9 us -> 9.64 us  [shifted(): lax.ppermute(x, 'head', [(m, (m + k) % head_count) for m in range(head_co...]
    pallas_call x2, Pallas kernels: 121 us -> 124 us  [exclusive_scan(): pl.pallas_call(functools.partial(scan_kernel, reverse, count), out_shape=...]
    unnamed x26 -> x24, local copies, waits for them, and re-layouts: 3.65 us -> 3.64 us
  transfers between devices with their start and end apart: 9 -> 9, of which waited for: 4 -> 5; matrix products, arithmetic and copies ran while one was open for 7% -> 6% of each run, Pallas kernels for 0% -> 0%
where the time goes in v15:
time: 176 us; the launch traced here: 175 us
  Pallas kernels  124 us (70%)
  matrix products  24.9 us (14%)
  starting transfers between devices  9.64 us (5%)
  waiting for transfers between devices  8.14 us (5%)
  local copies, waits for them, and re-layouts  5.13 us (3%)
  other arithmetic  1.8 us (1%)
    pallas_call x2, Pallas kernels, exclusive_scan(): pl.pallas_call(functools.partial(scan_kernel, reverse, count), out_shape=...  124 us
    ppermute x9, starting transfers between devices, shifted(): lax.ppermute(x, 'head', [(m, (m + k) % head_count) for m in range(head_co...  9.64 us
    ppermute x9, waiting for transfers between devices, shifted(): lax.ppermute(x, 'head', [(m, (m + k) % head_count) for m in range(head_co...  8.14 us
    dot_general x3, matrix products, body(): jnp.dot(received[k], weight_rows((head_index - k + head_count) % head_cou...  6.33 us
    dot_general x4, matrix products, block_term(): lax.dot_general(dlogit, weight_rows(owner), (((1,), (1,)), ((), ())), pre...  4.95 us
    unnamed x24, local copies, waits for them, and re-layouts  3.64 us
  transfers between devices with their start and end apart: 9, of which 5 were waited for; matrix products, arithmetic and copies ran while one was open for 6% of the time, Pallas kernels for 0%

profile of v15, /device:TPU:1, one launch (start us, length us, event | category | flops | bytes accessed | tf_op | source)
XLA Modules:
  0.0 174.8 jit_solution(8228623923855392877)
XLA Ops:
  0.7 1.0 copy.41
  2.0 1.0 fusion.45.state_ref
  3.0 38.5 %shard_map.111 = f32[8,128,128]{2,1,0:T(8,128)} custom-call(f32[8,128,128]{2,1,0:T(8,128)} %fusion.45.state_ref), custom_call_target="tpu_custom_call" | custom-call | tf_op jit(solution)/shard_map/pallas_call | solution.py:127
  41.5 1.6 convolution_bitcast_fusion.5
  43.1 1.3 convolution_multiply_fusion.1
  45.1 1.2 collective-permute-start
  46.3 1.5 collective-permute-start.2
  48.0 2.2 %fusion.14 = f32[128,1024]{1,0:T(8,128)S(1)} fusion(bf16[128,1024]{0,1:T(8,128)(2,1)S(1)} %bitcast.122, bf16[4096,1024]{1,0:T(8,128)(2,1)} %param.11, s32[]{:T(128)S(6)} %select_n.48), kind=kOutput, calls=%fused_computation.14 | convolution fusion | flops 268435456 | bytes 2883588 | tf_op jit(solution)/shard_map/dot_general | solution.py:181
  50.3 3.1 %collective-permute-done = bf16[128,1024]{0,1:T(8,128)(2,1)S(1)} collective-permute-done((bf16[128,1024]{0,1:T(8,128)(2,1)S(1)}, bf16[128,1024]{0,1:T(8,128)(2,1)S(1)}, u32[]{:S(2)}, u32[]{:S(2)}) %collective-permute-start) | collective-permute-done | bytes 262176 | tf_op jit(solution)/shard_map/ppermute | solution.py:176
  53.4 2.1 %fusion.2 = f32[128,1024]{1,0:T(8,128)S(1)} fusion(bf16[128,1024]{0,1:T(8,128)(2,1)S(1)} %collective-permute-done.2, bf16[4096,1024]{1,0:T(8,128)(2,1)} %param.11, s32[]{:T(128)S(6)} %select_n.54), kind=kOutput, calls=%fused_computation.2 | convolution fusion | flops 268435456 | bytes 2883588 | tf_op jit(solution)/shard_map/dot_general | solution.py:188
  55.4 2.2 %fusion.16 = f32[128,1024]{1,0:T(8,128)S(1)} fusion(f32[128,1024]{1,0:T(8,128)S(1)} %fusion.14, bf16[128,1024]{0,1:T(8,128)(2,1)S(1)} %collective-permute-done, bf16[4096,1024]{1,0:T(8,128)(2,1)} %param.11, s32[]{:T(128)S(6)} %select_n.50), kind=kOutput, calls=%fused_computation.16 | convolution fusion | flops 268566528 | bytes 3407876 | tf_op jit(solution)/shard_map/dot_general | solution.py:188
  57.7 3.0 %collective-permute-done.1 = bf16[128,1024]{0,1:T(8,128)(2,1)S(1)} collective-permute-done((bf16[128,1024]{0,1:T(8,128)(2,1)S(1)}, bf16[128,1024]{0,1:T(8,128)(2,1)S(1)}, u32[]{:S(2)}, u32[]{:S(2)}) %collective-permute-start.1) | collective-permute-done | bytes 262176 | tf_op jit(solution)/shard_map/ppermute | solution.py:176
  60.6 2.1 %fusion.26 = f32[128,1024]{1,0:T(8,128)S(1)} fusion(f32[128,1024]{1,0:T(8,128)S(1)} %fusion.2, f32[128,1024]{1,0:T(8,128)S(1)} %fusion.16, bf16[128,1024]{0,1:T(8,128)(2,1)S(1)} %collective-permute-done.1, bf16[4096,1024]{1,0:T(8,128)(2,1)} %param.11, s32[]{:T(128)S(6)} %select_n.52), kind=kOutput, calls=%fused_computation.32 | convolution fusion | flops 268697600 | bytes 3932164 | tf_op jit(solution)/shard_map/dot_general | solution.py:188
  63.8 2.5 %fusion.32 = bf16[128,1024]{1,0:T(8,128)(2,1)S(1)} fusion(bf16[128,1024]{1,0:T(8,128)(2,1)S(1)} %get-tuple-element.9, bf16[4096,1024]{1,0:T(8,128)(2,1)} %param.11, s32[]{:T(128)S(6)} %select_n.52), kind=kOutput, calls=%fused_computation.37 | convolution fusion | flops 268566528 | bytes 2621444 | tf_op jit(solution)/shard_map/dot_general | solution.py:207
  66.4 1.4 collective-permute-start.6
  67.9 2.5 %collective-permute-start.8 = (f32[128]{0:T(128)S(1)}, f32[128]{0:T(128)S(1)}, u32[]{:S(2)}, u32[]{:S(2)}) collective-permute-start(f32[128]{0:T(128)S(1)} %multiply_subtract_fusion), channel_id=1, source_target_pairs={{0,3},{1,0},{2,1},{3,2},{4,7},{5,4},{6,5},{7,6},{8,11},{9,8},{10,9... | collective-permute-start | bytes 1544 | tf_op jit(solution)/shard_map/ppermute | solution.py:176
  72.4 2.6 %collective-permute-start.5 = (bf16[128,1024]{1,0:T(8,128)(2,1)S(1)}, bf16[128,1024]{1,0:T(8,128)(2,1)S(1)}, u32[]{:S(2)}, u32[]{:S(2)}) collective-permute-start(bf16[128,1024]{1,0:T(8,128)(2,1)S(1)} %add_convert_fusion), channel_id=1, source_target_pairs={{0,3},{1,0},{2,1},{3,2},{4,7},{5,4},{6,5},{7,6},{8,11},{9,8},{10,9... | collective-permute-start | bytes 786440 | tf_op jit(solution)/shard_map/ppermute | solution.py:176
  76.4 1.5 collective-permute-done.3
  78.4 0.9 convert_add_fusion
  79.3 1.2 copy.19
  81.0 1.1 convolution_bitcast_fusion.1.state_ref
  82.8 85.6 %shard_map.112 = f32[8,128,128]{2,1,0:T(8,128)} custom-call(f32[8,128,128]{2,1,0:T(8,128)} %convolution_bitcast_fusion.1.state_ref), custom_call_target="tpu_custom_call" | custom-call | tf_op jit(solution)/shard_map/pallas_call | solution.py:127
  168.3 1.5 convolution_bitcast_fusion
  169.9 1.5 fusion.29
  (58 shorter events, 10.6 us)
Async XLA Ops:
  0.6 1.3 copy-start
  0.6 47.2 %copy-start.4 = (f32[32,1024]{1,0:T(8,128)S(1)}, f32[32,1024]{1,0:T(8,128)}, u32[]{:S(2)}) copy-start(f32[32,1024]{1,0:T(8,128)} %param.12) | copy-start | bytes 393220
  0.7 47.2 %copy-start.5 = (s32[128]{0:T(128)S(1)}, s32[128]{0:T(128)}, u32[]{:S(2)}) copy-start(s32[128]{0:T(128)} %param.14) | copy-start | bytes 1540
  44.4 18.3 %copy-start.6 = (s32[128]{0:T(128)S(1)}, s32[128]{0:T(128)}, u32[]{:S(2)}) copy-start(s32[128]{0:T(128)} %param.15) | copy-start | bytes 1540
  44.5 18.3 %copy-start.7 = (s32[128]{0:T(128)S(1)}, s32[128]{0:T(128)}, u32[]{:S(2)}) copy-start(s32[128]{0:T(128)} %param.13) | copy-start | bytes 1540
  45.1 8.3 %collective-permute-start = (bf16[128,1024]{0,1:T(8,128)(2,1)S(1)}, bf16[128,1024]{0,1:T(8,128)(2,1)S(1)}, u32[]{:S(2)}, u32[]{:S(2)}) collective-permute-start(bf16[128,1024]{0,1:T(8,128)(2,1)S(1)} %bitcast.120), channel_id=1, source_target_pairs={{0,1},{1,2},{2,3},{3,0},{4,5},{5,6},{6,7},{7,4},{8,9},{9,10},{10,1... | collective-permute-start | bytes 786440 | tf_op jit(solution)/shard_map/ppermute | solution.py:176
  46.3 7.0 %collective-permute-start.2 = (bf16[128,1024]{0,1:T(8,128)(2,1)S(1)}, bf16[128,1024]{0,1:T(8,128)(2,1)S(1)}, u32[]{:S(2)}, u32[]{:S(2)}) collective-permute-start(bf16[128,1024]{0,1:T(8,128)(2,1)S(1)} %bitcast.121), channel_id=1, source_target_pairs={{0,3},{1,0},{2,1},{3,2},{4,7},{5,4},{6,5},{7,6},{8,11},{9,8},{10,9... | collective-permute-start | bytes 786440 | tf_op jit(solution)/shard_map/ppermute | solution.py:176
  48.0 22.3 %slice-start = ((s8[8388608]{0:T(1024)(128)(4,1)}), s8[4194304]{0:T(1024)(128)(4,1)S(1)}, s32[]{:S(2)}) async-start(s8[8388608]{0:T(1024)(128)(4,1)} %bitcast.117), calls=%async_computation | async-start | bytes 8388608
  53.4 7.3 %collective-permute-start.1 = (bf16[128,1024]{0,1:T(8,128)(2,1)S(1)}, bf16[128,1024]{0,1:T(8,128)(2,1)S(1)}, u32[]{:S(2)}, u32[]{:S(2)}) collective-permute-start(bf16[128,1024]{0,1:T(8,128)(2,1)S(1)} %collective-permute-done), channel_id=1, source_target_pairs={{0,1},{1,2},{2,3},{3,0},{4,5},{5,6},{6,7},{7,4},{8,9},{9,10},{10,1... | collective-permute-start | bytes 786440 | tf_op jit(solution)/shard_map/ppermute | solution.py:176
  55.4 14.9 %slice-start.1 = ((s8[8388608]{0:T(1024)(128)(4,1)}), s8[4194304]{0:T(1024)(128)(4,1)S(1)}, s32[]{:S(2)}) async-start(s8[8388608]{0:T(1024)(128)(4,1)} %bitcast.117), calls=%async_computation.1 | async-start | bytes 8388608
  63.8 17.2 %copy-start.2 = (bf16[128,1024]{1,0:T(8,128)(2,1)S(1)}, bf16[128,1024]{1,0:T(8,128)(2,1)}, u32[]{:S(2)}) copy-start(bf16[128,1024]{1,0:T(8,128)(2,1)} %param.8) | copy-start | bytes 786436
  66.3 5.3 %collective-permute-start.4 = (bf16[128,1024]{1,0:T(8,128)(2,1)S(1)}, bf16[128,1024]{1,0:T(8,128)(2,1)S(1)}, u32[]{:S(2)}, u32[]{:S(2)}) collective-permute-start(bf16[128,1024]{1,0:T(8,128)(2,1)S(1)} %fusion.32), channel_id=1, source_target_pairs={{0,3},{1,0},{2,1},{3,2},{4,7},{5,4},{6,5},{7,6},{8,11},{9,8},{10,9... | collective-permute-start | bytes 786440 | tf_op jit(solution)/shard_map/ppermute | solution.py:176
  66.4 16.1 %copy-start.1 = (f32[8,128,128]{2,1,0:T(8,128)S(1)}, f32[8,128,128]{2,1,0:T(8,128)}, u32[]{:S(2)}) copy-start(f32[8,128,128]{2,1,0:T(8,128)} %shard_map.111) | copy-start | bytes 1572868
  66.4 9.5 %collective-permute-start.6 = (f32[128]{0:T(128)S(1)}, f32[128]{0:T(128)S(1)}, u32[]{:S(2)}, u32[]{:S(2)}) collective-permute-start(f32[128]{0:T(128)S(1)} %multiply_subtract_fusion), channel_id=1, source_target_pairs={{0,1},{1,2},{2,3},{3,0},{4,5},{5,6},{6,7},{7,4},{8,9},{9,10},{10,1... | collective-permute-start | bytes 1544 | tf_op jit(solution)/shard_map/ppermute | solution.py:176
  67.8 8.0 %collective-permute-start.7 = (f32[128]{0:T(128)S(1)}, f32[128]{0:T(128)S(1)}, u32[]{:S(2)}, u32[]{:S(2)}) collective-permute-start(f32[128]{0:T(128)S(1)} %multiply_subtract_fusion), channel_id=1, source_target_pairs={{0,2},{1,3},{2,0},{3,1},{4,6},{5,7},{6,4},{7,5},{8,10},{9,11},{10,... | collective-permute-start | bytes 1544 | tf_op jit(solution)/shard_map/ppermute | solution.py:176
  67.9 8.1 %collective-permute-start.8 = (f32[128]{0:T(128)S(1)}, f32[128]{0:T(128)S(1)}, u32[]{:S(2)}, u32[]{:S(2)}) collective-permute-start(f32[128]{0:T(128)S(1)} %multiply_subtract_fusion), channel_id=1, source_target_pairs={{0,3},{1,0},{2,1},{3,2},{4,7},{5,4},{6,5},{7,6},{8,11},{9,8},{10,9... | collective-permute-start | bytes 1544 | tf_op jit(solution)/shard_map/ppermute | solution.py:176
  71.2 98.7 %copy-start.3 = (bf16[128,1024]{1,0:T(8,128)(2,1)S(1)}, bf16[128,1024]{1,0:T(8,128)(2,1)}, u32[]{:S(2)}) copy-start(bf16[128,1024]{1,0:T(8,128)(2,1)} %param.9) | copy-start | bytes 786436
  71.2 6.7 %collective-permute-start.3 = (bf16[128,1024]{1,0:T(8,128)(2,1)S(1)}, bf16[128,1024]{1,0:T(8,128)(2,1)S(1)}, u32[]{:S(2)}, u32[]{:S(2)}) collective-permute-start(bf16[128,1024]{1,0:T(8,128)(2,1)S(1)} %fusion.35), channel_id=1, source_target_pairs={{0,1},{1,2},{2,3},{3,0},{4,5},{5,6},{6,7},{7,4},{8,9},{9,10},{10,1... | collective-permute-start | bytes 786440 | tf_op jit(solution)/shard_map/ppermute | solution.py:176
  72.4 5.9 %collective-permute-start.5 = (bf16[128,1024]{1,0:T(8,128)(2,1)S(1)}, bf16[128,1024]{1,0:T(8,128)(2,1)S(1)}, u32[]{:S(2)}, u32[]{:S(2)}) collective-permute-start(bf16[128,1024]{1,0:T(8,128)(2,1)S(1)} %add_convert_fusion), channel_id=1, source_target_pairs={{0,3},{1,0},{2,1},{3,2},{4,7},{5,4},{6,5},{7,6},{8,11},{9,8},{10,9... | collective-permute-start | bytes 786440 | tf_op jit(solution)/shard_map/ppermute | solution.py:176

commit v16 on v14

--- a/solution.py
+++ b/solution.py
@@ -179,12 +179,31 @@
         return lax.dynamic_slice_in_dim(hazard_weight, owner * width_here, width_here, 0)
 
     log_rate = jnp.dot(hidden, weight_rows(head_index), preferred_element_type=f32)
-    for k in range(1, head_count):
+    if head_count == 4:
+        split = width_here // 2
+        behind = shifted(hidden, 1)
+        ahead = shifted(hidden, 3)
+        far = (head_index + 2) % 4
+        near_half = shifted(behind[:, :split], 1)
+        other_half = shifted(ahead[:, split:], 3)
+        far_rows = weight_rows(far)
         log_rate = log_rate + jnp.dot(
-            shifted(hidden, k),
-            weight_rows((head_index - k + head_count) % head_count),
-            preferred_element_type=f32,
-        )
+            behind, weight_rows((head_index + 3) % 4), preferred_element_type=f32
+        )
+        log_rate = log_rate + (
+            jnp.dot(near_half, far_rows[:split], preferred_element_type=f32)
+            + jnp.dot(other_half, far_rows[split:], preferred_element_type=f32)
+        )
+        log_rate = log_rate + jnp.dot(
+            ahead, weight_rows((head_index + 1) % 4), preferred_element_type=f32
+        )
+    else:
+        for k in range(1, head_count):
+            log_rate = log_rate + jnp.dot(
+                shifted(hidden, k),
+                weight_rows((head_index - k + head_count) % head_count),
+                preferred_element_type=f32,
+            )
     offset = head_index * tasks_here
     cum_base = jnp.cumsum(jnp.exp(log_base), axis=0)
     bin_hot = (time_bin[:, None] == jnp.arange(BINS, dtype=jnp.int32)[None, :]).astype(f32)

time: 180 us -> 176 us (0.978)
  the two profiles are of different devices: /device:TPU:1 before, /device:TPU:47 now
where the time goes in v16:
time: 176 us
  Pallas kernels  122 us (69%)
  matrix products  25.8 us (15%)
  starting transfers between devices  10.1 us (6%)
  waiting for transfers between devices  8.6 us (5%)
  local copies, waits for them, and re-layouts  5.15 us (3%)
  other arithmetic  2.43 us (1%)
    pallas_call x2, Pallas kernels, exclusive_scan(): pl.pallas_call(functools.partial(scan_kernel, reverse, count), out_shape=...  122 us
    ppermute x10, starting transfers between devices, shifted(): lax.ppermute(x, 'head', [(m, (m + k) % head_count) for m in range(head_co...  10.1 us
    ppermute x10, waiting for transfers between devices, shifted(): lax.ppermute(x, 'head', [(m, (m + k) % head_count) for m in range(head_co...  8.6 us
    dot_general x4, matrix products, block_term(): lax.dot_general(dlogit, weight_rows(owner), (((1,), (1,)), ((), ())), pre...  4.92 us
    unnamed x24, local copies, waits for them, and re-layouts  3.65 us
  transfers between devices with their start and end apart: 10, of which 4 were waited for; matrix products, arithmetic and copies ran while one was open for 7% of the time, Pallas kernels for 0%

profile of v16, /device:TPU:47, one launch (start us, length us, event | category | flops | bytes accessed | tf_op | source)
XLA Modules:
  0.0 175.7 jit_solution(13917849902141940216)
XLA Ops:
  0.7 1.0 copy.41
  2.0 1.0 fusion.42.state_ref
  3.0 52.5 %shard_map.111 = f32[8,128,128]{2,1,0:T(8,128)} custom-call(f32[8,128,128]{2,1,0:T(8,128)} %fusion.42.state_ref), custom_call_target="tpu_custom_call" | custom-call | tf_op jit(solution)/shard_map/pallas_call | solution.py:127
  55.5 1.6 convolution_bitcast_fusion.5
  57.1 1.3 convolution_multiply_fusion.1
  59.2 2.7 %collective-permute-start = (bf16[128,1024]{0,1:T(8,128)(2,1)S(1)}, bf16[128,1024]{0,1:T(8,128)(2,1)S(1)}, u32[]{:S(2)}, u32[]{:S(2)}) collective-permute-start(bf16[128,1024]{0,1:T(8,128)(2,1)S(1)} %bitcast.122), channel_id=1, source_target_pairs={{0,1},{1,2},{2,3},{3,0},{4,5},{5,6},{6,7},{7,4},{8,9},{9,10},{10,1... | collective-permute-start | bytes 786440 | tf_op jit(solution)/shard_map/ppermute | solution.py:176
  62.7 2.1 %fusion.12 = f32[128,1024]{1,0:T(8,128)S(1)} fusion(bf16[128,1024]{0,1:T(8,128)(2,1)S(1)} %bitcast.123, bf16[4096,1024]{1,0:T(8,128)(2,1)} %param.11, s32[]{:T(128)S(6)} %select_n.48), kind=kOutput, calls=%fused_computation.12 | convolution fusion | flops 268435456 | bytes 2883588 | tf_op jit(solution)/shard_map/dot_general | solution.py:181
  64.7 2.4 %collective-permute-done.2 = bf16[128,1024]{0,1:T(8,128)(2,1)S(1)} collective-permute-done((bf16[128,1024]{0,1:T(8,128)(2,1)S(1)}, bf16[128,1024]{0,1:T(8,128)(2,1)S(1)}, u32[]{:S(2)}, u32[]{:S(2)}) %collective-permute-start.2) | collective-permute-done | bytes 262176 | tf_op jit(solution)/shard_map/ppermute | solution.py:176
  67.3 2.7 %collective-permute-start.1 = (bf16[128,512]{0,1:T(8,128)(2,1)S(1)}, bf16[128,512]{0,1:T(8,128)(2,1)S(1)}, u32[]{:S(2)}, u32[]{:S(2)}) collective-permute-start(bf16[128,512]{0,1:T(8,128)(2,1)S(1)} %slice.16), channel_id=1, source_target_pairs={{0,1},{1,2},{2,3},{3,0},{4,5},{5,6},{6,7},{7,4},{8,9},{9,10},{10,1... | collective-permute-start | bytes 393224 | tf_op jit(solution)/shard_map/ppermute | solution.py:176
  70.0 2.1 %fusion.16 = f32[128,1024]{1,0:T(8,128)S(1)} fusion(f32[128,1024]{1,0:T(8,128)S(1)} %fusion.12, bf16[128,1024]{0,1:T(8,128)(2,1)S(1)} %collective-permute-done, bf16[4096,1024]{1,0:T(8,128)(2,1)} %param.11, s32[]{:T(128)S(6)} %select_n.50), kind=kOutput, calls=%fused_computation.17 | convolution fusion | flops 268566528 | bytes 3407876 | tf_op jit(solution)/shard_map/dot_general | solution.py:190
  72.1 2.1 %fusion.4 = f32[128,1024]{1,0:T(8,128)S(1)} fusion(bf16[128,1024]{0,1:T(8,128)(2,1)S(1)} %collective-permute-done.2, bf16[4096,1024]{1,0:T(8,128)(2,1)} %param.11, s32[]{:T(128)S(6)} %select_n.54), kind=kOutput, calls=%fused_computation.4 | convolution fusion | flops 268435456 | bytes 2883588 | tf_op jit(solution)/shard_map/dot_general | solution.py:197
  74.2 1.7 fusion.33
  75.9 1.6 fusion.15
  78.6 2.4 %fusion.29 = bf16[128,1024]{1,0:T(8,128)(2,1)S(1)} fusion(bf16[128,1024]{1,0:T(8,128)(2,1)S(1)} %get-tuple-element.9, bf16[4096,1024]{1,0:T(8,128)(2,1)} %param.11, s32[]{:T(128)S(6)} %select_n.52), kind=kOutput, calls=%fused_computation.37 | convolution fusion | flops 268566528 | bytes 2621444 | tf_op jit(solution)/shard_map/dot_general | solution.py:221
  81.2 3.7 %collective-permute-start.8 = (f32[128]{0:T(128)S(1)}, f32[128]{0:T(128)S(1)}, u32[]{:S(2)}, u32[]{:S(2)}) collective-permute-start(f32[128]{0:T(128)S(1)} %multiply_subtract_fusion), channel_id=1, source_target_pairs={{0,2},{1,3},{2,0},{3,1},{4,6},{5,7},{6,4},{7,5},{8,10},{9,11},{10,... | collective-permute-start | bytes 1544 | tf_op jit(solution)/shard_map/ppermute | solution.py:176
  86.3 1.2 collective-permute-done.5
  89.9 1.7 collective-permute-done.4
  91.5 3.4 %collective-permute-done.6 = bf16[128,1024]{1,0:T(8,128)(2,1)S(1)} collective-permute-done((bf16[128,1024]{1,0:T(8,128)(2,1)S(1)}, bf16[128,1024]{1,0:T(8,128)(2,1)S(1)}, u32[]{:S(2)}, u32[]{:S(2)}) %collective-permute-start.6) | collective-permute-done | bytes 262176 | tf_op jit(solution)/shard_map/ppermute | solution.py:176
  94.9 0.9 convert_add_fusion
  95.8 1.2 copy.19
  97.8 1.1 convolution_bitcast_fusion.1.state_ref
  100.6 69.9 %shard_map.112 = f32[8,128,128]{2,1,0:T(8,128)} custom-call(f32[8,128,128]{2,1,0:T(8,128)} %convolution_bitcast_fusion.1.state_ref), custom_call_target="tpu_custom_call" | custom-call | tf_op jit(solution)/shard_map/pallas_call | solution.py:127
  170.6 1.5 convolution_bitcast_fusion
  173.3 1.5 fusion.23
  (63 shorter events, 11.3 us)
Async XLA Ops:
  0.6 1.3 copy-start
  0.6 61.8 %copy-start.4 = (f32[32,1024]{1,0:T(8,128)S(1)}, f32[32,1024]{1,0:T(8,128)}, u32[]{:S(2)}) copy-start(f32[32,1024]{1,0:T(8,128)} %param.12) | copy-start | bytes 393220
  59.0 18.5 %copy-start.6 = (s32[128]{0:T(128)S(1)}, s32[128]{0:T(128)}, u32[]{:S(2)}) copy-start(s32[128]{0:T(128)} %param.15) | copy-start | bytes 1540
  59.0 18.5 %copy-start.7 = (s32[128]{0:T(128)S(1)}, s32[128]{0:T(128)}, u32[]{:S(2)}) copy-start(s32[128]{0:T(128)} %param.13) | copy-start | bytes 1540
  59.1 8.1 %collective-permute-start.2 = (bf16[128,1024]{0,1:T(8,128)(2,1)S(1)}, bf16[128,1024]{0,1:T(8,128)(2,1)S(1)}, u32[]{:S(2)}, u32[]{:S(2)}) collective-permute-start(bf16[128,1024]{0,1:T(8,128)(2,1)S(1)} %bitcast.121), channel_id=1, source_target_pairs={{0,3},{1,0},{2,1},{3,2},{4,7},{5,4},{6,5},{7,6},{8,11},{9,8},{10,9... | collective-permute-start | bytes 786440 | tf_op jit(solution)/shard_map/ppermute | solution.py:176
  59.2 8.1 %collective-permute-start = (bf16[128,1024]{0,1:T(8,128)(2,1)S(1)}, bf16[128,1024]{0,1:T(8,128)(2,1)S(1)}, u32[]{:S(2)}, u32[]{:S(2)}) collective-permute-start(bf16[128,1024]{0,1:T(8,128)(2,1)S(1)} %bitcast.122), channel_id=1, source_target_pairs={{0,1},{1,2},{2,3},{3,0},{4,5},{5,6},{6,7},{7,4},{8,9},{9,10},{10,1... | collective-permute-start | bytes 786440 | tf_op jit(solution)/shard_map/ppermute | solution.py:176
  64.7 16.4 %copy-start.5 = (s32[128]{0:T(128)S(1)}, s32[128]{0:T(128)}, u32[]{:S(2)}) copy-start(s32[128]{0:T(128)} %param.14) | copy-start | bytes 1540
  64.7 20.2 %slice-start = ((s8[8388608]{0:T(1024)(128)(4,1)}), s8[4194304]{0:T(1024)(128)(4,1)S(1)}, s32[]{:S(2)}) async-start(s8[8388608]{0:T(1024)(128)(4,1)} %bitcast.118), calls=%async_computation | async-start | bytes 8388608
  67.1 7.0 %collective-permute-start.3 = (bf16[128,512]{0,1:T(8,128)(2,1)S(1)}, bf16[128,512]{0,1:T(8,128)(2,1)S(1)}, u32[]{:S(2)}, u32[]{:S(2)}) collective-permute-start(bf16[128,512]{0,1:T(8,128)(2,1)S(1)} %slice.17), channel_id=1, source_target_pairs={{0,3},{1,0},{2,1},{3,2},{4,7},{5,4},{6,5},{7,6},{8,11},{9,8},{10,9... | collective-permute-start | bytes 393224 | tf_op jit(solution)/shard_map/ppermute | solution.py:176
  67.3 8.6 %collective-permute-start.1 = (bf16[128,512]{0,1:T(8,128)(2,1)S(1)}, bf16[128,512]{0,1:T(8,128)(2,1)S(1)}, u32[]{:S(2)}, u32[]{:S(2)}) collective-permute-start(bf16[128,512]{0,1:T(8,128)(2,1)S(1)} %slice.16), channel_id=1, source_target_pairs={{0,1},{1,2},{2,3},{3,0},{4,5},{5,6},{6,7},{7,4},{8,9},{9,10},{10,1... | collective-permute-start | bytes 393224 | tf_op jit(solution)/shard_map/ppermute | solution.py:176
  74.1 10.8 %slice-start.1 = ((s8[8388608]{0:T(1024)(128)(4,1)}), s8[4194304]{0:T(1024)(128)(4,1)S(1)}, s32[]{:S(2)}) async-start(s8[8388608]{0:T(1024)(128)(4,1)} %bitcast.118), calls=%async_computation.1 | async-start | bytes 8388608
  78.0 19.2 %copy-start.1 = (f32[8,128,128]{2,1,0:T(8,128)S(1)}, f32[8,128,128]{2,1,0:T(8,128)}, u32[]{:S(2)}) copy-start(f32[8,128,128]{2,1,0:T(8,128)} %shard_map.111) | copy-start | bytes 1572868
  81.0 16.8 %copy-start.2 = (bf16[128,1024]{1,0:T(8,128)(2,1)S(1)}, bf16[128,1024]{1,0:T(8,128)(2,1)}, u32[]{:S(2)}) copy-start(bf16[128,1024]{1,0:T(8,128)(2,1)} %param.8) | copy-start | bytes 786436
  81.0 6.5 %collective-permute-start.5 = (bf16[128,1024]{1,0:T(8,128)(2,1)S(1)}, bf16[128,1024]{1,0:T(8,128)(2,1)S(1)}, u32[]{:S(2)}, u32[]{:S(2)}) collective-permute-start(bf16[128,1024]{1,0:T(8,128)(2,1)S(1)} %fusion.29), channel_id=1, source_target_pairs={{0,3},{1,0},{2,1},{3,2},{4,7},{5,4},{6,5},{7,6},{8,11},{9,8},{10,9... | collective-permute-start | bytes 786440 | tf_op jit(solution)/shard_map/ppermute | solution.py:176
  81.1 8.2 %collective-permute-start.9 = (f32[128]{0:T(128)S(1)}, f32[128]{0:T(128)S(1)}, u32[]{:S(2)}, u32[]{:S(2)}) collective-permute-start(f32[128]{0:T(128)S(1)} %multiply_subtract_fusion), channel_id=1, source_target_pairs={{0,3},{1,0},{2,1},{3,2},{4,7},{5,4},{6,5},{7,6},{8,11},{9,8},{10,9... | collective-permute-start | bytes 1544 | tf_op jit(solution)/shard_map/ppermute | solution.py:176
  81.2 8.1 %collective-permute-start.8 = (f32[128]{0:T(128)S(1)}, f32[128]{0:T(128)S(1)}, u32[]{:S(2)}, u32[]{:S(2)}) collective-permute-start(f32[128]{0:T(128)S(1)} %multiply_subtract_fusion), channel_id=1, source_target_pairs={{0,2},{1,3},{2,0},{3,1},{4,6},{5,7},{6,4},{7,5},{8,10},{9,11},{10,... | collective-permute-start | bytes 1544 | tf_op jit(solution)/shard_map/ppermute | solution.py:176
  85.0 4.4 %collective-permute-start.7 = (f32[128]{0:T(128)S(1)}, f32[128]{0:T(128)S(1)}, u32[]{:S(2)}, u32[]{:S(2)}) collective-permute-start(f32[128]{0:T(128)S(1)} %multiply_subtract_fusion), channel_id=1, source_target_pairs={{0,1},{1,2},{2,3},{3,0},{4,5},{5,6},{6,7},{7,4},{8,9},{9,10},{10,1... | collective-permute-start | bytes 1544 | tf_op jit(solution)/shard_map/ppermute | solution.py:176
  85.8 5.7 %collective-permute-start.4 = (bf16[128,1024]{1,0:T(8,128)(2,1)S(1)}, bf16[128,1024]{1,0:T(8,128)(2,1)S(1)}, u32[]{:S(2)}, u32[]{:S(2)}) collective-permute-start(bf16[128,1024]{1,0:T(8,128)(2,1)S(1)} %fusion.26), channel_id=1, source_target_pairs={{0,1},{1,2},{2,3},{3,0},{4,5},{5,6},{6,7},{7,4},{8,9},{9,10},{10,1... | collective-permute-start | bytes 786440 | tf_op jit(solution)/shard_map/ppermute | solution.py:176
  88.4 6.5 %collective-permute-start.6 = (bf16[128,1024]{1,0:T(8,128)(2,1)S(1)}, bf16[128,1024]{1,0:T(8,128)(2,1)S(1)}, u32[]{:S(2)}, u32[]{:S(2)}) collective-permute-start(bf16[128,1024]{1,0:T(8,128)(2,1)S(1)} %add_convert_fusion), channel_id=1, source_target_pairs={{0,3},{1,0},{2,1},{3,2},{4,7},{5,4},{6,5},{7,6},{8,11},{9,8},{10,9... | collective-permute-start | bytes 786440 | tf_op jit(solution)/shard_map/ppermute | solution.py:176
  89.3 84.0 %copy-start.3 = (bf16[128,1024]{1,0:T(8,128)(2,1)S(1)}, bf16[128,1024]{1,0:T(8,128)(2,1)}, u32[]{:S(2)}) copy-start(bf16[128,1024]{1,0:T(8,128)(2,1)} %param.9) | copy-start | bytes 786436

commit v17 on v15

--- a/solution.py
+++ b/solution.py
@@ -26,16 +26,41 @@
     wire = outgoing.dtype
     rounds = scan_rounds(count)
     step = -1 if reverse else 1
-    flat = [(r, d) for r, group in enumerate(rounds) for d in group]
-    targets = [me + step * d for _, d in flat]
-    sources = [me - step * d for _, d in flat]
-    sends = [(t >= 0) & (t < count) for t in targets]
-    receives = [(s >= 0) & (s < count) for s in sources]
+    plan = []
+    for r, group in enumerate(rounds):
+        if len(group) == 3:
+            w = group[0]
+            plan.append((r, w, None, 0))
+            plan.append((r, 3 * w, None, 0))
+            plan.append((r, w, len(plan) - 2, w))
+        else:
+            plan.append((r, group[0], None, 0))
+
+    def inside(i):
+        return (i >= 0) & (i < count)
+
+    targets = [me + step * d for _, d, _, _ in plan]
+    sends = []
+    receives = []
+    for _, d, origin, extra in plan:
+        if origin is None:
+            sends.append(inside(me + step * d))
+            receives.append(inside(me - step * d))
+        else:
+            sends.append(inside(me + step * d) & inside(me - step * extra))
+            receives.append(inside(me - step * (d + extra)))
+    fresh = [c for c, (_, _, origin, _) in enumerate(plan) if origin is None]
 
     barrier = pltpu.get_barrier_semaphore()
     pl.semaphore_signal(barrier, 1, device_id=(mate, head), device_id_type=MESH)
     expected = jnp.int32(1)
-    for target, source, send, receive in zip(targets, sources, sends, receives):
+    for c in fresh:
+        d = plan[c][1]
+        source = me - step * d
+        send = inside(targets[c])
+        receive = inside(source)
+        target = targets[c]
+
         @pl.when(send)
         def _():
             pl.semaphore_signal(barrier, 1, device_id=(target, head), device_id_type=MESH)
@@ -56,12 +81,18 @@
     running[...] = state_ref[mine] + other[mine]
     exclusive[...] = jnp.zeros_like(exclusive)
     copies = []
-    for r, group in enumerate(rounds):
+    for r in range(len(rounds)):
         outgoing[r] = running[...].astype(wire)
-        members = [c for c, (owner, _) in enumerate(flat) if owner == r]
+        members = [c for c, entry in enumerate(plan) if entry[0] == r]
         for c in members:
+            origin = plan[c][2]
+            if origin is not None:
+                @pl.when(receives[origin])
+                def _():
+                    copies[origin].wait_recv()
+            source_ref = outgoing.at[r] if origin is None else arrived.at[origin]
             copy = pltpu.make_async_remote_copy(
-                outgoing.at[r], arrived.at[c], send_sems.at[c + 1], recv_sems.at[c + 1],
+                source_ref, arrived.at[c], send_sems.at[c + 1], recv_sems.at[c + 1],
                 device_id=(targets[c], head), device_id_type=MESH,
             )
             copies.append(copy)
@@ -71,13 +102,21 @@
                 copy.start()
 
         for c in members:
+            origin_of = [e[2] for e in plan]
+            if c in origin_of:
+                continue_wait = False
+            else:
+                continue_wait = True
+
             @pl.when(receives[c])
             def _():
-                copies[c].wait_recv()
+                if continue_wait:
+                    copies[c].wait_recv()
                 got = arrived[c].astype(running.dtype)
                 running[...] = running[...] + got
                 exclusive[...] = exclusive[...] + got
 
+    flat = plan
     last = len(flat) + 1
     handed[...] = exclusive[...].astype(wire)
     back = pltpu.make_async_remote_copy(

time: 176 us -> 184 us (1.045); the launches traced: 175 us -> 181 us
  Pallas kernels: 124 us -> 130 us
    pallas_call x2, Pallas kernels: 124 us -> 130 us  [exclusive_scan(): pl.pallas_call(functools.partial(scan_kernel, reverse, count), out_shape=...]
  transfers between devices with their start and end apart: 9 -> 9, of which waited for: 5 -> 5; matrix products, arithmetic and copies ran while one was open for 6% -> 5% of each run, Pallas kernels for 0% -> 0%
where the time goes in v17:
time: 184 us; the launch traced here: 181 us
  Pallas kernels  130 us (71%)
  matrix products  24.9 us (14%)
  starting transfers between devices  9.66 us (5%)
  waiting for transfers between devices  8.44 us (5%)
  local copies, waits for them, and re-layouts  5.13 us (3%)
    pallas_call x2, Pallas kernels, exclusive_scan(): pl.pallas_call(functools.partial(scan_kernel, reverse, count), out_shape=...  130 us
    ppermute x9, starting transfers between devices, shifted(): lax.ppermute(x, 'head', [(m, (m + k) % head_count) for m in range(head_co...  9.66 us
    ppermute x9, waiting for transfers between devices, shifted(): lax.ppermute(x, 'head', [(m, (m + k) % head_count) for m in range(head_co...  8.44 us
    dot_general x3, matrix products, body(): jnp.dot(received[k], weight_rows((head_index - k + head_count) % head_cou...  6.34 us
    dot_general x4, matrix products, block_term(): lax.dot_general(dlogit, weight_rows(owner), (((1,), (1,)), ((), ())), pre...  4.95 us
  transfers between devices with their start and end apart: 9, of which 5 were waited for; matrix products, arithmetic and copies ran while one was open for 5% of the time, Pallas kernels for 0%

profile of v17, /device:TPU:1, one launch (start us, length us, event | category | flops | bytes accessed | tf_op | source)
XLA Modules:
  0.0 180.8 jit_solution(6059305621111651363)
XLA Ops:
  0.7 1.0 copy.41
  2.0 1.0 fusion.45.state_ref
  3.0 35.5 %shard_map.111 = f32[8,128,128]{2,1,0:T(8,128)} custom-call(f32[8,128,128]{2,1,0:T(8,128)} %fusion.45.state_ref), custom_call_target="tpu_custom_call" | custom-call | tf_op jit(solution)/shard_map/pallas_call | solution.py:166
  38.5 1.6 convolution_bitcast_fusion.5
  40.0 1.3 convolution_multiply_fusion.1
  42.8 1.9 %collective-permute-start.2 = (bf16[128,1024]{0,1:T(8,128)(2,1)S(1)}, bf16[128,1024]{0,1:T(8,128)(2,1)S(1)}, u32[]{:S(2)}, u32[]{:S(2)}) collective-permute-start(bf16[128,1024]{0,1:T(8,128)(2,1)S(1)} %bitcast.121), channel_id=1, source_target_pairs={{0,3},{1,0},{2,1},{3,2},{4,7},{5,4},{6,5},{7,6},{8,11},{9,8},{10,9... | collective-permute-start | bytes 786440 | tf_op jit(solution)/shard_map/ppermute | solution.py:215
  45.0 2.2 %fusion.14 = f32[128,1024]{1,0:T(8,128)S(1)} fusion(bf16[128,1024]{0,1:T(8,128)(2,1)S(1)} %bitcast.122, bf16[4096,1024]{1,0:T(8,128)(2,1)} %param.11, s32[]{:T(128)S(6)} %select_n.48), kind=kOutput, calls=%fused_computation.14 | convolution fusion | flops 268435456 | bytes 2883588 | tf_op jit(solution)/shard_map/dot_general | solution.py:220
  47.2 3.2 %collective-permute-done = bf16[128,1024]{0,1:T(8,128)(2,1)S(1)} collective-permute-done((bf16[128,1024]{0,1:T(8,128)(2,1)S(1)}, bf16[128,1024]{0,1:T(8,128)(2,1)S(1)}, u32[]{:S(2)}, u32[]{:S(2)}) %collective-permute-start) | collective-permute-done | bytes 262176 | tf_op jit(solution)/shard_map/ppermute | solution.py:215
  50.4 2.1 %fusion.2 = f32[128,1024]{1,0:T(8,128)S(1)} fusion(bf16[128,1024]{0,1:T(8,128)(2,1)S(1)} %collective-permute-done.2, bf16[4096,1024]{1,0:T(8,128)(2,1)} %param.11, s32[]{:T(128)S(6)} %select_n.54), kind=kOutput, calls=%fused_computation.2 | convolution fusion | flops 268435456 | bytes 2883588 | tf_op jit(solution)/shard_map/dot_general | solution.py:227
  52.5 2.2 %fusion.16 = f32[128,1024]{1,0:T(8,128)S(1)} fusion(f32[128,1024]{1,0:T(8,128)S(1)} %fusion.14, bf16[128,1024]{0,1:T(8,128)(2,1)S(1)} %collective-permute-done, bf16[4096,1024]{1,0:T(8,128)(2,1)} %param.11, s32[]{:T(128)S(6)} %select_n.50), kind=kOutput, calls=%fused_computation.16 | convolution fusion | flops 268566528 | bytes 3407876 | tf_op jit(solution)/shard_map/dot_general | solution.py:227
  54.7 3.1 %collective-permute-done.1 = bf16[128,1024]{0,1:T(8,128)(2,1)S(1)} collective-permute-done((bf16[128,1024]{0,1:T(8,128)(2,1)S(1)}, bf16[128,1024]{0,1:T(8,128)(2,1)S(1)}, u32[]{:S(2)}, u32[]{:S(2)}) %collective-permute-start.1) | collective-permute-done | bytes 262176 | tf_op jit(solution)/shard_map/ppermute | solution.py:215
  57.9 2.1 %fusion.26 = f32[128,1024]{1,0:T(8,128)S(1)} fusion(f32[128,1024]{1,0:T(8,128)S(1)} %fusion.2, f32[128,1024]{1,0:T(8,128)S(1)} %fusion.16, bf16[128,1024]{0,1:T(8,128)(2,1)S(1)} %collective-permute-done.1, bf16[4096,1024]{1,0:T(8,128)(2,1)} %param.11, s32[]{:T(128)S(6)} %select_n.52), kind=kOutput, calls=%fused_computation.32 | convolution fusion | flops 268697600 | bytes 3932164 | tf_op jit(solution)/shard_map/dot_general | solution.py:227
  61.1 2.5 %fusion.32 = bf16[128,1024]{1,0:T(8,128)(2,1)S(1)} fusion(bf16[128,1024]{1,0:T(8,128)(2,1)S(1)} %get-tuple-element.9, bf16[4096,1024]{1,0:T(8,128)(2,1)} %param.11, s32[]{:T(128)S(6)} %select_n.52), kind=kOutput, calls=%fused_computation.37 | convolution fusion | flops 268566528 | bytes 2621444 | tf_op jit(solution)/shard_map/dot_general | solution.py:246
  63.7 1.4 collective-permute-start.6
  65.1 2.5 %collective-permute-start.8 = (f32[128]{0:T(128)S(1)}, f32[128]{0:T(128)S(1)}, u32[]{:S(2)}, u32[]{:S(2)}) collective-permute-start(f32[128]{0:T(128)S(1)} %multiply_subtract_fusion), channel_id=1, source_target_pairs={{0,3},{1,0},{2,1},{3,2},{4,7},{5,4},{6,5},{7,6},{8,11},{9,8},{10,9... | collective-permute-start | bytes 1544 | tf_op jit(solution)/shard_map/ppermute | solution.py:215
  69.7 2.6 %collective-permute-start.5 = (bf16[128,1024]{1,0:T(8,128)(2,1)S(1)}, bf16[128,1024]{1,0:T(8,128)(2,1)S(1)}, u32[]{:S(2)}, u32[]{:S(2)}) collective-permute-start(bf16[128,1024]{1,0:T(8,128)(2,1)S(1)} %add_convert_fusion), channel_id=1, source_target_pairs={{0,3},{1,0},{2,1},{3,2},{4,7},{5,4},{6,5},{7,6},{8,11},{9,8},{10,9... | collective-permute-start | bytes 786440 | tf_op jit(solution)/shard_map/ppermute | solution.py:215
  73.7 1.5 collective-permute-done.3
  75.6 0.9 convert_add_fusion
  76.5 1.2 copy.19
  78.2 1.1 convolution_bitcast_fusion.1.state_ref
  80.0 94.3 %shard_map.112 = f32[8,128,128]{2,1,0:T(8,128)} custom-call(f32[8,128,128]{2,1,0:T(8,128)} %convolution_bitcast_fusion.1.state_ref), custom_call_target="tpu_custom_call" | custom-call | tf_op jit(solution)/shard_map/pallas_call | solution.py:166
  174.3 1.5 convolution_bitcast_fusion
  175.9 1.5 fusion.29
  177.4 0.9 copy.32
  (58 shorter events, 10.6 us)
Async XLA Ops:
  0.6 1.3 copy-start
  0.6 44.1 %copy-start.4 = (f32[32,1024]{1,0:T(8,128)S(1)}, f32[32,1024]{1,0:T(8,128)}, u32[]{:S(2)}) copy-start(f32[32,1024]{1,0:T(8,128)} %param.12) | copy-start | bytes 393220
  0.7 44.1 %copy-start.5 = (s32[128]{0:T(128)S(1)}, s32[128]{0:T(128)}, u32[]{:S(2)}) copy-start(s32[128]{0:T(128)} %param.14) | copy-start | bytes 1540
  41.4 18.6 %copy-start.6 = (s32[128]{0:T(128)S(1)}, s32[128]{0:T(128)}, u32[]{:S(2)}) copy-start(s32[128]{0:T(128)} %param.15) | copy-start | bytes 1540
  41.4 18.6 %copy-start.7 = (s32[128]{0:T(128)S(1)}, s32[128]{0:T(128)}, u32[]{:S(2)}) copy-start(s32[128]{0:T(128)} %param.13) | copy-start | bytes 1540
  42.0 8.4 %collective-permute-start = (bf16[128,1024]{0,1:T(8,128)(2,1)S(1)}, bf16[128,1024]{0,1:T(8,128)(2,1)S(1)}, u32[]{:S(2)}, u32[]{:S(2)}) collective-permute-start(bf16[128,1024]{0,1:T(8,128)(2,1)S(1)} %bitcast.120), channel_id=1, source_target_pairs={{0,1},{1,2},{2,3},{3,0},{4,5},{5,6},{6,7},{7,4},{8,9},{9,10},{10,1... | collective-permute-start | bytes 786440 | tf_op jit(solution)/shard_map/ppermute | solution.py:215
  42.8 7.6 %collective-permute-start.2 = (bf16[128,1024]{0,1:T(8,128)(2,1)S(1)}, bf16[128,1024]{0,1:T(8,128)(2,1)S(1)}, u32[]{:S(2)}, u32[]{:S(2)}) collective-permute-start(bf16[128,1024]{0,1:T(8,128)(2,1)S(1)} %bitcast.121), channel_id=1, source_target_pairs={{0,3},{1,0},{2,1},{3,2},{4,7},{5,4},{6,5},{7,6},{8,11},{9,8},{10,9... | collective-permute-start | bytes 786440 | tf_op jit(solution)/shard_map/ppermute | solution.py:215
  45.0 22.6 %slice-start = ((s8[8388608]{0:T(1024)(128)(4,1)}), s8[4194304]{0:T(1024)(128)(4,1)S(1)}, s32[]{:S(2)}) async-start(s8[8388608]{0:T(1024)(128)(4,1)} %bitcast.117), calls=%async_computation | async-start | bytes 8388608
  50.4 7.4 %collective-permute-start.1 = (bf16[128,1024]{0,1:T(8,128)(2,1)S(1)}, bf16[128,1024]{0,1:T(8,128)(2,1)S(1)}, u32[]{:S(2)}, u32[]{:S(2)}) collective-permute-start(bf16[128,1024]{0,1:T(8,128)(2,1)S(1)} %collective-permute-done), channel_id=1, source_target_pairs={{0,1},{1,2},{2,3},{3,0},{4,5},{5,6},{6,7},{7,4},{8,9},{9,10},{10,1... | collective-permute-start | bytes 786440 | tf_op jit(solution)/shard_map/ppermute | solution.py:215
  52.5 15.1 %slice-start.1 = ((s8[8388608]{0:T(1024)(128)(4,1)}), s8[4194304]{0:T(1024)(128)(4,1)S(1)}, s32[]{:S(2)}) async-start(s8[8388608]{0:T(1024)(128)(4,1)} %bitcast.117), calls=%async_computation.1 | async-start | bytes 8388608
  61.1 17.2 %copy-start.2 = (bf16[128,1024]{1,0:T(8,128)(2,1)S(1)}, bf16[128,1024]{1,0:T(8,128)(2,1)}, u32[]{:S(2)}) copy-start(bf16[128,1024]{1,0:T(8,128)(2,1)} %param.8) | copy-start | bytes 786436
  63.5 5.3 %collective-permute-start.4 = (bf16[128,1024]{1,0:T(8,128)(2,1)S(1)}, bf16[128,1024]{1,0:T(8,128)(2,1)S(1)}, u32[]{:S(2)}, u32[]{:S(2)}) collective-permute-start(bf16[128,1024]{1,0:T(8,128)(2,1)S(1)} %fusion.32), channel_id=1, source_target_pairs={{0,3},{1,0},{2,1},{3,2},{4,7},{5,4},{6,5},{7,6},{8,11},{9,8},{10,9... | collective-permute-start | bytes 786440 | tf_op jit(solution)/shard_map/ppermute | solution.py:215
  63.7 16.0 %copy-start.1 = (f32[8,128,128]{2,1,0:T(8,128)S(1)}, f32[8,128,128]{2,1,0:T(8,128)}, u32[]{:S(2)}) copy-start(f32[8,128,128]{2,1,0:T(8,128)} %shard_map.111) | copy-start | bytes 1572868
  63.7 9.5 %collective-permute-start.6 = (f32[128]{0:T(128)S(1)}, f32[128]{0:T(128)S(1)}, u32[]{:S(2)}, u32[]{:S(2)}) collective-permute-start(f32[128]{0:T(128)S(1)} %multiply_subtract_fusion), channel_id=1, source_target_pairs={{0,1},{1,2},{2,3},{3,0},{4,5},{5,6},{6,7},{7,4},{8,9},{9,10},{10,1... | collective-permute-start | bytes 1544 | tf_op jit(solution)/shard_map/ppermute | solution.py:215
  65.1 8.0 %collective-permute-start.7 = (f32[128]{0:T(128)S(1)}, f32[128]{0:T(128)S(1)}, u32[]{:S(2)}, u32[]{:S(2)}) collective-permute-start(f32[128]{0:T(128)S(1)} %multiply_subtract_fusion), channel_id=1, source_target_pairs={{0,2},{1,3},{2,0},{3,1},{4,6},{5,7},{6,4},{7,5},{8,10},{9,11},{10,... | collective-permute-start | bytes 1544 | tf_op jit(solution)/shard_map/ppermute | solution.py:215
  65.1 8.1 %collective-permute-start.8 = (f32[128]{0:T(128)S(1)}, f32[128]{0:T(128)S(1)}, u32[]{:S(2)}, u32[]{:S(2)}) collective-permute-start(f32[128]{0:T(128)S(1)} %multiply_subtract_fusion), channel_id=1, source_target_pairs={{0,3},{1,0},{2,1},{3,2},{4,7},{5,4},{6,5},{7,6},{8,11},{9,8},{10,9... | collective-permute-start | bytes 1544 | tf_op jit(solution)/shard_map/ppermute | solution.py:215
  68.4 107.4 %copy-start.3 = (bf16[128,1024]{1,0:T(8,128)(2,1)S(1)}, bf16[128,1024]{1,0:T(8,128)(2,1)}, u32[]{:S(2)}) copy-start(bf16[128,1024]{1,0:T(8,128)(2,1)} %param.9) | copy-start | bytes 786436
  68.4 6.7 %collective-permute-start.3 = (bf16[128,1024]{1,0:T(8,128)(2,1)S(1)}, bf16[128,1024]{1,0:T(8,128)(2,1)S(1)}, u32[]{:S(2)}, u32[]{:S(2)}) collective-permute-start(bf16[128,1024]{1,0:T(8,128)(2,1)S(1)} %fusion.35), channel_id=1, source_target_pairs={{0,1},{1,2},{2,3},{3,0},{4,5},{5,6},{6,7},{7,4},{8,9},{9,10},{10,1... | collective-permute-start | bytes 786440 | tf_op jit(solution)/shard_map/ppermute | solution.py:215
  69.7 5.9 %collective-permute-start.5 = (bf16[128,1024]{1,0:T(8,128)(2,1)S(1)}, bf16[128,1024]{1,0:T(8,128)(2,1)S(1)}, u32[]{:S(2)}, u32[]{:S(2)}) collective-permute-start(bf16[128,1024]{1,0:T(8,128)(2,1)S(1)} %add_convert_fusion), channel_id=1, source_target_pairs={{0,3},{1,0},{2,1},{3,2},{4,7},{5,4},{6,5},{7,6},{8,11},{9,8},{10,9... | collective-permute-start | bytes 786440 | tf_op jit(solution)/shard_map/ppermute | solution.py:215

commit v18 on v15

--- a/solution.py
+++ b/solution.py
@@ -209,9 +209,7 @@
         )
 
     grad_hidden = block_term(head_index)
-    event_loss = partial_value
-    for k in range(1, head_count):
-        event_loss = event_loss + shifted(partial_value, k)
+    loss_parts = [shifted(partial_value, k) for k in range(1, head_count)]
     if head_count == 4:
         ahead = shifted(block_term((head_index + 1) % 4).astype(jnp.bfloat16), 1)
         relay = shifted(block_term((head_index + 2) % 4).astype(jnp.bfloat16), 3)
@@ -228,6 +226,10 @@
     grad_out = grad_raw.astype(jnp.bfloat16)
     local_adjoint = jnp.einsum("thd,the->hde", query_rows, grad_out, preferred_element_type=f32)
     suffix = exclusive_scan(local_adjoint, "seq", reverse=True)
+    loss_parts, suffix = lax.optimization_barrier((loss_parts, suffix))
+    event_loss = partial_value
+    for part in loss_parts:
+        event_loss = event_loss + part
     back_scores = (
         jnp.einsum("the,she->hts", grad_out, value_rows, preferred_element_type=f32) * causal
     )

time: 176 us -> 175 us (level)
  transfers between devices with their start and end apart: 9 -> 9, of which waited for: 5 -> 4; matrix products, arithmetic and copies ran while one was open for 6% -> 8% of each run, Pallas kernels for 0% -> 49%
where the time goes in v18:
time: 175 us
  Pallas kernels  125 us (71%)
  matrix products  24.9 us (14%)
  waiting for transfers between devices  8.87 us (5%)
  starting transfers between devices  8.31 us (5%)
  local copies, waits for them, and re-layouts  5.13 us (3%)
  other arithmetic  1.8 us (1%)
    pallas_call x2, Pallas kernels, exclusive_scan(): pl.pallas_call(functools.partial(scan_kernel, reverse, count), out_shape=...  125 us
    ppermute x9, waiting for transfers between devices, shifted(): lax.ppermute(x, 'head', [(m, (m + k) % head_count) for m in range(head_co...  8.87 us
    ppermute x9, starting transfers between devices, shifted(): lax.ppermute(x, 'head', [(m, (m + k) % head_count) for m in range(head_co...  8.31 us
    dot_general x3, matrix products, body(): jnp.dot(received[k], weight_rows((head_index - k + head_count) % head_cou...  6.33 us
    dot_general x4, matrix products, block_term(): lax.dot_general(dlogit, weight_rows(owner), (((1,), (1,)), ((), ())), pre...  4.91 us
    unnamed x24, local copies, waits for them, and re-layouts  3.65 us
  transfers between devices with their start and end apart: 9, of which 4 were waited for; matrix products, arithmetic and copies ran while one was open for 8% of the time, Pallas kernels for 49%

profile of v18, /device:TPU:1, one launch (start us, length us, event | category | flops | bytes accessed | tf_op | source)
XLA Modules:
  0.0 174.7 jit_solution(3373825099608468488)
XLA Ops:
  0.7 1.0 copy.41
  2.0 1.0 fusion.45.state_ref
  3.0 38.5 %shard_map.111 = f32[8,128,128]{2,1,0:T(8,128)} custom-call(f32[8,128,128]{2,1,0:T(8,128)} %fusion.45.state_ref), custom_call_target="tpu_custom_call" | custom-call | tf_op jit(solution)/shard_map/pallas_call | solution.py:127
  41.5 1.6 convolution_bitcast_fusion.5
  43.1 1.3 convolution_multiply_fusion.1
  45.1 1.2 collective-permute-start
  46.3 1.5 collective-permute-start.2
  48.0 2.2 %fusion.14 = f32[128,1024]{1,0:T(8,128)S(1)} fusion(bf16[128,1024]{0,1:T(8,128)(2,1)S(1)} %bitcast.122, bf16[4096,1024]{1,0:T(8,128)(2,1)} %param.11, s32[]{:T(128)S(6)} %select_n.48), kind=kOutput, calls=%fused_computation.14 | convolution fusion | flops 268435456 | bytes 2883588 | tf_op jit(solution)/shard_map/dot_general | solution.py:181
  50.3 3.1 %collective-permute-done = bf16[128,1024]{0,1:T(8,128)(2,1)S(1)} collective-permute-done((bf16[128,1024]{0,1:T(8,128)(2,1)S(1)}, bf16[128,1024]{0,1:T(8,128)(2,1)S(1)}, u32[]{:S(2)}, u32[]{:S(2)}) %collective-permute-start) | collective-permute-done | bytes 262176 | tf_op jit(solution)/shard_map/ppermute | solution.py:176
  53.4 2.1 %fusion.2 = f32[128,1024]{1,0:T(8,128)S(1)} fusion(bf16[128,1024]{0,1:T(8,128)(2,1)S(1)} %collective-permute-done.2, bf16[4096,1024]{1,0:T(8,128)(2,1)} %param.11, s32[]{:T(128)S(6)} %select_n.54), kind=kOutput, calls=%fused_computation.2 | convolution fusion | flops 268435456 | bytes 2883588 | tf_op jit(solution)/shard_map/dot_general | solution.py:188
  55.4 2.2 %fusion.16 = f32[128,1024]{1,0:T(8,128)S(1)} fusion(f32[128,1024]{1,0:T(8,128)S(1)} %fusion.14, bf16[128,1024]{0,1:T(8,128)(2,1)S(1)} %collective-permute-done, bf16[4096,1024]{1,0:T(8,128)(2,1)} %param.11, s32[]{:T(128)S(6)} %select_n.50), kind=kOutput, calls=%fused_computation.16 | convolution fusion | flops 268566528 | bytes 3407876 | tf_op jit(solution)/shard_map/dot_general | solution.py:188
  57.7 3.0 %collective-permute-done.1 = bf16[128,1024]{0,1:T(8,128)(2,1)S(1)} collective-permute-done((bf16[128,1024]{0,1:T(8,128)(2,1)S(1)}, bf16[128,1024]{0,1:T(8,128)(2,1)S(1)}, u32[]{:S(2)}, u32[]{:S(2)}) %collective-permute-start.1) | collective-permute-done | bytes 262176 | tf_op jit(solution)/shard_map/ppermute | solution.py:176
  60.6 2.1 %fusion.26 = f32[128,1024]{1,0:T(8,128)S(1)} fusion(f32[128,1024]{1,0:T(8,128)S(1)} %fusion.2, f32[128,1024]{1,0:T(8,128)S(1)} %fusion.16, bf16[128,1024]{0,1:T(8,128)(2,1)S(1)} %collective-permute-done.1, bf16[4096,1024]{1,0:T(8,128)(2,1)} %param.11, s32[]{:T(128)S(6)} %select_n.52), kind=kOutput, calls=%fused_computation.32 | convolution fusion | flops 268697600 | bytes 3932164 | tf_op jit(solution)/shard_map/dot_general | solution.py:188
  63.3 2.4 %fusion.32 = bf16[128,1024]{1,0:T(8,128)(2,1)S(1)} fusion(bf16[128,1024]{1,0:T(8,128)(2,1)S(1)} %get-tuple-element.17, bf16[4096,1024]{1,0:T(8,128)(2,1)} %param.11, s32[]{:T(128)S(6)} %select_n.52), kind=kOutput, calls=%fused_computation.37 | convolution fusion | flops 268566528 | bytes 2621444 | tf_op jit(solution)/shard_map/dot_general | solution.py:207
  66.7 1.5 collective-permute-start.3
  68.7 2.3 %collective-permute-done.4 = bf16[128,1024]{1,0:T(8,128)(2,1)S(1)} collective-permute-done((bf16[128,1024]{1,0:T(8,128)(2,1)S(1)}, bf16[128,1024]{1,0:T(8,128)(2,1)S(1)}, u32[]{:S(2)}, u32[]{:S(2)}) %collective-permute-start.4) | collective-permute-done | bytes 262176 | tf_op jit(solution)/shard_map/ppermute | solution.py:176
  71.9 1.3 collective-permute-start.5
  73.4 1.0 collective-permute-start.7
  74.5 1.4 collective-permute-start.8
  78.1 1.2 copy.19
  80.5 1.1 convolution_bitcast_fusion.1.state_ref
  81.6 86.1 %shard_map.112 = f32[8,128,128]{2,1,0:T(8,128)} custom-call(f32[8,128,128]{2,1,0:T(8,128)} %convolution_bitcast_fusion.1.state_ref), custom_call_target="tpu_custom_call" | custom-call | tf_op jit(solution)/shard_map/pallas_call | solution.py:127
  167.7 1.5 fusion.29
  170.4 1.5 fusion.30
  (58 shorter events, 11.4 us)
Async XLA Ops:
  0.6 1.3 copy-start
  0.6 47.2 %copy-start.4 = (f32[32,1024]{1,0:T(8,128)S(1)}, f32[32,1024]{1,0:T(8,128)}, u32[]{:S(2)}) copy-start(f32[32,1024]{1,0:T(8,128)} %param.12) | copy-start | bytes 393220
  0.7 47.2 %copy-start.5 = (s32[128]{0:T(128)S(1)}, s32[128]{0:T(128)}, u32[]{:S(2)}) copy-start(s32[128]{0:T(128)} %param.14) | copy-start | bytes 1540
  44.4 18.3 %copy-start.6 = (s32[128]{0:T(128)S(1)}, s32[128]{0:T(128)}, u32[]{:S(2)}) copy-start(s32[128]{0:T(128)} %param.15) | copy-start | bytes 1540
  44.5 18.3 %copy-start.7 = (s32[128]{0:T(128)S(1)}, s32[128]{0:T(128)}, u32[]{:S(2)}) copy-start(s32[128]{0:T(128)} %param.13) | copy-start | bytes 1540
  45.1 8.3 %collective-permute-start = (bf16[128,1024]{0,1:T(8,128)(2,1)S(1)}, bf16[128,1024]{0,1:T(8,128)(2,1)S(1)}, u32[]{:S(2)}, u32[]{:S(2)}) collective-permute-start(bf16[128,1024]{0,1:T(8,128)(2,1)S(1)} %bitcast.120), channel_id=1, source_target_pairs={{0,1},{1,2},{2,3},{3,0},{4,5},{5,6},{6,7},{7,4},{8,9},{9,10},{10,1... | collective-permute-start | bytes 786440 | tf_op jit(solution)/shard_map/ppermute | solution.py:176
  46.3 7.0 %collective-permute-start.2 = (bf16[128,1024]{0,1:T(8,128)(2,1)S(1)}, bf16[128,1024]{0,1:T(8,128)(2,1)S(1)}, u32[]{:S(2)}, u32[]{:S(2)}) collective-permute-start(bf16[128,1024]{0,1:T(8,128)(2,1)S(1)} %bitcast.121), channel_id=1, source_target_pairs={{0,3},{1,0},{2,1},{3,2},{4,7},{5,4},{6,5},{7,6},{8,11},{9,8},{10,9... | collective-permute-start | bytes 786440 | tf_op jit(solution)/shard_map/ppermute | solution.py:176
  48.0 17.8 %slice-start = ((s8[8388608]{0:T(1024)(128)(4,1)}), s8[4194304]{0:T(1024)(128)(4,1)S(1)}, s32[]{:S(2)}) async-start(s8[8388608]{0:T(1024)(128)(4,1)} %bitcast.117), calls=%async_computation | async-start | bytes 8388608
  53.4 7.3 %collective-permute-start.1 = (bf16[128,1024]{0,1:T(8,128)(2,1)S(1)}, bf16[128,1024]{0,1:T(8,128)(2,1)S(1)}, u32[]{:S(2)}, u32[]{:S(2)}) collective-permute-start(bf16[128,1024]{0,1:T(8,128)(2,1)S(1)} %collective-permute-done), channel_id=1, source_target_pairs={{0,1},{1,2},{2,3},{3,0},{4,5},{5,6},{6,7},{7,4},{8,9},{9,10},{10,1... | collective-permute-start | bytes 786440 | tf_op jit(solution)/shard_map/ppermute | solution.py:176
  55.4 10.4 %slice-start.1 = ((s8[8388608]{0:T(1024)(128)(4,1)}), s8[4194304]{0:T(1024)(128)(4,1)S(1)}, s32[]{:S(2)}) async-start(s8[8388608]{0:T(1024)(128)(4,1)} %bitcast.117), calls=%async_computation.1 | async-start | bytes 8388608
  65.7 14.4 %copy-start.1 = (f32[8,128,128]{2,1,0:T(8,128)S(1)}, f32[8,128,128]{2,1,0:T(8,128)}, u32[]{:S(2)}) copy-start(f32[8,128,128]{2,1,0:T(8,128)} %shard_map.111) | copy-start | bytes 1572868
  65.7 14.7 %copy-start.2 = (bf16[128,1024]{1,0:T(8,128)(2,1)S(1)}, bf16[128,1024]{1,0:T(8,128)(2,1)}, u32[]{:S(2)}) copy-start(bf16[128,1024]{1,0:T(8,128)(2,1)} %param.8) | copy-start | bytes 786436
  65.7 5.3 %collective-permute-start.4 = (bf16[128,1024]{1,0:T(8,128)(2,1)S(1)}, bf16[128,1024]{1,0:T(8,128)(2,1)S(1)}, u32[]{:S(2)}, u32[]{:S(2)}) collective-permute-start(bf16[128,1024]{1,0:T(8,128)(2,1)S(1)} %fusion.32), channel_id=1, source_target_pairs={{0,3},{1,0},{2,1},{3,2},{4,7},{5,4},{6,5},{7,6},{8,11},{9,8},{10,9... | collective-permute-start | bytes 786440 | tf_op jit(solution)/shard_map/ppermute | solution.py:176
  66.7 10.0 %collective-permute-start.3 = (bf16[128,1024]{1,0:T(8,128)(2,1)S(1)}, bf16[128,1024]{1,0:T(8,128)(2,1)S(1)}, u32[]{:S(2)}, u32[]{:S(2)}) collective-permute-start(bf16[128,1024]{1,0:T(8,128)(2,1)S(1)} %fusion.35), channel_id=1, source_target_pairs={{0,1},{1,2},{2,3},{3,0},{4,5},{5,6},{6,7},{7,4},{8,9},{9,10},{10,1... | collective-permute-start | bytes 786440 | tf_op jit(solution)/shard_map/ppermute | solution.py:176
  68.7 99.0 %copy-start.3 = (bf16[128,1024]{1,0:T(8,128)(2,1)S(1)}, bf16[128,1024]{1,0:T(8,128)(2,1)}, u32[]{:S(2)}) copy-start(bf16[128,1024]{1,0:T(8,128)(2,1)} %param.9) | copy-start | bytes 786436
  71.9 5.3 %collective-permute-start.5 = (bf16[128,1024]{1,0:T(8,128)(2,1)S(1)}, bf16[128,1024]{1,0:T(8,128)(2,1)S(1)}, u32[]{:S(2)}, u32[]{:S(2)}) collective-permute-start(bf16[128,1024]{1,0:T(8,128)(2,1)S(1)} %add_convert_fusion), channel_id=1, source_target_pairs={{0,3},{1,0},{2,1},{3,2},{4,7},{5,4},{6,5},{7,6},{8,11},{9,8},{10,9... | collective-permute-start | bytes 786440 | tf_op jit(solution)/shard_map/ppermute | solution.py:176
  73.2 94.5 %collective-permute-start.6 = (f32[128]{0:T(128)S(1)}, f32[128]{0:T(128)S(1)}, u32[]{:S(2)}, u32[]{:S(2)}) collective-permute-start(f32[128]{0:T(128)S(1)} %multiply_subtract_fusion), channel_id=1, source_target_pairs={{0,1},{1,2},{2,3},{3,0},{4,5},{5,6},{6,7},{7,4},{8,9},{9,10},{10,1... | collective-permute-start | bytes 1544 | tf_op jit(solution)/shard_map/ppermute | solution.py:176
  73.4 94.3 %collective-permute-start.7 = (f32[128]{0:T(128)S(1)}, f32[128]{0:T(128)S(1)}, u32[]{:S(2)}, u32[]{:S(2)}) collective-permute-start(f32[128]{0:T(128)S(1)} %multiply_subtract_fusion), channel_id=1, source_target_pairs={{0,2},{1,3},{2,0},{3,1},{4,6},{5,7},{6,4},{7,5},{8,10},{9,11},{10,... | collective-permute-start | bytes 1544 | tf_op jit(solution)/shard_map/ppermute | solution.py:176
  74.5 93.2 %collective-permute-start.8 = (f32[128]{0:T(128)S(1)}, f32[128]{0:T(128)S(1)}, u32[]{:S(2)}, u32[]{:S(2)}) collective-permute-start(f32[128]{0:T(128)S(1)} %multiply_subtract_fusion), channel_id=1, source_target_pairs={{0,3},{1,0},{2,1},{3,2},{4,7},{5,4},{6,5},{7,6},{8,11},{9,8},{10,9... | collective-permute-start | bytes 1544 | tf_op jit(solution)/shard_map/ppermute | solution.py:176

commit v19 on v18

--- a/solution.py
+++ b/solution.py
@@ -225,20 +225,22 @@
     ) / root_mean
     grad_out = grad_raw.astype(jnp.bfloat16)
     local_adjoint = jnp.einsum("thd,the->hde", query_rows, grad_out, preferred_element_type=f32)
+    back_scores = (
+        jnp.einsum("the,she->hts", grad_out, value_rows, preferred_element_type=f32) * causal
+    )
+    grad_query = jnp.einsum(
+        "hts,shd->thd", back_scores, key_rows, precision=three_pass, preferred_element_type=f32
+    )
+    grad_query = grad_query + jnp.einsum(
+        "the,hde->thd", grad_out, prefix, precision=three_pass, preferred_element_type=f32
+    )
+    grad_queries = grad_query.reshape(rows_here, width_here).astype(jnp.bfloat16)
+    grad_queries, local_adjoint = lax.optimization_barrier((grad_queries, local_adjoint))
     suffix = exclusive_scan(local_adjoint, "seq", reverse=True)
     loss_parts, suffix = lax.optimization_barrier((loss_parts, suffix))
     event_loss = partial_value
     for part in loss_parts:
         event_loss = event_loss + part
-    back_scores = (
-        jnp.einsum("the,she->hts", grad_out, value_rows, preferred_element_type=f32) * causal
-    )
-    grad_query = jnp.einsum(
-        "hts,shd->thd", back_scores, key_rows, precision=three_pass, preferred_element_type=f32
-    )
-    grad_query = grad_query + jnp.einsum(
-        "the,hde->thd", grad_out, prefix, precision=three_pass, preferred_element_type=f32
-    )
     grad_key = jnp.einsum(
         "hts,thd->shd", back_scores, query_rows, precision=three_pass, preferred_element_type=f32
     )
@@ -251,7 +253,6 @@
     grad_value = grad_value + jnp.einsum(
         "shd,hde->she", key_rows, suffix, precision=three_pass, preferred_element_type=f32
     )
-    grad_queries = grad_query.reshape(rows_here, width_here).astype(jnp.bfloat16)
     grad_keys = grad_key.reshape(rows_here, width_here).astype(jnp.bfloat16)
     grad_values = grad_value.reshape(rows_here, width_here).astype(jnp.bfloat16)
     return (grad_queries, grad_keys, grad_values, event_loss)

time: 175 us -> 176 us (level)
    unnamed x24 -> x22, local copies, waits for them, and re-layouts: 3.65 us -> 3.6 us
where the time goes in v19:
time: 176 us
  Pallas kernels  125 us (71%)
  matrix products  24.8 us (14%)
  waiting for transfers between devices  8.88 us (5%)
  starting transfers between devices  8.31 us (5%)
  local copies, waits for them, and re-layouts  6.24 us (4%)
  other arithmetic  1.79 us (1%)
    pallas_call x2, Pallas kernels, exclusive_scan(): pl.pallas_call(functools.partial(scan_kernel, reverse, count), out_shape=...  125 us
    ppermute x9, waiting for transfers between devices, shifted(): lax.ppermute(x, 'head', [(m, (m + k) % head_count) for m in range(head_co...  8.88 us
    ppermute x9, starting transfers between devices, shifted(): lax.ppermute(x, 'head', [(m, (m + k) % head_count) for m in range(head_co...  8.31 us
    dot_general x3, matrix products, body(): jnp.dot(received[k], weight_rows((head_index - k + head_count) % head_cou...  6.35 us
    dot_general x4, matrix products, block_term(): lax.dot_general(dlogit, weight_rows(owner), (((1,), (1,)), ((), ())), pre...  4.97 us
    unnamed x22, local copies, waits for them, and re-layouts  3.6 us
  transfers between devices with their start and end apart: 9, of which 4 were waited for; matrix products, arithmetic and copies ran while one was open for 8% of the time, Pallas kernels for 49%

profile of v19, /device:TPU:1, one launch (start us, length us, event | category | flops | bytes accessed | tf_op | source)
XLA Modules:
  0.0 175.5 jit_solution(9707883850037552826)
XLA Ops:
  0.7 1.2 copy.38
  3.1 1.0 fusion.45.state_ref
  4.1 38.5 %shard_map.111 = f32[8,128,128]{2,1,0:T(8,128)} custom-call(f32[8,128,128]{2,1,0:T(8,128)} %fusion.45.state_ref), custom_call_target="tpu_custom_call" | custom-call | tf_op jit(solution)/shard_map/pallas_call | solution.py:127
  42.6 1.5 convolution_bitcast_fusion.5
  44.1 1.3 convolution_multiply_fusion.1
  46.1 1.2 collective-permute-start
  47.3 1.5 collective-permute-start.2
  49.0 2.2 %fusion.14 = f32[128,1024]{1,0:T(8,128)S(1)} fusion(bf16[128,1024]{0,1:T(8,128)(2,1)S(1)} %bitcast.109, bf16[4096,1024]{1,0:T(8,128)(2,1)} %param.11, s32[]{:T(128)S(6)} %select_n.48), kind=kOutput, calls=%fused_computation.14 | convolution fusion | flops 268435456 | bytes 2883588 | tf_op jit(solution)/shard_map/dot_general | solution.py:181
  51.2 3.1 %collective-permute-done = bf16[128,1024]{0,1:T(8,128)(2,1)S(1)} collective-permute-done((bf16[128,1024]{0,1:T(8,128)(2,1)S(1)}, bf16[128,1024]{0,1:T(8,128)(2,1)S(1)}, u32[]{:S(2)}, u32[]{:S(2)}) %collective-permute-start) | collective-permute-done | bytes 262176 | tf_op jit(solution)/shard_map/ppermute | solution.py:176
  54.3 2.1 %fusion.2 = f32[128,1024]{1,0:T(8,128)S(1)} fusion(bf16[128,1024]{0,1:T(8,128)(2,1)S(1)} %collective-permute-done.2, bf16[4096,1024]{1,0:T(8,128)(2,1)} %param.11, s32[]{:T(128)S(6)} %select_n.54), kind=kOutput, calls=%fused_computation.2 | convolution fusion | flops 268435456 | bytes 2883588 | tf_op jit(solution)/shard_map/dot_general | solution.py:188
  56.4 2.2 %fusion.16 = f32[128,1024]{1,0:T(8,128)S(1)} fusion(f32[128,1024]{1,0:T(8,128)S(1)} %fusion.14, bf16[128,1024]{0,1:T(8,128)(2,1)S(1)} %collective-permute-done, bf16[4096,1024]{1,0:T(8,128)(2,1)} %param.11, s32[]{:T(128)S(6)} %select_n.50), kind=kOutput, calls=%fused_computation.16 | convolution fusion | flops 268566528 | bytes 3407876 | tf_op jit(solution)/shard_map/dot_general | solution.py:188
  58.7 3.0 %collective-permute-done.1 = bf16[128,1024]{0,1:T(8,128)(2,1)S(1)} collective-permute-done((bf16[128,1024]{0,1:T(8,128)(2,1)S(1)}, bf16[128,1024]{0,1:T(8,128)(2,1)S(1)}, u32[]{:S(2)}, u32[]{:S(2)}) %collective-permute-start.1) | collective-permute-done | bytes 262176 | tf_op jit(solution)/shard_map/ppermute | solution.py:176
  61.6 2.1 %fusion.26 = f32[128,1024]{1,0:T(8,128)S(1)} fusion(f32[128,1024]{1,0:T(8,128)S(1)} %fusion.2, f32[128,1024]{1,0:T(8,128)S(1)} %fusion.16, bf16[128,1024]{0,1:T(8,128)(2,1)S(1)} %collective-permute-done.1, bf16[4096,1024]{1,0:T(8,128)(2,1)} %param.11, s32[]{:T(128)S(6)} %select_n.52), kind=kOutput, calls=%fused_computation.32 | convolution fusion | flops 268697600 | bytes 3932164 | tf_op jit(solution)/shard_map/dot_general | solution.py:188
  64.3 2.5 %fusion.32 = bf16[128,1024]{1,0:T(8,128)(2,1)S(1)} fusion(bf16[128,1024]{1,0:T(8,128)(2,1)S(1)} %get-tuple-element.21, bf16[4096,1024]{1,0:T(8,128)(2,1)} %param.11, s32[]{:T(128)S(6)} %select_n.52), kind=kOutput, calls=%fused_computation.37 | convolution fusion | flops 268566528 | bytes 2621444 | tf_op jit(solution)/shard_map/dot_general | solution.py:207
  67.8 1.5 collective-permute-start.3
  69.8 2.3 %collective-permute-done.4 = bf16[128,1024]{1,0:T(8,128)(2,1)S(1)} collective-permute-done((bf16[128,1024]{1,0:T(8,128)(2,1)S(1)}, bf16[128,1024]{1,0:T(8,128)(2,1)S(1)}, u32[]{:S(2)}, u32[]{:S(2)}) %collective-permute-start.4) | collective-permute-done | bytes 262176 | tf_op jit(solution)/shard_map/ppermute | solution.py:176
  72.9 1.3 collective-permute-start.5
  74.5 1.0 collective-permute-start.7
  75.5 1.4 collective-permute-start.8
  79.1 1.2 copy.19
  82.3 1.1 convolution_bitcast_fusion.2.state_ref
  83.4 86.0 %shard_map.112 = f32[8,128,128]{2,1,0:T(8,128)} custom-call(f32[8,128,128]{2,1,0:T(8,128)} %convolution_bitcast_fusion.2.state_ref), custom_call_target="tpu_custom_call" | custom-call | tf_op jit(solution)/shard_map/pallas_call | solution.py:127
  169.4 1.5 fusion.29
  171.8 1.5 fusion.30
  (57 shorter events, 12.3 us)
Async XLA Ops:
  0.6 2.5 %copy-start = (bf16[128,1024]{1,0:T(8,128)(2,1)S(1)}, bf16[128,1024]{1,0:T(8,128)(2,1)}, u32[]{:S(2)}) copy-start(bf16[128,1024]{1,0:T(8,128)(2,1)} %param.10) | copy-start | bytes 786436
  0.6 48.2 %copy-start.3 = (f32[32,1024]{1,0:T(8,128)S(1)}, f32[32,1024]{1,0:T(8,128)}, u32[]{:S(2)}) copy-start(f32[32,1024]{1,0:T(8,128)} %param.12) | copy-start | bytes 393220
  0.7 48.2 %copy-start.4 = (s32[128]{0:T(128)S(1)}, s32[128]{0:T(128)}, u32[]{:S(2)}) copy-start(s32[128]{0:T(128)} %param.14) | copy-start | bytes 1540
  45.4 18.3 %copy-start.5 = (s32[128]{0:T(128)S(1)}, s32[128]{0:T(128)}, u32[]{:S(2)}) copy-start(s32[128]{0:T(128)} %param.15) | copy-start | bytes 1540
  45.4 18.3 %copy-start.6 = (s32[128]{0:T(128)S(1)}, s32[128]{0:T(128)}, u32[]{:S(2)}) copy-start(s32[128]{0:T(128)} %param.13) | copy-start | bytes 1540
  46.1 8.3 %collective-permute-start = (bf16[128,1024]{0,1:T(8,128)(2,1)S(1)}, bf16[128,1024]{0,1:T(8,128)(2,1)S(1)}, u32[]{:S(2)}, u32[]{:S(2)}) collective-permute-start(bf16[128,1024]{0,1:T(8,128)(2,1)S(1)} %bitcast.107), channel_id=1, source_target_pairs={{0,1},{1,2},{2,3},{3,0},{4,5},{5,6},{6,7},{7,4},{8,9},{9,10},{10,1... | collective-permute-start | bytes 786440 | tf_op jit(solution)/shard_map/ppermute | solution.py:176
  47.3 7.1 %collective-permute-start.2 = (bf16[128,1024]{0,1:T(8,128)(2,1)S(1)}, bf16[128,1024]{0,1:T(8,128)(2,1)S(1)}, u32[]{:S(2)}, u32[]{:S(2)}) collective-permute-start(bf16[128,1024]{0,1:T(8,128)(2,1)S(1)} %bitcast.108), channel_id=1, source_target_pairs={{0,3},{1,0},{2,1},{3,2},{4,7},{5,4},{6,5},{7,6},{8,11},{9,8},{10,9... | collective-permute-start | bytes 786440 | tf_op jit(solution)/shard_map/ppermute | solution.py:176
  49.0 17.9 %slice-start = ((s8[8388608]{0:T(1024)(128)(4,1)}), s8[4194304]{0:T(1024)(128)(4,1)S(1)}, s32[]{:S(2)}) async-start(s8[8388608]{0:T(1024)(128)(4,1)} %bitcast.100), calls=%async_computation | async-start | bytes 8388608
  54.3 7.3 %collective-permute-start.1 = (bf16[128,1024]{0,1:T(8,128)(2,1)S(1)}, bf16[128,1024]{0,1:T(8,128)(2,1)S(1)}, u32[]{:S(2)}, u32[]{:S(2)}) collective-permute-start(bf16[128,1024]{0,1:T(8,128)(2,1)S(1)} %collective-permute-done), channel_id=1, source_target_pairs={{0,1},{1,2},{2,3},{3,0},{4,5},{5,6},{6,7},{7,4},{8,9},{9,10},{10,1... | collective-permute-start | bytes 786440 | tf_op jit(solution)/shard_map/ppermute | solution.py:176
  56.4 10.5 %slice-start.1 = ((s8[8388608]{0:T(1024)(128)(4,1)}), s8[4194304]{0:T(1024)(128)(4,1)S(1)}, s32[]{:S(2)}) async-start(s8[8388608]{0:T(1024)(128)(4,1)} %bitcast.100), calls=%async_computation.1 | async-start | bytes 8388608
  64.3 16.6 %copy-start.1 = (f32[8,128,128]{2,1,0:T(8,128)S(1)}, f32[8,128,128]{2,1,0:T(8,128)}, u32[]{:S(2)}) copy-start(f32[8,128,128]{2,1,0:T(8,128)} %shard_map.111) | copy-start | bytes 1572868
  66.8 5.3 %collective-permute-start.4 = (bf16[128,1024]{1,0:T(8,128)(2,1)S(1)}, bf16[128,1024]{1,0:T(8,128)(2,1)S(1)}, u32[]{:S(2)}, u32[]{:S(2)}) collective-permute-start(bf16[128,1024]{1,0:T(8,128)(2,1)S(1)} %fusion.32), channel_id=1, source_target_pairs={{0,3},{1,0},{2,1},{3,2},{4,7},{5,4},{6,5},{7,6},{8,11},{9,8},{10,9... | collective-permute-start | bytes 786440 | tf_op jit(solution)/shard_map/ppermute | solution.py:176
  67.8 10.0 %collective-permute-start.3 = (bf16[128,1024]{1,0:T(8,128)(2,1)S(1)}, bf16[128,1024]{1,0:T(8,128)(2,1)S(1)}, u32[]{:S(2)}, u32[]{:S(2)}) collective-permute-start(bf16[128,1024]{1,0:T(8,128)(2,1)S(1)} %fusion.35), channel_id=1, source_target_pairs={{0,1},{1,2},{2,3},{3,0},{4,5},{5,6},{6,7},{7,4},{8,9},{9,10},{10,1... | collective-permute-start | bytes 786440 | tf_op jit(solution)/shard_map/ppermute | solution.py:176
  72.9 96.5 %copy-start.2 = (bf16[128,1024]{1,0:T(8,128)(2,1)S(1)}, bf16[128,1024]{1,0:T(8,128)(2,1)}, u32[]{:S(2)}) copy-start(bf16[128,1024]{1,0:T(8,128)(2,1)} %param.9) | copy-start | bytes 786436
  72.9 5.3 %collective-permute-start.5 = (bf16[128,1024]{1,0:T(8,128)(2,1)S(1)}, bf16[128,1024]{1,0:T(8,128)(2,1)S(1)}, u32[]{:S(2)}, u32[]{:S(2)}) collective-permute-start(bf16[128,1024]{1,0:T(8,128)(2,1)S(1)} %add_convert_fusion), channel_id=1, source_target_pairs={{0,3},{1,0},{2,1},{3,2},{4,7},{5,4},{6,5},{7,6},{8,11},{9,8},{10,9... | collective-permute-start | bytes 786440 | tf_op jit(solution)/shard_map/ppermute | solution.py:176
  74.2 95.2 %collective-permute-start.6 = (f32[128]{0:T(128)S(1)}, f32[128]{0:T(128)S(1)}, u32[]{:S(2)}, u32[]{:S(2)}) collective-permute-start(f32[128]{0:T(128)S(1)} %multiply_subtract_fusion), channel_id=1, source_target_pairs={{0,1},{1,2},{2,3},{3,0},{4,5},{5,6},{6,7},{7,4},{8,9},{9,10},{10,1... | collective-permute-start | bytes 1544 | tf_op jit(solution)/shard_map/ppermute | solution.py:176
  74.5 94.9 %collective-permute-start.7 = (f32[128]{0:T(128)S(1)}, f32[128]{0:T(128)S(1)}, u32[]{:S(2)}, u32[]{:S(2)}) collective-permute-start(f32[128]{0:T(128)S(1)} %multiply_subtract_fusion), channel_id=1, source_target_pairs={{0,2},{1,3},{2,0},{3,1},{4,6},{5,7},{6,4},{7,5},{8,10},{9,11},{10,... | collective-permute-start | bytes 1544 | tf_op jit(solution)/shard_map/ppermute | solution.py:176
  75.5 93.9 %collective-permute-start.8 = (f32[128]{0:T(128)S(1)}, f32[128]{0:T(128)S(1)}, u32[]{:S(2)}, u32[]{:S(2)}) collective-permute-start(f32[128]{0:T(128)S(1)} %multiply_subtract_fusion), channel_id=1, source_target_pairs={{0,3},{1,0},{2,1},{3,2},{4,7},{5,4},{6,5},{7,6},{8,11},{9,8},{10,9... | collective-permute-start | bytes 1544 | tf_op jit(solution)/shard_map/ppermute | solution.py:176
